TPU v7x, 256 devices: a whole 4x4x8 slice. The times are simulated.
256 devices in a mesh: blk: 16 (over y, x_lo, core), head: 16 (over x_hi, z).
Axes of the slice: x: 4 (x_hi: 2, x_lo: 2; x = x_hi * 2 + x_lo), y: 4, z: 8, core: 2. Of those that a mesh axis runs over, the one named last changes fastest.
Arguments:
- query: bfloat16 [8192, 8192], P(('blk', 'head')), may hold values from -6 to 6
- key: bfloat16 [8192, 1024], P(('blk', 'head')), may hold values from -6 to 6
- value: bfloat16 [8192, 1024], P(('blk', 'head')), may hold values from -6 to 6
- output: bfloat16 [8192, 8192], P(('blk', 'head')), may hold values from -1.5 to 1.5
- out_grad: bfloat16 [8192, 8192], P(('blk', 'head')), may hold values from -6 to 6
- lse: float32 [8192, 64], P(('blk', 'head')), may hold values from 3.5 to 6
- doc_lengths: int32 [7], replicated, may hold values from 1 to 2048, as said below
- block_keep: int32 [64, 17], P('blk'), may hold values 0 or 1
Outputs:
- query_grad: bfloat16 [8192, 8192], P(('blk', 'head'))
- key_grad: bfloat16 [8192, 1024], P(('blk', 'head'))
- value_grad: bfloat16 [8192, 1024], P(('blk', 'head'))
Inputs may be any that keep to these rules, and one draw needn't show every extreme that they name: `doc_lengths`: whole document lengths that sum to 8192; the sequence is cut into aligned windows of 2048 tokens, each but the last split into two documents, the last one document of exactly 2048.
All inputs are finite; a program needn't handle non-finite values. No bound on the sum of `block_keep` on one device may be relied on, other than what follows from the above.
Results may differ from a plain program's by a relative error of at most 0.015.
Values may be sent and summed in bfloat16 or wider, within the bound.
No kernel may reach another device: no remote copies, remote signals or barrier semaphores. Data moves between devices by JAX's collectives and lax.ppermute only.
A program may use at most 128 MiB of HBM per device.

v0:
```python
import math

import jax
import jax.numpy as jnp
from jax import lax
from jax.sharding import PartitionSpec as P

KVH = 8
HD = 128
DOC_MAX = 2048
BLOCK = 128


def from_behind(value, axis, by):
    length = lax.axis_size(axis)
    pairs = [(i, i + by) for i in range(length) if 0 <= i + by < length]
    return lax.ppermute(value, axis, pairs)


def passed_along(value, axis, by):
    length = lax.axis_size(axis)
    return lax.ppermute(value, axis, [(i, (i + by) % length) for i in range(length)])


def for_sending(value):
    return jax.tree.map(lambda a: a.astype(jnp.bfloat16) if a.dtype == jnp.float32 else a, value)


def doc_index(positions, starts):
    return jnp.sum((positions[:, None] >= starts[None, :]).astype(jnp.int32), axis=1) - 1


def block_table(first_query, first_key, rows, count_query, count_key):
    query_blocks = first_query // BLOCK + jnp.arange(count_query // BLOCK, dtype=jnp.int32)
    key_blocks = first_key // BLOCK + jnp.arange(count_key // BLOCK, dtype=jnp.int32)
    distance = query_blocks[:, None] - key_blocks[None, :]
    offsets = jnp.arange(rows.shape[1], dtype=jnp.int32)
    table = (
        jnp.sum(
            jnp.where(distance[:, :, None] == offsets[None, None, :], rows[:, None, :], 0), axis=2
        )
        > 0
    )
    return jnp.repeat(jnp.repeat(table, BLOCK, axis=0), BLOCK, axis=1)


def piece_grads(q_group, g_group, lse_group, delta_group, keys, values, allowed, scale):
    f32 = jnp.float32
    scores = jnp.einsum("tcgd,scd->cgts", q_group, keys, preferred_element_type=f32) * scale
    probs = jnp.where(allowed[None, None], jnp.exp(scores - lse_group[..., None]), 0.0)
    dprobs = jnp.einsum("tcgd,scd->cgts", g_group, values, preferred_element_type=f32)
    dscores = probs * (dprobs - delta_group[..., None])
    probs_b = probs.astype(jnp.bfloat16)
    dscores_b = dscores.astype(jnp.bfloat16)
    dv_part = jnp.einsum("cgts,tcgd->scd", probs_b, g_group, preferred_element_type=f32)
    dk_part = jnp.einsum("cgts,tcgd->scd", dscores_b, q_group, preferred_element_type=f32)
    dq_part = jnp.einsum("cgts,scd->tcgd", dscores_b, keys, preferred_element_type=f32)
    return (dq_part, dk_part, dv_part)


def shards(query, key, value, output, out_grad, lse, doc_lengths, block_keep):
    f32 = jnp.float32
    heads_axis = lax.axis_size("head")
    repeat = max(1, heads_axis // KVH)
    local_rows = query.shape[0]
    scale = 1.0 / math.sqrt(HD)
    q_range, o_range, g_range = (
        lax.all_to_all(query, "head", split_axis=1, concat_axis=0, tiled=True),
        lax.all_to_all(output, "head", split_axis=1, concat_axis=0, tiled=True),
        lax.all_to_all(out_grad, "head", split_axis=1, concat_axis=0, tiled=True),
    )
    lse_range = lax.all_to_all(lse, "head", split_axis=1, concat_axis=0, tiled=True)
    width = q_range.shape[1] // HD
    delta_range = jnp.sum(
        g_range.reshape(-1, width, HD).astype(f32) * o_range.reshape(-1, width, HD).astype(f32),
        axis=2,
    )
    key_rep = jnp.repeat(key.reshape(local_rows, KVH, HD), repeat, axis=1).reshape(
        local_rows, KVH * repeat * HD
    )
    value_rep = jnp.repeat(value.reshape(local_rows, KVH, HD), repeat, axis=1).reshape(
        local_rows, KVH * repeat * HD
    )
    key_range, value_range = (
        lax.all_to_all(key_rep, "head", split_axis=1, concat_axis=0, tiled=True),
        lax.all_to_all(value_rep, "head", split_axis=1, concat_axis=0, tiled=True),
    )
    range_rows = q_range.shape[0]
    local_heads = q_range.shape[1] // HD
    local_kv = key_range.shape[1] // HD
    group = local_heads // local_kv
    q_group = q_range.reshape(range_rows, local_kv, group, HD)
    g_group = g_range.reshape(range_rows, local_kv, group, HD)
    lse_group = lse_range.reshape(range_rows, local_kv, group).transpose(1, 2, 0)
    delta_group = delta_range.reshape(range_rows, local_kv, group).transpose(1, 2, 0)
    keys_own = key_range.reshape(range_rows, local_kv, HD)
    values_own = value_range.reshape(range_rows, local_kv, HD)
    starts = jnp.cumsum(doc_lengths) - doc_lengths
    position = lax.axis_index("blk")
    first_query = position * range_rows
    q_pos = first_query + jnp.arange(range_rows, dtype=jnp.int32)
    q_doc = doc_index(q_pos, starts)

    def allowed_for(first_key):
        k_pos = first_key + jnp.arange(range_rows, dtype=jnp.int32)
        same = q_doc[:, None] == doc_index(k_pos, starts)[None, :]
        causal = k_pos[None, :] <= q_pos[:, None]
        return (
            same & causal & block_table(first_query, first_key, block_keep, range_rows, range_rows)
        )

    reach = DOC_MAX // range_rows
    half = range_rows // 2
    own_allowed = allowed_for(first_query)
    dq_upper, dk_upper, dv_upper = piece_grads(
        q_group[:half],
        g_group[:half],
        lse_group[..., :half],
        delta_group[..., :half],
        keys_own[:half],
        values_own[:half],
        own_allowed[:half, :half],
        scale,
    )
    dq_lower, dk_lower, dv_lower = piece_grads(
        q_group[half:],
        g_group[half:],
        lse_group[..., half:],
        delta_group[..., half:],
        keys_own,
        values_own,
        own_allowed[half:],
        scale,
    )
    dq_total = jnp.concatenate([dq_upper, dq_lower], axis=0)
    filler = jnp.zeros((range_rows - half,) + dk_upper.shape[1:], f32)
    dk_home = dk_lower + jnp.concatenate([dk_upper, filler], axis=0)
    dv_home = dv_lower + jnp.concatenate([dv_upper, filler], axis=0)
    moving = (keys_own, values_own)
    carried = (dk_home, dv_home)
    for step in range(1, reach + 1):
        moving = from_behind((moving[0], moving[1]), "blk", 1)
        carried = passed_along((carried[0], carried[1]), "blk", 1)
        dq_part, dk_part, dv_part = piece_grads(
            q_group,
            g_group,
            lse_group,
            delta_group,
            moving[0],
            moving[1],
            allowed_for((position - step) * range_rows),
            scale,
        )
        dq_total = dq_total + dq_part
        carried = (carried[0] + dk_part, carried[1] + dv_part)
    dk_final, dv_final = (
        passed_along(carried[0].astype(jnp.bfloat16), "blk", -reach).astype(jnp.float32),
        passed_along(carried[1].astype(jnp.bfloat16), "blk", -reach).astype(jnp.float32),
    )
    dk_rows = (dk_final * scale).reshape(range_rows, local_kv * HD)
    dv_rows = dv_final.reshape(range_rows, local_kv * HD)
    dk_back, dv_back = (
        lax.all_to_all(
            for_sending(dk_rows), "head", split_axis=0, concat_axis=1, tiled=True
        ).astype(dk_rows.dtype),
        lax.all_to_all(
            for_sending(dv_rows), "head", split_axis=0, concat_axis=1, tiled=True
        ).astype(dv_rows.dtype),
    )
    key_grad = jnp.sum(dk_back.reshape(local_rows, KVH, repeat, HD), axis=2).reshape(
        local_rows, KVH * HD
    )
    value_grad = jnp.sum(dv_back.reshape(local_rows, KVH, repeat, HD), axis=2).reshape(
        local_rows, KVH * HD
    )
    dq_rows = (dq_total * scale).astype(jnp.bfloat16).reshape(range_rows, local_heads * HD)
    query_grad = lax.all_to_all(dq_rows, "head", split_axis=0, concat_axis=1, tiled=True)
    return (query_grad, key_grad.astype(jnp.bfloat16), value_grad.astype(jnp.bfloat16))


def solution(mesh):
    in_specs = (
        P(("blk", "head"), None),
        P(("blk", "head"), None),
        P(("blk", "head"), None),
        P(("blk", "head"), None),
        P(("blk", "head"), None),
        P(("blk", "head"), None),
        P(),
        P("blk", None),
    )
    out_specs = (P(("blk", "head"), None), P(("blk", "head"), None), P(("blk", "head"), None))
    return jax.shard_map(shards, mesh=mesh, in_specs=in_specs, out_specs=out_specs, check_vma=False)
```

profile of v0, /device:TPU:8, one launch (start us, length us, event | category | flops | bytes accessed | tf_op | source)
XLA Modules:
  0.0 239.5 jit_solution(15776605030406222535)
XLA Ops:
  2.2 11.0 %all-to-all-start.2 = ((f32[16,1,128]{2,1,0:T(1,128)}), f32[16,1,128]{2,1,0:T(1,128)S(1)}, u32[]{:S(2)}, u32[]{:S(2)}) async-start(f32[16,1,128]{2,1,0:T(1,128)} %reshape.904), calls=%async_computation.2 | async-start | bytes 16384 | tf_op jit(solution)/shard_map/all_to_all | solution.py:72
  14.7 8.4 %all-to-all-done.2 = f32[16,1,128]{2,1,0:T(1,128)S(1)} async-done(((f32[16,1,128]{2,1,0:T(1,128)}), f32[16,1,128]{2,1,0:T(1,128)S(1)}, u32[]{:S(2)}, u32[]{:S(2)}) %all-to-all-start.2) | async-done | bytes 8224 | tf_op jit(solution)/shard_map/all_to_all | solution.py:72
  23.8 3.5 %all-to-all-start = ((bf16[32,16,128]{2,0,1:T(8,128)(2,1)}), bf16[32,16,128]{2,0,1:T(8,128)(2,1)S(1)}, u32[]{:S(2)}, u32[]{:S(2)}) async-start(bf16[32,16,128]{2,0,1:T(8,128)(2,1)} %bitcast.3), calls=%async_computation | async-start | bytes 262144 | tf_op jit(solution)/shard_map/all_to_all | solution.py:85
  28.2 9.3 %all-to-all-done = bf16[32,16,128]{2,0,1:T(8,128)(2,1)S(1)} async-done(((bf16[32,16,128]{2,0,1:T(8,128)(2,1)}), bf16[32,16,128]{2,0,1:T(8,128)(2,1)S(1)}, u32[]{:S(2)}, u32[]{:S(2)}) %all-to-all-start) | async-done | bytes 131104 | tf_op jit(solution)/shard_map/all_to_all | solution.py:85
  38.2 3.5 %all-to-all-start.3 = ((bf16[32,16,128]{2,0,1:T(8,128)(2,1)}), bf16[32,16,128]{2,0,1:T(8,128)(2,1)S(1)}, u32[]{:S(2)}, u32[]{:S(2)}) async-start(bf16[32,16,128]{2,0,1:T(8,128)(2,1)} %bitcast.14), calls=%async_computation.3 | async-start | bytes 262144 | tf_op jit(solution)/shard_map/all_to_all | solution.py:86
  48.8 3.0 %all-to-all-done.3 = bf16[32,16,128]{2,0,1:T(8,128)(2,1)S(1)} async-done(((bf16[32,16,128]{2,0,1:T(8,128)(2,1)}), bf16[32,16,128]{2,0,1:T(8,128)(2,1)S(1)}, u32[]{:S(2)}, u32[]{:S(2)}) %all-to-all-start.3) | async-done | bytes 131104 | tf_op jit(solution)/shard_map/all_to_all | solution.py:86
  51.7 6.6 %all-to-all-start.1 = ((bf16[32,16,512]{2,0,1:T(8,128)(2,1)}), bf16[32,16,512]{2,0,1:T(8,128)(2,1)S(1)}, u32[]{:S(2)}, u32[]{:S(2)}) async-start(bf16[32,16,512]{2,0,1:T(8,128)(2,1)} %bitcast.565), calls=%async_computation.1 | async-start | bytes 1048576 | tf_op jit(solution)/shard_map/all_to_all | solution.py:68
  58.6 14.0 %all-to-all-done.1 = bf16[32,16,512]{2,0,1:T(8,128)(2,1)S(1)} async-done(((bf16[32,16,512]{2,0,1:T(8,128)(2,1)}), bf16[32,16,512]{2,0,1:T(8,128)(2,1)S(1)}, u32[]{:S(2)}, u32[]{:S(2)}) %all-to-all-start.1) | async-done | bytes 524320 | tf_op jit(solution)/shard_map/all_to_all | solution.py:68
  72.6 4.6 %all-to-all-start.4 = ((bf16[32,16,512]{2,0,1:T(8,128)(2,1)}), bf16[32,16,512]{2,0,1:T(8,128)(2,1)S(1)}, u32[]{:S(2)}, u32[]{:S(2)}) async-start(bf16[32,16,512]{2,0,1:T(8,128)(2,1)} %bitcast.564), calls=%async_computation.4 | async-start | bytes 1048576 | tf_op jit(solution)/shard_map/all_to_all | solution.py:70
  82.0 8.8 %all-to-all-done.4 = bf16[32,16,512]{2,0,1:T(8,128)(2,1)S(1)} async-done(((bf16[32,16,512]{2,0,1:T(8,128)(2,1)}), bf16[32,16,512]{2,0,1:T(8,128)(2,1)S(1)}, u32[]{:S(2)}, u32[]{:S(2)}) %all-to-all-start.4) | async-done | bytes 524320 | tf_op jit(solution)/shard_map/all_to_all | solution.py:70
  90.8 4.6 %all-to-all-start.5 = ((bf16[32,16,512]{2,0,1:T(8,128)(2,1)}), bf16[32,16,512]{2,0,1:T(8,128)(2,1)}, u32[]{:S(2)}, u32[]{:S(2)}) async-start(bf16[32,16,512]{2,0,1:T(8,128)(2,1)} %bitcast.563), calls=%async_computation.5 | async-start | bytes 1048576 | tf_op jit(solution)/shard_map/all_to_all | solution.py:69
  105.2 2.9 %collective-permute-done.3 = bf16[512,1,128]{2,0,1:T(8,128)(2,1)S(1)} collective-permute-done((bf16[512,1,128]{2,0,1:T(8,128)(2,1)S(1)}, bf16[512,1,128]{2,0,1:T(8,128)(2,1)S(1)}, u32[]{:S(2)}, u32[]{:S(2)}) %collective-permute-start.3) | collective-permute-done | bytes 131104 | tf_op jit(solution)/shard_map/ppermute | solution.py:17
  117.3 3.0 %collective-permute-start.6 = (bf16[512,1,128]{2,0,1:T(8,128)(2,1)}, bf16[512,1,128]{2,0,1:T(8,128)(2,1)}, u32[]{:S(2)}, u32[]{:S(2)}) collective-permute-start(bf16[512,1,128]{2,0,1:T(8,128)(2,1)} %collective-permute-done.4), channel_id=1, source_target_pairs={{0,16},{16,32},{32,48},{48,64},{64,80},{80,96},{96,112},{112,128},... | collective-permute-start | bytes 393224 | tf_op jit(solution)/shard_map/ppermute | solution.py:17
  141.8 2.7 %fusion.5 = bf16[1,4,512,512]{2,3,1,0:T(8,128)(2,1)S(1)} fusion(f32[512,512,4]{1,0,2:T(8,128)S(1)} %fusion.145, f32[4,512]{1,0:T(4,128)S(1)} %copy.201, f32[4,512]{1,0:T(4,128)S(1)} %bitcast.596, pred[512,512]{0,1:T(8,128)(4,1)S(1)} %copy-done.24, bf16[512,1,128]{2,0,1:T(8,128)(2,1)} %collective-permute-done.5, bf16[512,4,128]{2,1,0:T(4,128)(2,1)S(1)} %reshape.842), kind=kOutput, calls=%fused_computation.8 | convolution fusion | flops 274726912 | bytes 7225344 | tf_op jit(solution)/shard_map/tcgd,scd->cgts/dot_general | solution.py:51
  152.5 2.7 %fusion.1 = bf16[1,4,512,512]{2,3,1,0:T(8,128)(2,1)S(1)} fusion(f32[512,512,4]{1,0,2:T(8,128)S(1)} %fusion.141, f32[4,512]{1,0:T(4,128)S(1)} %copy.201, f32[4,512]{1,0:T(4,128)S(1)} %bitcast.598, pred[512,512]{0,1:T(8,128)(4,1)S(1)} %copy-done.20, bf16[512,1,128]{2,0,1:T(8,128)(2,1)} %collective-permute-done.7, bf16[512,4,128]{2,1,0:T(4,128)(2,1)S(1)} %reshape.842), kind=kOutput, calls=%fused_computation.2 | convolution fusion | flops 274726912 | bytes 7225344 | tf_op jit(solution)/shard_map/tcgd,scd->cgts/dot_general | solution.py:51
  160.3 9.3 %all-to-all-start.6 = ((bf16[16,32,512]{2,1,0:T(8,128)(2,1)}), bf16[16,32,512]{2,1,0:T(8,128)(2,1)}, u32[]{:S(2)}, u32[]{:S(2)}) async-start(bf16[16,32,512]{2,1,0:T(8,128)(2,1)} %all_to_all.117), calls=%async_computation.6 | async-start | bytes 1048576 | tf_op jit(solution)/shard_map/all_to_all | solution.py:177
  176.3 6.2 %collective-permute-done.9 = f32[512,1,128]{2,0,1:T(8,128)S(1)} collective-permute-done((f32[512,1,128]{2,0,1:T(8,128)S(1)}, f32[512,1,128]{2,0,1:T(8,128)S(1)}, u32[]{:S(2)}, u32[]{:S(2)}) %collective-permute-start.9) | collective-permute-done | bytes 262176 | tf_op jit(solution)/shard_map/ppermute | solution.py:22
  185.8 3.5 %collective-permute-done.10 = f32[512,1,128]{2,0,1:T(8,128)S(1)} collective-permute-done((f32[512,1,128]{2,0,1:T(8,128)S(1)}, f32[512,1,128]{2,0,1:T(8,128)S(1)}, u32[]{:S(2)}, u32[]{:S(2)}) %collective-permute-start.10) | collective-permute-done | bytes 262176 | tf_op jit(solution)/shard_map/ppermute | solution.py:22
  192.6 3.5 %collective-permute-done.11 = f32[512,1,128]{2,0,1:T(8,128)S(1)} collective-permute-done((f32[512,1,128]{2,0,1:T(8,128)S(1)}, f32[512,1,128]{2,0,1:T(8,128)S(1)}, u32[]{:S(2)}, u32[]{:S(2)}) %collective-permute-start.11) | collective-permute-done | bytes 262176 | tf_op jit(solution)/shard_map/ppermute | solution.py:22
  196.2 4.4 %collective-permute-start.12 = (bf16[512,1,128]{2,0,1:T(8,128)(2,1)S(1)}, bf16[512,1,128]{2,0,1:T(8,128)(2,1)S(1)}, u32[]{:S(2)}, u32[]{:S(2)}) collective-permute-start(bf16[512,1,128]{2,0,1:T(8,128)(2,1)S(1)} %add_convert_fusion.1), channel_id=1, source_target_pairs={{0,192},{16,208},{32,224},{48,240},{64,0},{80,16},{96,32},{112,48}... | collective-permute-start | bytes 393224 | tf_op jit(solution)/shard_map/ppermute | solution.py:22
  203.8 10.1 %all-to-all-start.7 = ((bf16[16,32,128]{2,1,0:T(8,128)(2,1)}), bf16[16,32,128]{2,1,0:T(8,128)(2,1)S(1)}, u32[]{:S(2)}, u32[]{:S(2)}) async-start(bf16[16,32,128]{2,1,0:T(8,128)(2,1)} %bitcast.125), calls=%async_computation.7 | async-start | bytes 262144 | tf_op jit(solution)/shard_map/all_to_all | solution.py:163
  219.1 4.9 %all-to-all-done.7 = bf16[16,32,128]{2,1,0:T(8,128)(2,1)S(1)} async-done(((bf16[16,32,128]{2,1,0:T(8,128)(2,1)}), bf16[16,32,128]{2,1,0:T(8,128)(2,1)S(1)}, u32[]{:S(2)}, u32[]{:S(2)}) %all-to-all-start.7) | async-done | bytes 131104 | tf_op jit(solution)/shard_map/all_to_all | solution.py:163
  224.0 4.7 %all-to-all-start.8 = ((bf16[16,32,128]{2,1,0:T(8,128)(2,1)}), bf16[16,32,128]{2,1,0:T(8,128)(2,1)S(1)}, u32[]{:S(2)}, u32[]{:S(2)}) async-start(bf16[16,32,128]{2,1,0:T(8,128)(2,1)} %bitcast.158), calls=%async_computation.8 | async-start | bytes 262144 | tf_op jit(solution)/shard_map/all_to_all | solution.py:166
  229.4 9.4 %all-to-all-done.8 = bf16[16,32,128]{2,1,0:T(8,128)(2,1)S(1)} async-done(((bf16[16,32,128]{2,1,0:T(8,128)(2,1)}), bf16[16,32,128]{2,1,0:T(8,128)(2,1)S(1)}, u32[]{:S(2)}, u32[]{:S(2)}) %all-to-all-start.8) | async-done | bytes 131104 | tf_op jit(solution)/shard_map/all_to_all | solution.py:166
  (214 shorter events, 92.9 us)
Async XLA Ops:
  2.2 20.9 %all-to-all-start.2 = ((f32[16,1,128]{2,1,0:T(1,128)}), f32[16,1,128]{2,1,0:T(1,128)S(1)}, u32[]{:S(2)}, u32[]{:S(2)}) async-start(f32[16,1,128]{2,1,0:T(1,128)} %reshape.904), calls=%async_computation.2 | async-start | bytes 16384 | tf_op jit(solution)/shard_map/all_to_all | solution.py:72
  23.8 13.7 %all-to-all-start = ((bf16[32,16,128]{2,0,1:T(8,128)(2,1)}), bf16[32,16,128]{2,0,1:T(8,128)(2,1)S(1)}, u32[]{:S(2)}, u32[]{:S(2)}) async-start(bf16[32,16,128]{2,0,1:T(8,128)(2,1)} %bitcast.3), calls=%async_computation | async-start | bytes 262144 | tf_op jit(solution)/shard_map/all_to_all | solution.py:85
  38.2 13.5 %all-to-all-start.3 = ((bf16[32,16,128]{2,0,1:T(8,128)(2,1)}), bf16[32,16,128]{2,0,1:T(8,128)(2,1)S(1)}, u32[]{:S(2)}, u32[]{:S(2)}) async-start(bf16[32,16,128]{2,0,1:T(8,128)(2,1)} %bitcast.14), calls=%async_computation.3 | async-start | bytes 262144 | tf_op jit(solution)/shard_map/all_to_all | solution.py:86
  51.7 20.9 %all-to-all-start.1 = ((bf16[32,16,512]{2,0,1:T(8,128)(2,1)}), bf16[32,16,512]{2,0,1:T(8,128)(2,1)S(1)}, u32[]{:S(2)}, u32[]{:S(2)}) async-start(bf16[32,16,512]{2,0,1:T(8,128)(2,1)} %bitcast.565), calls=%async_computation.1 | async-start | bytes 1048576 | tf_op jit(solution)/shard_map/all_to_all | solution.py:68
  72.6 18.2 %all-to-all-start.4 = ((bf16[32,16,512]{2,0,1:T(8,128)(2,1)}), bf16[32,16,512]{2,0,1:T(8,128)(2,1)S(1)}, u32[]{:S(2)}, u32[]{:S(2)}) async-start(bf16[32,16,512]{2,0,1:T(8,128)(2,1)} %bitcast.564), calls=%async_computation.4 | async-start | bytes 1048576 | tf_op jit(solution)/shard_map/all_to_all | solution.py:70
  77.4 23.1 %collective-permute-start.1 = (bf16[512,1,128]{2,0,1:T(8,128)(2,1)S(1)}, bf16[512,1,128]{2,0,1:T(8,128)(2,1)S(1)}, u32[]{:S(2)}, u32[]{:S(2)}) collective-permute-start(bf16[512,1,128]{2,0,1:T(8,128)(2,1)S(1)} %bitcast.577), channel_id=1, source_target_pairs={{0,16},{16,32},{32,48},{48,64},{64,80},{80,96},{96,112},{112,128},... | collective-permute-start | bytes 393224 | tf_op jit(solution)/shard_map/ppermute | solution.py:17
  79.4 23.1 %collective-permute-start = (bf16[512,1,128]{2,0,1:T(8,128)(2,1)S(1)}, bf16[512,1,128]{2,0,1:T(8,128)(2,1)S(1)}, u32[]{:S(2)}, u32[]{:S(2)}) collective-permute-start(bf16[512,1,128]{2,0,1:T(8,128)(2,1)S(1)} %bitcast.580), channel_id=1, source_target_pairs={{0,16},{16,32},{32,48},{48,64},{64,80},{80,96},{96,112},{112,128},... | collective-permute-start | bytes 393224 | tf_op jit(solution)/shard_map/ppermute | solution.py:17
  90.8 31.5 %all-to-all-start.5 = ((bf16[32,16,512]{2,0,1:T(8,128)(2,1)}), bf16[32,16,512]{2,0,1:T(8,128)(2,1)}, u32[]{:S(2)}, u32[]{:S(2)}) async-start(bf16[32,16,512]{2,0,1:T(8,128)(2,1)} %bitcast.563), calls=%async_computation.5 | async-start | bytes 1048576 | tf_op jit(solution)/shard_map/all_to_all | solution.py:69
  100.6 7.5 %collective-permute-start.3 = (bf16[512,1,128]{2,0,1:T(8,128)(2,1)S(1)}, bf16[512,1,128]{2,0,1:T(8,128)(2,1)S(1)}, u32[]{:S(2)}, u32[]{:S(2)}) collective-permute-start(bf16[512,1,128]{2,0,1:T(8,128)(2,1)S(1)} %collective-permute-done.1), channel_id=1, source_target_pairs={{0,16},{16,32},{32,48},{48,64},{64,80},{80,96},{96,112},{112,128},... | collective-permute-start | bytes 393224 | tf_op jit(solution)/shard_map/ppermute | solution.py:17
  102.5 7.5 %collective-permute-start.2 = (bf16[512,1,128]{2,0,1:T(8,128)(2,1)S(1)}, bf16[512,1,128]{2,0,1:T(8,128)(2,1)S(1)}, u32[]{:S(2)}, u32[]{:S(2)}) collective-permute-start(bf16[512,1,128]{2,0,1:T(8,128)(2,1)S(1)} %collective-permute-done), channel_id=1, source_target_pairs={{0,16},{16,32},{32,48},{48,64},{64,80},{80,96},{96,112},{112,128},... | collective-permute-start | bytes 393224 | tf_op jit(solution)/shard_map/ppermute | solution.py:17
  108.1 7.3 %collective-permute-start.5 = (bf16[512,1,128]{2,0,1:T(8,128)(2,1)S(1)}, bf16[512,1,128]{2,0,1:T(8,128)(2,1)}, u32[]{:S(2)}, u32[]{:S(2)}) collective-permute-start(bf16[512,1,128]{2,0,1:T(8,128)(2,1)S(1)} %collective-permute-done.3), channel_id=1, source_target_pairs={{0,16},{16,32},{32,48},{48,64},{64,80},{80,96},{96,112},{112,128},... | collective-permute-start | bytes 393224 | tf_op jit(solution)/shard_map/ppermute | solution.py:17
  110.1 7.3 %collective-permute-start.4 = (bf16[512,1,128]{2,0,1:T(8,128)(2,1)S(1)}, bf16[512,1,128]{2,0,1:T(8,128)(2,1)}, u32[]{:S(2)}, u32[]{:S(2)}) collective-permute-start(bf16[512,1,128]{2,0,1:T(8,128)(2,1)S(1)} %collective-permute-done.2), channel_id=1, source_target_pairs={{0,16},{16,32},{32,48},{48,64},{64,80},{80,96},{96,112},{112,128},... | collective-permute-start | bytes 393224 | tf_op jit(solution)/shard_map/ppermute | solution.py:17
  115.4 37.1 %collective-permute-start.7 = (bf16[512,1,128]{2,0,1:T(8,128)(2,1)}, bf16[512,1,128]{2,0,1:T(8,128)(2,1)}, u32[]{:S(2)}, u32[]{:S(2)}) collective-permute-start(bf16[512,1,128]{2,0,1:T(8,128)(2,1)} %collective-permute-done.5), channel_id=1, source_target_pairs={{0,16},{16,32},{32,48},{48,64},{64,80},{80,96},{96,112},{112,128},... | collective-permute-start | bytes 393224 | tf_op jit(solution)/shard_map/ppermute | solution.py:17
  117.3 28.4 %collective-permute-start.6 = (bf16[512,1,128]{2,0,1:T(8,128)(2,1)}, bf16[512,1,128]{2,0,1:T(8,128)(2,1)}, u32[]{:S(2)}, u32[]{:S(2)}) collective-permute-start(bf16[512,1,128]{2,0,1:T(8,128)(2,1)} %collective-permute-done.4), channel_id=1, source_target_pairs={{0,16},{16,32},{32,48},{48,64},{64,80},{80,96},{96,112},{112,128},... | collective-permute-start | bytes 393224 | tf_op jit(solution)/shard_map/ppermute | solution.py:17
  133.0 39.0 %collective-permute-start.8 = (f32[512,1,128]{2,0,1:T(8,128)}, f32[512,1,128]{2,0,1:T(8,128)}, u32[]{:S(2)}, u32[]{:S(2)}) collective-permute-start(f32[512,1,128]{2,0,1:T(8,128)} %fusion.122), channel_id=1, source_target_pairs={{0,16},{16,32},{32,48},{48,64},{64,80},{80,96},{96,112},{112,128},... | collective-permute-start | bytes 786440 | tf_op jit(solution)/shard_map/ppermute | solution.py:22
  133.0 40.8 %collective-permute-start.13 = (f32[512,1,128]{2,0,1:T(8,128)}, f32[512,1,128]{2,0,1:T(8,128)}, u32[]{:S(2)}, u32[]{:S(2)}) collective-permute-start(f32[512,1,128]{2,0,1:T(8,128)} %fusion.123), channel_id=1, source_target_pairs={{0,16},{16,32},{32,48},{48,64},{64,80},{80,96},{96,112},{112,128},... | collective-permute-start | bytes 786440 | tf_op jit(solution)/shard_map/ppermute | solution.py:22
  160.3 43.5 %all-to-all-start.6 = ((bf16[16,32,512]{2,1,0:T(8,128)(2,1)}), bf16[16,32,512]{2,1,0:T(8,128)(2,1)}, u32[]{:S(2)}, u32[]{:S(2)}) async-start(bf16[16,32,512]{2,1,0:T(8,128)(2,1)} %all_to_all.117), calls=%async_computation.6 | async-start | bytes 1048576 | tf_op jit(solution)/shard_map/all_to_all | solution.py:177
  173.8 8.8 %collective-permute-start.9 = (f32[512,1,128]{2,0,1:T(8,128)S(1)}, f32[512,1,128]{2,0,1:T(8,128)S(1)}, u32[]{:S(2)}, u32[]{:S(2)}) collective-permute-start(f32[512,1,128]{2,0,1:T(8,128)S(1)} %fusion.110), channel_id=1, source_target_pairs={{0,16},{16,32},{32,48},{48,64},{64,80},{80,96},{96,112},{112,128},... | collective-permute-start | bytes 786440 | tf_op jit(solution)/shard_map/ppermute | solution.py:22
  176.1 9.6 %collective-permute-start.14 = (f32[512,1,128]{2,0,1:T(8,128)S(1)}, f32[512,1,128]{2,0,1:T(8,128)S(1)}, u32[]{:S(2)}, u32[]{:S(2)}) collective-permute-start(f32[512,1,128]{2,0,1:T(8,128)S(1)} %fusion.124), channel_id=1, source_target_pairs={{0,16},{16,32},{32,48},{48,64},{64,80},{80,96},{96,112},{112,128},... | collective-permute-start | bytes 786440 | tf_op jit(solution)/shard_map/ppermute | solution.py:22
  182.6 6.8 %collective-permute-start.10 = (f32[512,1,128]{2,0,1:T(8,128)S(1)}, f32[512,1,128]{2,0,1:T(8,128)S(1)}, u32[]{:S(2)}, u32[]{:S(2)}) collective-permute-start(f32[512,1,128]{2,0,1:T(8,128)S(1)} %add.246), channel_id=1, source_target_pairs={{0,16},{16,32},{32,48},{48,64},{64,80},{80,96},{96,112},{112,128},... | collective-permute-start | bytes 786440 | tf_op jit(solution)/shard_map/ppermute | solution.py:22
  192.5 21.4 %collective-permute-start.16 = (f32[512,1,128]{2,0,1:T(8,128)S(1)}, f32[512,1,128]{2,0,1:T(8,128)S(1)}, u32[]{:S(2)}, u32[]{:S(2)}) collective-permute-start(f32[512,1,128]{2,0,1:T(8,128)S(1)} %add.252), channel_id=1, source_target_pairs={{0,16},{16,32},{32,48},{48,64},{64,80},{80,96},{96,112},{112,128},... | collective-permute-start | bytes 786440 | tf_op jit(solution)/shard_map/ppermute | solution.py:22
  196.2 6.9 %collective-permute-start.12 = (bf16[512,1,128]{2,0,1:T(8,128)(2,1)S(1)}, bf16[512,1,128]{2,0,1:T(8,128)(2,1)S(1)}, u32[]{:S(2)}, u32[]{:S(2)}) collective-permute-start(bf16[512,1,128]{2,0,1:T(8,128)(2,1)S(1)} %add_convert_fusion.1), channel_id=1, source_target_pairs={{0,192},{16,208},{32,224},{48,240},{64,0},{80,16},{96,32},{112,48}... | collective-permute-start | bytes 393224 | tf_op jit(solution)/shard_map/ppermute | solution.py:22
  203.8 20.2 %all-to-all-start.7 = ((bf16[16,32,128]{2,1,0:T(8,128)(2,1)}), bf16[16,32,128]{2,1,0:T(8,128)(2,1)S(1)}, u32[]{:S(2)}, u32[]{:S(2)}) async-start(bf16[16,32,128]{2,1,0:T(8,128)(2,1)} %bitcast.125), calls=%async_computation.7 | async-start | bytes 262144 | tf_op jit(solution)/shard_map/all_to_all | solution.py:163
  224.0 14.8 %all-to-all-start.8 = ((bf16[16,32,128]{2,1,0:T(8,128)(2,1)}), bf16[16,32,128]{2,1,0:T(8,128)(2,1)S(1)}, u32[]{:S(2)}, u32[]{:S(2)}) async-start(bf16[16,32,128]{2,1,0:T(8,128)(2,1)} %bitcast.158), calls=%async_computation.8 | async-start | bytes 262144 | tf_op jit(solution)/shard_map/all_to_all | solution.py:166
  (37 other events, 440.5 us)
where the time goes:
time: 243 us; the launch traced here: 239 us
  starting transfers between devices  85.5 us (35%)
  waiting for transfers between devices  83 us (34%)
  matrix products  36.1 us (15%)
  local copies, waits for them, and re-layouts  24.8 us (10%)
  other arithmetic  8.06 us (3%)
    ppermute x10, waiting for transfers between devices, passed_along(): lax.ppermute(value, axis, [(i, (i + by) % length) for i in range(length)])  20.2 us
    ppermute x8, starting transfers between devices, from_behind(): return lax.ppermute(value, axis, pairs)  17.7 us
    all_to_all x1, waiting for transfers between devices, shards(): lax.all_to_all(query, 'head', split_axis=1, concat_axis=0, tiled=True)  14 us
    all_to_all x1, starting transfers between devices, shards(): lax.all_to_all(lse, 'head', split_axis=1, concat_axis=0, tiled=True)  11 us
    all_to_all x1, starting transfers between devices, shards(): lax.all_to_all(for_sending(dk_rows), 'head', split_axis=0, concat_axis=1,...  10.1 us
    ppermute x10, starting transfers between devices, passed_along(): lax.ppermute(value, axis, [(i, (i + by) % length) for i in range(length)])  9.8 us
    all_to_all x1, waiting for transfers between devices, shards(): lax.all_to_all(for_sending(dv_rows), 'head', split_axis=0, concat_axis=1,...  9.42 us
    dot_general x6, matrix products, piece_grads(): jnp.einsum('tcgd,scd->cgts', g_group, values, preferred_element_type=f32)  9.35 us
  transfers between devices with their start and end apart: 27, of which 16 were waited for; matrix products, arithmetic and copies ran while one was open for 26% of the time, Pallas kernels for 0%

commit v1 on v0

--- a/solution.py
+++ b/solution.py
@@ -95,7 +95,10 @@
     delta_group = delta_range.reshape(range_rows, local_kv, group).transpose(1, 2, 0)
     keys_own = key_range.reshape(range_rows, local_kv, HD)
     values_own = value_range.reshape(range_rows, local_kv, HD)
-    starts = jnp.cumsum(doc_lengths) - doc_lengths
+    documents = jnp.arange(doc_lengths.shape[0], dtype=jnp.int32)
+    starts = jnp.sum(
+        jnp.where(documents[None, :] < documents[:, None], doc_lengths[None, :], 0), axis=1
+    )
     position = lax.axis_index("blk")
     first_query = position * range_rows
     q_pos = first_query + jnp.arange(range_rows, dtype=jnp.int32)

time: 243 us -> 242 us (level)
  no operation moved by 1% of the time
where the time goes in v1:
time: 242 us; the launch traced here: 239 us
  starting transfers between devices  84.7 us (35%)
  waiting for transfers between devices  83.7 us (35%)
  matrix products  36.1 us (15%)
  local copies, waits for them, and re-layouts  24.8 us (10%)
  other arithmetic  7.34 us (3%)
    ppermute x10, waiting for transfers between devices, passed_along(): lax.ppermute(value, axis, [(i, (i + by) % length) for i in range(length)])  20.2 us
    ppermute x8, starting transfers between devices, from_behind(): return lax.ppermute(value, axis, pairs)  17.7 us
    all_to_all x1, waiting for transfers between devices, shards(): lax.all_to_all(query, 'head', split_axis=1, concat_axis=0, tiled=True)  13.9 us
    all_to_all x1, starting transfers between devices, shards(): lax.all_to_all(lse, 'head', split_axis=1, concat_axis=0, tiled=True)  11 us
    all_to_all x1, starting transfers between devices, shards(): lax.all_to_all(for_sending(dk_rows), 'head', split_axis=0, concat_axis=1,...  10.1 us
    ppermute x10, starting transfers between devices, passed_along(): lax.ppermute(value, axis, [(i, (i + by) % length) for i in range(length)])  9.8 us
    all_to_all x1, waiting for transfers between devices, shards(): lax.all_to_all(for_sending(dv_rows), 'head', split_axis=0, concat_axis=1,...  9.42 us
    dot_general x6, matrix products, piece_grads(): jnp.einsum('tcgd,scd->cgts', g_group, values, preferred_element_type=f32)  9.36 us
  transfers between devices with their start and end apart: 27, of which 16 were waited for; matrix products, arithmetic and copies ran while one was open for 26% of the time, Pallas kernels for 0%

profile of v1, /device:TPU:8, one launch (start us, length us, event | category | flops | bytes accessed | tf_op | source)
XLA Modules:
  0.0 238.6 jit_solution(12676364072740974371)
XLA Ops:
  2.2 11.0 %all-to-all-start.2 = ((f32[16,1,128]{2,1,0:T(1,128)}), f32[16,1,128]{2,1,0:T(1,128)S(1)}, u32[]{:S(2)}, u32[]{:S(2)}) async-start(f32[16,1,128]{2,1,0:T(1,128)} %reshape.877), calls=%async_computation.2 | async-start | bytes 16384 | tf_op jit(solution)/shard_map/all_to_all | solution.py:72
  14.7 8.4 %all-to-all-done.2 = f32[16,1,128]{2,1,0:T(1,128)S(1)} async-done(((f32[16,1,128]{2,1,0:T(1,128)}), f32[16,1,128]{2,1,0:T(1,128)S(1)}, u32[]{:S(2)}, u32[]{:S(2)}) %all-to-all-start.2) | async-done | bytes 8224 | tf_op jit(solution)/shard_map/all_to_all | solution.py:72
  23.8 3.5 %all-to-all-start = ((bf16[32,16,128]{2,0,1:T(8,128)(2,1)}), bf16[32,16,128]{2,0,1:T(8,128)(2,1)S(1)}, u32[]{:S(2)}, u32[]{:S(2)}) async-start(bf16[32,16,128]{2,0,1:T(8,128)(2,1)} %bitcast.1), calls=%async_computation | async-start | bytes 262144 | tf_op jit(solution)/shard_map/all_to_all | solution.py:85
  28.2 9.3 %all-to-all-done = bf16[32,16,128]{2,0,1:T(8,128)(2,1)S(1)} async-done(((bf16[32,16,128]{2,0,1:T(8,128)(2,1)}), bf16[32,16,128]{2,0,1:T(8,128)(2,1)S(1)}, u32[]{:S(2)}, u32[]{:S(2)}) %all-to-all-start) | async-done | bytes 131104 | tf_op jit(solution)/shard_map/all_to_all | solution.py:85
  38.2 3.5 %all-to-all-start.3 = ((bf16[32,16,128]{2,0,1:T(8,128)(2,1)}), bf16[32,16,128]{2,0,1:T(8,128)(2,1)S(1)}, u32[]{:S(2)}, u32[]{:S(2)}) async-start(bf16[32,16,128]{2,0,1:T(8,128)(2,1)} %bitcast.12), calls=%async_computation.3 | async-start | bytes 262144 | tf_op jit(solution)/shard_map/all_to_all | solution.py:86
  48.0 3.8 %all-to-all-done.3 = bf16[32,16,128]{2,0,1:T(8,128)(2,1)S(1)} async-done(((bf16[32,16,128]{2,0,1:T(8,128)(2,1)}), bf16[32,16,128]{2,0,1:T(8,128)(2,1)S(1)}, u32[]{:S(2)}, u32[]{:S(2)}) %all-to-all-start.3) | async-done | bytes 131104 | tf_op jit(solution)/shard_map/all_to_all | solution.py:86
  51.7 5.8 %all-to-all-start.1 = ((bf16[32,16,512]{2,0,1:T(8,128)(2,1)}), bf16[32,16,512]{2,0,1:T(8,128)(2,1)S(1)}, u32[]{:S(2)}, u32[]{:S(2)}) async-start(bf16[32,16,512]{2,0,1:T(8,128)(2,1)} %bitcast.562), calls=%async_computation.1 | async-start | bytes 1048576 | tf_op jit(solution)/shard_map/all_to_all | solution.py:68
  57.9 13.9 %all-to-all-done.1 = bf16[32,16,512]{2,0,1:T(8,128)(2,1)S(1)} async-done(((bf16[32,16,512]{2,0,1:T(8,128)(2,1)}), bf16[32,16,512]{2,0,1:T(8,128)(2,1)S(1)}, u32[]{:S(2)}, u32[]{:S(2)}) %all-to-all-start.1) | async-done | bytes 524320 | tf_op jit(solution)/shard_map/all_to_all | solution.py:68
  71.8 4.6 %all-to-all-start.4 = ((bf16[32,16,512]{2,0,1:T(8,128)(2,1)}), bf16[32,16,512]{2,0,1:T(8,128)(2,1)S(1)}, u32[]{:S(2)}, u32[]{:S(2)}) async-start(bf16[32,16,512]{2,0,1:T(8,128)(2,1)} %bitcast.561), calls=%async_computation.4 | async-start | bytes 1048576 | tf_op jit(solution)/shard_map/all_to_all | solution.py:70
  81.1 8.8 %all-to-all-done.4 = bf16[32,16,512]{2,0,1:T(8,128)(2,1)S(1)} async-done(((bf16[32,16,512]{2,0,1:T(8,128)(2,1)}), bf16[32,16,512]{2,0,1:T(8,128)(2,1)S(1)}, u32[]{:S(2)}, u32[]{:S(2)}) %all-to-all-start.4) | async-done | bytes 524320 | tf_op jit(solution)/shard_map/all_to_all | solution.py:70
  90.0 4.6 %all-to-all-start.5 = ((bf16[32,16,512]{2,0,1:T(8,128)(2,1)}), bf16[32,16,512]{2,0,1:T(8,128)(2,1)}, u32[]{:S(2)}, u32[]{:S(2)}) async-start(bf16[32,16,512]{2,0,1:T(8,128)(2,1)} %bitcast.560), calls=%async_computation.5 | async-start | bytes 1048576 | tf_op jit(solution)/shard_map/all_to_all | solution.py:69
  104.4 2.9 %collective-permute-done.3 = bf16[512,1,128]{2,0,1:T(8,128)(2,1)S(1)} collective-permute-done((bf16[512,1,128]{2,0,1:T(8,128)(2,1)S(1)}, bf16[512,1,128]{2,0,1:T(8,128)(2,1)S(1)}, u32[]{:S(2)}, u32[]{:S(2)}) %collective-permute-start.3) | collective-permute-done | bytes 131104 | tf_op jit(solution)/shard_map/ppermute | solution.py:17
  116.5 3.0 %collective-permute-start.6 = (bf16[512,1,128]{2,0,1:T(8,128)(2,1)}, bf16[512,1,128]{2,0,1:T(8,128)(2,1)}, u32[]{:S(2)}, u32[]{:S(2)}) collective-permute-start(bf16[512,1,128]{2,0,1:T(8,128)(2,1)} %collective-permute-done.4), channel_id=1, source_target_pairs={{0,16},{16,32},{32,48},{48,64},{64,80},{80,96},{96,112},{112,128},... | collective-permute-start | bytes 393224 | tf_op jit(solution)/shard_map/ppermute | solution.py:17
  141.0 2.7 %fusion.5 = bf16[1,4,512,512]{2,3,1,0:T(8,128)(2,1)S(1)} fusion(f32[512,512,4]{1,0,2:T(8,128)S(1)} %fusion.145, f32[4,512]{1,0:T(4,128)S(1)} %copy.201, f32[4,512]{1,0:T(4,128)S(1)} %bitcast.593, pred[512,512]{0,1:T(8,128)(4,1)S(1)} %copy-done.24, bf16[512,1,128]{2,0,1:T(8,128)(2,1)} %collective-permute-done.5, bf16[512,4,128]{2,1,0:T(4,128)(2,1)S(1)} %reshape.815), kind=kOutput, calls=%fused_computation.8 | convolution fusion | flops 274726912 | bytes 7225344 | tf_op jit(solution)/shard_map/tcgd,scd->cgts/dot_general | solution.py:51
  151.7 2.7 %fusion.1 = bf16[1,4,512,512]{2,3,1,0:T(8,128)(2,1)S(1)} fusion(f32[512,512,4]{1,0,2:T(8,128)S(1)} %fusion.141, f32[4,512]{1,0:T(4,128)S(1)} %copy.201, f32[4,512]{1,0:T(4,128)S(1)} %bitcast.595, pred[512,512]{0,1:T(8,128)(4,1)S(1)} %copy-done.20, bf16[512,1,128]{2,0,1:T(8,128)(2,1)} %collective-permute-done.7, bf16[512,4,128]{2,1,0:T(4,128)(2,1)S(1)} %reshape.815), kind=kOutput, calls=%fused_computation.2 | convolution fusion | flops 274726912 | bytes 7225344 | tf_op jit(solution)/shard_map/tcgd,scd->cgts/dot_general | solution.py:51
  159.5 9.3 %all-to-all-start.6 = ((bf16[16,32,512]{2,1,0:T(8,128)(2,1)}), bf16[16,32,512]{2,1,0:T(8,128)(2,1)}, u32[]{:S(2)}, u32[]{:S(2)}) async-start(bf16[16,32,512]{2,1,0:T(8,128)(2,1)} %all_to_all.117), calls=%async_computation.6 | async-start | bytes 1048576 | tf_op jit(solution)/shard_map/all_to_all | solution.py:180
  175.5 6.2 %collective-permute-done.9 = f32[512,1,128]{2,0,1:T(8,128)S(1)} collective-permute-done((f32[512,1,128]{2,0,1:T(8,128)S(1)}, f32[512,1,128]{2,0,1:T(8,128)S(1)}, u32[]{:S(2)}, u32[]{:S(2)}) %collective-permute-start.9) | collective-permute-done | bytes 262176 | tf_op jit(solution)/shard_map/ppermute | solution.py:22
  185.0 3.5 %collective-permute-done.10 = f32[512,1,128]{2,0,1:T(8,128)S(1)} collective-permute-done((f32[512,1,128]{2,0,1:T(8,128)S(1)}, f32[512,1,128]{2,0,1:T(8,128)S(1)}, u32[]{:S(2)}, u32[]{:S(2)}) %collective-permute-start.10) | collective-permute-done | bytes 262176 | tf_op jit(solution)/shard_map/ppermute | solution.py:22
  191.8 3.5 %collective-permute-done.11 = f32[512,1,128]{2,0,1:T(8,128)S(1)} collective-permute-done((f32[512,1,128]{2,0,1:T(8,128)S(1)}, f32[512,1,128]{2,0,1:T(8,128)S(1)}, u32[]{:S(2)}, u32[]{:S(2)}) %collective-permute-start.11) | collective-permute-done | bytes 262176 | tf_op jit(solution)/shard_map/ppermute | solution.py:22
  195.4 4.4 %collective-permute-start.12 = (bf16[512,1,128]{2,0,1:T(8,128)(2,1)S(1)}, bf16[512,1,128]{2,0,1:T(8,128)(2,1)S(1)}, u32[]{:S(2)}, u32[]{:S(2)}) collective-permute-start(bf16[512,1,128]{2,0,1:T(8,128)(2,1)S(1)} %add_convert_fusion.1), channel_id=1, source_target_pairs={{0,192},{16,208},{32,224},{48,240},{64,0},{80,16},{96,32},{112,48}... | collective-permute-start | bytes 393224 | tf_op jit(solution)/shard_map/ppermute | solution.py:22
  203.0 10.1 %all-to-all-start.7 = ((bf16[16,32,128]{2,1,0:T(8,128)(2,1)}), bf16[16,32,128]{2,1,0:T(8,128)(2,1)S(1)}, u32[]{:S(2)}, u32[]{:S(2)}) async-start(bf16[16,32,128]{2,1,0:T(8,128)(2,1)} %bitcast.123), calls=%async_computation.7 | async-start | bytes 262144 | tf_op jit(solution)/shard_map/all_to_all | solution.py:166
  218.3 4.9 %all-to-all-done.7 = bf16[16,32,128]{2,1,0:T(8,128)(2,1)S(1)} async-done(((bf16[16,32,128]{2,1,0:T(8,128)(2,1)}), bf16[16,32,128]{2,1,0:T(8,128)(2,1)S(1)}, u32[]{:S(2)}, u32[]{:S(2)}) %all-to-all-start.7) | async-done | bytes 131104 | tf_op jit(solution)/shard_map/all_to_all | solution.py:166
  223.1 4.7 %all-to-all-start.8 = ((bf16[16,32,128]{2,1,0:T(8,128)(2,1)}), bf16[16,32,128]{2,1,0:T(8,128)(2,1)S(1)}, u32[]{:S(2)}, u32[]{:S(2)}) async-start(bf16[16,32,128]{2,1,0:T(8,128)(2,1)} %bitcast.156), calls=%async_computation.8 | async-start | bytes 262144 | tf_op jit(solution)/shard_map/all_to_all | solution.py:169
  228.6 9.4 %all-to-all-done.8 = bf16[16,32,128]{2,1,0:T(8,128)(2,1)S(1)} async-done(((bf16[16,32,128]{2,1,0:T(8,128)(2,1)}), bf16[16,32,128]{2,1,0:T(8,128)(2,1)S(1)}, u32[]{:S(2)}, u32[]{:S(2)}) %all-to-all-start.8) | async-done | bytes 131104 | tf_op jit(solution)/shard_map/all_to_all | solution.py:169
  (213 shorter events, 92.1 us)
Async XLA Ops:
  2.2 20.9 %all-to-all-start.2 = ((f32[16,1,128]{2,1,0:T(1,128)}), f32[16,1,128]{2,1,0:T(1,128)S(1)}, u32[]{:S(2)}, u32[]{:S(2)}) async-start(f32[16,1,128]{2,1,0:T(1,128)} %reshape.877), calls=%async_computation.2 | async-start | bytes 16384 | tf_op jit(solution)/shard_map/all_to_all | solution.py:72
  23.8 13.7 %all-to-all-start = ((bf16[32,16,128]{2,0,1:T(8,128)(2,1)}), bf16[32,16,128]{2,0,1:T(8,128)(2,1)S(1)}, u32[]{:S(2)}, u32[]{:S(2)}) async-start(bf16[32,16,128]{2,0,1:T(8,128)(2,1)} %bitcast.1), calls=%async_computation | async-start | bytes 262144 | tf_op jit(solution)/shard_map/all_to_all | solution.py:85
  38.2 13.5 %all-to-all-start.3 = ((bf16[32,16,128]{2,0,1:T(8,128)(2,1)}), bf16[32,16,128]{2,0,1:T(8,128)(2,1)S(1)}, u32[]{:S(2)}, u32[]{:S(2)}) async-start(bf16[32,16,128]{2,0,1:T(8,128)(2,1)} %bitcast.12), calls=%async_computation.3 | async-start | bytes 262144 | tf_op jit(solution)/shard_map/all_to_all | solution.py:86
  51.7 20.0 %all-to-all-start.1 = ((bf16[32,16,512]{2,0,1:T(8,128)(2,1)}), bf16[32,16,512]{2,0,1:T(8,128)(2,1)S(1)}, u32[]{:S(2)}, u32[]{:S(2)}) async-start(bf16[32,16,512]{2,0,1:T(8,128)(2,1)} %bitcast.562), calls=%async_computation.1 | async-start | bytes 1048576 | tf_op jit(solution)/shard_map/all_to_all | solution.py:68
  71.8 18.2 %all-to-all-start.4 = ((bf16[32,16,512]{2,0,1:T(8,128)(2,1)}), bf16[32,16,512]{2,0,1:T(8,128)(2,1)S(1)}, u32[]{:S(2)}, u32[]{:S(2)}) async-start(bf16[32,16,512]{2,0,1:T(8,128)(2,1)} %bitcast.561), calls=%async_computation.4 | async-start | bytes 1048576 | tf_op jit(solution)/shard_map/all_to_all | solution.py:70
  76.6 23.1 %collective-permute-start.1 = (bf16[512,1,128]{2,0,1:T(8,128)(2,1)S(1)}, bf16[512,1,128]{2,0,1:T(8,128)(2,1)S(1)}, u32[]{:S(2)}, u32[]{:S(2)}) collective-permute-start(bf16[512,1,128]{2,0,1:T(8,128)(2,1)S(1)} %bitcast.574), channel_id=1, source_target_pairs={{0,16},{16,32},{32,48},{48,64},{64,80},{80,96},{96,112},{112,128},... | collective-permute-start | bytes 393224 | tf_op jit(solution)/shard_map/ppermute | solution.py:17
  78.5 23.1 %collective-permute-start = (bf16[512,1,128]{2,0,1:T(8,128)(2,1)S(1)}, bf16[512,1,128]{2,0,1:T(8,128)(2,1)S(1)}, u32[]{:S(2)}, u32[]{:S(2)}) collective-permute-start(bf16[512,1,128]{2,0,1:T(8,128)(2,1)S(1)} %bitcast.577), channel_id=1, source_target_pairs={{0,16},{16,32},{32,48},{48,64},{64,80},{80,96},{96,112},{112,128},... | collective-permute-start | bytes 393224 | tf_op jit(solution)/shard_map/ppermute | solution.py:17
  90.0 31.5 %all-to-all-start.5 = ((bf16[32,16,512]{2,0,1:T(8,128)(2,1)}), bf16[32,16,512]{2,0,1:T(8,128)(2,1)}, u32[]{:S(2)}, u32[]{:S(2)}) async-start(bf16[32,16,512]{2,0,1:T(8,128)(2,1)} %bitcast.560), calls=%async_computation.5 | async-start | bytes 1048576 | tf_op jit(solution)/shard_map/all_to_all | solution.py:69
  99.7 7.5 %collective-permute-start.3 = (bf16[512,1,128]{2,0,1:T(8,128)(2,1)S(1)}, bf16[512,1,128]{2,0,1:T(8,128)(2,1)S(1)}, u32[]{:S(2)}, u32[]{:S(2)}) collective-permute-start(bf16[512,1,128]{2,0,1:T(8,128)(2,1)S(1)} %collective-permute-done.1), channel_id=1, source_target_pairs={{0,16},{16,32},{32,48},{48,64},{64,80},{80,96},{96,112},{112,128},... | collective-permute-start | bytes 393224 | tf_op jit(solution)/shard_map/ppermute | solution.py:17
  101.7 7.5 %collective-permute-start.2 = (bf16[512,1,128]{2,0,1:T(8,128)(2,1)S(1)}, bf16[512,1,128]{2,0,1:T(8,128)(2,1)S(1)}, u32[]{:S(2)}, u32[]{:S(2)}) collective-permute-start(bf16[512,1,128]{2,0,1:T(8,128)(2,1)S(1)} %collective-permute-done), channel_id=1, source_target_pairs={{0,16},{16,32},{32,48},{48,64},{64,80},{80,96},{96,112},{112,128},... | collective-permute-start | bytes 393224 | tf_op jit(solution)/shard_map/ppermute | solution.py:17
  107.3 7.3 %collective-permute-start.5 = (bf16[512,1,128]{2,0,1:T(8,128)(2,1)S(1)}, bf16[512,1,128]{2,0,1:T(8,128)(2,1)}, u32[]{:S(2)}, u32[]{:S(2)}) collective-permute-start(bf16[512,1,128]{2,0,1:T(8,128)(2,1)S(1)} %collective-permute-done.3), channel_id=1, source_target_pairs={{0,16},{16,32},{32,48},{48,64},{64,80},{80,96},{96,112},{112,128},... | collective-permute-start | bytes 393224 | tf_op jit(solution)/shard_map/ppermute | solution.py:17
  109.2 7.3 %collective-permute-start.4 = (bf16[512,1,128]{2,0,1:T(8,128)(2,1)S(1)}, bf16[512,1,128]{2,0,1:T(8,128)(2,1)}, u32[]{:S(2)}, u32[]{:S(2)}) collective-permute-start(bf16[512,1,128]{2,0,1:T(8,128)(2,1)S(1)} %collective-permute-done.2), channel_id=1, source_target_pairs={{0,16},{16,32},{32,48},{48,64},{64,80},{80,96},{96,112},{112,128},... | collective-permute-start | bytes 393224 | tf_op jit(solution)/shard_map/ppermute | solution.py:17
  114.6 37.1 %collective-permute-start.7 = (bf16[512,1,128]{2,0,1:T(8,128)(2,1)}, bf16[512,1,128]{2,0,1:T(8,128)(2,1)}, u32[]{:S(2)}, u32[]{:S(2)}) collective-permute-start(bf16[512,1,128]{2,0,1:T(8,128)(2,1)} %collective-permute-done.5), channel_id=1, source_target_pairs={{0,16},{16,32},{32,48},{48,64},{64,80},{80,96},{96,112},{112,128},... | collective-permute-start | bytes 393224 | tf_op jit(solution)/shard_map/ppermute | solution.py:17
  116.5 28.4 %collective-permute-start.6 = (bf16[512,1,128]{2,0,1:T(8,128)(2,1)}, bf16[512,1,128]{2,0,1:T(8,128)(2,1)}, u32[]{:S(2)}, u32[]{:S(2)}) collective-permute-start(bf16[512,1,128]{2,0,1:T(8,128)(2,1)} %collective-permute-done.4), channel_id=1, source_target_pairs={{0,16},{16,32},{32,48},{48,64},{64,80},{80,96},{96,112},{112,128},... | collective-permute-start | bytes 393224 | tf_op jit(solution)/shard_map/ppermute | solution.py:17
  132.2 39.0 %collective-permute-start.8 = (f32[512,1,128]{2,0,1:T(8,128)}, f32[512,1,128]{2,0,1:T(8,128)}, u32[]{:S(2)}, u32[]{:S(2)}) collective-permute-start(f32[512,1,128]{2,0,1:T(8,128)} %fusion.122), channel_id=1, source_target_pairs={{0,16},{16,32},{32,48},{48,64},{64,80},{80,96},{96,112},{112,128},... | collective-permute-start | bytes 786440 | tf_op jit(solution)/shard_map/ppermute | solution.py:22
  132.2 40.8 %collective-permute-start.13 = (f32[512,1,128]{2,0,1:T(8,128)}, f32[512,1,128]{2,0,1:T(8,128)}, u32[]{:S(2)}, u32[]{:S(2)}) collective-permute-start(f32[512,1,128]{2,0,1:T(8,128)} %fusion.123), channel_id=1, source_target_pairs={{0,16},{16,32},{32,48},{48,64},{64,80},{80,96},{96,112},{112,128},... | collective-permute-start | bytes 786440 | tf_op jit(solution)/shard_map/ppermute | solution.py:22
  159.5 43.5 %all-to-all-start.6 = ((bf16[16,32,512]{2,1,0:T(8,128)(2,1)}), bf16[16,32,512]{2,1,0:T(8,128)(2,1)}, u32[]{:S(2)}, u32[]{:S(2)}) async-start(bf16[16,32,512]{2,1,0:T(8,128)(2,1)} %all_to_all.117), calls=%async_computation.6 | async-start | bytes 1048576 | tf_op jit(solution)/shard_map/all_to_all | solution.py:180
  172.9 8.8 %collective-permute-start.9 = (f32[512,1,128]{2,0,1:T(8,128)S(1)}, f32[512,1,128]{2,0,1:T(8,128)S(1)}, u32[]{:S(2)}, u32[]{:S(2)}) collective-permute-start(f32[512,1,128]{2,0,1:T(8,128)S(1)} %fusion.110), channel_id=1, source_target_pairs={{0,16},{16,32},{32,48},{48,64},{64,80},{80,96},{96,112},{112,128},... | collective-permute-start | bytes 786440 | tf_op jit(solution)/shard_map/ppermute | solution.py:22
  175.2 9.6 %collective-permute-start.14 = (f32[512,1,128]{2,0,1:T(8,128)S(1)}, f32[512,1,128]{2,0,1:T(8,128)S(1)}, u32[]{:S(2)}, u32[]{:S(2)}) collective-permute-start(f32[512,1,128]{2,0,1:T(8,128)S(1)} %fusion.124), channel_id=1, source_target_pairs={{0,16},{16,32},{32,48},{48,64},{64,80},{80,96},{96,112},{112,128},... | collective-permute-start | bytes 786440 | tf_op jit(solution)/shard_map/ppermute | solution.py:22
  181.8 6.8 %collective-permute-start.10 = (f32[512,1,128]{2,0,1:T(8,128)S(1)}, f32[512,1,128]{2,0,1:T(8,128)S(1)}, u32[]{:S(2)}, u32[]{:S(2)}) collective-permute-start(f32[512,1,128]{2,0,1:T(8,128)S(1)} %add.246), channel_id=1, source_target_pairs={{0,16},{16,32},{32,48},{48,64},{64,80},{80,96},{96,112},{112,128},... | collective-permute-start | bytes 786440 | tf_op jit(solution)/shard_map/ppermute | solution.py:22
  191.7 21.4 %collective-permute-start.16 = (f32[512,1,128]{2,0,1:T(8,128)S(1)}, f32[512,1,128]{2,0,1:T(8,128)S(1)}, u32[]{:S(2)}, u32[]{:S(2)}) collective-permute-start(f32[512,1,128]{2,0,1:T(8,128)S(1)} %add.252), channel_id=1, source_target_pairs={{0,16},{16,32},{32,48},{48,64},{64,80},{80,96},{96,112},{112,128},... | collective-permute-start | bytes 786440 | tf_op jit(solution)/shard_map/ppermute | solution.py:22
  195.4 6.9 %collective-permute-start.12 = (bf16[512,1,128]{2,0,1:T(8,128)(2,1)S(1)}, bf16[512,1,128]{2,0,1:T(8,128)(2,1)S(1)}, u32[]{:S(2)}, u32[]{:S(2)}) collective-permute-start(bf16[512,1,128]{2,0,1:T(8,128)(2,1)S(1)} %add_convert_fusion.1), channel_id=1, source_target_pairs={{0,192},{16,208},{32,224},{48,240},{64,0},{80,16},{96,32},{112,48}... | collective-permute-start | bytes 393224 | tf_op jit(solution)/shard_map/ppermute | solution.py:22
  203.0 20.2 %all-to-all-start.7 = ((bf16[16,32,128]{2,1,0:T(8,128)(2,1)}), bf16[16,32,128]{2,1,0:T(8,128)(2,1)S(1)}, u32[]{:S(2)}, u32[]{:S(2)}) async-start(bf16[16,32,128]{2,1,0:T(8,128)(2,1)} %bitcast.123), calls=%async_computation.7 | async-start | bytes 262144 | tf_op jit(solution)/shard_map/all_to_all | solution.py:166
  223.1 14.8 %all-to-all-start.8 = ((bf16[16,32,128]{2,1,0:T(8,128)(2,1)}), bf16[16,32,128]{2,1,0:T(8,128)(2,1)S(1)}, u32[]{:S(2)}, u32[]{:S(2)}) async-start(bf16[16,32,128]{2,1,0:T(8,128)(2,1)} %bitcast.156), calls=%async_computation.8 | async-start | bytes 262144 | tf_op jit(solution)/shard_map/all_to_all | solution.py:169
  (37 other events, 438.0 us)

commit v2 on v0

v2 whole, which is shorter than its diff:
```python
import functools
import math

import jax
import jax.numpy as jnp
from jax import lax
from jax.experimental import pallas as pl
from jax.experimental.pallas import tpu as pltpu
from jax.sharding import Mesh
from jax.sharding import PartitionSpec as P

KVH = 8
HD = 128
GROUP = 8
BLOCK = 128
WINDOW = 2048
TOK = 32
ZS = 8
AS = 8
CHUNK = TOK * ZS
ROWS = TOK * GROUP
SCALE = 1.0 / math.sqrt(HD)
LOG2E = math.log2(math.e)
BIG = 1e30
HEADS = ("xl", "c", "xh")
F32 = jnp.float32
BF16 = jnp.bfloat16
OFFSETS = (0, 1, -1, 2, -2, 3, -3, 4)


def along_z(value, by):
    return lax.ppermute(value, "z", [(i, (i + by) % ZS) for i in range(ZS)])


def exchange(value):
    return lax.all_to_all(value, HEADS, split_axis=0, concat_axis=0, tiled=True)


def pack_kv_kernel(k_ref, v_ref, out_ref):
    for a in range(AS):
        out_ref[a, :, :HD] = k_ref[:, a * HD : (a + 1) * HD]
        out_ref[a, :, HD:] = v_ref[:, a * HD : (a + 1) * HD]


def pack_queries_kernel(q_ref, g_ref, extra_ref, out_ref):
    out_ref[0, :TOK, :] = q_ref[...]
    out_ref[0, TOK : 2 * TOK, :] = g_ref[...]
    out_ref[0, 2 * TOK :, :ROWS] = extra_ref[0]
    out_ref[0, 2 * TOK :, ROWS:] = jnp.zeros((16, GROUP * HD - ROWS), BF16)


def attention_kernel(keep_ref, span_ref, z_ref, message_ref, start_ref, *refs):
    kv_refs, refs = refs[:ZS], refs[ZS:]
    dq_ref, refs = refs[0], refs[1:]
    dkv_refs, refs = refs[:ZS], refs[ZS:]
    acc_ref, kt_ref, q_ref, g_ref, qt_ref, gt_ref, dqt_ref = refs
    z = z_ref[0]
    sources = [lax.rem(z - off + ZS, ZS) for off in OFFSETS]

    def keys_of(a, lanes):
        return jnp.concatenate([kv[a, :, lanes] for kv in kv_refs], axis=0)

    def prepare(a, _):
        kt_ref[a] = keys_of(a, pl.ds(0, HD)).T
        acc_ref[a] = jnp.zeros((CHUNK, 2 * HD), F32)
        return 0

    lax.fori_loop(0, AS, prepare, 0)

    def chunk(i, _):
        for h in range(GROUP):
            q_ref[h * TOK : (h + 1) * TOK, :] = message_ref[i, :TOK, h * HD : (h + 1) * HD]
            g_ref[h * TOK : (h + 1) * TOK, :] = message_ref[i, TOK : 2 * TOK, h * HD : (h + 1) * HD]
        qt_ref[...] = q_ref[...].T
        gt_ref[...] = g_ref[...].T
        extra = message_ref[i, 2 * TOK :, :ROWS].astype(F32)
        lse = extra[0:1] + extra[1:2]
        delta = extra[2:3] + extra[3:4]
        start = start_ref[i]
        q_pos = i * CHUNK + z * TOK + lax.rem(lax.broadcasted_iota(jnp.int32, (1, ROWS), 1), TOK)
        dqt_ref[...] = jnp.zeros((HD, ROWS), F32)

        def tile(a, masked):
            scores = jnp.dot(keys_of(a, pl.ds(0, HD)), qt_ref[...], preferred_element_type=F32)
            dprobs = jnp.dot(keys_of(a, pl.ds(HD, HD)), gt_ref[...], preferred_element_type=F32)
            probs_b, dscores_b = [], []
            for r in range(ZS):
                rows = slice(r * TOK, (r + 1) * TOK)
                distance = 2 * (i - a) + z // 4 - sources[r] // 4
                kept = keep_ref[i, jnp.maximum(distance, 0)] > 0
                lse_piece = lse + jnp.where(kept, 0.0, BIG)
                probs = jnp.exp2(scores[rows] * (SCALE * LOG2E) - lse_piece)
                if masked:
                    k_pos = (
                        a * CHUNK
                        + sources[r] * TOK
                        + lax.broadcasted_iota(jnp.int32, (TOK, ROWS), 0)
                    )
                    probs = jnp.where((k_pos >= start) & (k_pos <= q_pos), probs, 0.0)
                probs_b.append(probs.astype(BF16))
                dscores_b.append((probs * (dprobs[rows] - delta)).astype(BF16))
            probs_b = jnp.concatenate(probs_b, axis=0)
            dscores_b = jnp.concatenate(dscores_b, axis=0)
            acc_ref[a, :, :HD] += jnp.dot(dscores_b, q_ref[...], preferred_element_type=F32)
            acc_ref[a, :, HD:] += jnp.dot(probs_b, g_ref[...], preferred_element_type=F32)
            dqt_ref[...] += jnp.dot(kt_ref[a], dscores_b, preferred_element_type=F32)

        def step(a, _):
            masked = (a == i) | (span_ref[i, 1] > a * CHUNK)

            @pl.when(masked)
            def _():
                tile(a, True)

            @pl.when(jnp.logical_not(masked))
            def _():
                tile(a, False)

            return 0

        lax.fori_loop(span_ref[i, 0] // CHUNK, i + 1, step, 0)
        dq = (dqt_ref[...] * SCALE).T.astype(BF16)
        for h in range(GROUP):
            dq_ref[i, :, h * HD : (h + 1) * HD] = dq[h * TOK : (h + 1) * TOK]
        return 0

    lax.fori_loop(0, AS, chunk, 0)

    def finish(a, _):
        for r in range(ZS):
            piece = acc_ref[a, r * TOK : (r + 1) * TOK, :]
            dkv_refs[r][a, :, :HD] = (piece[:, :HD] * SCALE).astype(BF16)
            dkv_refs[r][a, :, HD:] = piece[:, HD:].astype(BF16)
        return 0

    lax.fori_loop(0, AS, finish, 0)


def sum_kernel(*refs):
    total = refs[0][...].astype(F32)
    for ref in refs[1:-1]:
        total = total + ref[...].astype(F32)
    refs[-1][...] = total.astype(BF16)


def unpack_queries_kernel(in_ref, out_ref):
    out_ref[...] = in_ref[0]


def unpack_kv_kernel(in_ref, dk_ref, dv_ref):
    for a in range(AS):
        dk_ref[:, a * HD : (a + 1) * HD] = in_ref[a, :, :HD]
        dv_ref[:, a * HD : (a + 1) * HD] = in_ref[a, :, HD:]


def in_vmem():
    return pl.BlockSpec(memory_space=pltpu.VMEM)


def in_smem():
    return pl.BlockSpec(memory_space=pltpu.SMEM)


def shards(query, key, value, output, out_grad, lse, doc_lengths, block_keep):
    i32 = jnp.int32
    z = lax.axis_index("z").astype(i32)
    columns = GROUP * HD

    kv_send = pl.pallas_call(
        pack_kv_kernel,
        out_shape=jax.ShapeDtypeStruct((AS, TOK, 2 * HD), BF16),
        in_specs=[in_vmem(), in_vmem()],
        out_specs=in_vmem(),
        cost_estimate=pl.CostEstimate(flops=0, bytes_accessed=262144, transcendentals=0),
    )(key, value)
    kv_own = exchange(kv_send)

    delta = jnp.sum(
        out_grad.reshape(TOK, -1, HD).astype(F32) * output.reshape(TOK, -1, HD).astype(F32), axis=2
    )
    both = jnp.stack([lse * LOG2E, delta])
    high = lax.reduce_precision(both, 8, 7)
    parts = jnp.stack([high, both - high], axis=1).astype(BF16)
    parts = parts.reshape(4, TOK, AS, GROUP).transpose(2, 0, 3, 1).reshape(AS, 4, ROWS)
    local_block = lax.axis_index("xh") * 2 + z // 4
    keep_row = lax.dynamic_slice_in_dim(block_keep, local_block, 1, 0).astype(BF16)
    reach = keep_row.shape[1]
    keep_row = jnp.broadcast_to(jnp.pad(keep_row, ((0, 0), (0, ROWS - reach)))[None], (AS, 1, ROWS))
    extra = jnp.concatenate([parts, keep_row, jnp.zeros((AS, 11, ROWS), BF16)], axis=1)
    message_send = pl.pallas_call(
        pack_queries_kernel,
        grid=(AS,),
        out_shape=jax.ShapeDtypeStruct((AS, 2 * TOK + 16, columns), BF16),
        in_specs=[
            pl.BlockSpec((TOK, columns), lambda a: (0, a)),
            pl.BlockSpec((TOK, columns), lambda a: (0, a)),
            pl.BlockSpec((1, 16, ROWS), lambda a: (a, 0, 0)),
        ],
        out_specs=pl.BlockSpec((1, 2 * TOK + 16, columns), lambda a: (a, 0, 0)),
        cost_estimate=pl.CostEstimate(flops=0, bytes_accessed=2600000, transcendentals=0),
    )(query, out_grad, extra)
    message = exchange(message_send)

    pieces = {0: kv_own}
    for off in (1, 2, 3, 4):
        pieces[off] = along_z(pieces[off - 1], 1)
        if off < 4:
            pieces[-off] = along_z(pieces[1 - off], -1)

    keep = message[:, 2 * TOK + 4, :reach].astype(i32)
    ends = jnp.arange(doc_lengths.shape[0], dtype=i32)
    starts = jnp.sum(jnp.where(ends[None, :] < ends[:, None], doc_lengths[None, :], 0), axis=1)
    base = lax.axis_index("y").astype(i32) * WINDOW
    positions = (
        base
        + jnp.arange(AS, dtype=i32)[:, None] * CHUNK
        + z * TOK
        + (jnp.arange(ROWS, dtype=i32) % TOK)[None, :]
    )
    start_of = jnp.max(
        jnp.where(starts[None, None, :] <= positions[:, :, None], starts[None, None, :], 0), axis=2
    )
    start_of = jnp.maximum(start_of - base, 0)
    span = jnp.stack([start_of[:, 0], start_of[:, TOK - 1]], axis=1)

    piece_shape = jax.ShapeDtypeStruct((AS, TOK, 2 * HD), BF16)
    results = pl.pallas_call(
        attention_kernel,
        out_shape=[jax.ShapeDtypeStruct((AS, TOK, columns), BF16)] + [piece_shape] * ZS,
        in_specs=[in_smem()] * 3 + [in_vmem()] * (2 + ZS),
        out_specs=[in_vmem()] * (1 + ZS),
        scratch_shapes=[
            pltpu.VMEM((AS, CHUNK, 2 * HD), F32),
            pltpu.VMEM((AS, HD, CHUNK), BF16),
            pltpu.VMEM((ROWS, HD), BF16),
            pltpu.VMEM((ROWS, HD), BF16),
            pltpu.VMEM((HD, ROWS), BF16),
            pltpu.VMEM((HD, ROWS), BF16),
            pltpu.VMEM((HD, ROWS), F32),
        ],
        compiler_params=pltpu.CompilerParams(vmem_limit_bytes=24 * 2**20),
        cost_estimate=pl.CostEstimate(
            flops=3000000000, bytes_accessed=4000000, transcendentals=2360000
        ),
    )(keep, span, z.reshape(1), message, start_of.reshape(AS, 1, ROWS), *[pieces[o] for o in OFFSETS])
    dq, partials = results[0], results[1:]

    returned = [
        partials[r] if off == 0 else along_z(partials[r], -off) for r, off in enumerate(OFFSETS)
    ]
    dq_back = exchange(dq)
    query_grad = pl.pallas_call(
        unpack_queries_kernel,
        grid=(AS,),
        out_shape=jax.ShapeDtypeStruct((TOK, AS * columns), BF16),
        in_specs=[pl.BlockSpec((1, TOK, columns), lambda a: (a, 0, 0))],
        out_specs=pl.BlockSpec((TOK, columns), lambda a: (0, a)),
        cost_estimate=pl.CostEstimate(flops=0, bytes_accessed=1048576, transcendentals=0),
    )(dq_back)
    summed = pl.pallas_call(
        sum_kernel,
        out_shape=piece_shape,
        in_specs=[in_vmem()] * ZS,
        out_specs=in_vmem(),
        cost_estimate=pl.CostEstimate(flops=524288, bytes_accessed=1179648, transcendentals=0),
    )(*returned)
    grads = exchange(summed)
    half = jax.ShapeDtypeStruct((TOK, KVH * HD), BF16)
    key_grad, value_grad = pl.pallas_call(
        unpack_kv_kernel,
        out_shape=[half, half],
        in_specs=[in_vmem()],
        out_specs=[in_vmem(), in_vmem()],
        cost_estimate=pl.CostEstimate(flops=0, bytes_accessed=262144, transcendentals=0),
    )(grads)
    return (query_grad, key_grad, value_grad)


def solution(mesh):
    fine = Mesh(mesh.devices.reshape(4, 2, 2, 2, ZS), ("y", "xl", "c", "xh", "z"))
    tokens = P(("y", "xl", "c", "xh", "z"), None)
    in_specs = (tokens,) * 6 + (P(), P(("y", "xl", "c"), None))
    return jax.shard_map(
        shards, mesh=fine, in_specs=in_specs, out_specs=(tokens,) * 3, check_vma=False
    )
```

time: 243 us -> 128 us (0.53)
  starting transfers between devices: 85.5 us -> 37.6 us
  waiting for transfers between devices: 83 us -> 35.8 us
  matrix products: 36.1 us -> 0 us
  Pallas kernels: 0 us -> 34.2 us
  local copies, waits for them, and re-layouts: 24.8 us -> 2.7 us
  blocking collectives: 0 us -> 11 us
  other arithmetic: 8.06 us -> 4.15 us
    all_to_all x9 -> x3, waiting for transfers between devices: 57.7 us -> 8.1 us  [exchange(): return lax.all_to_all(value, HEADS, split_axis=0, concat_axis=0, tiled=True)]
    all_to_all x9 -> x3, starting transfers between devices: 58 us -> 12.7 us  [exchange(): return lax.all_to_all(value, HEADS, split_axis=0, concat_axis=0, tiled=True)]
    dot_general x30 -> x0, matrix products: 36.1 us -> none  [the longest x6 9.35 us: piece_grads(): jnp.einsum('tcgd,scd->cgts', g_group, values, preferred_element_type=f32)]
    pallas_call x0 -> x6, Pallas kernels: none -> 34.2 us  [the longest x1 19.1 us: shards(): pl.pallas_call(attention_kernel, out_shape=[jax.ShapeDtypeStruct((AS, TOK...]
    all_to_all x0 -> x1, blocking collectives: none -> 11 us  [exchange(): return lax.all_to_all(value, HEADS, split_axis=0, concat_axis=0, tiled=True)]
    all_to_all x8 -> x0, local copies, waits for them, and re-layouts: 10.1 us -> none  [the longest x2 3.9 us: shards(): lax.all_to_all(dq_rows, 'head', split_axis=0, concat_axis=1, tiled=True)]
    another operation x5 -> x1, local copies, waits for them, and re-layouts: 3.05 us -> 0.1 us  [shards(): parts = jnp.stack([high, both - high], axis=1).astype(BF16)]
    convert_element_type x4 -> x0, local copies, waits for them, and re-layouts: 2.83 us -> none  [the longest x1 1.2 us: shards(): (dq_total * scale).astype(jnp.bfloat16)]
  transfers between devices with their start and end apart: 27 -> 17, of which waited for: 16 -> 9; matrix products, arithmetic and copies ran while one was open for 26% -> 4% of each run, Pallas kernels for 0% -> 5%
where the time goes in v2:
time: 128 us; the launch traced here: 126 us
  starting transfers between devices  37.6 us (29%)
  waiting for transfers between devices  35.8 us (28%)
  Pallas kernels  34.2 us (27%)
  blocking collectives  11 us (9%)
  other arithmetic  4.15 us (3%)
  local copies, waits for them, and re-layouts  2.7 us (2%)
    ppermute x14, waiting for transfers between devices, along_z(): return lax.ppermute(value, 'z', [(i, (i + by) % ZS) for i in range(ZS)])  27.7 us
    ppermute x14, starting transfers between devices, along_z(): return lax.ppermute(value, 'z', [(i, (i + by) % ZS) for i in range(ZS)])  24.9 us
    pallas_call x1, Pallas kernels, shards(): pl.pallas_call(attention_kernel, out_shape=[jax.ShapeDtypeStruct((AS, TOK...  19.1 us
    all_to_all x3, starting transfers between devices, exchange(): return lax.all_to_all(value, HEADS, split_axis=0, concat_axis=0, tiled=True)  12.7 us
    all_to_all x1, blocking collectives, exchange(): return lax.all_to_all(value, HEADS, split_axis=0, concat_axis=0, tiled=True)  11 us
    all_to_all x3, waiting for transfers between devices, exchange(): return lax.all_to_all(value, HEADS, split_axis=0, concat_axis=0, tiled=True)  8.1 us
    pallas_call x1, Pallas kernels, shards(): pl.pallas_call(pack_queries_kernel, grid=(AS,), out_shape=jax.ShapeDtypeS...  5.12 us
    pallas_call x1, Pallas kernels, shards(): pl.pallas_call(unpack_queries_kernel, grid=(AS,), out_shape=jax.ShapeDtyp...  4.74 us
  transfers between devices with their start and end apart: 17, of which 9 were waited for; matrix products, arithmetic and copies ran while one was open for 4% of the time, Pallas kernels for 5%

profile of v2, /device:TPU:8, one launch (start us, length us, event | category | flops | bytes accessed | tf_op | source)
XLA Modules:
  0.0 126.2 jit_solution(5885819544049916628)
XLA Ops:
  2.2 4.3 %all-to-all-start.1 = ((bf16[8,32,256]{2,1,0:T(8,128)(2,1)}), bf16[8,32,256]{2,1,0:T(8,128)(2,1)S(1)}, u32[]{:S(2)}, u32[]{:S(2)}) async-start(bf16[8,32,256]{2,1,0:T(8,128)(2,1)} %shard_map.104), calls=%async_computation.1 | async-start | bytes 262144 | tf_op jit(solution)/shard_map/all_to_all | solution.py:36
  10.8 5.1 %shard_map.103 = bf16[8,80,1024]{2,1,0:T(8,128)(2,1)} custom-call(bf16[32,8192]{1,0:T(8,128)(2,1)} %q_ref.1, bf16[32,8192]{1,0:T(8,128)(2,1)} %g_ref.1, bf16[8,16,256]{2,1,0:T(8,128)(2,1)} %maximum_maximum_fusion.extra_ref), custom_call_target="tpu_custom_call" | custom-call | bytes 2600000 | tf_op jit(solution)/shard_map/pallas_call | solution.py:190
  16.0 4.9 %all-to-all-start = ((bf16[8,80,1024]{2,1,0:T(8,128)(2,1)}), bf16[8,80,1024]{2,1,0:T(8,128)(2,1)S(1)}, u32[]{:S(2)}, u32[]{:S(2)}) async-start(bf16[8,80,1024]{2,1,0:T(8,128)(2,1)} %shard_map.103), calls=%async_computation | async-start | bytes 2621440 | tf_op jit(solution)/shard_map/all_to_all | solution.py:36
  23.1 4.0 %collective-permute-start.1 = (bf16[8,32,256]{2,1,0:T(8,128)(2,1)S(1)}, bf16[8,32,256]{2,1,0:T(8,128)(2,1)S(1)}, u32[]{:S(2)}, u32[]{:S(2)}) collective-permute-start(bf16[8,32,256]{2,1,0:T(8,128)(2,1)S(1)} %all-to-all-done.1.refs_0_), channel_id=1, source_target_pairs={{0,7},{1,0},{2,1},{3,2},{4,3},{5,4},{6,5},{7,6},{8,15},{9,8},{10,9... | collective-permute-start | bytes 393224 | tf_op jit(solution)/shard_map/ppermute | solution.py:32
  27.2 3.9 %collective-permute-done.refs_1_ = bf16[8,32,256]{2,1,0:T(8,128)(2,1)S(1)} collective-permute-done((bf16[8,32,256]{2,1,0:T(8,128)(2,1)S(1)}, bf16[8,32,256]{2,1,0:T(8,128)(2,1)S(1)}, u32[]{:S(2)}, u32[]{:S(2)}) %collective-permute-start) | collective-permute-done | bytes 131104 | tf_op jit(solution)/shard_map/ppermute | solution.py:32
  31.0 3.2 %collective-permute-start.3 = (bf16[8,32,256]{2,1,0:T(8,128)(2,1)S(1)}, bf16[8,32,256]{2,1,0:T(8,128)(2,1)S(1)}, u32[]{:S(2)}, u32[]{:S(2)}) collective-permute-start(bf16[8,32,256]{2,1,0:T(8,128)(2,1)S(1)} %collective-permute-done.1.refs_2_), channel_id=1, source_target_pairs={{0,7},{1,0},{2,1},{3,2},{4,3},{5,4},{6,5},{7,6},{8,15},{9,8},{10,9... | collective-permute-start | bytes 393224 | tf_op jit(solution)/shard_map/ppermute | solution.py:32
  34.3 3.3 %collective-permute-done.2.refs_3_ = bf16[8,32,256]{2,1,0:T(8,128)(2,1)S(1)} collective-permute-done((bf16[8,32,256]{2,1,0:T(8,128)(2,1)S(1)}, bf16[8,32,256]{2,1,0:T(8,128)(2,1)S(1)}, u32[]{:S(2)}, u32[]{:S(2)}) %collective-permute-start.2) | collective-permute-done | bytes 131104 | tf_op jit(solution)/shard_map/ppermute | solution.py:32
  37.7 3.3 %collective-permute-start.5 = (bf16[8,32,256]{2,1,0:T(8,128)(2,1)S(1)}, bf16[8,32,256]{2,1,0:T(8,128)(2,1)S(1)}, u32[]{:S(2)}, u32[]{:S(2)}) collective-permute-start(bf16[8,32,256]{2,1,0:T(8,128)(2,1)S(1)} %collective-permute-done.3.refs_4_), channel_id=1, source_target_pairs={{0,7},{1,0},{2,1},{3,2},{4,3},{5,4},{6,5},{7,6},{8,15},{9,8},{10,9... | collective-permute-start | bytes 393224 | tf_op jit(solution)/shard_map/ppermute | solution.py:32
  41.0 2.8 %collective-permute-done.4.refs_5_ = bf16[8,32,256]{2,1,0:T(8,128)(2,1)S(1)} collective-permute-done((bf16[8,32,256]{2,1,0:T(8,128)(2,1)S(1)}, bf16[8,32,256]{2,1,0:T(8,128)(2,1)S(1)}, u32[]{:S(2)}, u32[]{:S(2)}) %collective-permute-start.4) | collective-permute-done | bytes 131104 | tf_op jit(solution)/shard_map/ppermute | solution.py:32
  43.8 6.1 %collective-permute-done.6.refs_7_ = bf16[8,32,256]{2,1,0:T(8,128)(2,1)S(1)} collective-permute-done((bf16[8,32,256]{2,1,0:T(8,128)(2,1)S(1)}, bf16[8,32,256]{2,1,0:T(8,128)(2,1)S(1)}, u32[]{:S(2)}, u32[]{:S(2)}) %collective-permute-start.6) | collective-permute-done | bytes 131104 | tf_op jit(solution)/shard_map/ppermute | solution.py:32
  49.9 19.1 %shard_map.105 = (bf16[8,32,1024]{2,1,0:T(8,128)(2,1)}, bf16[8,32,256]{2,1,0:T(8,128)(2,1)S(1)}, bf16[8,32,256]{2,1,0:T(8,128)(2,1)S(1)}, bf16[8,32,256]{2,1,0:T...) custom-call(s32[8,17]{1,0:T(8,128)S(1)} %bitcast.15, ...), custom_call_target="tpu_custom_call" | custom-call | flops 3000000000 | bytes 4000000 | tf_op jit(solution)/shard_map/pallas_call | solution.py:227
  69.7 2.0 %collective-permute-start.8 = (bf16[8,32,256]{2,1,0:T(8,128)(2,1)S(1)}, bf16[8,32,256]{2,1,0:T(8,128)(2,1)S(1)}, u32[]{:S(2)}, u32[]{:S(2)}) collective-permute-start(bf16[8,32,256]{2,1,0:T(8,128)(2,1)S(1)} %get-tuple-element.17), channel_id=1, source_target_pairs={{0,1},{1,2},{2,3},{3,4},{4,5},{5,6},{6,7},{7,0},{8,9},{9,10},{10,1... | collective-permute-start | bytes 393224 | tf_op jit(solution)/shard_map/ppermute | solution.py:32
  71.7 2.9 %collective-permute-start.10 = (bf16[8,32,256]{2,1,0:T(8,128)(2,1)S(1)}, bf16[8,32,256]{2,1,0:T(8,128)(2,1)S(1)}, u32[]{:S(2)}, u32[]{:S(2)}) collective-permute-start(bf16[8,32,256]{2,1,0:T(8,128)(2,1)S(1)} %get-tuple-element.19), channel_id=1, source_target_pairs={{0,2},{1,3},{2,4},{3,5},{4,6},{5,7},{6,0},{7,1},{8,10},{9,11},{10,... | collective-permute-start | bytes 393224 | tf_op jit(solution)/shard_map/ppermute | solution.py:32
  74.7 2.6 %collective-permute-start.11 = (bf16[8,32,256]{2,1,0:T(8,128)(2,1)S(1)}, bf16[8,32,256]{2,1,0:T(8,128)(2,1)S(1)}, u32[]{:S(2)}, u32[]{:S(2)}) collective-permute-start(bf16[8,32,256]{2,1,0:T(8,128)(2,1)S(1)} %get-tuple-element.20), channel_id=1, source_target_pairs={{0,5},{1,6},{2,7},{3,0},{4,1},{5,2},{6,3},{7,4},{8,13},{9,14},{10,... | collective-permute-start | bytes 393224 | tf_op jit(solution)/shard_map/ppermute | solution.py:32
  77.9 1.9 %collective-permute-start.12 = (bf16[8,32,256]{2,1,0:T(8,128)(2,1)S(1)}, bf16[8,32,256]{2,1,0:T(8,128)(2,1)S(1)}, u32[]{:S(2)}, u32[]{:S(2)}) collective-permute-start(bf16[8,32,256]{2,1,0:T(8,128)(2,1)S(1)} %get-tuple-element.21), channel_id=1, source_target_pairs={{0,3},{1,4},{2,5},{3,6},{4,7},{5,0},{6,1},{7,2},{8,11},{9,12},{10,... | collective-permute-start | bytes 393224 | tf_op jit(solution)/shard_map/ppermute | solution.py:32
  79.9 2.9 %collective-permute-start.13 = (bf16[8,32,256]{2,1,0:T(8,128)(2,1)S(1)}, bf16[8,32,256]{2,1,0:T(8,128)(2,1)S(1)}, u32[]{:S(2)}, u32[]{:S(2)}) collective-permute-start(bf16[8,32,256]{2,1,0:T(8,128)(2,1)S(1)} %get-tuple-element.22), channel_id=1, source_target_pairs={{0,4},{1,5},{2,6},{3,7},{4,0},{5,1},{6,2},{7,3},{8,12},{9,13},{10,... | collective-permute-start | bytes 393224 | tf_op jit(solution)/shard_map/ppermute | solution.py:32
  82.8 2.8 %collective-permute-done.10.refs_4_ = bf16[8,32,256]{2,1,0:T(8,128)(2,1)S(1)} collective-permute-done((bf16[8,32,256]{2,1,0:T(8,128)(2,1)S(1)}, bf16[8,32,256]{2,1,0:T(8,128)(2,1)S(1)}, u32[]{:S(2)}, u32[]{:S(2)}) %collective-permute-start.10) | collective-permute-done | bytes 131104 | tf_op jit(solution)/shard_map/ppermute | solution.py:32
  85.6 3.8 %collective-permute-done.11.refs_5_ = bf16[8,32,256]{2,1,0:T(8,128)(2,1)S(1)} collective-permute-done((bf16[8,32,256]{2,1,0:T(8,128)(2,1)S(1)}, bf16[8,32,256]{2,1,0:T(8,128)(2,1)S(1)}, u32[]{:S(2)}, u32[]{:S(2)}) %collective-permute-start.11) | collective-permute-done | bytes 131104 | tf_op jit(solution)/shard_map/ppermute | solution.py:32
  89.4 4.4 %collective-permute-done.13.refs_7_ = bf16[8,32,256]{2,1,0:T(8,128)(2,1)S(1)} collective-permute-done((bf16[8,32,256]{2,1,0:T(8,128)(2,1)S(1)}, bf16[8,32,256]{2,1,0:T(8,128)(2,1)S(1)}, u32[]{:S(2)}, u32[]{:S(2)}) %collective-permute-start.13) | collective-permute-done | bytes 131104 | tf_op jit(solution)/shard_map/ppermute | solution.py:32
  94.5 2.1 %shard_map.107 = bf16[8,32,256]{2,1,0:T(8,128)(2,1)} custom-call(bf16[8,32,256]{2,1,0:T(8,128)(2,1)} %copy-done, bf16[8,32,256]{2,1,0:T(8,128)(2,1)} %copy-done.2, bf16[8,32,256]{2,1,0:T(8,128)(2,1)} %copy-done.3, bf16[8,32,256]{2,1,0:T(8,128)(2,1)} %copy-done.4, bf16[8,32,256]{2,1,0:T(8,128)(2,1)} %copy-done.5, bf16[8,32,256]{2,1,0:T(8,128)(2,1)} %copy-done.6, ...), custom_call_target="tpu_custom_call" | custom-call | flops 524288 | bytes 1179648 | tf_op jit(solution)/shard_map/pallas_call | solution.py:260
  96.5 11.0 %all_to_all.20.in_ref = bf16[8,32,256]{2,1,0:T(8,128)(2,1)} all-to-all(bf16[8,32,256]{2,1,0:T(8,128)(2,1)} %shard_map.107), channel_id=1, replica_groups=mesh['y'=4,'xl'=2,'c'=2,'xh'=2,'z'=8] {'xl','c','xh'}, dimensions={0} | all-to-all | bytes 262144 | tf_op jit(solution)/shard_map/all_to_all | solution.py:36
  107.5 3.5 %all-to-all-start.2 = ((bf16[8,32,1024]{2,1,0:T(8,128)(2,1)}), bf16[8,32,1024]{2,1,0:T(8,128)(2,1)S(1)}, u32[]{:S(2)}, u32[]{:S(2)}) async-start(bf16[8,32,1024]{2,1,0:T(8,128)(2,1)} %get-tuple-element.14), calls=%async_computation.2 | async-start | bytes 1048576 | tf_op jit(solution)/shard_map/all_to_all | solution.py:36
  112.6 8.1 %all-to-all-done.2.in_ref = bf16[8,32,1024]{2,1,0:T(8,128)(2,1)S(1)} async-done(((bf16[8,32,1024]{2,1,0:T(8,128)(2,1)}), bf16[8,32,1024]{2,1,0:T(8,128)(2,1)S(1)}, u32[]{:S(2)}, u32[]{:S(2)}) %all-to-all-start.2) | async-done | bytes 524320 | tf_op jit(solution)/shard_map/all_to_all | solution.py:36
  121.5 4.7 %shard_map.106 = bf16[32,8192]{1,0:T(8,128)(2,1)} custom-call(bf16[8,32,1024]{2,1,0:T(8,128)(2,1)} %copy-done.1), custom_call_target="tpu_custom_call" | custom-call | bytes 1048576 | tf_op jit(solution)/shard_map/pallas_call | solution.py:252
  (62 shorter events, 12.6 us)
Async XLA Ops:
  2.2 13.8 %all-to-all-start.1 = ((bf16[8,32,256]{2,1,0:T(8,128)(2,1)}), bf16[8,32,256]{2,1,0:T(8,128)(2,1)S(1)}, u32[]{:S(2)}, u32[]{:S(2)}) async-start(bf16[8,32,256]{2,1,0:T(8,128)(2,1)} %shard_map.104), calls=%async_computation.1 | async-start | bytes 262144 | tf_op jit(solution)/shard_map/all_to_all | solution.py:36
  16.0 7.0 %copy-start.9 = (s32[7]{0:T(128)S(1)}, s32[7]{0:T(128)}, u32[]{:S(2)}) copy-start(s32[7]{0:T(128)} %param.14) | copy-start | bytes 88
  16.0 27.8 %all-to-all-start = ((bf16[8,80,1024]{2,1,0:T(8,128)(2,1)}), bf16[8,80,1024]{2,1,0:T(8,128)(2,1)S(1)}, u32[]{:S(2)}, u32[]{:S(2)}) async-start(bf16[8,80,1024]{2,1,0:T(8,128)(2,1)} %shard_map.103), calls=%async_computation | async-start | bytes 2621440 | tf_op jit(solution)/shard_map/all_to_all | solution.py:36
  21.0 10.0 %collective-permute-start = (bf16[8,32,256]{2,1,0:T(8,128)(2,1)S(1)}, bf16[8,32,256]{2,1,0:T(8,128)(2,1)S(1)}, u32[]{:S(2)}, u32[]{:S(2)}) collective-permute-start(bf16[8,32,256]{2,1,0:T(8,128)(2,1)S(1)} %all-to-all-done.1.refs_0_), channel_id=1, source_target_pairs={{0,1},{1,2},{2,3},{3,4},{4,5},{5,6},{6,7},{7,0},{8,9},{9,10},{10,1... | collective-permute-start | bytes 393224 | tf_op jit(solution)/shard_map/ppermute | solution.py:32
  23.1 7.9 %collective-permute-start.1 = (bf16[8,32,256]{2,1,0:T(8,128)(2,1)S(1)}, bf16[8,32,256]{2,1,0:T(8,128)(2,1)S(1)}, u32[]{:S(2)}, u32[]{:S(2)}) collective-permute-start(bf16[8,32,256]{2,1,0:T(8,128)(2,1)S(1)} %all-to-all-done.1.refs_0_), channel_id=1, source_target_pairs={{0,7},{1,0},{2,1},{3,2},{4,3},{5,4},{6,5},{7,6},{8,15},{9,8},{10,9... | collective-permute-start | bytes 393224 | tf_op jit(solution)/shard_map/ppermute | solution.py:32
  31.0 6.5 %collective-permute-start.2 = (bf16[8,32,256]{2,1,0:T(8,128)(2,1)S(1)}, bf16[8,32,256]{2,1,0:T(8,128)(2,1)S(1)}, u32[]{:S(2)}, u32[]{:S(2)}) collective-permute-start(bf16[8,32,256]{2,1,0:T(8,128)(2,1)S(1)} %collective-permute-done.refs_1_), channel_id=1, source_target_pairs={{0,1},{1,2},{2,3},{3,4},{4,5},{5,6},{6,7},{7,0},{8,9},{9,10},{10,1... | collective-permute-start | bytes 393224 | tf_op jit(solution)/shard_map/ppermute | solution.py:32
  31.0 6.7 %collective-permute-start.3 = (bf16[8,32,256]{2,1,0:T(8,128)(2,1)S(1)}, bf16[8,32,256]{2,1,0:T(8,128)(2,1)S(1)}, u32[]{:S(2)}, u32[]{:S(2)}) collective-permute-start(bf16[8,32,256]{2,1,0:T(8,128)(2,1)S(1)} %collective-permute-done.1.refs_2_), channel_id=1, source_target_pairs={{0,7},{1,0},{2,1},{3,2},{4,3},{5,4},{6,5},{7,6},{8,15},{9,8},{10,9... | collective-permute-start | bytes 393224 | tf_op jit(solution)/shard_map/ppermute | solution.py:32
  37.6 6.2 %collective-permute-start.4 = (bf16[8,32,256]{2,1,0:T(8,128)(2,1)S(1)}, bf16[8,32,256]{2,1,0:T(8,128)(2,1)S(1)}, u32[]{:S(2)}, u32[]{:S(2)}) collective-permute-start(bf16[8,32,256]{2,1,0:T(8,128)(2,1)S(1)} %collective-permute-done.2.refs_3_), channel_id=1, source_target_pairs={{0,1},{1,2},{2,3},{3,4},{4,5},{5,6},{6,7},{7,0},{8,9},{9,10},{10,1... | collective-permute-start | bytes 393224 | tf_op jit(solution)/shard_map/ppermute | solution.py:32
  37.7 6.0 %collective-permute-start.5 = (bf16[8,32,256]{2,1,0:T(8,128)(2,1)S(1)}, bf16[8,32,256]{2,1,0:T(8,128)(2,1)S(1)}, u32[]{:S(2)}, u32[]{:S(2)}) collective-permute-start(bf16[8,32,256]{2,1,0:T(8,128)(2,1)S(1)} %collective-permute-done.3.refs_4_), channel_id=1, source_target_pairs={{0,7},{1,0},{2,1},{3,2},{4,3},{5,4},{6,5},{7,6},{8,15},{9,8},{10,9... | collective-permute-start | bytes 393224 | tf_op jit(solution)/shard_map/ppermute | solution.py:32
  43.7 6.2 %collective-permute-start.6 = (bf16[8,32,256]{2,1,0:T(8,128)(2,1)S(1)}, bf16[8,32,256]{2,1,0:T(8,128)(2,1)S(1)}, u32[]{:S(2)}, u32[]{:S(2)}) collective-permute-start(bf16[8,32,256]{2,1,0:T(8,128)(2,1)S(1)} %collective-permute-done.4.refs_5_), channel_id=1, source_target_pairs={{0,1},{1,2},{2,3},{3,4},{4,5},{5,6},{6,7},{7,0},{8,9},{9,10},{10,1... | collective-permute-start | bytes 393224 | tf_op jit(solution)/shard_map/ppermute | solution.py:32
  69.7 8.2 %collective-permute-start.7 = (bf16[8,32,256]{2,1,0:T(8,128)(2,1)S(1)}, bf16[8,32,256]{2,1,0:T(8,128)(2,1)S(1)}, u32[]{:S(2)}, u32[]{:S(2)}) collective-permute-start(bf16[8,32,256]{2,1,0:T(8,128)(2,1)S(1)} %get-tuple-element.16), channel_id=1, source_target_pairs={{0,7},{1,0},{2,1},{3,2},{4,3},{5,4},{6,5},{7,6},{8,15},{9,8},{10,9... | collective-permute-start | bytes 393224 | tf_op jit(solution)/shard_map/ppermute | solution.py:32
  69.7 10.2 %collective-permute-start.8 = (bf16[8,32,256]{2,1,0:T(8,128)(2,1)S(1)}, bf16[8,32,256]{2,1,0:T(8,128)(2,1)S(1)}, u32[]{:S(2)}, u32[]{:S(2)}) collective-permute-start(bf16[8,32,256]{2,1,0:T(8,128)(2,1)S(1)} %get-tuple-element.17), channel_id=1, source_target_pairs={{0,1},{1,2},{2,3},{3,4},{4,5},{5,6},{6,7},{7,0},{8,9},{9,10},{10,1... | collective-permute-start | bytes 393224 | tf_op jit(solution)/shard_map/ppermute | solution.py:32
  71.7 11.0 %collective-permute-start.9 = (bf16[8,32,256]{2,1,0:T(8,128)(2,1)S(1)}, bf16[8,32,256]{2,1,0:T(8,128)(2,1)S(1)}, u32[]{:S(2)}, u32[]{:S(2)}) collective-permute-start(bf16[8,32,256]{2,1,0:T(8,128)(2,1)S(1)} %get-tuple-element.18), channel_id=1, source_target_pairs={{0,6},{1,7},{2,0},{3,1},{4,2},{5,3},{6,4},{7,5},{8,14},{9,15},{10,... | collective-permute-start | bytes 393224 | tf_op jit(solution)/shard_map/ppermute | solution.py:32
  71.7 13.8 %collective-permute-start.10 = (bf16[8,32,256]{2,1,0:T(8,128)(2,1)S(1)}, bf16[8,32,256]{2,1,0:T(8,128)(2,1)S(1)}, u32[]{:S(2)}, u32[]{:S(2)}) collective-permute-start(bf16[8,32,256]{2,1,0:T(8,128)(2,1)S(1)} %get-tuple-element.19), channel_id=1, source_target_pairs={{0,2},{1,3},{2,4},{3,5},{4,6},{5,7},{6,0},{7,1},{8,10},{9,11},{10,... | collective-permute-start | bytes 393224 | tf_op jit(solution)/shard_map/ppermute | solution.py:32
  74.7 14.7 %collective-permute-start.11 = (bf16[8,32,256]{2,1,0:T(8,128)(2,1)S(1)}, bf16[8,32,256]{2,1,0:T(8,128)(2,1)S(1)}, u32[]{:S(2)}, u32[]{:S(2)}) collective-permute-start(bf16[8,32,256]{2,1,0:T(8,128)(2,1)S(1)} %get-tuple-element.20), channel_id=1, source_target_pairs={{0,5},{1,6},{2,7},{3,0},{4,1},{5,2},{6,3},{7,4},{8,13},{9,14},{10,... | collective-permute-start | bytes 393224 | tf_op jit(solution)/shard_map/ppermute | solution.py:32
  77.9 15.9 %copy-start.2 = (bf16[8,32,256]{2,1,0:T(8,128)(2,1)}, bf16[8,32,256]{2,1,0:T(8,128)(2,1)S(1)}, u32[]{:S(2)}) copy-start(bf16[8,32,256]{2,1,0:T(8,128)(2,1)S(1)} %collective-permute-done.7.refs_1_) | copy-start | bytes 393220
  77.9 11.4 %collective-permute-start.12 = (bf16[8,32,256]{2,1,0:T(8,128)(2,1)S(1)}, bf16[8,32,256]{2,1,0:T(8,128)(2,1)S(1)}, u32[]{:S(2)}, u32[]{:S(2)}) collective-permute-start(bf16[8,32,256]{2,1,0:T(8,128)(2,1)S(1)} %get-tuple-element.21), channel_id=1, source_target_pairs={{0,3},{1,4},{2,5},{3,6},{4,7},{5,0},{6,1},{7,2},{8,11},{9,12},{10,... | collective-permute-start | bytes 393224 | tf_op jit(solution)/shard_map/ppermute | solution.py:32
  79.9 13.9 %copy-start.3 = (bf16[8,32,256]{2,1,0:T(8,128)(2,1)}, bf16[8,32,256]{2,1,0:T(8,128)(2,1)S(1)}, u32[]{:S(2)}) copy-start(bf16[8,32,256]{2,1,0:T(8,128)(2,1)S(1)} %collective-permute-done.8.refs_2_) | copy-start | bytes 393220
  79.9 13.9 %collective-permute-start.13 = (bf16[8,32,256]{2,1,0:T(8,128)(2,1)S(1)}, bf16[8,32,256]{2,1,0:T(8,128)(2,1)S(1)}, u32[]{:S(2)}, u32[]{:S(2)}) collective-permute-start(bf16[8,32,256]{2,1,0:T(8,128)(2,1)S(1)} %get-tuple-element.22), channel_id=1, source_target_pairs={{0,4},{1,5},{2,6},{3,7},{4,0},{5,1},{6,2},{7,3},{8,12},{9,13},{10,... | collective-permute-start | bytes 393224 | tf_op jit(solution)/shard_map/ppermute | solution.py:32
  82.8 11.0 %copy-start.4 = (bf16[8,32,256]{2,1,0:T(8,128)(2,1)}, bf16[8,32,256]{2,1,0:T(8,128)(2,1)S(1)}, u32[]{:S(2)}) copy-start(bf16[8,32,256]{2,1,0:T(8,128)(2,1)S(1)} %collective-permute-done.9.refs_3_) | copy-start | bytes 393220
  85.6 8.2 %copy-start.5 = (bf16[8,32,256]{2,1,0:T(8,128)(2,1)}, bf16[8,32,256]{2,1,0:T(8,128)(2,1)S(1)}, u32[]{:S(2)}) copy-start(bf16[8,32,256]{2,1,0:T(8,128)(2,1)S(1)} %collective-permute-done.10.refs_4_) | copy-start | bytes 393220
  89.4 4.5 %copy-start.6 = (bf16[8,32,256]{2,1,0:T(8,128)(2,1)}, bf16[8,32,256]{2,1,0:T(8,128)(2,1)S(1)}, u32[]{:S(2)}) copy-start(bf16[8,32,256]{2,1,0:T(8,128)(2,1)S(1)} %collective-permute-done.11.refs_5_) | copy-start | bytes 393220
  89.4 4.5 %copy-start.7 = (bf16[8,32,256]{2,1,0:T(8,128)(2,1)}, bf16[8,32,256]{2,1,0:T(8,128)(2,1)S(1)}, u32[]{:S(2)}) copy-start(bf16[8,32,256]{2,1,0:T(8,128)(2,1)S(1)} %collective-permute-done.12.refs_6_) | copy-start | bytes 393220
  107.5 13.2 %all-to-all-start.2 = ((bf16[8,32,1024]{2,1,0:T(8,128)(2,1)}), bf16[8,32,1024]{2,1,0:T(8,128)(2,1)S(1)}, u32[]{:S(2)}, u32[]{:S(2)}) async-start(bf16[8,32,1024]{2,1,0:T(8,128)(2,1)} %get-tuple-element.14), calls=%async_computation.2 | async-start | bytes 1048576 | tf_op jit(solution)/shard_map/all_to_all | solution.py:36
  (3 other events, 2.1 us)

commit v3 on v2

--- a/solution.py
+++ b/solution.py
@@ -22,6 +22,7 @@
 SCALE = 1.0 / math.sqrt(HD)
 LOG2E = math.log2(math.e)
 BIG = 1e30
+EXTRA = 8
 HEADS = ("xl", "c", "xh")
 F32 = jnp.float32
 BF16 = jnp.bfloat16
@@ -42,11 +43,52 @@
         out_ref[a, :, HD:] = v_ref[:, a * HD : (a + 1) * HD]
 
 
-def pack_queries_kernel(q_ref, g_ref, extra_ref, out_ref):
-    out_ref[0, :TOK, :] = q_ref[...]
-    out_ref[0, TOK : 2 * TOK, :] = g_ref[...]
-    out_ref[0, 2 * TOK :, :ROWS] = extra_ref[0]
-    out_ref[0, 2 * TOK :, ROWS:] = jnp.zeros((16, GROUP * HD - ROWS), BF16)
+def split(value):
+    high = value.astype(BF16)
+    return high, (value - high.astype(F32)).astype(BF16)
+
+
+def pack_queries_kernel(place_ref, keep_ref, q_ref, g_ref, o_ref, lse_ref, out_ref):
+    ones = jnp.ones((EXTRA, 2 * HD), BF16)
+    lane = lax.broadcasted_iota(jnp.int32, (TOK, ROWS), 1)
+    spread = (lane % TOK == lax.broadcasted_iota(jnp.int32, (TOK, ROWS), 0)).astype(F32).astype(BF16)
+    head_lane = lax.broadcasted_iota(jnp.int32, (GROUP, ROWS), 1) // TOK
+    own_head = head_lane == lax.broadcasted_iota(jnp.int32, (GROUP, ROWS), 0)
+    row = lax.broadcasted_iota(jnp.int32, (EXTRA, ROWS), 0)
+    flag_lane = lax.broadcasted_iota(jnp.int32, (1, ROWS), 1)
+    flags = jnp.zeros((1, ROWS), F32)
+    for d in range(keep_ref.shape[1]):
+        flags = jnp.where(flag_lane == d, keep_ref[place_ref[0], d].astype(F32), flags)
+    high, low = split(lse_ref[...])
+    low, lower = low, split(lse_ref[...] - high.astype(F32) - low.astype(F32))[0]
+    lse_all = sum(jnp.dot(p, spread, preferred_element_type=F32) for p in (high, low, lower))
+    for a in range(AS):
+        columns = slice(a * GROUP * HD, (a + 1) * GROUP * HD)
+        q_block, g_block = q_ref[:, columns], g_ref[:, columns]
+        out_ref[a, :TOK, :] = q_block
+        out_ref[a, TOK : 2 * TOK, :] = g_block
+        product = g_block.astype(F32) * o_ref[:, columns].astype(F32)
+        high, low = split(product)
+        stacked = jnp.concatenate(
+            [
+                jnp.concatenate([p[:, h * HD : (h + 1) * HD] for h in range(GROUP)], axis=0)
+                for p in (high, low)
+            ],
+            axis=1,
+        )
+        delta = lax.dot_general(
+            ones, stacked, (((1,), (1,)), ((), ())), preferred_element_type=F32
+        )[:1]
+        lse = jnp.sum(
+            jnp.where(own_head, lse_all[a * GROUP : (a + 1) * GROUP], 0.0), axis=0, keepdims=True
+        )
+        lse_high, lse_low = split(lse)
+        delta_high, delta_low = split(delta)
+        extra = jnp.zeros((EXTRA, ROWS), F32)
+        for n, part in enumerate((lse_high, lse_low, delta_high, delta_low, flags)):
+            extra = jnp.where(row == n, part.astype(F32), extra)
+        out_ref[a, 2 * TOK :, :ROWS] = extra.astype(BF16)
+        out_ref[a, 2 * TOK :, ROWS:] = jnp.zeros((EXTRA, GROUP * HD - ROWS), BF16)
 
 
 def attention_kernel(keep_ref, span_ref, z_ref, message_ref, start_ref, *refs):
@@ -144,7 +186,8 @@
 
 
 def unpack_queries_kernel(in_ref, out_ref):
-    out_ref[...] = in_ref[0]
+    for a in range(AS):
+        out_ref[:, a * GROUP * HD : (a + 1) * GROUP * HD] = in_ref[a]
 
 
 def unpack_kv_kernel(in_ref, dk_ref, dv_ref):
@@ -171,34 +214,21 @@
         out_shape=jax.ShapeDtypeStruct((AS, TOK, 2 * HD), BF16),
         in_specs=[in_vmem(), in_vmem()],
         out_specs=in_vmem(),
+        compiler_params=pltpu.CompilerParams(vmem_limit_bytes=4 * 2**20),
         cost_estimate=pl.CostEstimate(flops=0, bytes_accessed=262144, transcendentals=0),
     )(key, value)
     kv_own = exchange(kv_send)
 
-    delta = jnp.sum(
-        out_grad.reshape(TOK, -1, HD).astype(F32) * output.reshape(TOK, -1, HD).astype(F32), axis=2
-    )
-    both = jnp.stack([lse * LOG2E, delta])
-    high = lax.reduce_precision(both, 8, 7)
-    parts = jnp.stack([high, both - high], axis=1).astype(BF16)
-    parts = parts.reshape(4, TOK, AS, GROUP).transpose(2, 0, 3, 1).reshape(AS, 4, ROWS)
-    local_block = lax.axis_index("xh") * 2 + z // 4
-    keep_row = lax.dynamic_slice_in_dim(block_keep, local_block, 1, 0).astype(BF16)
-    reach = keep_row.shape[1]
-    keep_row = jnp.broadcast_to(jnp.pad(keep_row, ((0, 0), (0, ROWS - reach)))[None], (AS, 1, ROWS))
-    extra = jnp.concatenate([parts, keep_row, jnp.zeros((AS, 11, ROWS), BF16)], axis=1)
+    place = (lax.axis_index("xh") * 2 + z // 4).astype(i32).reshape(1)
+    reach = block_keep.shape[1]
     message_send = pl.pallas_call(
         pack_queries_kernel,
-        grid=(AS,),
-        out_shape=jax.ShapeDtypeStruct((AS, 2 * TOK + 16, columns), BF16),
-        in_specs=[
-            pl.BlockSpec((TOK, columns), lambda a: (0, a)),
-            pl.BlockSpec((TOK, columns), lambda a: (0, a)),
-            pl.BlockSpec((1, 16, ROWS), lambda a: (a, 0, 0)),
-        ],
-        out_specs=pl.BlockSpec((1, 2 * TOK + 16, columns), lambda a: (a, 0, 0)),
-        cost_estimate=pl.CostEstimate(flops=0, bytes_accessed=2600000, transcendentals=0),
-    )(query, out_grad, extra)
+        out_shape=jax.ShapeDtypeStruct((AS, 2 * TOK + EXTRA, columns), BF16),
+        in_specs=[in_smem(), in_smem()] + [in_vmem()] * 4,
+        out_specs=in_vmem(),
+        compiler_params=pltpu.CompilerParams(vmem_limit_bytes=16 * 2**20),
+        cost_estimate=pl.CostEstimate(flops=67108864, bytes_accessed=2800000, transcendentals=0),
+    )(place, block_keep, query, out_grad, output, lse.T * LOG2E)
     message = exchange(message_send)
 
     pieces = {0: kv_own}
@@ -249,12 +279,13 @@
         partials[r] if off == 0 else along_z(partials[r], -off) for r, off in enumerate(OFFSETS)
     ]
     dq_back = exchange(dq)
+    returned, dq_back = lax.optimization_barrier((returned, dq_back))
     query_grad = pl.pallas_call(
         unpack_queries_kernel,
-        grid=(AS,),
         out_shape=jax.ShapeDtypeStruct((TOK, AS * columns), BF16),
-        in_specs=[pl.BlockSpec((1, TOK, columns), lambda a: (a, 0, 0))],
-        out_specs=pl.BlockSpec((TOK, columns), lambda a: (0, a)),
+        in_specs=[in_vmem()],
+        out_specs=in_vmem(),
+        compiler_params=pltpu.CompilerParams(vmem_limit_bytes=4 * 2**20),
         cost_estimate=pl.CostEstimate(flops=0, bytes_accessed=1048576, transcendentals=0),
     )(dq_back)
     summed = pl.pallas_call(
@@ -262,6 +293,7 @@
         out_shape=piece_shape,
         in_specs=[in_vmem()] * ZS,
         out_specs=in_vmem(),
+        compiler_params=pltpu.CompilerParams(vmem_limit_bytes=4 * 2**20),
         cost_estimate=pl.CostEstimate(flops=524288, bytes_accessed=1179648, transcendentals=0),
     )(*returned)
     grads = exchange(summed)
@@ -271,6 +303,7 @@
         out_shape=[half, half],
         in_specs=[in_vmem()],
         out_specs=[in_vmem(), in_vmem()],
+        compiler_params=pltpu.CompilerParams(vmem_limit_bytes=4 * 2**20),
         cost_estimate=pl.CostEstimate(flops=0, bytes_accessed=262144, transcendentals=0),
     )(grads)
     return (query_grad, key_grad, value_grad)

time: 128 us -> 112 us (0.88)
  the two profiles are of different devices: /device:TPU:8 before, /device:TPU:57 now
where the time goes in v3:
time: 112 us; the launch traced here: 111 us
  starting transfers between devices  44 us (39%)
  waiting for transfers between devices  35.3 us (32%)
  Pallas kernels  24.2 us (22%)
  local copies, waits for them, and re-layouts  6.35 us (6%)
    ppermute x14, waiting for transfers between devices, along_z(): return lax.ppermute(value, 'z', [(i, (i + by) % ZS) for i in range(ZS)])  30.8 us
    all_to_all x4, starting transfers between devices, exchange(): return lax.all_to_all(value, HEADS, split_axis=0, concat_axis=0, tiled=True)  22.6 us
    ppermute x14, starting transfers between devices, along_z(): return lax.ppermute(value, 'z', [(i, (i + by) % ZS) for i in range(ZS)])  21.4 us
    pallas_call x1, Pallas kernels, shards(): pl.pallas_call(attention_kernel, out_shape=[jax.ShapeDtypeStruct((AS, TOK...  19.2 us
    unnamed x15, local copies, waits for them, and re-layouts  6.27 us
    all_to_all x4, waiting for transfers between devices, exchange(): return lax.all_to_all(value, HEADS, split_axis=0, concat_axis=0, tiled=True)  4.45 us
  transfers between devices with their start and end apart: 18, of which 12 were waited for; matrix products, arithmetic and copies ran while one was open for 1% of the time, Pallas kernels for 3%

profile of v3, /device:TPU:57, one launch (start us, length us, event | category | flops | bytes accessed | tf_op | source)
XLA Modules:
  0.0 110.9 jit_solution(8125003586258286264)
XLA Ops:
  3.0 5.0 %all-to-all-start.1 = ((bf16[8,32,256]{2,1,0:T(8,128)(2,1)}), bf16[8,32,256]{2,1,0:T(8,128)(2,1)S(1)}, u32[]{:S(2)}, u32[]{:S(2)}) async-start(bf16[8,32,256]{2,1,0:T(8,128)(2,1)} %shard_map.104), calls=%async_computation.1 | async-start | bytes 262144 | tf_op jit(solution)/shard_map/all_to_all | solution.py:37
  12.6 2.1 %shard_map.103 = bf16[8,72,1024]{2,1,0:T(8,128)(2,1)} custom-call(s32[1]{0:T(128)} %bitcast.place_ref, s32[4,17]{1,0:T(4,128)S(1)} %copy-done.5, bf16[32,8192]{1,0:T(8,128)(2,1)S(1)} %copy-done, bf16[32,8192]{1,0:T(8,128)(2,1)S(1)} %copy-done.1, bf16[32,8192]{1,0:T(8,128)(2,1)S(1)} %copy-done.2, f32[64,32]{1,0:T(8,128)S(1)} %multiply_bitcast_fusion.lse_ref), custom_call_target="tpu_custom_call" | custom-call | flops 67108864 | bytes 2800000 | tf_op jit(solution)/shard_map/pallas_call | solution.py:224
  14.7 4.8 %all-to-all-start = ((bf16[8,72,1024]{2,1,0:T(8,128)(2,1)}), bf16[8,72,1024]{2,1,0:T(8,128)(2,1)S(1)}, u32[]{:S(2)}, u32[]{:S(2)}) async-start(bf16[8,72,1024]{2,1,0:T(8,128)(2,1)} %shard_map.103), calls=%async_computation | async-start | bytes 2359296 | tf_op jit(solution)/shard_map/all_to_all | solution.py:37
  19.6 1.6 %collective-permute-start = (bf16[8,32,256]{2,1,0:T(8,128)(2,1)S(1)}, bf16[8,32,256]{2,1,0:T(8,128)(2,1)S(1)}, u32[]{:S(2)}, u32[]{:S(2)}) collective-permute-start(bf16[8,32,256]{2,1,0:T(8,128)(2,1)S(1)} %all-to-all-done.1.refs_0_), channel_id=1, source_target_pairs={{0,1},{1,2},{2,3},{3,4},{4,5},{5,6},{6,7},{7,0},{8,9},{9,10},{10,1... | collective-permute-start | bytes 393224 | tf_op jit(solution)/shard_map/ppermute | solution.py:33
  21.5 3.2 %collective-permute-done.refs_1_ = bf16[8,32,256]{2,1,0:T(8,128)(2,1)S(1)} collective-permute-done((bf16[8,32,256]{2,1,0:T(8,128)(2,1)S(1)}, bf16[8,32,256]{2,1,0:T(8,128)(2,1)S(1)}, u32[]{:S(2)}, u32[]{:S(2)}) %collective-permute-start) | collective-permute-done | bytes 131104 | tf_op jit(solution)/shard_map/ppermute | solution.py:33
  24.7 1.6 %collective-permute-start.2 = (bf16[8,32,256]{2,1,0:T(8,128)(2,1)S(1)}, bf16[8,32,256]{2,1,0:T(8,128)(2,1)S(1)}, u32[]{:S(2)}, u32[]{:S(2)}) collective-permute-start(bf16[8,32,256]{2,1,0:T(8,128)(2,1)S(1)} %collective-permute-done.refs_1_), channel_id=1, source_target_pairs={{0,1},{1,2},{2,3},{3,4},{4,5},{5,6},{6,7},{7,0},{8,9},{9,10},{10,1... | collective-permute-start | bytes 393224 | tf_op jit(solution)/shard_map/ppermute | solution.py:33
  26.7 2.3 %collective-permute-start.3 = (bf16[8,32,256]{2,1,0:T(8,128)(2,1)S(1)}, bf16[8,32,256]{2,1,0:T(8,128)(2,1)S(1)}, u32[]{:S(2)}, u32[]{:S(2)}) collective-permute-start(bf16[8,32,256]{2,1,0:T(8,128)(2,1)S(1)} %collective-permute-done.1.refs_2_), channel_id=1, source_target_pairs={{0,7},{1,0},{2,1},{3,2},{4,3},{5,4},{6,5},{7,6},{8,15},{9,8},{10,9... | collective-permute-start | bytes 393224 | tf_op jit(solution)/shard_map/ppermute | solution.py:33
  28.9 3.2 %collective-permute-done.2.refs_3_ = bf16[8,32,256]{2,1,0:T(8,128)(2,1)S(1)} collective-permute-done((bf16[8,32,256]{2,1,0:T(8,128)(2,1)S(1)}, bf16[8,32,256]{2,1,0:T(8,128)(2,1)S(1)}, u32[]{:S(2)}, u32[]{:S(2)}) %collective-permute-start.2) | collective-permute-done | bytes 131104 | tf_op jit(solution)/shard_map/ppermute | solution.py:33
  32.7 2.0 %collective-permute-start.5 = (bf16[8,32,256]{2,1,0:T(8,128)(2,1)S(1)}, bf16[8,32,256]{2,1,0:T(8,128)(2,1)S(1)}, u32[]{:S(2)}, u32[]{:S(2)}) collective-permute-start(bf16[8,32,256]{2,1,0:T(8,128)(2,1)S(1)} %collective-permute-done.3.refs_4_), channel_id=1, source_target_pairs={{0,7},{1,0},{2,1},{3,2},{4,3},{5,4},{6,5},{7,6},{8,15},{9,8},{10,9... | collective-permute-start | bytes 393224 | tf_op jit(solution)/shard_map/ppermute | solution.py:33
  34.7 2.2 %collective-permute-done.4.refs_5_ = bf16[8,32,256]{2,1,0:T(8,128)(2,1)S(1)} collective-permute-done((bf16[8,32,256]{2,1,0:T(8,128)(2,1)S(1)}, bf16[8,32,256]{2,1,0:T(8,128)(2,1)S(1)}, u32[]{:S(2)}, u32[]{:S(2)}) %collective-permute-start.4) | collective-permute-done | bytes 131104 | tf_op jit(solution)/shard_map/ppermute | solution.py:33
  37.5 4.4 %collective-permute-done.6.refs_7_ = bf16[8,32,256]{2,1,0:T(8,128)(2,1)S(1)} collective-permute-done((bf16[8,32,256]{2,1,0:T(8,128)(2,1)S(1)}, bf16[8,32,256]{2,1,0:T(8,128)(2,1)S(1)}, u32[]{:S(2)}, u32[]{:S(2)}) %collective-permute-start.6) | collective-permute-done | bytes 131104 | tf_op jit(solution)/shard_map/ppermute | solution.py:33
  41.9 19.2 %shard_map.105 = (bf16[8,32,1024]{2,1,0:T(8,128)(2,1)}, bf16[8,32,256]{2,1,0:T(8,128)(2,1)S(1)}, bf16[8,32,256]{2,1,0:T(8,128)(2,1)S(1)}, bf16[8,32,256]{2,1,0:T...) custom-call(s32[8,17]{1,0:T(8,128)S(1)} %bitcast.5, ...), custom_call_target="tpu_custom_call" | custom-call | flops 3000000000 | bytes 4000000 | tf_op jit(solution)/shard_map/pallas_call | solution.py:257
  61.1 7.6 %all-to-all-start.2 = ((bf16[8,32,1024]{2,1,0:T(8,128)(2,1)}), bf16[8,32,1024]{2,1,0:T(8,128)(2,1)S(1)}, u32[]{:S(2)}, u32[]{:S(2)}) async-start(bf16[8,32,1024]{2,1,0:T(8,128)(2,1)} %get-tuple-element.31), calls=%async_computation.2 | async-start | bytes 1048576 | tf_op jit(solution)/shard_map/all_to_all | solution.py:37
  68.7 2.9 %collective-permute-start.7 = (bf16[8,32,256]{2,1,0:T(8,128)(2,1)S(1)}, bf16[8,32,256]{2,1,0:T(8,128)(2,1)S(1)}, u32[]{:S(2)}, u32[]{:S(2)}) collective-permute-start(bf16[8,32,256]{2,1,0:T(8,128)(2,1)S(1)} %get-tuple-element.24), channel_id=1, source_target_pairs={{0,7},{1,0},{2,1},{3,2},{4,3},{5,4},{6,5},{7,6},{8,15},{9,8},{10,9... | collective-permute-start | bytes 393224 | tf_op jit(solution)/shard_map/ppermute | solution.py:33
  71.6 2.4 %collective-permute-start.9 = (bf16[8,32,256]{2,1,0:T(8,128)(2,1)S(1)}, bf16[8,32,256]{2,1,0:T(8,128)(2,1)S(1)}, u32[]{:S(2)}, u32[]{:S(2)}) collective-permute-start(bf16[8,32,256]{2,1,0:T(8,128)(2,1)S(1)} %get-tuple-element.26), channel_id=1, source_target_pairs={{0,6},{1,7},{2,0},{3,1},{4,2},{5,3},{6,4},{7,5},{8,14},{9,15},{10,... | collective-permute-start | bytes 393224 | tf_op jit(solution)/shard_map/ppermute | solution.py:33
  74.7 2.3 %collective-permute-start.11 = (bf16[8,32,256]{2,1,0:T(8,128)(2,1)S(1)}, bf16[8,32,256]{2,1,0:T(8,128)(2,1)S(1)}, u32[]{:S(2)}, u32[]{:S(2)}) collective-permute-start(bf16[8,32,256]{2,1,0:T(8,128)(2,1)S(1)} %get-tuple-element.28), channel_id=1, source_target_pairs={{0,5},{1,6},{2,7},{3,0},{4,1},{5,2},{6,3},{7,4},{8,13},{9,14},{10,... | collective-permute-start | bytes 393224 | tf_op jit(solution)/shard_map/ppermute | solution.py:33
  77.1 2.5 %collective-permute-start.12 = (bf16[8,32,256]{2,1,0:T(8,128)(2,1)S(1)}, bf16[8,32,256]{2,1,0:T(8,128)(2,1)S(1)}, u32[]{:S(2)}, u32[]{:S(2)}) collective-permute-start(bf16[8,32,256]{2,1,0:T(8,128)(2,1)S(1)} %get-tuple-element.29), channel_id=1, source_target_pairs={{0,3},{1,4},{2,5},{3,6},{4,7},{5,0},{6,1},{7,2},{8,11},{9,12},{10,... | collective-permute-start | bytes 393224 | tf_op jit(solution)/shard_map/ppermute | solution.py:33
  79.5 2.9 %collective-permute-start.13 = (bf16[8,32,256]{2,1,0:T(8,128)(2,1)S(1)}, bf16[8,32,256]{2,1,0:T(8,128)(2,1)S(1)}, u32[]{:S(2)}, u32[]{:S(2)}) collective-permute-start(bf16[8,32,256]{2,1,0:T(8,128)(2,1)S(1)} %get-tuple-element.30), channel_id=1, source_target_pairs={{0,4},{1,5},{2,6},{3,7},{4,0},{5,1},{6,2},{7,3},{8,12},{9,13},{10,... | collective-permute-start | bytes 393224 | tf_op jit(solution)/shard_map/ppermute | solution.py:33
  82.5 2.1 %collective-permute-done.10.refs_4_ = bf16[8,32,256]{2,1,0:T(8,128)(2,1)S(1)} collective-permute-done((bf16[8,32,256]{2,1,0:T(8,128)(2,1)S(1)}, bf16[8,32,256]{2,1,0:T(8,128)(2,1)S(1)}, u32[]{:S(2)}, u32[]{:S(2)}) %collective-permute-start.10) | collective-permute-done | bytes 131104 | tf_op jit(solution)/shard_map/ppermute | solution.py:33
  84.5 5.0 %collective-permute-done.11.refs_5_ = bf16[8,32,256]{2,1,0:T(8,128)(2,1)S(1)} collective-permute-done((bf16[8,32,256]{2,1,0:T(8,128)(2,1)S(1)}, bf16[8,32,256]{2,1,0:T(8,128)(2,1)S(1)}, u32[]{:S(2)}, u32[]{:S(2)}) %collective-permute-start.11) | collective-permute-done | bytes 131104 | tf_op jit(solution)/shard_map/ppermute | solution.py:33
  89.6 2.6 %collective-permute-done.12.refs_6_ = bf16[8,32,256]{2,1,0:T(8,128)(2,1)S(1)} collective-permute-done((bf16[8,32,256]{2,1,0:T(8,128)(2,1)S(1)}, bf16[8,32,256]{2,1,0:T(8,128)(2,1)S(1)}, u32[]{:S(2)}, u32[]{:S(2)}) %collective-permute-start.12) | collective-permute-done | bytes 131104 | tf_op jit(solution)/shard_map/ppermute | solution.py:33
  92.2 6.8 %collective-permute-done.13.refs_7_ = bf16[8,32,256]{2,1,0:T(8,128)(2,1)S(1)} collective-permute-done((bf16[8,32,256]{2,1,0:T(8,128)(2,1)S(1)}, bf16[8,32,256]{2,1,0:T(8,128)(2,1)S(1)}, u32[]{:S(2)}, u32[]{:S(2)}) %collective-permute-start.13) | collective-permute-done | bytes 131104 | tf_op jit(solution)/shard_map/ppermute | solution.py:33
  99.7 5.2 %all-to-all-start.3 = ((bf16[8,32,256]{2,1,0:T(8,128)(2,1)}), bf16[8,32,256]{2,1,0:T(8,128)(2,1)S(1)}, u32[]{:S(2)}, u32[]{:S(2)}) async-start(bf16[8,32,256]{2,1,0:T(8,128)(2,1)} %shard_map.107), calls=%async_computation.3 | async-start | bytes 262144 | tf_op jit(solution)/shard_map/all_to_all | solution.py:37
  105.7 4.4 %all-to-all-done.3.in_ref = bf16[8,32,256]{2,1,0:T(8,128)(2,1)S(1)} async-done(((bf16[8,32,256]{2,1,0:T(8,128)(2,1)}), bf16[8,32,256]{2,1,0:T(8,128)(2,1)S(1)}, u32[]{:S(2)}, u32[]{:S(2)}) %all-to-all-start.3) | async-done | bytes 131104 | tf_op jit(solution)/shard_map/all_to_all | solution.py:37
  (44 shorter events, 11.8 us)
Async XLA Ops:
  0.6 0.8 copy-start.3
  1.5 0.8 copy-start.4
  3.0 11.7 %all-to-all-start.1 = ((bf16[8,32,256]{2,1,0:T(8,128)(2,1)}), bf16[8,32,256]{2,1,0:T(8,128)(2,1)S(1)}, u32[]{:S(2)}, u32[]{:S(2)}) async-start(bf16[8,32,256]{2,1,0:T(8,128)(2,1)} %shard_map.104), calls=%async_computation.1 | async-start | bytes 262144 | tf_op jit(solution)/shard_map/all_to_all | solution.py:37
  8.8 1.0 copy-start
  9.8 1.0 copy-start.1
  10.9 1.0 copy-start.2
  14.7 6.5 %copy-start.6 = (s32[7]{0:T(128)S(1)}, s32[7]{0:T(128)}, u32[]{:S(2)}) copy-start(s32[7]{0:T(128)} %param.14) | copy-start | bytes 88
  14.7 22.2 %all-to-all-start = ((bf16[8,72,1024]{2,1,0:T(8,128)(2,1)}), bf16[8,72,1024]{2,1,0:T(8,128)(2,1)S(1)}, u32[]{:S(2)}, u32[]{:S(2)}) async-start(bf16[8,72,1024]{2,1,0:T(8,128)(2,1)} %shard_map.103), calls=%async_computation | async-start | bytes 2359296 | tf_op jit(solution)/shard_map/all_to_all | solution.py:37
  19.6 5.1 %collective-permute-start = (bf16[8,32,256]{2,1,0:T(8,128)(2,1)S(1)}, bf16[8,32,256]{2,1,0:T(8,128)(2,1)S(1)}, u32[]{:S(2)}, u32[]{:S(2)}) collective-permute-start(bf16[8,32,256]{2,1,0:T(8,128)(2,1)S(1)} %all-to-all-done.1.refs_0_), channel_id=1, source_target_pairs={{0,1},{1,2},{2,3},{3,4},{4,5},{5,6},{6,7},{7,0},{8,9},{9,10},{10,1... | collective-permute-start | bytes 393224 | tf_op jit(solution)/shard_map/ppermute | solution.py:33
  21.4 5.3 %collective-permute-start.1 = (bf16[8,32,256]{2,1,0:T(8,128)(2,1)S(1)}, bf16[8,32,256]{2,1,0:T(8,128)(2,1)S(1)}, u32[]{:S(2)}, u32[]{:S(2)}) collective-permute-start(bf16[8,32,256]{2,1,0:T(8,128)(2,1)S(1)} %all-to-all-done.1.refs_0_), channel_id=1, source_target_pairs={{0,7},{1,0},{2,1},{3,2},{4,3},{5,4},{6,5},{7,6},{8,15},{9,8},{10,9... | collective-permute-start | bytes 393224 | tf_op jit(solution)/shard_map/ppermute | solution.py:33
  24.7 7.5 %collective-permute-start.2 = (bf16[8,32,256]{2,1,0:T(8,128)(2,1)S(1)}, bf16[8,32,256]{2,1,0:T(8,128)(2,1)S(1)}, u32[]{:S(2)}, u32[]{:S(2)}) collective-permute-start(bf16[8,32,256]{2,1,0:T(8,128)(2,1)S(1)} %collective-permute-done.refs_1_), channel_id=1, source_target_pairs={{0,1},{1,2},{2,3},{3,4},{4,5},{5,6},{6,7},{7,0},{8,9},{9,10},{10,1... | collective-permute-start | bytes 393224 | tf_op jit(solution)/shard_map/ppermute | solution.py:33
  26.7 6.0 %collective-permute-start.3 = (bf16[8,32,256]{2,1,0:T(8,128)(2,1)S(1)}, bf16[8,32,256]{2,1,0:T(8,128)(2,1)S(1)}, u32[]{:S(2)}, u32[]{:S(2)}) collective-permute-start(bf16[8,32,256]{2,1,0:T(8,128)(2,1)S(1)} %collective-permute-done.1.refs_2_), channel_id=1, source_target_pairs={{0,7},{1,0},{2,1},{3,2},{4,3},{5,4},{6,5},{7,6},{8,15},{9,8},{10,9... | collective-permute-start | bytes 393224 | tf_op jit(solution)/shard_map/ppermute | solution.py:33
  32.2 4.7 %collective-permute-start.4 = (bf16[8,32,256]{2,1,0:T(8,128)(2,1)S(1)}, bf16[8,32,256]{2,1,0:T(8,128)(2,1)S(1)}, u32[]{:S(2)}, u32[]{:S(2)}) collective-permute-start(bf16[8,32,256]{2,1,0:T(8,128)(2,1)S(1)} %collective-permute-done.2.refs_3_), channel_id=1, source_target_pairs={{0,1},{1,2},{2,3},{3,4},{4,5},{5,6},{6,7},{7,0},{8,9},{9,10},{10,1... | collective-permute-start | bytes 393224 | tf_op jit(solution)/shard_map/ppermute | solution.py:33
  32.7 4.7 %collective-permute-start.5 = (bf16[8,32,256]{2,1,0:T(8,128)(2,1)S(1)}, bf16[8,32,256]{2,1,0:T(8,128)(2,1)S(1)}, u32[]{:S(2)}, u32[]{:S(2)}) collective-permute-start(bf16[8,32,256]{2,1,0:T(8,128)(2,1)S(1)} %collective-permute-done.3.refs_4_), channel_id=1, source_target_pairs={{0,7},{1,0},{2,1},{3,2},{4,3},{5,4},{6,5},{7,6},{8,15},{9,8},{10,9... | collective-permute-start | bytes 393224 | tf_op jit(solution)/shard_map/ppermute | solution.py:33
  36.9 5.0 %collective-permute-start.6 = (bf16[8,32,256]{2,1,0:T(8,128)(2,1)S(1)}, bf16[8,32,256]{2,1,0:T(8,128)(2,1)S(1)}, u32[]{:S(2)}, u32[]{:S(2)}) collective-permute-start(bf16[8,32,256]{2,1,0:T(8,128)(2,1)S(1)} %collective-permute-done.4.refs_5_), channel_id=1, source_target_pairs={{0,1},{1,2},{2,3},{3,4},{4,5},{5,6},{6,7},{7,0},{8,9},{9,10},{10,1... | collective-permute-start | bytes 393224 | tf_op jit(solution)/shard_map/ppermute | solution.py:33
  61.1 37.9 %all-to-all-start.2 = ((bf16[8,32,1024]{2,1,0:T(8,128)(2,1)}), bf16[8,32,1024]{2,1,0:T(8,128)(2,1)S(1)}, u32[]{:S(2)}, u32[]{:S(2)}) async-start(bf16[8,32,1024]{2,1,0:T(8,128)(2,1)} %get-tuple-element.31), calls=%async_computation.2 | async-start | bytes 1048576 | tf_op jit(solution)/shard_map/all_to_all | solution.py:37
  68.7 8.4 %collective-permute-start.7 = (bf16[8,32,256]{2,1,0:T(8,128)(2,1)S(1)}, bf16[8,32,256]{2,1,0:T(8,128)(2,1)S(1)}, u32[]{:S(2)}, u32[]{:S(2)}) collective-permute-start(bf16[8,32,256]{2,1,0:T(8,128)(2,1)S(1)} %get-tuple-element.24), channel_id=1, source_target_pairs={{0,7},{1,0},{2,1},{3,2},{4,3},{5,4},{6,5},{7,6},{8,15},{9,8},{10,9... | collective-permute-start | bytes 393224 | tf_op jit(solution)/shard_map/ppermute | solution.py:33
  71.6 7.9 %collective-permute-start.8 = (bf16[8,32,256]{2,1,0:T(8,128)(2,1)S(1)}, bf16[8,32,256]{2,1,0:T(8,128)(2,1)S(1)}, u32[]{:S(2)}, u32[]{:S(2)}) collective-permute-start(bf16[8,32,256]{2,1,0:T(8,128)(2,1)S(1)} %get-tuple-element.25), channel_id=1, source_target_pairs={{0,1},{1,2},{2,3},{3,4},{4,5},{5,6},{6,7},{7,0},{8,9},{9,10},{10,1... | collective-permute-start | bytes 393224 | tf_op jit(solution)/shard_map/ppermute | solution.py:33
  71.6 10.8 %collective-permute-start.9 = (bf16[8,32,256]{2,1,0:T(8,128)(2,1)S(1)}, bf16[8,32,256]{2,1,0:T(8,128)(2,1)S(1)}, u32[]{:S(2)}, u32[]{:S(2)}) collective-permute-start(bf16[8,32,256]{2,1,0:T(8,128)(2,1)S(1)} %get-tuple-element.26), channel_id=1, source_target_pairs={{0,6},{1,7},{2,0},{3,1},{4,2},{5,3},{6,4},{7,5},{8,14},{9,15},{10,... | collective-permute-start | bytes 393224 | tf_op jit(solution)/shard_map/ppermute | solution.py:33
  74.1 10.5 %collective-permute-start.10 = (bf16[8,32,256]{2,1,0:T(8,128)(2,1)S(1)}, bf16[8,32,256]{2,1,0:T(8,128)(2,1)S(1)}, u32[]{:S(2)}, u32[]{:S(2)}) collective-permute-start(bf16[8,32,256]{2,1,0:T(8,128)(2,1)S(1)} %get-tuple-element.27), channel_id=1, source_target_pairs={{0,2},{1,3},{2,4},{3,5},{4,6},{5,7},{6,0},{7,1},{8,10},{9,11},{10,... | collective-permute-start | bytes 393224 | tf_op jit(solution)/shard_map/ppermute | solution.py:33
  74.7 14.9 %collective-permute-start.11 = (bf16[8,32,256]{2,1,0:T(8,128)(2,1)S(1)}, bf16[8,32,256]{2,1,0:T(8,128)(2,1)S(1)}, u32[]{:S(2)}, u32[]{:S(2)}) collective-permute-start(bf16[8,32,256]{2,1,0:T(8,128)(2,1)S(1)} %get-tuple-element.28), channel_id=1, source_target_pairs={{0,5},{1,6},{2,7},{3,0},{4,1},{5,2},{6,3},{7,4},{8,13},{9,14},{10,... | collective-permute-start | bytes 393224 | tf_op jit(solution)/shard_map/ppermute | solution.py:33
  77.1 15.1 %collective-permute-start.12 = (bf16[8,32,256]{2,1,0:T(8,128)(2,1)S(1)}, bf16[8,32,256]{2,1,0:T(8,128)(2,1)S(1)}, u32[]{:S(2)}, u32[]{:S(2)}) collective-permute-start(bf16[8,32,256]{2,1,0:T(8,128)(2,1)S(1)} %get-tuple-element.29), channel_id=1, source_target_pairs={{0,3},{1,4},{2,5},{3,6},{4,7},{5,0},{6,1},{7,2},{8,11},{9,12},{10,... | collective-permute-start | bytes 393224 | tf_op jit(solution)/shard_map/ppermute | solution.py:33
  79.5 19.4 %collective-permute-start.13 = (bf16[8,32,256]{2,1,0:T(8,128)(2,1)S(1)}, bf16[8,32,256]{2,1,0:T(8,128)(2,1)S(1)}, u32[]{:S(2)}, u32[]{:S(2)}) collective-permute-start(bf16[8,32,256]{2,1,0:T(8,128)(2,1)S(1)} %get-tuple-element.30), channel_id=1, source_target_pairs={{0,4},{1,5},{2,6},{3,7},{4,0},{5,1},{6,2},{7,3},{8,12},{9,13},{10,... | collective-permute-start | bytes 393224 | tf_op jit(solution)/shard_map/ppermute | solution.py:33
  99.7 10.5 %all-to-all-start.3 = ((bf16[8,32,256]{2,1,0:T(8,128)(2,1)}), bf16[8,32,256]{2,1,0:T(8,128)(2,1)S(1)}, u32[]{:S(2)}, u32[]{:S(2)}) async-start(bf16[8,32,256]{2,1,0:T(8,128)(2,1)} %shard_map.107), calls=%async_computation.3 | async-start | bytes 262144 | tf_op jit(solution)/shard_map/all_to_all | solution.py:37
  (1 other events, 0.7 us)

commit v4 on v3

v4 whole, which is shorter than its diff:
```python
import math

import jax
import jax.numpy as jnp
from jax import lax
from jax.experimental import pallas as pl
from jax.experimental.pallas import tpu as pltpu
from jax.sharding import Mesh
from jax.sharding import PartitionSpec as P

KVH = 8
HD = 128
GROUP = 8
BLOCK = 128
WINDOW = 2048
TOK = 32
ZS = 8
AS = 8
CHUNK = TOK * ZS
ROWS = TOK * GROUP
SCALE = 1.0 / math.sqrt(HD)
LOG2E = math.log2(math.e)
BIG = 1e30
PAIR = 2
EXTRA = 8
HEADS = ("xl", "c", "xh")
F32 = jnp.float32
BF16 = jnp.bfloat16
OFFSETS = (0, 1, -1, 2, -2, 3, -3, 4)


def along_z(value, by):
    return lax.ppermute(value, "z", [(i, (i + by) % ZS) for i in range(ZS)])


def exchange(value):
    return lax.all_to_all(value, HEADS, split_axis=0, concat_axis=0, tiled=True)


def run_copies(copies):
    for copy in copies:
        copy.start()
    for copy in copies:
        copy.wait()


def pack_kv_kernel(k_ref, v_ref, out_ref, sems):
    run_copies(
        [
            pltpu.make_async_copy(
                ref.at[:, pl.ds(a * HD, HD)], out_ref.at[a, :, pl.ds(n * HD, HD)], sems.at[n, a]
            )
            for n, ref in enumerate((k_ref, v_ref))
            for a in range(AS)
        ]
    )


def split(value):
    high = value.astype(BF16)
    return high, (value - high.astype(F32)).astype(BF16)


def pack_queries_kernel(
    q_hbm, g_hbm, o_hbm, lse_hbm, keep_hbm, out_ref, o_ref, lse_ref, keep_ref, row_ref, sems, small
):
    wide = GROUP * HD
    copies = [[], []]
    small_copies = [
        pltpu.make_async_copy(lse_hbm, lse_ref, small.at[0]),
        pltpu.make_async_copy(keep_hbm, keep_ref, small.at[1]),
    ]
    for copy in small_copies:
        copy.start()
    for a in range(AS):
        columns = pl.ds(a * wide, wide)
        for n, (src, dst) in enumerate(
            (
                (g_hbm, out_ref.at[a, pl.ds(TOK, TOK), :]),
                (o_hbm, o_ref.at[:, columns]),
            )
        ):
            copies[0].append(pltpu.make_async_copy(src.at[:, columns], dst, sems.at[n, a]))
        copies[1].append(
            pltpu.make_async_copy(
                q_hbm.at[:, columns], out_ref.at[a, pl.ds(0, TOK), :], sems.at[2, a]
            )
        )
    for copy in copies[0] + copies[1]:
        copy.start()
    ones = jnp.ones((EXTRA, 2 * HD), BF16)
    lane = lax.broadcasted_iota(jnp.int32, (TOK, ROWS), 1)
    spread = (lane % TOK == lax.broadcasted_iota(jnp.int32, (TOK, ROWS), 0)).astype(F32).astype(BF16)
    head_lane = lax.broadcasted_iota(jnp.int32, (GROUP, ROWS), 1) // TOK
    own_head = head_lane == lax.broadcasted_iota(jnp.int32, (GROUP, ROWS), 0)
    row = lax.broadcasted_iota(jnp.int32, (EXTRA, ROWS), 0)
    for copy in small_copies:
        copy.wait()
    place = lax.axis_index("xh") * 2 + lax.axis_index("z") // 4
    kept = keep_ref[...].astype(F32)
    at_place = lax.broadcasted_iota(jnp.int32, kept.shape, 0) == place
    row_ref[...] = jnp.zeros(row_ref.shape, F32)
    row_ref[0:1, : kept.shape[1]] = jnp.sum(jnp.where(at_place, kept, 0.0), axis=0, keepdims=True)
    flags = row_ref[0:1]
    scaled = lse_ref[...].T * LOG2E
    high, low = split(scaled)
    lower = split(scaled - high.astype(F32) - low.astype(F32))[0]
    lse_all = sum(jnp.dot(p, spread, preferred_element_type=F32) for p in (high, low, lower))
    for a in range(AS):
        copies[0][2 * a].wait()
        copies[0][2 * a + 1].wait()
        columns = slice(a * wide, (a + 1) * wide)
        product = out_ref[a, TOK : 2 * TOK, :].astype(F32) * o_ref[:, columns].astype(F32)
        high, low = split(product)
        stacked = jnp.concatenate(
            [
                jnp.concatenate([p[:, h * HD : (h + 1) * HD] for h in range(GROUP)], axis=0)
                for p in (high, low)
            ],
            axis=1,
        )
        delta = lax.dot_general(
            ones, stacked, (((1,), (1,)), ((), ())), preferred_element_type=F32
        )[:1]
        lse = jnp.sum(
            jnp.where(own_head, lse_all[a * GROUP : (a + 1) * GROUP], 0.0), axis=0, keepdims=True
        )
        lse_high, lse_low = split(lse)
        delta_high, delta_low = split(delta)
        extra = jnp.zeros((EXTRA, ROWS), F32)
        for n, part in enumerate((lse_high, lse_low, delta_high, delta_low, flags)):
            extra = jnp.where(row == n, part.astype(F32), extra)
        out_ref[a, 2 * TOK :, :ROWS] = extra.astype(BF16)
        out_ref[a, 2 * TOK :, ROWS:] = jnp.zeros((EXTRA, wide - ROWS), BF16)
    for copy in copies[1]:
        copy.wait()


def attention_kernel(keep_ref, span_ref, message_ref, start_ref, *refs):
    kv_refs, refs = refs[:ZS], refs[ZS:]
    dq_ref, refs = refs[0], refs[1:]
    dkv_refs, refs = refs[:ZS], refs[ZS:]
    acc_ref, kt_ref, q_ref, g_ref, qt_ref, gt_ref, dqt_ref = refs
    z = lax.axis_index("z")
    sources = [lax.rem(z - off + ZS, ZS) for off in OFFSETS]
    lane_token = lax.rem(lax.broadcasted_iota(jnp.int32, (1, ROWS), 1), TOK)
    sublane = lax.broadcasted_iota(jnp.int32, (TOK, ROWS), 0)

    def keys_of(b, lanes):
        return jnp.concatenate(
            [kv[b * PAIR + c, :, lanes] for c in range(PAIR) for kv in kv_refs], axis=0
        )

    def prepare(b, _):
        kt_ref[b] = keys_of(b, pl.ds(0, HD)).T
        acc_ref[b] = jnp.zeros((PAIR * CHUNK, 2 * HD), F32)
        return 0

    lax.fori_loop(0, AS // PAIR, prepare, 0)

    def pair_of_chunks(j, _):
        lse, delta, start, q_pos = [], [], [], []
        for c in range(PAIR):
            i = j * PAIR + c
            for h in range(GROUP):
                rows = pl.ds(c * ROWS + h * TOK, TOK)
                q_ref[rows, :] = message_ref[i, :TOK, h * HD : (h + 1) * HD]
                g_ref[rows, :] = message_ref[i, TOK : 2 * TOK, h * HD : (h + 1) * HD]
            extra = message_ref[i, 2 * TOK :, :ROWS].astype(F32)
            lse.append(extra[0:1] + extra[1:2])
            delta.append(extra[2:3] + extra[3:4])
            start.append(start_ref[i])
            q_pos.append(i * CHUNK + z * TOK + lane_token)
        qt_ref[...] = q_ref[...].T
        gt_ref[...] = g_ref[...].T
        dqt_ref[...] = jnp.zeros((HD, PAIR * ROWS), F32)

        def tile(b, masked):
            scores = jnp.dot(keys_of(b, pl.ds(0, HD)), qt_ref[...], preferred_element_type=F32)
            dprobs = jnp.dot(keys_of(b, pl.ds(HD, HD)), gt_ref[...], preferred_element_type=F32)
            probs_b, dscores_b = [], []
            for k in range(PAIR * ZS):
                a, r = b * PAIR + k // ZS, k % ZS
                rows = slice(k * TOK, (k + 1) * TOK)
                probs_row, dscores_row = [], []
                for c in range(PAIR):
                    i = j * PAIR + c
                    columns = slice(c * ROWS, (c + 1) * ROWS)
                    distance = 2 * (i - a) + z // 4 - sources[r] // 4
                    kept = keep_ref[i, jnp.maximum(distance, 0)] > 0
                    shift = lse[c] + jnp.where(kept, 0.0, BIG)
                    probs = jnp.exp2(scores[rows, columns] * (SCALE * LOG2E) - shift)
                    if masked:
                        k_pos = a * CHUNK + sources[r] * TOK + sublane
                        probs = jnp.where((k_pos >= start[c]) & (k_pos <= q_pos[c]), probs, 0.0)
                    probs_row.append(probs.astype(BF16))
                    dscores_row.append((probs * (dprobs[rows, columns] - delta[c])).astype(BF16))
                probs_b.append(jnp.concatenate(probs_row, axis=1))
                dscores_b.append(jnp.concatenate(dscores_row, axis=1))
            probs_b = jnp.concatenate(probs_b, axis=0)
            dscores_b = jnp.concatenate(dscores_b, axis=0)
            acc_ref[b, :, :HD] += jnp.dot(dscores_b, q_ref[...], preferred_element_type=F32)
            acc_ref[b, :, HD:] += jnp.dot(probs_b, g_ref[...], preferred_element_type=F32)
            dqt_ref[...] += jnp.dot(kt_ref[b], dscores_b, preferred_element_type=F32)

        def step(b, _):
            masked = (b == j) | (span_ref[j * PAIR + PAIR - 1, 1] > b * PAIR * CHUNK)

            @pl.when(masked)
            def _():
                tile(b, True)

            @pl.when(jnp.logical_not(masked))
            def _():
                tile(b, False)

            return 0

        lax.fori_loop(span_ref[j * PAIR, 0] // (PAIR * CHUNK), j + 1, step, 0)
        dq = (dqt_ref[...] * SCALE).T.astype(BF16)
        for c in range(PAIR):
            for h in range(GROUP):
                first = c * ROWS + h * TOK
                dq_ref[j * PAIR + c, :, h * HD : (h + 1) * HD] = dq[first : first + TOK]
        return 0

    lax.fori_loop(0, AS // PAIR, pair_of_chunks, 0)

    def finish(b, _):
        for k in range(PAIR * ZS):
            piece = acc_ref[b, k * TOK : (k + 1) * TOK, :]
            out = dkv_refs[k % ZS].at[b * PAIR + k // ZS]
            out[:, :HD] = (piece[:, :HD] * SCALE).astype(BF16)
            out[:, HD:] = piece[:, HD:].astype(BF16)
        return 0

    lax.fori_loop(0, AS // PAIR, finish, 0)


def sum_kernel(*refs):
    total = refs[0][...].astype(F32)
    for ref in refs[1:-1]:
        total = total + ref[...].astype(F32)
    refs[-1][...] = total.astype(BF16)


def unpack_queries_kernel(in_ref, out_ref, sems):
    wide = GROUP * HD
    run_copies(
        [
            pltpu.make_async_copy(in_ref.at[a], out_ref.at[:, pl.ds(a * wide, wide)], sems.at[a])
            for a in range(AS)
        ]
    )


def unpack_kv_kernel(in_ref, dk_ref, dv_ref, sems):
    run_copies(
        [
            pltpu.make_async_copy(
                in_ref.at[a, :, pl.ds(n * HD, HD)], ref.at[:, pl.ds(a * HD, HD)], sems.at[n, a]
            )
            for n, ref in enumerate((dk_ref, dv_ref))
            for a in range(AS)
        ]
    )


def in_hbm():
    return pl.BlockSpec(memory_space=pltpu.HBM)


def anywhere():
    return pl.BlockSpec(memory_space=pl.ANY)


def in_vmem():
    return pl.BlockSpec(memory_space=pltpu.VMEM)


def in_smem():
    return pl.BlockSpec(memory_space=pltpu.SMEM)


def partial_sum(*values):
    shape = values[0].shape
    return pl.pallas_call(
        sum_kernel,
        out_shape=jax.ShapeDtypeStruct(shape, BF16),
        in_specs=[in_vmem()] * len(values),
        out_specs=in_vmem(),
        compiler_params=pltpu.CompilerParams(vmem_limit_bytes=4 * 2**20),
        cost_estimate=pl.CostEstimate(
            flops=65536 * len(values), bytes_accessed=131072 * (1 + len(values)), transcendentals=0
        ),
    )(*values)


def shards(query, key, value, output, out_grad, lse, doc_lengths, block_keep):
    i32 = jnp.int32
    z = lax.axis_index("z").astype(i32)
    columns = GROUP * HD
    dma = pltpu.SemaphoreType.DMA
    small_kernel = pltpu.CompilerParams(vmem_limit_bytes=4 * 2**20)

    kv_send = pl.pallas_call(
        pack_kv_kernel,
        out_shape=jax.ShapeDtypeStruct((AS, TOK, 2 * HD), BF16),
        in_specs=[in_hbm(), in_hbm()],
        out_specs=anywhere(),
        scratch_shapes=[dma((2, AS))],
        compiler_params=small_kernel,
        cost_estimate=pl.CostEstimate(flops=0, bytes_accessed=262144, transcendentals=0),
    )(key, value)
    kv_own = exchange(kv_send)

    reach = block_keep.shape[1]
    message_send = pl.pallas_call(
        pack_queries_kernel,
        out_shape=jax.ShapeDtypeStruct((AS, 2 * TOK + EXTRA, columns), BF16),
        in_specs=[in_hbm()] * 5,
        out_specs=in_vmem(),
        scratch_shapes=[
            pltpu.VMEM((TOK, AS * columns), BF16),
            pltpu.VMEM(lse.shape, F32),
            pltpu.VMEM(block_keep.shape, i32),
            pltpu.VMEM((8, ROWS), F32),
            dma((3, AS)),
            dma((2,)),
        ],
        compiler_params=pltpu.CompilerParams(vmem_limit_bytes=8 * 2**20),
        cost_estimate=pl.CostEstimate(flops=67108864, bytes_accessed=2800000, transcendentals=0),
    )(query, out_grad, output, lse, block_keep)
    message = exchange(message_send)

    pieces = {0: kv_own}
    for off in (1, -1, 2, -2):
        pieces[off] = along_z(kv_own, off)
    pieces[3] = along_z(pieces[2], 1)
    pieces[-3] = along_z(pieces[-2], -1)
    pieces[4] = along_z(pieces[2], 2)

    keep = message[:, 2 * TOK + 4, :reach].astype(i32)
    ends = jnp.arange(doc_lengths.shape[0], dtype=i32)
    starts = jnp.sum(jnp.where(ends[None, :] < ends[:, None], doc_lengths[None, :], 0), axis=1)
    base = lax.axis_index("y").astype(i32) * WINDOW
    positions = (
        base
        + jnp.arange(AS, dtype=i32)[:, None] * CHUNK
        + z * TOK
        + (jnp.arange(ROWS, dtype=i32) % TOK)[None, :]
    )
    start_of = jnp.max(
        jnp.where(starts[None, None, :] <= positions[:, :, None], starts[None, None, :], 0), axis=2
    )
    start_of = jnp.maximum(start_of - base, 0)
    span = jnp.stack([start_of[:, 0], start_of[:, TOK - 1]], axis=1)

    piece_shape = jax.ShapeDtypeStruct((AS, TOK, 2 * HD), BF16)
    results = pl.pallas_call(
        attention_kernel,
        out_shape=[jax.ShapeDtypeStruct((AS, TOK, columns), BF16)] + [piece_shape] * ZS,
        in_specs=[in_smem()] * 2 + [in_vmem()] * (2 + ZS),
        out_specs=[in_vmem()] * (1 + ZS),
        scratch_shapes=[
            pltpu.VMEM((AS // PAIR, PAIR * CHUNK, 2 * HD), F32),
            pltpu.VMEM((AS // PAIR, HD, PAIR * CHUNK), BF16),
            pltpu.VMEM((PAIR * ROWS, HD), BF16),
            pltpu.VMEM((PAIR * ROWS, HD), BF16),
            pltpu.VMEM((HD, PAIR * ROWS), BF16),
            pltpu.VMEM((HD, PAIR * ROWS), BF16),
            pltpu.VMEM((HD, PAIR * ROWS), F32),
        ],
        compiler_params=pltpu.CompilerParams(vmem_limit_bytes=24 * 2**20),
        cost_estimate=pl.CostEstimate(
            flops=3000000000, bytes_accessed=4000000, transcendentals=2360000
        ),
    )(keep, span, message, start_of.reshape(AS, 1, ROWS), *[pieces[o] for o in OFFSETS])
    dq, part = results[0], dict(zip(OFFSETS, results[1:]))

    from_three, from_four = along_z(part[3], -1), along_z(part[4], -2)
    from_minus_three = along_z(part[-3], 1)
    dq_back = exchange(dq)
    one, minus_one = along_z(part[1], -1), along_z(part[-1], 1)
    two = along_z(partial_sum(part[2], from_three, from_four), -2)
    minus_two = along_z(partial_sum(part[-2], from_minus_three), 2)
    returned = (part[0], one, minus_one, two, minus_two)
    returned, dq_back = lax.optimization_barrier((returned, dq_back))
    query_grad = pl.pallas_call(
        unpack_queries_kernel,
        out_shape=jax.ShapeDtypeStruct((TOK, AS * columns), BF16),
        in_specs=[anywhere()],
        out_specs=anywhere(),
        scratch_shapes=[dma((AS,))],
        compiler_params=small_kernel,
        cost_estimate=pl.CostEstimate(flops=0, bytes_accessed=1048576, transcendentals=0),
    )(dq_back)
    grads = exchange(partial_sum(*returned))
    half = jax.ShapeDtypeStruct((TOK, KVH * HD), BF16)
    key_grad, value_grad = pl.pallas_call(
        unpack_kv_kernel,
        out_shape=[half, half],
        in_specs=[anywhere()],
        out_specs=[anywhere(), anywhere()],
        scratch_shapes=[dma((2, AS))],
        compiler_params=small_kernel,
        cost_estimate=pl.CostEstimate(flops=0, bytes_accessed=262144, transcendentals=0),
    )(grads)
    return (query_grad, key_grad, value_grad)


def solution(mesh):
    fine = Mesh(mesh.devices.reshape(4, 2, 2, 2, ZS), ("y", "xl", "c", "xh", "z"))
    tokens = P(("y", "xl", "c", "xh", "z"), None)
    in_specs = (tokens,) * 6 + (P(), P(("y", "xl", "c"), None))
    return jax.shard_map(
        shards, mesh=fine, in_specs=in_specs, out_specs=(tokens,) * 3, check_vma=False
    )
```

time: 112 us -> 101 us (0.902)
  the two profiles are of different devices: /device:TPU:57 before, /device:TPU:8 now
where the time goes in v4:
time: 101 us; the launch traced here: 99.3 us
  starting transfers between devices  39 us (39%)
  waiting for transfers between devices  34 us (34%)
  Pallas kernels  18.9 us (19%)
  local copies, waits for them, and re-layouts  6.27 us (6%)
    ppermute x14, waiting for transfers between devices, along_z(): return lax.ppermute(value, 'z', [(i, (i + by) % ZS) for i in range(ZS)])  29.3 us
    ppermute x14, starting transfers between devices, along_z(): return lax.ppermute(value, 'z', [(i, (i + by) % ZS) for i in range(ZS)])  21.3 us
    all_to_all x4, starting transfers between devices, exchange(): return lax.all_to_all(value, HEADS, split_axis=0, concat_axis=0, tiled=True)  17.7 us
    pallas_call x1, Pallas kernels, shards(): pl.pallas_call(attention_kernel, out_shape=[jax.ShapeDtypeStruct((AS, TOK...  12 us
    unnamed x16, local copies, waits for them, and re-layouts  6.2 us
    all_to_all x4, waiting for transfers between devices, exchange(): return lax.all_to_all(value, HEADS, split_axis=0, concat_axis=0, tiled=True)  4.71 us
    pallas_call x1, Pallas kernels, shards(): pl.pallas_call(pack_queries_kernel, out_shape=jax.ShapeDtypeStruct((AS, 2...  3.63 us
  transfers between devices with their start and end apart: 18, of which 9 were waited for; matrix products, arithmetic and copies ran while one was open for 0% of the time, Pallas kernels for 5%

profile of v4, /device:TPU:8, one launch (start us, length us, event | category | flops | bytes accessed | tf_op | source)
XLA Modules:
  0.0 99.3 jit_solution(6816737315194405466)
XLA Ops:
  3.1 4.3 %all-to-all-start.1 = ((bf16[8,32,256]{2,1,0:T(8,128)(2,1)}), bf16[8,32,256]{2,1,0:T(8,128)(2,1)S(1)}, u32[]{:S(2)}, u32[]{:S(2)}) async-start(bf16[8,32,256]{2,1,0:T(8,128)(2,1)} %shard_map.104), calls=%async_computation.1 | async-start | bytes 262144 | tf_op jit(solution)/shard_map/all_to_all | solution.py:37
  8.5 1.0 %copy-done.1 = bf16[32,8192]{1,0:T(8,128)(2,1)S(1)} copy-done((bf16[32,8192]{1,0:T(8,128)(2,1)S(1)}, bf16[32,8192]{1,0:T(8,128)(2,1)}, u32[]{:S(2)}) %copy-start.1) | copy-done | bytes 524312
  9.5 1.0 %copy-done.2 = bf16[32,8192]{1,0:T(8,128)(2,1)S(1)} copy-done((bf16[32,8192]{1,0:T(8,128)(2,1)S(1)}, bf16[32,8192]{1,0:T(8,128)(2,1)}, u32[]{:S(2)}) %copy-start.2) | copy-done | bytes 524312
  12.0 3.6 %shard_map.103 = bf16[8,72,1024]{2,1,0:T(8,128)(2,1)} custom-call(bf16[32,8192]{1,0:T(8,128)(2,1)S(1)} %copy-done, bf16[32,8192]{1,0:T(8,128)(2,1)S(1)} %copy-done.1, bf16[32,8192]{1,0:T(8,128)(2,1)S(1)} %copy-done.2, f32[32,64]{1,0:T(8,128)S(1)} %copy-done.5, s32[4,17]{1,0:T(4,128)S(1)} %copy-done.6), custom_call_target="tpu_custom_call" | custom-call | flops 67108864 | bytes 2800000 | tf_op jit(solution)/shard_map/pallas_call | solution.py:318
  15.6 4.8 %all-to-all-start = ((bf16[8,72,1024]{2,1,0:T(8,128)(2,1)}), bf16[8,72,1024]{2,1,0:T(8,128)(2,1)S(1)}, u32[]{:S(2)}, u32[]{:S(2)}) async-start(bf16[8,72,1024]{2,1,0:T(8,128)(2,1)} %shard_map.103), calls=%async_computation | async-start | bytes 2359296 | tf_op jit(solution)/shard_map/all_to_all | solution.py:37
  20.8 6.4 %collective-permute-start.3 = (bf16[8,32,256]{2,1,0:T(8,128)(2,1)S(1)}, bf16[8,32,256]{2,1,0:T(8,128)(2,1)S(1)}, u32[]{:S(2)}, u32[]{:S(2)}) collective-permute-start(bf16[8,32,256]{2,1,0:T(8,128)(2,1)S(1)} %all-to-all-done.1.refs_0_), channel_id=1, source_target_pairs={{0,6},{1,7},{2,0},{3,1},{4,2},{5,3},{6,4},{7,5},{8,14},{9,15},{10,... | collective-permute-start | bytes 393224 | tf_op jit(solution)/shard_map/ppermute | solution.py:33
  27.3 3.7 %collective-permute-start.1 = (bf16[8,32,256]{2,1,0:T(8,128)(2,1)S(1)}, bf16[8,32,256]{2,1,0:T(8,128)(2,1)S(1)}, u32[]{:S(2)}, u32[]{:S(2)}) collective-permute-start(bf16[8,32,256]{2,1,0:T(8,128)(2,1)S(1)} %all-to-all-done.1.refs_0_), channel_id=1, source_target_pairs={{0,7},{1,0},{2,1},{3,2},{4,3},{5,4},{6,5},{7,6},{8,15},{9,8},{10,9... | collective-permute-start | bytes 393224 | tf_op jit(solution)/shard_map/ppermute | solution.py:33
  31.0 6.8 %collective-permute-done.2.refs_3_ = bf16[8,32,256]{2,1,0:T(8,128)(2,1)S(1)} collective-permute-done((bf16[8,32,256]{2,1,0:T(8,128)(2,1)S(1)}, bf16[8,32,256]{2,1,0:T(8,128)(2,1)S(1)}, u32[]{:S(2)}, u32[]{:S(2)}) %collective-permute-start.2) | collective-permute-done | bytes 131104 | tf_op jit(solution)/shard_map/ppermute | solution.py:33
  37.8 1.3 %collective-permute-start.4 = (bf16[8,32,256]{2,1,0:T(8,128)(2,1)S(1)}, bf16[8,32,256]{2,1,0:T(8,128)(2,1)S(1)}, u32[]{:S(2)}, u32[]{:S(2)}) collective-permute-start(bf16[8,32,256]{2,1,0:T(8,128)(2,1)S(1)} %collective-permute-done.2.refs_3_), channel_id=1, source_target_pairs={{0,1},{1,2},{2,3},{3,4},{4,5},{5,6},{6,7},{7,0},{8,9},{9,10},{10,1... | collective-permute-start | bytes 393224 | tf_op jit(solution)/shard_map/ppermute | solution.py:33
  39.1 2.7 %collective-permute-start.5 = (bf16[8,32,256]{2,1,0:T(8,128)(2,1)S(1)}, bf16[8,32,256]{2,1,0:T(8,128)(2,1)S(1)}, u32[]{:S(2)}, u32[]{:S(2)}) collective-permute-start(bf16[8,32,256]{2,1,0:T(8,128)(2,1)S(1)} %collective-permute-done.3.refs_4_), channel_id=1, source_target_pairs={{0,7},{1,0},{2,1},{3,2},{4,3},{5,4},{6,5},{7,6},{8,15},{9,8},{10,9... | collective-permute-start | bytes 393224 | tf_op jit(solution)/shard_map/ppermute | solution.py:33
  41.8 2.5 %collective-permute-done.5.refs_6_ = bf16[8,32,256]{2,1,0:T(8,128)(2,1)S(1)} collective-permute-done((bf16[8,32,256]{2,1,0:T(8,128)(2,1)S(1)}, bf16[8,32,256]{2,1,0:T(8,128)(2,1)S(1)}, u32[]{:S(2)}, u32[]{:S(2)}) %collective-permute-start.5) | collective-permute-done | bytes 131104 | tf_op jit(solution)/shard_map/ppermute | solution.py:33
  44.3 3.1 %collective-permute-done.6.refs_7_ = bf16[8,32,256]{2,1,0:T(8,128)(2,1)S(1)} collective-permute-done((bf16[8,32,256]{2,1,0:T(8,128)(2,1)S(1)}, bf16[8,32,256]{2,1,0:T(8,128)(2,1)S(1)}, u32[]{:S(2)}, u32[]{:S(2)}) %collective-permute-start.6) | collective-permute-done | bytes 131104 | tf_op jit(solution)/shard_map/ppermute | solution.py:33
  47.4 1.5 %collective-permute-done.4.refs_5_ = bf16[8,32,256]{2,1,0:T(8,128)(2,1)S(1)} collective-permute-done((bf16[8,32,256]{2,1,0:T(8,128)(2,1)S(1)}, bf16[8,32,256]{2,1,0:T(8,128)(2,1)S(1)}, u32[]{:S(2)}, u32[]{:S(2)}) %collective-permute-start.4) | collective-permute-done | bytes 131104 | tf_op jit(solution)/shard_map/ppermute | solution.py:33
  48.9 12.0 %shard_map.105 = (bf16[8,32,1024]{2,1,0:T(8,128)(2,1)}, bf16[8,32,256]{2,1,0:T(8,128)(2,1)S(1)}, bf16[8,32,256]{2,1,0:T(8,128)(2,1)S(1)}, bf16[8,32,256]{2,1,0:T...) custom-call(s32[8,17]{1,0:T(8,128)S(1)} %bitcast.1, ...), custom_call_target="tpu_custom_call" | custom-call | flops 3000000000 | bytes 4000000 | tf_op jit(solution)/shard_map/pallas_call | solution.py:360
  60.8 4.3 %all-to-all-start.2 = ((bf16[8,32,1024]{2,1,0:T(8,128)(2,1)}), bf16[8,32,1024]{2,1,0:T(8,128)(2,1)S(1)}, u32[]{:S(2)}, u32[]{:S(2)}) async-start(bf16[8,32,1024]{2,1,0:T(8,128)(2,1)} %get-tuple-element.28), calls=%async_computation.2 | async-start | bytes 1048576 | tf_op jit(solution)/shard_map/all_to_all | solution.py:37
  66.1 1.0 %collective-permute-start.12 = (bf16[8,32,256]{2,1,0:T(8,128)(2,1)S(1)}, bf16[8,32,256]{2,1,0:T(8,128)(2,1)S(1)}, u32[]{:S(2)}, u32[]{:S(2)}) collective-permute-start(bf16[8,32,256]{2,1,0:T(8,128)(2,1)S(1)} %get-tuple-element.27), channel_id=1, source_target_pairs={{0,1},{1,2},{2,3},{3,4},{4,5},{5,6},{6,7},{7,0},{8,9},{9,10},{10,1... | collective-permute-start | bytes 393224 | tf_op jit(solution)/shard_map/ppermute | solution.py:33
  67.2 2.2 %collective-permute-start.7 = (bf16[8,32,256]{2,1,0:T(8,128)(2,1)S(1)}, bf16[8,32,256]{2,1,0:T(8,128)(2,1)S(1)}, u32[]{:S(2)}, u32[]{:S(2)}) collective-permute-start(bf16[8,32,256]{2,1,0:T(8,128)(2,1)S(1)} %get-tuple-element.21), channel_id=1, source_target_pairs={{0,7},{1,0},{2,1},{3,2},{4,3},{5,4},{6,5},{7,6},{8,15},{9,8},{10,9... | collective-permute-start | bytes 393224 | tf_op jit(solution)/shard_map/ppermute | solution.py:33
  69.4 2.5 %collective-permute-done.9.refs_1_ = bf16[8,32,256]{2,1,0:T(8,128)(2,1)S(1)} collective-permute-done((bf16[8,32,256]{2,1,0:T(8,128)(2,1)S(1)}, bf16[8,32,256]{2,1,0:T(8,128)(2,1)S(1)}, u32[]{:S(2)}, u32[]{:S(2)}) %collective-permute-start.9) | collective-permute-done | bytes 131104 | tf_op jit(solution)/shard_map/ppermute | solution.py:33
  71.8 4.7 %collective-permute-done.10.refs_2_ = bf16[8,32,256]{2,1,0:T(8,128)(2,1)S(1)} collective-permute-done((bf16[8,32,256]{2,1,0:T(8,128)(2,1)S(1)}, bf16[8,32,256]{2,1,0:T(8,128)(2,1)S(1)}, u32[]{:S(2)}, u32[]{:S(2)}) %collective-permute-start.10) | collective-permute-done | bytes 131104 | tf_op jit(solution)/shard_map/ppermute | solution.py:33
  76.6 2.1 %collective-permute-start.11 = (bf16[8,32,256]{2,1,0:T(8,128)(2,1)S(1)}, bf16[8,32,256]{2,1,0:T(8,128)(2,1)S(1)}, u32[]{:S(2)}, u32[]{:S(2)}) collective-permute-start(bf16[8,32,256]{2,1,0:T(8,128)(2,1)S(1)} %shard_map.106), channel_id=1, source_target_pairs={{0,6},{1,7},{2,0},{3,1},{4,2},{5,3},{6,4},{7,5},{8,14},{9,15},{10,... | collective-permute-start | bytes 393224 | tf_op jit(solution)/shard_map/ppermute | solution.py:33
  79.7 4.9 %collective-permute-done.11.refs_3_ = bf16[8,32,256]{2,1,0:T(8,128)(2,1)S(1)} collective-permute-done((bf16[8,32,256]{2,1,0:T(8,128)(2,1)S(1)}, bf16[8,32,256]{2,1,0:T(8,128)(2,1)S(1)}, u32[]{:S(2)}, u32[]{:S(2)}) %collective-permute-start.11) | collective-permute-done | bytes 131104 | tf_op jit(solution)/shard_map/ppermute | solution.py:33
  84.6 3.4 %collective-permute-done.13.refs_4_ = bf16[8,32,256]{2,1,0:T(8,128)(2,1)S(1)} collective-permute-done((bf16[8,32,256]{2,1,0:T(8,128)(2,1)S(1)}, bf16[8,32,256]{2,1,0:T(8,128)(2,1)S(1)}, u32[]{:S(2)}, u32[]{:S(2)}) %collective-permute-start.13) | collective-permute-done | bytes 131104 | tf_op jit(solution)/shard_map/ppermute | solution.py:33
  88.7 4.3 %all-to-all-start.3 = ((bf16[8,32,256]{2,1,0:T(8,128)(2,1)}), bf16[8,32,256]{2,1,0:T(8,128)(2,1)S(1)}, u32[]{:S(2)}, u32[]{:S(2)}) async-start(bf16[8,32,256]{2,1,0:T(8,128)(2,1)} %shard_map.109), calls=%async_computation.3 | async-start | bytes 262144 | tf_op jit(solution)/shard_map/all_to_all | solution.py:37
  93.8 4.7 %all-to-all-done.3.in_ref = bf16[8,32,256]{2,1,0:T(8,128)(2,1)S(1)} async-done(((bf16[8,32,256]{2,1,0:T(8,128)(2,1)}), bf16[8,32,256]{2,1,0:T(8,128)(2,1)S(1)}, u32[]{:S(2)}, u32[]{:S(2)}) %all-to-all-start.3) | async-done | bytes 131104 | tf_op jit(solution)/shard_map/all_to_all | solution.py:37
  (46 shorter events, 9.8 us)
Async XLA Ops:
  0.6 0.8 copy-start.3
  1.5 0.8 copy-start.4
  3.1 12.5 %all-to-all-start.1 = ((bf16[8,32,256]{2,1,0:T(8,128)(2,1)}), bf16[8,32,256]{2,1,0:T(8,128)(2,1)S(1)}, u32[]{:S(2)}, u32[]{:S(2)}) async-start(bf16[8,32,256]{2,1,0:T(8,128)(2,1)} %shard_map.104), calls=%async_computation.1 | async-start | bytes 262144 | tf_op jit(solution)/shard_map/all_to_all | solution.py:37
  7.4 1.0 %copy-start = (bf16[32,8192]{1,0:T(8,128)(2,1)S(1)}, bf16[32,8192]{1,0:T(8,128)(2,1)}, u32[]{:S(2)}) copy-start(bf16[32,8192]{1,0:T(8,128)(2,1)} %q_hbm.1) | copy-start | bytes 1572868
  8.5 1.0 %copy-start.1 = (bf16[32,8192]{1,0:T(8,128)(2,1)S(1)}, bf16[32,8192]{1,0:T(8,128)(2,1)}, u32[]{:S(2)}) copy-start(bf16[32,8192]{1,0:T(8,128)(2,1)} %g_hbm.1) | copy-start | bytes 1572868
  9.5 1.0 %copy-start.2 = (bf16[32,8192]{1,0:T(8,128)(2,1)S(1)}, bf16[32,8192]{1,0:T(8,128)(2,1)}, u32[]{:S(2)}) copy-start(bf16[32,8192]{1,0:T(8,128)(2,1)} %o_hbm.1) | copy-start | bytes 1572868
  15.6 4.8 %copy-start.7 = (s32[7]{0:T(128)S(1)}, s32[7]{0:T(128)}, u32[]{:S(2)}) copy-start(s32[7]{0:T(128)} %param.14) | copy-start | bytes 88
  15.6 26.1 %all-to-all-start = ((bf16[8,72,1024]{2,1,0:T(8,128)(2,1)}), bf16[8,72,1024]{2,1,0:T(8,128)(2,1)S(1)}, u32[]{:S(2)}, u32[]{:S(2)}) async-start(bf16[8,72,1024]{2,1,0:T(8,128)(2,1)} %shard_map.103), calls=%async_computation | async-start | bytes 2359296 | tf_op jit(solution)/shard_map/all_to_all | solution.py:37
  20.8 18.4 %collective-permute-start.3 = (bf16[8,32,256]{2,1,0:T(8,128)(2,1)S(1)}, bf16[8,32,256]{2,1,0:T(8,128)(2,1)S(1)}, u32[]{:S(2)}, u32[]{:S(2)}) collective-permute-start(bf16[8,32,256]{2,1,0:T(8,128)(2,1)S(1)} %all-to-all-done.1.refs_0_), channel_id=1, source_target_pairs={{0,6},{1,7},{2,0},{3,1},{4,2},{5,3},{6,4},{7,5},{8,14},{9,15},{10,... | collective-permute-start | bytes 393224 | tf_op jit(solution)/shard_map/ppermute | solution.py:33
  27.1 10.7 %collective-permute-start.2 = (bf16[8,32,256]{2,1,0:T(8,128)(2,1)S(1)}, bf16[8,32,256]{2,1,0:T(8,128)(2,1)S(1)}, u32[]{:S(2)}, u32[]{:S(2)}) collective-permute-start(bf16[8,32,256]{2,1,0:T(8,128)(2,1)S(1)} %all-to-all-done.1.refs_0_), channel_id=1, source_target_pairs={{0,2},{1,3},{2,4},{3,5},{4,6},{5,7},{6,0},{7,1},{8,10},{9,11},{10,... | collective-permute-start | bytes 393224 | tf_op jit(solution)/shard_map/ppermute | solution.py:33
  27.3 14.5 %collective-permute-start.1 = (bf16[8,32,256]{2,1,0:T(8,128)(2,1)S(1)}, bf16[8,32,256]{2,1,0:T(8,128)(2,1)S(1)}, u32[]{:S(2)}, u32[]{:S(2)}) collective-permute-start(bf16[8,32,256]{2,1,0:T(8,128)(2,1)S(1)} %all-to-all-done.1.refs_0_), channel_id=1, source_target_pairs={{0,7},{1,0},{2,1},{3,2},{4,3},{5,4},{6,5},{7,6},{8,15},{9,8},{10,9... | collective-permute-start | bytes 393224 | tf_op jit(solution)/shard_map/ppermute | solution.py:33
  31.0 10.8 %collective-permute-start = (bf16[8,32,256]{2,1,0:T(8,128)(2,1)S(1)}, bf16[8,32,256]{2,1,0:T(8,128)(2,1)S(1)}, u32[]{:S(2)}, u32[]{:S(2)}) collective-permute-start(bf16[8,32,256]{2,1,0:T(8,128)(2,1)S(1)} %all-to-all-done.1.refs_0_), channel_id=1, source_target_pairs={{0,1},{1,2},{2,3},{3,4},{4,5},{5,6},{6,7},{7,0},{8,9},{9,10},{10,1... | collective-permute-start | bytes 393224 | tf_op jit(solution)/shard_map/ppermute | solution.py:33
  37.8 9.5 %collective-permute-start.6 = (bf16[8,32,256]{2,1,0:T(8,128)(2,1)S(1)}, bf16[8,32,256]{2,1,0:T(8,128)(2,1)S(1)}, u32[]{:S(2)}, u32[]{:S(2)}) collective-permute-start(bf16[8,32,256]{2,1,0:T(8,128)(2,1)S(1)} %collective-permute-done.2.refs_3_), channel_id=1, source_target_pairs={{0,2},{1,3},{2,4},{3,5},{4,6},{5,7},{6,0},{7,1},{8,10},{9,11},{10,... | collective-permute-start | bytes 393224 | tf_op jit(solution)/shard_map/ppermute | solution.py:33
  37.8 11.0 %collective-permute-start.4 = (bf16[8,32,256]{2,1,0:T(8,128)(2,1)S(1)}, bf16[8,32,256]{2,1,0:T(8,128)(2,1)S(1)}, u32[]{:S(2)}, u32[]{:S(2)}) collective-permute-start(bf16[8,32,256]{2,1,0:T(8,128)(2,1)S(1)} %collective-permute-done.2.refs_3_), channel_id=1, source_target_pairs={{0,1},{1,2},{2,3},{3,4},{4,5},{5,6},{6,7},{7,0},{8,9},{9,10},{10,1... | collective-permute-start | bytes 393224 | tf_op jit(solution)/shard_map/ppermute | solution.py:33
  39.1 5.2 %collective-permute-start.5 = (bf16[8,32,256]{2,1,0:T(8,128)(2,1)S(1)}, bf16[8,32,256]{2,1,0:T(8,128)(2,1)S(1)}, u32[]{:S(2)}, u32[]{:S(2)}) collective-permute-start(bf16[8,32,256]{2,1,0:T(8,128)(2,1)S(1)} %collective-permute-done.3.refs_4_), channel_id=1, source_target_pairs={{0,7},{1,0},{2,1},{3,2},{4,3},{5,4},{6,5},{7,6},{8,15},{9,8},{10,9... | collective-permute-start | bytes 393224 | tf_op jit(solution)/shard_map/ppermute | solution.py:33
  60.8 27.1 %all-to-all-start.2 = ((bf16[8,32,1024]{2,1,0:T(8,128)(2,1)}), bf16[8,32,1024]{2,1,0:T(8,128)(2,1)S(1)}, u32[]{:S(2)}, u32[]{:S(2)}) async-start(bf16[8,32,1024]{2,1,0:T(8,128)(2,1)} %get-tuple-element.28), calls=%async_computation.2 | async-start | bytes 1048576 | tf_op jit(solution)/shard_map/all_to_all | solution.py:37
  65.1 6.7 %collective-permute-start.9 = (bf16[8,32,256]{2,1,0:T(8,128)(2,1)S(1)}, bf16[8,32,256]{2,1,0:T(8,128)(2,1)S(1)}, u32[]{:S(2)}, u32[]{:S(2)}) collective-permute-start(bf16[8,32,256]{2,1,0:T(8,128)(2,1)S(1)} %get-tuple-element.24), channel_id=1, source_target_pairs={{0,7},{1,0},{2,1},{3,2},{4,3},{5,4},{6,5},{7,6},{8,15},{9,8},{10,9... | collective-permute-start | bytes 393224 | tf_op jit(solution)/shard_map/ppermute | solution.py:33
  65.2 11.4 %collective-permute-start.10 = (bf16[8,32,256]{2,1,0:T(8,128)(2,1)S(1)}, bf16[8,32,256]{2,1,0:T(8,128)(2,1)S(1)}, u32[]{:S(2)}, u32[]{:S(2)}) collective-permute-start(bf16[8,32,256]{2,1,0:T(8,128)(2,1)S(1)} %get-tuple-element.25), channel_id=1, source_target_pairs={{0,6},{1,7},{2,0},{3,1},{4,2},{5,3},{6,4},{7,5},{8,14},{9,15},{10,... | collective-permute-start | bytes 393224 | tf_op jit(solution)/shard_map/ppermute | solution.py:33
  66.1 12.6 %collective-permute-start.12 = (bf16[8,32,256]{2,1,0:T(8,128)(2,1)S(1)}, bf16[8,32,256]{2,1,0:T(8,128)(2,1)S(1)}, u32[]{:S(2)}, u32[]{:S(2)}) collective-permute-start(bf16[8,32,256]{2,1,0:T(8,128)(2,1)S(1)} %get-tuple-element.27), channel_id=1, source_target_pairs={{0,1},{1,2},{2,3},{3,4},{4,5},{5,6},{6,7},{7,0},{8,9},{9,10},{10,1... | collective-permute-start | bytes 393224 | tf_op jit(solution)/shard_map/ppermute | solution.py:33
  67.2 12.6 %collective-permute-start.7 = (bf16[8,32,256]{2,1,0:T(8,128)(2,1)S(1)}, bf16[8,32,256]{2,1,0:T(8,128)(2,1)S(1)}, u32[]{:S(2)}, u32[]{:S(2)}) collective-permute-start(bf16[8,32,256]{2,1,0:T(8,128)(2,1)S(1)} %get-tuple-element.21), channel_id=1, source_target_pairs={{0,7},{1,0},{2,1},{3,2},{4,3},{5,4},{6,5},{7,6},{8,15},{9,8},{10,9... | collective-permute-start | bytes 393224 | tf_op jit(solution)/shard_map/ppermute | solution.py:33
  69.4 10.4 %collective-permute-start.8 = (bf16[8,32,256]{2,1,0:T(8,128)(2,1)S(1)}, bf16[8,32,256]{2,1,0:T(8,128)(2,1)S(1)}, u32[]{:S(2)}, u32[]{:S(2)}) collective-permute-start(bf16[8,32,256]{2,1,0:T(8,128)(2,1)S(1)} %get-tuple-element.22), channel_id=1, source_target_pairs={{0,1},{1,2},{2,3},{3,4},{4,5},{5,6},{6,7},{7,0},{8,9},{9,10},{10,1... | collective-permute-start | bytes 393224 | tf_op jit(solution)/shard_map/ppermute | solution.py:33
  76.6 8.0 %collective-permute-start.11 = (bf16[8,32,256]{2,1,0:T(8,128)(2,1)S(1)}, bf16[8,32,256]{2,1,0:T(8,128)(2,1)S(1)}, u32[]{:S(2)}, u32[]{:S(2)}) collective-permute-start(bf16[8,32,256]{2,1,0:T(8,128)(2,1)S(1)} %shard_map.106), channel_id=1, source_target_pairs={{0,6},{1,7},{2,0},{3,1},{4,2},{5,3},{6,4},{7,5},{8,14},{9,15},{10,... | collective-permute-start | bytes 393224 | tf_op jit(solution)/shard_map/ppermute | solution.py:33
  78.8 9.2 %collective-permute-start.13 = (bf16[8,32,256]{2,1,0:T(8,128)(2,1)S(1)}, bf16[8,32,256]{2,1,0:T(8,128)(2,1)S(1)}, u32[]{:S(2)}, u32[]{:S(2)}) collective-permute-start(bf16[8,32,256]{2,1,0:T(8,128)(2,1)S(1)} %shard_map.107), channel_id=1, source_target_pairs={{0,2},{1,3},{2,4},{3,5},{4,6},{5,7},{6,0},{7,1},{8,10},{9,11},{10,... | collective-permute-start | bytes 393224 | tf_op jit(solution)/shard_map/ppermute | solution.py:33
  88.7 9.8 %all-to-all-start.3 = ((bf16[8,32,256]{2,1,0:T(8,128)(2,1)}), bf16[8,32,256]{2,1,0:T(8,128)(2,1)S(1)}, u32[]{:S(2)}, u32[]{:S(2)}) async-start(bf16[8,32,256]{2,1,0:T(8,128)(2,1)} %shard_map.109), calls=%async_computation.3 | async-start | bytes 262144 | tf_op jit(solution)/shard_map/all_to_all | solution.py:37
  (2 other events, 1.4 us)

commit v5 on v4

--- a/solution.py
+++ b/solution.py
@@ -1,3 +1,4 @@
+import functools
 import math
 
 import jax
@@ -22,11 +23,13 @@
 LOG2E = math.log2(math.e)
 BIG = 1e30
 PAIR = 2
+SPAN = 4
 EXTRA = 8
 HEADS = ("xl", "c", "xh")
 F32 = jnp.float32
 BF16 = jnp.bfloat16
-OFFSETS = (0, 1, -1, 2, -2, 3, -3, 4)
+FAR = (3, -3, 4, 2)
+NEAR = (0, 1, -1, -2)
 
 
 def along_z(value, by):
@@ -136,27 +139,31 @@
         copy.wait()
 
 
-def attention_kernel(keep_ref, span_ref, message_ref, start_ref, *refs):
-    kv_refs, refs = refs[:ZS], refs[ZS:]
+def attention_kernel(offsets, final, keep_ref, span_ref, message_ref, start_ref, *refs):
+    pieces = len(offsets)
+    kv_refs, refs = refs[:pieces], refs[pieces:]
+    if final:
+        dqt_in_ref, refs = refs[0], refs[1:]
     dq_ref, refs = refs[0], refs[1:]
-    dkv_refs, refs = refs[:ZS], refs[ZS:]
+    dkv_refs, refs = refs[:pieces], refs[pieces:]
     acc_ref, kt_ref, q_ref, g_ref, qt_ref, gt_ref, dqt_ref = refs
     z = lax.axis_index("z")
-    sources = [lax.rem(z - off + ZS, ZS) for off in OFFSETS]
+    sources = [lax.rem(z - off + ZS, ZS) for off in offsets]
     lane_token = lax.rem(lax.broadcasted_iota(jnp.int32, (1, ROWS), 1), TOK)
     sublane = lax.broadcasted_iota(jnp.int32, (TOK, ROWS), 0)
+    keys = SPAN * pieces * TOK
 
     def keys_of(b, lanes):
         return jnp.concatenate(
-            [kv[b * PAIR + c, :, lanes] for c in range(PAIR) for kv in kv_refs], axis=0
+            [kv[b * SPAN + c, :, lanes] for c in range(SPAN) for kv in kv_refs], axis=0
         )
 
     def prepare(b, _):
         kt_ref[b] = keys_of(b, pl.ds(0, HD)).T
-        acc_ref[b] = jnp.zeros((PAIR * CHUNK, 2 * HD), F32)
+        acc_ref[b] = jnp.zeros((keys, 2 * HD), F32)
         return 0
 
-    lax.fori_loop(0, AS // PAIR, prepare, 0)
+    lax.fori_loop(0, AS // SPAN, prepare, 0)
 
     def pair_of_chunks(j, _):
         lse, delta, start, q_pos = [], [], [], []
@@ -173,14 +180,17 @@
             q_pos.append(i * CHUNK + z * TOK + lane_token)
         qt_ref[...] = q_ref[...].T
         gt_ref[...] = g_ref[...].T
-        dqt_ref[...] = jnp.zeros((HD, PAIR * ROWS), F32)
+        if final:
+            dqt_ref[...] = dqt_in_ref[j]
+        else:
+            dqt_ref[...] = jnp.zeros((HD, PAIR * ROWS), F32)
 
         def tile(b, masked):
             scores = jnp.dot(keys_of(b, pl.ds(0, HD)), qt_ref[...], preferred_element_type=F32)
             dprobs = jnp.dot(keys_of(b, pl.ds(HD, HD)), gt_ref[...], preferred_element_type=F32)
             probs_b, dscores_b = [], []
-            for k in range(PAIR * ZS):
-                a, r = b * PAIR + k // ZS, k % ZS
+            for k in range(SPAN * pieces):
+                a, r = b * SPAN + k // pieces, k % pieces
                 rows = slice(k * TOK, (k + 1) * TOK)
                 probs_row, dscores_row = [], []
                 for c in range(PAIR):
@@ -204,7 +214,8 @@
             dqt_ref[...] += jnp.dot(kt_ref[b], dscores_b, preferred_element_type=F32)
 
         def step(b, _):
-            masked = (b == j) | (span_ref[j * PAIR + PAIR - 1, 1] > b * PAIR * CHUNK)
+            reaches_own = (b + 1) * SPAN > j * PAIR
+            masked = reaches_own | (span_ref[j * PAIR + PAIR - 1, 1] > b * SPAN * CHUNK)
 
             @pl.when(masked)
             def _():
@@ -216,25 +227,59 @@
 
             return 0
 
-        lax.fori_loop(span_ref[j * PAIR, 0] // (PAIR * CHUNK), j + 1, step, 0)
+        first = span_ref[j * PAIR, 0] // (SPAN * CHUNK)
+        lax.fori_loop(first, (j * PAIR + PAIR - 1) // SPAN + 1, step, 0)
+        if not final:
+            dq_ref[j] = dqt_ref[...]
+            return 0
         dq = (dqt_ref[...] * SCALE).T.astype(BF16)
         for c in range(PAIR):
             for h in range(GROUP):
-                first = c * ROWS + h * TOK
-                dq_ref[j * PAIR + c, :, h * HD : (h + 1) * HD] = dq[first : first + TOK]
+                at = c * ROWS + h * TOK
+                dq_ref[j * PAIR + c, :, h * HD : (h + 1) * HD] = dq[at : at + TOK]
         return 0
 
     lax.fori_loop(0, AS // PAIR, pair_of_chunks, 0)
 
     def finish(b, _):
-        for k in range(PAIR * ZS):
+        for k in range(SPAN * pieces):
             piece = acc_ref[b, k * TOK : (k + 1) * TOK, :]
-            out = dkv_refs[k % ZS].at[b * PAIR + k // ZS]
+            out = dkv_refs[k % pieces].at[b * SPAN + k // pieces]
             out[:, :HD] = (piece[:, :HD] * SCALE).astype(BF16)
             out[:, HD:] = piece[:, HD:].astype(BF16)
         return 0
 
-    lax.fori_loop(0, AS // PAIR, finish, 0)
+    lax.fori_loop(0, AS // SPAN, finish, 0)
+
+
+def attention(offsets, scalars, message, start, kv, dqt=None):
+    final = dqt is not None
+    pieces = len(offsets)
+    keys = SPAN * pieces * TOK
+    rows = PAIR * ROWS
+    dqt_shape = jax.ShapeDtypeStruct((AS // PAIR, HD, rows), F32)
+    dq_shape = jax.ShapeDtypeStruct((AS, TOK, GROUP * HD), BF16)
+    results = pl.pallas_call(
+        functools.partial(attention_kernel, offsets, final),
+        out_shape=[dq_shape if final else dqt_shape]
+        + [jax.ShapeDtypeStruct((AS, TOK, 2 * HD), BF16)] * pieces,
+        in_specs=[in_smem()] * 2 + [in_vmem()] * (2 + pieces + final),
+        out_specs=[in_vmem()] * (1 + pieces),
+        scratch_shapes=[
+            pltpu.VMEM((AS // SPAN, keys, 2 * HD), F32),
+            pltpu.VMEM((AS // SPAN, HD, keys), BF16),
+            pltpu.VMEM((rows, HD), BF16),
+            pltpu.VMEM((rows, HD), BF16),
+            pltpu.VMEM((HD, rows), BF16),
+            pltpu.VMEM((HD, rows), BF16),
+            pltpu.VMEM((HD, rows), F32),
+        ],
+        compiler_params=pltpu.CompilerParams(vmem_limit_bytes=24 * 2**20),
+        cost_estimate=pl.CostEstimate(
+            flops=400000000 * pieces, bytes_accessed=3000000, transcendentals=300000 * pieces
+        ),
+    )(*scalars, message, start, *[kv[o] for o in offsets], *([dqt] if final else []))
+    return results[0], dict(zip(offsets, results[1:]))
 
 
 def sum_kernel(*refs):
@@ -244,30 +289,50 @@
     refs[-1][...] = total.astype(BF16)
 
 
-def unpack_queries_kernel(in_ref, out_ref, sems):
+def pack_gradients_kernel(dq_ref, *refs):
+    pieces, (out_ref, rows_ref, sems) = refs[:-3], refs[-3:]
+    dq_copy = pltpu.make_async_copy(dq_ref, out_ref.at[:, pl.ds(0, TOK), :], sems.at[0])
+    dq_copy.start()
+    total = pieces[0][...].astype(F32)
+    for piece in pieces[1:]:
+        total = total + piece[...].astype(F32)
+    total = total.astype(BF16)
+    for n in range(TOK // 8):
+        rows_ref[:, :, n * 2 * HD : (n + 1) * 2 * HD] = total[:, n * 8 : (n + 1) * 8, :]
+    rows_copy = pltpu.make_async_copy(rows_ref, out_ref.at[:, pl.ds(TOK, 8), :], sems.at[1])
+    rows_copy.start()
+    dq_copy.wait()
+    rows_copy.wait()
+
+
+def unpack_gradients_kernel(in_ref, dq_ref, dk_ref, dv_ref, sems, small):
     wide = GROUP * HD
     run_copies(
         [
-            pltpu.make_async_copy(in_ref.at[a], out_ref.at[:, pl.ds(a * wide, wide)], sems.at[a])
+            pltpu.make_async_copy(
+                in_ref.at[a, pl.ds(0, TOK), :], dq_ref.at[:, pl.ds(a * wide, wide)], sems.at[a]
+            )
             for a in range(AS)
         ]
-    )
-
-
-def unpack_kv_kernel(in_ref, dk_ref, dv_ref, sems):
-    run_copies(
-        [
+        + [
             pltpu.make_async_copy(
-                in_ref.at[a, :, pl.ds(n * HD, HD)], ref.at[:, pl.ds(a * HD, HD)], sems.at[n, a]
+                in_ref.at[a, pl.ds(TOK, 8), pl.ds((2 * n + m) * HD, HD)],
+                ref.at[pl.ds(n * 8, 8), pl.ds(a * HD, HD)],
+                small.at[m, n, a],
             )
-            for n, ref in enumerate((dk_ref, dv_ref))
             for a in range(AS)
+            for n in range(TOK // 8)
+            for m, ref in enumerate((dk_ref, dv_ref))
         ]
     )
 
 
 def in_hbm():
     return pl.BlockSpec(memory_space=pltpu.HBM)
+
+
+def held_in_hbm(*values):
+    return [pltpu.with_memory_space_constraint(v, pltpu.HBM) for v in values]
 
 
 def anywhere():
@@ -311,7 +376,7 @@
         scratch_shapes=[dma((2, AS))],
         compiler_params=small_kernel,
         cost_estimate=pl.CostEstimate(flops=0, bytes_accessed=262144, transcendentals=0),
-    )(key, value)
+    )(*held_in_hbm(key, value))
     kv_own = exchange(kv_send)
 
     reach = block_keep.shape[1]
@@ -330,7 +395,7 @@
         ],
         compiler_params=pltpu.CompilerParams(vmem_limit_bytes=8 * 2**20),
         cost_estimate=pl.CostEstimate(flops=67108864, bytes_accessed=2800000, transcendentals=0),
-    )(query, out_grad, output, lse, block_keep)
+    )(*held_in_hbm(query, out_grad, output, lse, block_keep))
     message = exchange(message_send)
 
     pieces = {0: kv_own}
@@ -356,57 +421,34 @@
     start_of = jnp.maximum(start_of - base, 0)
     span = jnp.stack([start_of[:, 0], start_of[:, TOK - 1]], axis=1)
 
-    piece_shape = jax.ShapeDtypeStruct((AS, TOK, 2 * HD), BF16)
-    results = pl.pallas_call(
-        attention_kernel,
-        out_shape=[jax.ShapeDtypeStruct((AS, TOK, columns), BF16)] + [piece_shape] * ZS,
-        in_specs=[in_smem()] * 2 + [in_vmem()] * (2 + ZS),
-        out_specs=[in_vmem()] * (1 + ZS),
-        scratch_shapes=[
-            pltpu.VMEM((AS // PAIR, PAIR * CHUNK, 2 * HD), F32),
-            pltpu.VMEM((AS // PAIR, HD, PAIR * CHUNK), BF16),
-            pltpu.VMEM((PAIR * ROWS, HD), BF16),
-            pltpu.VMEM((PAIR * ROWS, HD), BF16),
-            pltpu.VMEM((HD, PAIR * ROWS), BF16),
-            pltpu.VMEM((HD, PAIR * ROWS), BF16),
-            pltpu.VMEM((HD, PAIR * ROWS), F32),
-        ],
-        compiler_params=pltpu.CompilerParams(vmem_limit_bytes=24 * 2**20),
-        cost_estimate=pl.CostEstimate(
-            flops=3000000000, bytes_accessed=4000000, transcendentals=2360000
-        ),
-    )(keep, span, message, start_of.reshape(AS, 1, ROWS), *[pieces[o] for o in OFFSETS])
-    dq, part = results[0], dict(zip(OFFSETS, results[1:]))
-
+    scalars, start = (keep, span), start_of.reshape(AS, 1, ROWS)
+    dqt, part = attention(FAR, scalars, message, start, pieces)
     from_three, from_four = along_z(part[3], -1), along_z(part[4], -2)
     from_minus_three = along_z(part[-3], 1)
-    dq_back = exchange(dq)
+    dq, near_part = attention(NEAR, scalars, message, start, pieces, dqt)
+    part.update(near_part)
     one, minus_one = along_z(part[1], -1), along_z(part[-1], 1)
     two = along_z(partial_sum(part[2], from_three, from_four), -2)
     minus_two = along_z(partial_sum(part[-2], from_minus_three), 2)
-    returned = (part[0], one, minus_one, two, minus_two)
-    returned, dq_back = lax.optimization_barrier((returned, dq_back))
-    query_grad = pl.pallas_call(
-        unpack_queries_kernel,
-        out_shape=jax.ShapeDtypeStruct((TOK, AS * columns), BF16),
+    gradients_send = pl.pallas_call(
+        pack_gradients_kernel,
+        out_shape=jax.ShapeDtypeStruct((AS, TOK + 8, columns), BF16),
+        in_specs=[anywhere()] + [in_vmem()] * 5,
+        out_specs=anywhere(),
+        scratch_shapes=[pltpu.VMEM((AS, 8, columns), BF16), dma((2,))],
+        compiler_params=small_kernel,
+        cost_estimate=pl.CostEstimate(flops=400000, bytes_accessed=1900000, transcendentals=0),
+    )(dq, part[0], one, minus_one, two, minus_two)
+    half = jax.ShapeDtypeStruct((TOK, KVH * HD), BF16)
+    return pl.pallas_call(
+        unpack_gradients_kernel,
+        out_shape=[jax.ShapeDtypeStruct((TOK, AS * columns), BF16), half, half],
         in_specs=[anywhere()],
-        out_specs=anywhere(),
-        scratch_shapes=[dma((AS,))],
+        out_specs=[anywhere()] * 3,
+        scratch_shapes=[dma((AS,)), dma((2, TOK // 8, AS))],
         compiler_params=small_kernel,
-        cost_estimate=pl.CostEstimate(flops=0, bytes_accessed=1048576, transcendentals=0),
-    )(dq_back)
-    grads = exchange(partial_sum(*returned))
-    half = jax.ShapeDtypeStruct((TOK, KVH * HD), BF16)
-    key_grad, value_grad = pl.pallas_call(
-        unpack_kv_kernel,
-        out_shape=[half, half],
-        in_specs=[anywhere()],
-        out_specs=[anywhere(), anywhere()],
-        scratch_shapes=[dma((2, AS))],
-        compiler_params=small_kernel,
-        cost_estimate=pl.CostEstimate(flops=0, bytes_accessed=262144, transcendentals=0),
-    )(grads)
-    return (query_grad, key_grad, value_grad)
+        cost_estimate=pl.CostEstimate(flops=0, bytes_accessed=1300000, transcendentals=0),
+    )(exchange(gradients_send))
 
 
 def solution(mesh):

time: 101 us -> 96.5 us (0.955)
  blocking collectives: 0 us -> 15.4 us
  waiting for transfers between devices: 34 us -> 19.5 us
  Pallas kernels: 18.9 us -> 26.1 us
  starting transfers between devices: 39 us -> 32.5 us
  local copies, waits for them, and re-layouts: 6.27 us -> 0.08 us
    all_to_all x0 -> x1, blocking collectives: none -> 15.4 us  [exchange(): return lax.all_to_all(value, HEADS, split_axis=0, concat_axis=0, tiled=True)]
    ppermute x14, waiting for transfers between devices: 29.3 us -> 18.3 us  [along_z(): return lax.ppermute(value, 'z', [(i, (i + by) % ZS) for i in range(ZS)])]
    all_to_all x4 -> x2, starting transfers between devices: 17.7 us -> 7.97 us  [exchange(): return lax.all_to_all(value, HEADS, split_axis=0, concat_axis=0, tiled=True)]
    unnamed x16 -> x2, local copies, waits for them, and re-layouts: 6.2 us -> 0.01 us
    pallas_call x1, Pallas kernels: 0.8 us -> 5.22 us  [shards(): pl.pallas_call(pack_kv_kernel, out_shape=jax.ShapeDtypeStruct((AS, TOK, 2...]
    all_to_all x4 -> x2, waiting for transfers between devices: 4.71 us -> 1.17 us  [exchange(): return lax.all_to_all(value, HEADS, split_axis=0, concat_axis=0, tiled=True)]
    ppermute x14, starting transfers between devices: 21.3 us -> 24.6 us  [along_z(): return lax.ppermute(value, 'z', [(i, (i + by) % ZS) for i in range(ZS)])]
    pallas_call x3 -> x4, Pallas kernels: 13.6 us -> 16.5 us  [the longest x2 14.6 us: attention(): pl.pallas_call(functools.partial(attention_kernel, offsets, final), out_s...]
  transfers between devices with their start and end apart: 18 -> 16, of which waited for: 9 -> 8; matrix products, arithmetic and copies ran while one was open for 0% -> 0% of each run, Pallas kernels for 5% -> 20%
where the time goes in v5:
time: 96.5 us; the launch traced here: 95 us
  starting transfers between devices  32.5 us (34%)
  Pallas kernels  26.1 us (27%)
  waiting for transfers between devices  19.5 us (20%)
  blocking collectives  15.4 us (16%)
    ppermute x14, starting transfers between devices, along_z(): return lax.ppermute(value, 'z', [(i, (i + by) % ZS) for i in range(ZS)])  24.6 us
    ppermute x14, waiting for transfers between devices, along_z(): return lax.ppermute(value, 'z', [(i, (i + by) % ZS) for i in range(ZS)])  18.3 us
    all_to_all x1, blocking collectives, exchange(): return lax.all_to_all(value, HEADS, split_axis=0, concat_axis=0, tiled=True)  15.4 us
    pallas_call x2, Pallas kernels, attention(): pl.pallas_call(functools.partial(attention_kernel, offsets, final), out_s...  14.6 us
    all_to_all x2, starting transfers between devices, exchange(): return lax.all_to_all(value, HEADS, split_axis=0, concat_axis=0, tiled=True)  7.97 us
    pallas_call x1, Pallas kernels, shards(): pl.pallas_call(pack_kv_kernel, out_shape=jax.ShapeDtypeStruct((AS, TOK, 2...  5.22 us
    pallas_call x1, Pallas kernels, shards(): pl.pallas_call(pack_queries_kernel, out_shape=jax.ShapeDtypeStruct((AS, 2...  4.35 us
  transfers between devices with their start and end apart: 16, of which 8 were waited for; matrix products, arithmetic and copies ran while one was open for 0% of the time, Pallas kernels for 20%

profile of v5, /device:TPU:8, one launch (start us, length us, event | category | flops | bytes accessed | tf_op | source)
XLA Modules:
  0.0 95.0 jit_solution(2736898786711114368)
XLA Ops:
  0.6 5.2 %shard_map.104 = bf16[8,32,256]{2,1,0:T(8,128)(2,1)} custom-call(bf16[32,1024]{1,0:T(8,128)(2,1)} %k_ref.1, bf16[32,1024]{1,0:T(8,128)(2,1)} %v_ref.1), custom_call_target="tpu_custom_call" | custom-call | bytes 262144 | tf_op jit(solution)/shard_map/pallas_call | solution.py:371
  5.9 4.3 %all-to-all-start.1 = ((bf16[8,32,256]{2,1,0:T(8,128)(2,1)}), bf16[8,32,256]{2,1,0:T(8,128)(2,1)S(1)}, u32[]{:S(2)}, u32[]{:S(2)}) async-start(bf16[8,32,256]{2,1,0:T(8,128)(2,1)} %shard_map.104), calls=%async_computation.1 | async-start | bytes 262144 | tf_op jit(solution)/shard_map/all_to_all | solution.py:40
  10.2 4.4 %shard_map.103 = bf16[8,72,1024]{2,1,0:T(8,128)(2,1)} custom-call(bf16[32,8192]{1,0:T(8,128)(2,1)} %q_hbm.1, bf16[32,8192]{1,0:T(8,128)(2,1)} %g_hbm.1, bf16[32,8192]{1,0:T(8,128)(2,1)} %o_hbm.1, f32[32,64]{1,0:T(8,128)} %lse_hbm.1, s32[4,17]{1,0:T(4,128)} %keep_hbm.1), custom_call_target="tpu_custom_call" | custom-call | flops 67108864 | bytes 2800000 | tf_op jit(solution)/shard_map/pallas_call | solution.py:383
  14.6 1.2 %all-to-all-done.1.refs_0_ = bf16[8,32,256]{2,1,0:T(8,128)(2,1)S(1)} async-done(((bf16[8,32,256]{2,1,0:T(8,128)(2,1)}), bf16[8,32,256]{2,1,0:T(8,128)(2,1)S(1)}, u32[]{:S(2)}, u32[]{:S(2)}) %all-to-all-start.1) | async-done | bytes 131104 | tf_op jit(solution)/shard_map/all_to_all | solution.py:40
  15.7 3.7 %all-to-all-start = ((bf16[8,72,1024]{2,1,0:T(8,128)(2,1)}), bf16[8,72,1024]{2,1,0:T(8,128)(2,1)S(1)}, u32[]{:S(2)}, u32[]{:S(2)}) async-start(bf16[8,72,1024]{2,1,0:T(8,128)(2,1)} %shard_map.103), calls=%async_computation | async-start | bytes 2359296 | tf_op jit(solution)/shard_map/all_to_all | solution.py:40
  19.7 3.3 %collective-permute-start.3 = (bf16[8,32,256]{2,1,0:T(8,128)(2,1)S(1)}, bf16[8,32,256]{2,1,0:T(8,128)(2,1)S(1)}, u32[]{:S(2)}, u32[]{:S(2)}) collective-permute-start(bf16[8,32,256]{2,1,0:T(8,128)(2,1)S(1)} %all-to-all-done.1.refs_0_), channel_id=1, source_target_pairs={{0,2},{1,3},{2,4},{3,5},{4,6},{5,7},{6,0},{7,1},{8,10},{9,11},{10,... | collective-permute-start | bytes 393224 | tf_op jit(solution)/shard_map/ppermute | solution.py:36
  23.0 3.1 %collective-permute-start.2 = (bf16[8,32,256]{2,1,0:T(8,128)(2,1)S(1)}, bf16[8,32,256]{2,1,0:T(8,128)(2,1)S(1)}, u32[]{:S(2)}, u32[]{:S(2)}) collective-permute-start(bf16[8,32,256]{2,1,0:T(8,128)(2,1)S(1)} %all-to-all-done.1.refs_0_), channel_id=1, source_target_pairs={{0,6},{1,7},{2,0},{3,1},{4,2},{5,3},{6,4},{7,5},{8,14},{9,15},{10,... | collective-permute-start | bytes 393224 | tf_op jit(solution)/shard_map/ppermute | solution.py:36
  26.3 2.4 %collective-permute-start.1 = (bf16[8,32,256]{2,1,0:T(8,128)(2,1)S(1)}, bf16[8,32,256]{2,1,0:T(8,128)(2,1)S(1)}, u32[]{:S(2)}, u32[]{:S(2)}) collective-permute-start(bf16[8,32,256]{2,1,0:T(8,128)(2,1)S(1)} %all-to-all-done.1.refs_0_), channel_id=1, source_target_pairs={{0,7},{1,0},{2,1},{3,2},{4,3},{5,4},{6,5},{7,6},{8,15},{9,8},{10,9... | collective-permute-start | bytes 393224 | tf_op jit(solution)/shard_map/ppermute | solution.py:36
  28.7 2.1 %collective-permute-done.3.refs_3_ = bf16[8,32,256]{2,1,0:T(8,128)(2,1)S(1)} collective-permute-done((bf16[8,32,256]{2,1,0:T(8,128)(2,1)S(1)}, bf16[8,32,256]{2,1,0:T(8,128)(2,1)S(1)}, u32[]{:S(2)}, u32[]{:S(2)}) %collective-permute-start.3) | collective-permute-done | bytes 131104 | tf_op jit(solution)/shard_map/ppermute | solution.py:36
  30.8 3.2 %collective-permute-start.6 = (bf16[8,32,256]{2,1,0:T(8,128)(2,1)S(1)}, bf16[8,32,256]{2,1,0:T(8,128)(2,1)S(1)}, u32[]{:S(2)}, u32[]{:S(2)}) collective-permute-start(bf16[8,32,256]{2,1,0:T(8,128)(2,1)S(1)} %collective-permute-done.3.refs_3_), channel_id=1, source_target_pairs={{0,2},{1,3},{2,4},{3,5},{4,6},{5,7},{6,0},{7,1},{8,10},{9,11},{10,... | collective-permute-start | bytes 393224 | tf_op jit(solution)/shard_map/ppermute | solution.py:36
  34.6 2.7 %collective-permute-start.5 = (bf16[8,32,256]{2,1,0:T(8,128)(2,1)S(1)}, bf16[8,32,256]{2,1,0:T(8,128)(2,1)S(1)}, u32[]{:S(2)}, u32[]{:S(2)}) collective-permute-start(bf16[8,32,256]{2,1,0:T(8,128)(2,1)S(1)} %collective-permute-done.2.refs_3_), channel_id=1, source_target_pairs={{0,7},{1,0},{2,1},{3,2},{4,3},{5,4},{6,5},{7,6},{8,15},{9,8},{10,9... | collective-permute-start | bytes 393224 | tf_op jit(solution)/shard_map/ppermute | solution.py:36
  37.3 5.9 %collective-permute-done.6.refs_2_ = bf16[8,32,256]{2,1,0:T(8,128)(2,1)S(1)} collective-permute-done((bf16[8,32,256]{2,1,0:T(8,128)(2,1)S(1)}, bf16[8,32,256]{2,1,0:T(8,128)(2,1)S(1)}, u32[]{:S(2)}, u32[]{:S(2)}) %collective-permute-start.6) | collective-permute-done | bytes 131104 | tf_op jit(solution)/shard_map/ppermute | solution.py:36
  43.2 1.6 %collective-permute-done.4.refs_0_ = bf16[8,32,256]{2,1,0:T(8,128)(2,1)S(1)} collective-permute-done((bf16[8,32,256]{2,1,0:T(8,128)(2,1)S(1)}, bf16[8,32,256]{2,1,0:T(8,128)(2,1)S(1)}, u32[]{:S(2)}, u32[]{:S(2)}) %collective-permute-start.4) | collective-permute-done | bytes 131104 | tf_op jit(solution)/shard_map/ppermute | solution.py:36
  44.8 7.1 %shard_map.105 = (f32[4,128,512]{2,1,0:T(8,128)S(1)}, bf16[8,32,256]{2,1,0:T(8,128)(2,1)S(1)}, bf16[8,32,256]{2,1,0:T(8,128)(2,1)S(1)}, bf16[8,32,256]{2,1,0:T(8,128)(2,1)S(1)}, bf16[8,32,256]{2,1,0:T(8,128)(2,1)S(1)}) custom-call(s32[8,17]{1,0:T(8,128)S(1)} %bitcast.1, s32[8,2]{1,0:T(8,128)S(1)} %pad_add_fusion.span_ref, ...), custom_call_target="tpu_custom_call" | custom-call | flops 1600000000 | bytes 3000000 | tf_op jit(solution)/shard_map/pallas_call | solution.py:262
  51.9 0.6 collective-permute-start.9
  52.5 2.5 %collective-permute-start.10 = (bf16[8,32,256]{2,1,0:T(8,128)(2,1)S(1)}, bf16[8,32,256]{2,1,0:T(8,128)(2,1)S(1)}, u32[]{:S(2)}, u32[]{:S(2)}) collective-permute-start(bf16[8,32,256]{2,1,0:T(8,128)(2,1)S(1)} %get-tuple-element.20), channel_id=1, source_target_pairs={{0,6},{1,7},{2,0},{3,1},{4,2},{5,3},{6,4},{7,5},{8,14},{9,15},{10,... | collective-permute-start | bytes 393224 | tf_op jit(solution)/shard_map/ppermute | solution.py:36
  55.7 7.5 %shard_map.106 = (bf16[8,32,1024]{2,1,0:T(8,128)(2,1)S(1)}, bf16[8,32,256]{2,1,0:T(8,128)(2,1)S(1)}, bf16[8,32,256]{2,1,0:T(8,128)(2,1)S(1)}, bf16[8,32,256]{2,1,0:T(8,128)(2,1)S(1)}, bf16[8,32,256]{2,1,0:T(8,128)(2,1)S(1)}) custom-call(s32[8,17]{1,0:T(8,128)S(1)} %bitcast.2, s32[8,2]{1,0:T(8,128)S(1)} %pad_add_fusion.span_ref, ...), custom_call_target="tpu_custom_call" | custom-call | flops 1600000000 | bytes 3000000 | tf_op jit(solution)/shard_map/pallas_call | solution.py:262
  63.2 2.7 %collective-permute-start.7 = (bf16[8,32,256]{2,1,0:T(8,128)(2,1)S(1)}, bf16[8,32,256]{2,1,0:T(8,128)(2,1)S(1)}, u32[]{:S(2)}, u32[]{:S(2)}) collective-permute-start(bf16[8,32,256]{2,1,0:T(8,128)(2,1)S(1)} %get-tuple-element.16), channel_id=1, source_target_pairs={{0,7},{1,0},{2,1},{3,2},{4,3},{5,4},{6,5},{7,6},{8,15},{9,8},{10,9... | collective-permute-start | bytes 393224 | tf_op jit(solution)/shard_map/ppermute | solution.py:36
  66.0 2.1 %collective-permute-start.11 = (bf16[8,32,256]{2,1,0:T(8,128)(2,1)S(1)}, bf16[8,32,256]{2,1,0:T(8,128)(2,1)S(1)}, u32[]{:S(2)}, u32[]{:S(2)}) collective-permute-start(bf16[8,32,256]{2,1,0:T(8,128)(2,1)S(1)} %shard_map.107), channel_id=1, source_target_pairs={{0,6},{1,7},{2,0},{3,1},{4,2},{5,3},{6,4},{7,5},{8,14},{9,15},{10,... | collective-permute-start | bytes 393224 | tf_op jit(solution)/shard_map/ppermute | solution.py:36
  68.1 1.0 %collective-permute-start.13 = (bf16[8,32,256]{2,1,0:T(8,128)(2,1)S(1)}, bf16[8,32,256]{2,1,0:T(8,128)(2,1)S(1)}, u32[]{:S(2)}, u32[]{:S(2)}) collective-permute-start(bf16[8,32,256]{2,1,0:T(8,128)(2,1)S(1)} %shard_map.108), channel_id=1, source_target_pairs={{0,2},{1,3},{2,4},{3,5},{4,6},{5,7},{6,0},{7,1},{8,10},{9,11},{10,... | collective-permute-start | bytes 393224 | tf_op jit(solution)/shard_map/ppermute | solution.py:36
  69.3 6.5 %collective-permute-done.8.refs_2_ = bf16[8,32,256]{2,1,0:T(8,128)(2,1)S(1)} collective-permute-done((bf16[8,32,256]{2,1,0:T(8,128)(2,1)S(1)}, bf16[8,32,256]{2,1,0:T(8,128)(2,1)S(1)}, u32[]{:S(2)}, u32[]{:S(2)}) %collective-permute-start.8) | collective-permute-done | bytes 131104 | tf_op jit(solution)/shard_map/ppermute | solution.py:36
  75.7 1.7 %collective-permute-done.13.refs_4_ = bf16[8,32,256]{2,1,0:T(8,128)(2,1)S(1)} collective-permute-done((bf16[8,32,256]{2,1,0:T(8,128)(2,1)S(1)}, bf16[8,32,256]{2,1,0:T(8,128)(2,1)S(1)}, u32[]{:S(2)}, u32[]{:S(2)}) %collective-permute-start.13) | collective-permute-done | bytes 131104 | tf_op jit(solution)/shard_map/ppermute | solution.py:36
  77.6 15.4 %all_to_all.15.in_ref = bf16[8,40,1024]{2,1,0:T(8,128)(2,1)S(1)} all-to-all(bf16[8,40,1024]{2,1,0:T(8,128)(2,1)S(1)} %shard_map.109), channel_id=1, replica_groups=mesh['y'=4,'xl'=2,'c'=2,'xh'=2,'z'=8] {'xl','c','xh'}, dimensions={0} | all-to-all | bytes 1310720 | tf_op jit(solution)/shard_map/all_to_all | solution.py:40
  93.0 1.8 %shard_map.110 = (bf16[32,8192]{1,0:T(8,128)(2,1)}, bf16[32,1024]{1,0:T(8,128)(2,1)}, bf16[32,1024]{1,0:T(8,128)(2,1)}) custom-call(bf16[8,40,1024]{2,1,0:T(8,128)(2,1)S(1)} %all_to_all.15.in_ref), custom_call_target="tpu_custom_call" | custom-call | bytes 1300000 | tf_op jit(solution)/shard_map/pallas_call | solution.py:443
  (29 shorter events, 2.0 us)
Async XLA Ops:
  5.9 9.9 %all-to-all-start.1 = ((bf16[8,32,256]{2,1,0:T(8,128)(2,1)}), bf16[8,32,256]{2,1,0:T(8,128)(2,1)S(1)}, u32[]{:S(2)}, u32[]{:S(2)}) async-start(bf16[8,32,256]{2,1,0:T(8,128)(2,1)} %shard_map.104), calls=%async_computation.1 | async-start | bytes 262144 | tf_op jit(solution)/shard_map/all_to_all | solution.py:40
  14.5 4.8 %copy-start = (s32[7]{0:T(128)S(1)}, s32[7]{0:T(128)}, u32[]{:S(2)}) copy-start(s32[7]{0:T(128)} %param.14) | copy-start | bytes 88
  15.7 21.6 %all-to-all-start = ((bf16[8,72,1024]{2,1,0:T(8,128)(2,1)}), bf16[8,72,1024]{2,1,0:T(8,128)(2,1)S(1)}, u32[]{:S(2)}, u32[]{:S(2)}) async-start(bf16[8,72,1024]{2,1,0:T(8,128)(2,1)} %shard_map.103), calls=%async_computation | async-start | bytes 2359296 | tf_op jit(solution)/shard_map/all_to_all | solution.py:40
  19.7 11.1 %collective-permute-start.3 = (bf16[8,32,256]{2,1,0:T(8,128)(2,1)S(1)}, bf16[8,32,256]{2,1,0:T(8,128)(2,1)S(1)}, u32[]{:S(2)}, u32[]{:S(2)}) collective-permute-start(bf16[8,32,256]{2,1,0:T(8,128)(2,1)S(1)} %all-to-all-done.1.refs_0_), channel_id=1, source_target_pairs={{0,2},{1,3},{2,4},{3,5},{4,6},{5,7},{6,0},{7,1},{8,10},{9,11},{10,... | collective-permute-start | bytes 393224 | tf_op jit(solution)/shard_map/ppermute | solution.py:36
  23.0 11.6 %collective-permute-start.2 = (bf16[8,32,256]{2,1,0:T(8,128)(2,1)S(1)}, bf16[8,32,256]{2,1,0:T(8,128)(2,1)S(1)}, u32[]{:S(2)}, u32[]{:S(2)}) collective-permute-start(bf16[8,32,256]{2,1,0:T(8,128)(2,1)S(1)} %all-to-all-done.1.refs_0_), channel_id=1, source_target_pairs={{0,6},{1,7},{2,0},{3,1},{4,2},{5,3},{6,4},{7,5},{8,14},{9,15},{10,... | collective-permute-start | bytes 393224 | tf_op jit(solution)/shard_map/ppermute | solution.py:36
  26.3 29.4 %collective-permute-start.1 = (bf16[8,32,256]{2,1,0:T(8,128)(2,1)S(1)}, bf16[8,32,256]{2,1,0:T(8,128)(2,1)S(1)}, u32[]{:S(2)}, u32[]{:S(2)}) collective-permute-start(bf16[8,32,256]{2,1,0:T(8,128)(2,1)S(1)} %all-to-all-done.1.refs_0_), channel_id=1, source_target_pairs={{0,7},{1,0},{2,1},{3,2},{4,3},{5,4},{6,5},{7,6},{8,15},{9,8},{10,9... | collective-permute-start | bytes 393224 | tf_op jit(solution)/shard_map/ppermute | solution.py:36
  28.7 27.0 %collective-permute-start = (bf16[8,32,256]{2,1,0:T(8,128)(2,1)S(1)}, bf16[8,32,256]{2,1,0:T(8,128)(2,1)S(1)}, u32[]{:S(2)}, u32[]{:S(2)}) collective-permute-start(bf16[8,32,256]{2,1,0:T(8,128)(2,1)S(1)} %all-to-all-done.1.refs_0_), channel_id=1, source_target_pairs={{0,1},{1,2},{2,3},{3,4},{4,5},{5,6},{6,7},{7,0},{8,9},{9,10},{10,1... | collective-permute-start | bytes 393224 | tf_op jit(solution)/shard_map/ppermute | solution.py:36
  30.8 12.4 %collective-permute-start.6 = (bf16[8,32,256]{2,1,0:T(8,128)(2,1)S(1)}, bf16[8,32,256]{2,1,0:T(8,128)(2,1)S(1)}, u32[]{:S(2)}, u32[]{:S(2)}) collective-permute-start(bf16[8,32,256]{2,1,0:T(8,128)(2,1)S(1)} %collective-permute-done.3.refs_3_), channel_id=1, source_target_pairs={{0,2},{1,3},{2,4},{3,5},{4,6},{5,7},{6,0},{7,1},{8,10},{9,11},{10,... | collective-permute-start | bytes 393224 | tf_op jit(solution)/shard_map/ppermute | solution.py:36
  34.1 10.7 %collective-permute-start.4 = (bf16[8,32,256]{2,1,0:T(8,128)(2,1)S(1)}, bf16[8,32,256]{2,1,0:T(8,128)(2,1)S(1)}, u32[]{:S(2)}, u32[]{:S(2)}) collective-permute-start(bf16[8,32,256]{2,1,0:T(8,128)(2,1)S(1)} %collective-permute-done.3.refs_3_), channel_id=1, source_target_pairs={{0,1},{1,2},{2,3},{3,4},{4,5},{5,6},{6,7},{7,0},{8,9},{9,10},{10,1... | collective-permute-start | bytes 393224 | tf_op jit(solution)/shard_map/ppermute | solution.py:36
  34.6 10.2 %collective-permute-start.5 = (bf16[8,32,256]{2,1,0:T(8,128)(2,1)S(1)}, bf16[8,32,256]{2,1,0:T(8,128)(2,1)S(1)}, u32[]{:S(2)}, u32[]{:S(2)}) collective-permute-start(bf16[8,32,256]{2,1,0:T(8,128)(2,1)S(1)} %collective-permute-done.2.refs_3_), channel_id=1, source_target_pairs={{0,7},{1,0},{2,1},{3,2},{4,3},{5,4},{6,5},{7,6},{8,15},{9,8},{10,9... | collective-permute-start | bytes 393224 | tf_op jit(solution)/shard_map/ppermute | solution.py:36
  51.9 14.0 %collective-permute-start.9 = (bf16[8,32,256]{2,1,0:T(8,128)(2,1)S(1)}, bf16[8,32,256]{2,1,0:T(8,128)(2,1)S(1)}, u32[]{:S(2)}, u32[]{:S(2)}) collective-permute-start(bf16[8,32,256]{2,1,0:T(8,128)(2,1)S(1)} %get-tuple-element.19), channel_id=1, source_target_pairs={{0,7},{1,0},{2,1},{3,2},{4,3},{5,4},{6,5},{7,6},{8,15},{9,8},{10,9... | collective-permute-start | bytes 393224 | tf_op jit(solution)/shard_map/ppermute | solution.py:36
  52.5 13.3 %collective-permute-start.10 = (bf16[8,32,256]{2,1,0:T(8,128)(2,1)S(1)}, bf16[8,32,256]{2,1,0:T(8,128)(2,1)S(1)}, u32[]{:S(2)}, u32[]{:S(2)}) collective-permute-start(bf16[8,32,256]{2,1,0:T(8,128)(2,1)S(1)} %get-tuple-element.20), channel_id=1, source_target_pairs={{0,6},{1,7},{2,0},{3,1},{4,2},{5,3},{6,4},{7,5},{8,14},{9,15},{10,... | collective-permute-start | bytes 393224 | tf_op jit(solution)/shard_map/ppermute | solution.py:36
  55.1 13.0 %collective-permute-start.12 = (bf16[8,32,256]{2,1,0:T(8,128)(2,1)S(1)}, bf16[8,32,256]{2,1,0:T(8,128)(2,1)S(1)}, u32[]{:S(2)}, u32[]{:S(2)}) collective-permute-start(bf16[8,32,256]{2,1,0:T(8,128)(2,1)S(1)} %get-tuple-element.22), channel_id=1, source_target_pairs={{0,1},{1,2},{2,3},{3,4},{4,5},{5,6},{6,7},{7,0},{8,9},{9,10},{10,1... | collective-permute-start | bytes 393224 | tf_op jit(solution)/shard_map/ppermute | solution.py:36
  63.2 6.1 %collective-permute-start.7 = (bf16[8,32,256]{2,1,0:T(8,128)(2,1)S(1)}, bf16[8,32,256]{2,1,0:T(8,128)(2,1)S(1)}, u32[]{:S(2)}, u32[]{:S(2)}) collective-permute-start(bf16[8,32,256]{2,1,0:T(8,128)(2,1)S(1)} %get-tuple-element.16), channel_id=1, source_target_pairs={{0,7},{1,0},{2,1},{3,2},{4,3},{5,4},{6,5},{7,6},{8,15},{9,8},{10,9... | collective-permute-start | bytes 393224 | tf_op jit(solution)/shard_map/ppermute | solution.py:36
  65.9 9.9 %collective-permute-start.8 = (bf16[8,32,256]{2,1,0:T(8,128)(2,1)S(1)}, bf16[8,32,256]{2,1,0:T(8,128)(2,1)S(1)}, u32[]{:S(2)}, u32[]{:S(2)}) collective-permute-start(bf16[8,32,256]{2,1,0:T(8,128)(2,1)S(1)} %get-tuple-element.17), channel_id=1, source_target_pairs={{0,1},{1,2},{2,3},{3,4},{4,5},{5,6},{6,7},{7,0},{8,9},{9,10},{10,1... | collective-permute-start | bytes 393224 | tf_op jit(solution)/shard_map/ppermute | solution.py:36
  66.0 9.8 %collective-permute-start.11 = (bf16[8,32,256]{2,1,0:T(8,128)(2,1)S(1)}, bf16[8,32,256]{2,1,0:T(8,128)(2,1)S(1)}, u32[]{:S(2)}, u32[]{:S(2)}) collective-permute-start(bf16[8,32,256]{2,1,0:T(8,128)(2,1)S(1)} %shard_map.107), channel_id=1, source_target_pairs={{0,6},{1,7},{2,0},{3,1},{4,2},{5,3},{6,4},{7,5},{8,14},{9,15},{10,... | collective-permute-start | bytes 393224 | tf_op jit(solution)/shard_map/ppermute | solution.py:36
  68.1 9.4 %collective-permute-start.13 = (bf16[8,32,256]{2,1,0:T(8,128)(2,1)S(1)}, bf16[8,32,256]{2,1,0:T(8,128)(2,1)S(1)}, u32[]{:S(2)}, u32[]{:S(2)}) collective-permute-start(bf16[8,32,256]{2,1,0:T(8,128)(2,1)S(1)} %shard_map.108), channel_id=1, source_target_pairs={{0,2},{1,3},{2,4},{3,5},{4,6},{5,7},{6,0},{7,1},{8,10},{9,11},{10,... | collective-permute-start | bytes 393224 | tf_op jit(solution)/shard_map/ppermute | solution.py:36

commit v6 on v5

--- a/solution.py
+++ b/solution.py
@@ -40,23 +40,25 @@
     return lax.all_to_all(value, HEADS, split_axis=0, concat_axis=0, tiled=True)
 
 
-def run_copies(copies):
+def own_place():
+    return (lax.axis_index("xl") * 2 + lax.axis_index("c")) * 2 + lax.axis_index("xh")
+
+
+def shifted(value, by):
+    return lax.ppermute(value, HEADS, [(i, (i + by) % AS) for i in range(AS)])
+
+
+def pack_kv_kernel(k_hbm, v_hbm, out_ref, k_ref, v_ref, sems):
+    copies = [
+        pltpu.make_async_copy(k_hbm, k_ref, sems.at[0]),
+        pltpu.make_async_copy(v_hbm, v_ref, sems.at[1]),
+    ]
     for copy in copies:
         copy.start()
-    for copy in copies:
+    for n, (copy, ref) in enumerate(zip(copies, (k_ref, v_ref))):
         copy.wait()
-
-
-def pack_kv_kernel(k_ref, v_ref, out_ref, sems):
-    run_copies(
-        [
-            pltpu.make_async_copy(
-                ref.at[:, pl.ds(a * HD, HD)], out_ref.at[a, :, pl.ds(n * HD, HD)], sems.at[n, a]
-            )
-            for n, ref in enumerate((k_ref, v_ref))
-            for a in range(AS)
-        ]
-    )
+        for a in range(AS):
+            out_ref[a, :, n * HD : (n + 1) * HD] = ref[:, a * HD : (a + 1) * HD]
 
 
 def split(value):
@@ -290,41 +292,54 @@
 
 
 def pack_gradients_kernel(dq_ref, *refs):
-    pieces, (out_ref, rows_ref, sems) = refs[:-3], refs[-3:]
-    dq_copy = pltpu.make_async_copy(dq_ref, out_ref.at[:, pl.ds(0, TOK), :], sems.at[0])
-    dq_copy.start()
+    pieces, out_refs, (total_ref, sems) = refs[:5], refs[5 : 5 + AS], refs[5 + AS :]
+    me = own_place()
+    copies = []
+    for k, out_ref in enumerate(out_refs):
+        there = lax.rem(me + k, AS)
+        copies.append(
+            pltpu.make_async_copy(dq_ref.at[there], out_ref.at[pl.ds(0, TOK), :], sems.at[k])
+        )
+    for copy in copies:
+        copy.start()
     total = pieces[0][...].astype(F32)
     for piece in pieces[1:]:
         total = total + piece[...].astype(F32)
-    total = total.astype(BF16)
-    for n in range(TOK // 8):
-        rows_ref[:, :, n * 2 * HD : (n + 1) * 2 * HD] = total[:, n * 8 : (n + 1) * 8, :]
-    rows_copy = pltpu.make_async_copy(rows_ref, out_ref.at[:, pl.ds(TOK, 8), :], sems.at[1])
-    rows_copy.start()
-    dq_copy.wait()
-    rows_copy.wait()
-
-
-def unpack_gradients_kernel(in_ref, dq_ref, dk_ref, dv_ref, sems, small):
+    total_ref[...] = total.astype(BF16)
+    for k, out_ref in enumerate(out_refs):
+        there = lax.rem(me + k, AS)
+        for n in range(TOK // 8):
+            columns = slice(n * 2 * HD, (n + 1) * 2 * HD)
+            out_ref[TOK:, columns] = total_ref[there, n * 8 : (n + 1) * 8, :]
+    for copy in copies:
+        copy.wait()
+
+
+def unpack_gradients_kernel(*refs):
+    in_refs, (dq_hbm, dk_hbm, dv_hbm, dk_ref, dv_ref, sems) = refs[:AS], refs[AS:]
     wide = GROUP * HD
-    run_copies(
-        [
-            pltpu.make_async_copy(
-                in_ref.at[a, pl.ds(0, TOK), :], dq_ref.at[:, pl.ds(a * wide, wide)], sems.at[a]
-            )
-            for a in range(AS)
-        ]
-        + [
-            pltpu.make_async_copy(
-                in_ref.at[a, pl.ds(TOK, 8), pl.ds((2 * n + m) * HD, HD)],
-                ref.at[pl.ds(n * 8, 8), pl.ds(a * HD, HD)],
-                small.at[m, n, a],
-            )
-            for a in range(AS)
-            for n in range(TOK // 8)
-            for m, ref in enumerate((dk_ref, dv_ref))
-        ]
-    )
+    me = own_place()
+    copies = []
+    for k, in_ref in enumerate(in_refs):
+        a = lax.rem(me - k + AS, AS)
+        columns = pl.ds(pl.multiple_of(a * wide, wide), wide)
+        copies.append(
+            pltpu.make_async_copy(in_ref.at[pl.ds(0, TOK), :], dq_hbm.at[:, columns], sems.at[k])
+        )
+        copies[-1].start()
+    for k, in_ref in enumerate(in_refs):
+        a = lax.rem(me - k + AS, AS)
+        columns = pl.ds(pl.multiple_of(a * HD, HD), HD)
+        for n in range(TOK // 8):
+            rows = slice(n * 8, (n + 1) * 8)
+            dk_ref[rows, columns] = in_ref[TOK:, 2 * n * HD : (2 * n + 1) * HD]
+            dv_ref[rows, columns] = in_ref[TOK:, (2 * n + 1) * HD : (2 * n + 2) * HD]
+    copies.append(pltpu.make_async_copy(dk_ref, dk_hbm, sems.at[AS]))
+    copies.append(pltpu.make_async_copy(dv_ref, dv_hbm, sems.at[AS + 1]))
+    copies[-2].start()
+    copies[-1].start()
+    for copy in copies:
+        copy.wait()
 
 
 def in_hbm():
@@ -372,8 +387,8 @@
         pack_kv_kernel,
         out_shape=jax.ShapeDtypeStruct((AS, TOK, 2 * HD), BF16),
         in_specs=[in_hbm(), in_hbm()],
-        out_specs=anywhere(),
-        scratch_shapes=[dma((2, AS))],
+        out_specs=in_vmem(),
+        scratch_shapes=[pltpu.VMEM(key.shape, BF16), pltpu.VMEM(key.shape, BF16), dma((2,))],
         compiler_params=small_kernel,
         cost_estimate=pl.CostEstimate(flops=0, bytes_accessed=262144, transcendentals=0),
     )(*held_in_hbm(key, value))
@@ -430,25 +445,30 @@
     one, minus_one = along_z(part[1], -1), along_z(part[-1], 1)
     two = along_z(partial_sum(part[2], from_three, from_four), -2)
     minus_two = along_z(partial_sum(part[-2], from_minus_three), 2)
-    gradients_send = pl.pallas_call(
+    gradients = pl.pallas_call(
         pack_gradients_kernel,
-        out_shape=jax.ShapeDtypeStruct((AS, TOK + 8, columns), BF16),
-        in_specs=[anywhere()] + [in_vmem()] * 5,
-        out_specs=anywhere(),
-        scratch_shapes=[pltpu.VMEM((AS, 8, columns), BF16), dma((2,))],
+        out_shape=[jax.ShapeDtypeStruct((TOK + 8, columns), BF16)] * AS,
+        in_specs=[in_vmem()] * 6,
+        out_specs=[in_vmem()] * AS,
+        scratch_shapes=[pltpu.VMEM((AS, TOK, 2 * HD), BF16), dma((AS,))],
         compiler_params=small_kernel,
         cost_estimate=pl.CostEstimate(flops=400000, bytes_accessed=1900000, transcendentals=0),
     )(dq, part[0], one, minus_one, two, minus_two)
+    gradients = [gradients[0]] + [shifted(gradients[k], k) for k in range(1, AS)]
     half = jax.ShapeDtypeStruct((TOK, KVH * HD), BF16)
     return pl.pallas_call(
         unpack_gradients_kernel,
         out_shape=[jax.ShapeDtypeStruct((TOK, AS * columns), BF16), half, half],
-        in_specs=[anywhere()],
-        out_specs=[anywhere()] * 3,
-        scratch_shapes=[dma((AS,)), dma((2, TOK // 8, AS))],
+        in_specs=[in_vmem()] * AS,
+        out_specs=[in_hbm()] * 3,
+        scratch_shapes=[
+            pltpu.VMEM(half.shape, BF16),
+            pltpu.VMEM(half.shape, BF16),
+            dma((AS + 2,)),
+        ],
         compiler_params=small_kernel,
         cost_estimate=pl.CostEstimate(flops=0, bytes_accessed=1300000, transcendentals=0),
-    )(exchange(gradients_send))
+    )(*gradients)
 
 
 def solution(mesh):

time: 96.5 us -> 90.1 us (0.934); the launches traced: 95 us -> 90 us
  blocking collectives: 15.4 us -> 0 us
  starting transfers between devices: 32.5 us -> 41 us
  waiting for transfers between devices: 19.5 us -> 25.2 us
  Pallas kernels: 26.1 us -> 22.3 us
    all_to_all x1 -> x0, blocking collectives: 15.4 us -> none  [exchange(): return lax.all_to_all(value, HEADS, split_axis=0, concat_axis=0, tiled=True)]
    ppermute x0 -> x7, starting transfers between devices: none -> 8.54 us  [shifted(): return lax.ppermute(value, HEADS, [(i, (i + by) % AS) for i in range(AS)])]
    ppermute x0 -> x7, waiting for transfers between devices: none -> 5.65 us  [shifted(): return lax.ppermute(value, HEADS, [(i, (i + by) % AS) for i in range(AS)])]
    pallas_call x1, Pallas kernels: 5.22 us -> 1.55 us  [shards(): pl.pallas_call(pack_kv_kernel, out_shape=jax.ShapeDtypeStruct((AS, TOK, 2...]
  transfers between devices with their start and end apart: 16 -> 23, of which waited for: 8 -> 13; matrix products, arithmetic and copies ran while one was open for 0% -> 0% of each run, Pallas kernels for 20% -> 21%
where the time goes in v6:
time: 90.1 us; the launch traced here: 90 us
  starting transfers between devices  41 us (46%)
  waiting for transfers between devices  25.2 us (28%)
  Pallas kernels  22.3 us (25%)
  between operations  0.92 us (1%)
    ppermute x14, starting transfers between devices, along_z(): return lax.ppermute(value, 'z', [(i, (i + by) % ZS) for i in range(ZS)])  24.5 us
    ppermute x14, waiting for transfers between devices, along_z(): return lax.ppermute(value, 'z', [(i, (i + by) % ZS) for i in range(ZS)])  18.4 us
    pallas_call x2, Pallas kernels, attention(): pl.pallas_call(functools.partial(attention_kernel, offsets, final), out_s...  14.6 us
    ppermute x7, starting transfers between devices, shifted(): return lax.ppermute(value, HEADS, [(i, (i + by) % AS) for i in range(AS)])  8.54 us
    all_to_all x2, starting transfers between devices, exchange(): return lax.all_to_all(value, HEADS, split_axis=0, concat_axis=0, tiled=True)  7.97 us
    ppermute x7, waiting for transfers between devices, shifted(): return lax.ppermute(value, HEADS, [(i, (i + by) % AS) for i in range(AS)])  5.65 us
    pallas_call x1, Pallas kernels, shards(): pl.pallas_call(pack_queries_kernel, out_shape=jax.ShapeDtypeStruct((AS, 2...  4.35 us
  transfers between devices with their start and end apart: 23, of which 13 were waited for; matrix products, arithmetic and copies ran while one was open for 0% of the time, Pallas kernels for 21%

profile of v6, /device:TPU:8, one launch (start us, length us, event | category | flops | bytes accessed | tf_op | source)
XLA Modules:
  0.0 90.0 jit_solution(12347520650757140750)
XLA Ops:
  0.6 1.6 %shard_map.104 = bf16[8,32,256]{2,1,0:T(8,128)(2,1)} custom-call(bf16[32,1024]{1,0:T(8,128)(2,1)} %k_hbm.1, bf16[32,1024]{1,0:T(8,128)(2,1)} %v_hbm.1), custom_call_target="tpu_custom_call" | custom-call | bytes 262144 | tf_op jit(solution)/shard_map/pallas_call | solution.py:386
  2.2 4.3 %all-to-all-start.1 = ((bf16[8,32,256]{2,1,0:T(8,128)(2,1)}), bf16[8,32,256]{2,1,0:T(8,128)(2,1)S(1)}, u32[]{:S(2)}, u32[]{:S(2)}) async-start(bf16[8,32,256]{2,1,0:T(8,128)(2,1)} %shard_map.104), calls=%async_computation.1 | async-start | bytes 262144 | tf_op jit(solution)/shard_map/all_to_all | solution.py:40
  6.5 4.3 %shard_map.103 = bf16[8,72,1024]{2,1,0:T(8,128)(2,1)} custom-call(bf16[32,8192]{1,0:T(8,128)(2,1)} %q_hbm.1, bf16[32,8192]{1,0:T(8,128)(2,1)} %g_hbm.1, bf16[32,8192]{1,0:T(8,128)(2,1)} %o_hbm.1, f32[32,64]{1,0:T(8,128)} %lse_hbm.1, s32[4,17]{1,0:T(4,128)} %keep_hbm.1), custom_call_target="tpu_custom_call" | custom-call | flops 67108864 | bytes 2800000 | tf_op jit(solution)/shard_map/pallas_call | solution.py:398
  12.1 3.7 %all-to-all-start = ((bf16[8,72,1024]{2,1,0:T(8,128)(2,1)}), bf16[8,72,1024]{2,1,0:T(8,128)(2,1)S(1)}, u32[]{:S(2)}, u32[]{:S(2)}) async-start(bf16[8,72,1024]{2,1,0:T(8,128)(2,1)} %shard_map.103), calls=%async_computation | async-start | bytes 2359296 | tf_op jit(solution)/shard_map/all_to_all | solution.py:40
  16.0 3.3 %collective-permute-start.3 = (bf16[8,32,256]{2,1,0:T(8,128)(2,1)S(1)}, bf16[8,32,256]{2,1,0:T(8,128)(2,1)S(1)}, u32[]{:S(2)}, u32[]{:S(2)}) collective-permute-start(bf16[8,32,256]{2,1,0:T(8,128)(2,1)S(1)} %all-to-all-done.1.refs_0_), channel_id=1, source_target_pairs={{0,2},{1,3},{2,4},{3,5},{4,6},{5,7},{6,0},{7,1},{8,10},{9,11},{10,... | collective-permute-start | bytes 393224 | tf_op jit(solution)/shard_map/ppermute | solution.py:36
  19.4 3.1 %collective-permute-start.2 = (bf16[8,32,256]{2,1,0:T(8,128)(2,1)S(1)}, bf16[8,32,256]{2,1,0:T(8,128)(2,1)S(1)}, u32[]{:S(2)}, u32[]{:S(2)}) collective-permute-start(bf16[8,32,256]{2,1,0:T(8,128)(2,1)S(1)} %all-to-all-done.1.refs_0_), channel_id=1, source_target_pairs={{0,6},{1,7},{2,0},{3,1},{4,2},{5,3},{6,4},{7,5},{8,14},{9,15},{10,... | collective-permute-start | bytes 393224 | tf_op jit(solution)/shard_map/ppermute | solution.py:36
  22.6 2.4 %collective-permute-start.1 = (bf16[8,32,256]{2,1,0:T(8,128)(2,1)S(1)}, bf16[8,32,256]{2,1,0:T(8,128)(2,1)S(1)}, u32[]{:S(2)}, u32[]{:S(2)}) collective-permute-start(bf16[8,32,256]{2,1,0:T(8,128)(2,1)S(1)} %all-to-all-done.1.refs_0_), channel_id=1, source_target_pairs={{0,7},{1,0},{2,1},{3,2},{4,3},{5,4},{6,5},{7,6},{8,15},{9,8},{10,9... | collective-permute-start | bytes 393224 | tf_op jit(solution)/shard_map/ppermute | solution.py:36
  25.0 2.1 %collective-permute-done.3.refs_3_ = bf16[8,32,256]{2,1,0:T(8,128)(2,1)S(1)} collective-permute-done((bf16[8,32,256]{2,1,0:T(8,128)(2,1)S(1)}, bf16[8,32,256]{2,1,0:T(8,128)(2,1)S(1)}, u32[]{:S(2)}, u32[]{:S(2)}) %collective-permute-start.3) | collective-permute-done | bytes 131104 | tf_op jit(solution)/shard_map/ppermute | solution.py:36
  27.1 3.2 %collective-permute-start.6 = (bf16[8,32,256]{2,1,0:T(8,128)(2,1)S(1)}, bf16[8,32,256]{2,1,0:T(8,128)(2,1)S(1)}, u32[]{:S(2)}, u32[]{:S(2)}) collective-permute-start(bf16[8,32,256]{2,1,0:T(8,128)(2,1)S(1)} %collective-permute-done.3.refs_3_), channel_id=1, source_target_pairs={{0,2},{1,3},{2,4},{3,5},{4,6},{5,7},{6,0},{7,1},{8,10},{9,11},{10,... | collective-permute-start | bytes 393224 | tf_op jit(solution)/shard_map/ppermute | solution.py:36
  30.9 2.7 %collective-permute-start.5 = (bf16[8,32,256]{2,1,0:T(8,128)(2,1)S(1)}, bf16[8,32,256]{2,1,0:T(8,128)(2,1)S(1)}, u32[]{:S(2)}, u32[]{:S(2)}) collective-permute-start(bf16[8,32,256]{2,1,0:T(8,128)(2,1)S(1)} %collective-permute-done.2.refs_3_), channel_id=1, source_target_pairs={{0,7},{1,0},{2,1},{3,2},{4,3},{5,4},{6,5},{7,6},{8,15},{9,8},{10,9... | collective-permute-start | bytes 393224 | tf_op jit(solution)/shard_map/ppermute | solution.py:36
  33.7 5.9 %collective-permute-done.6.refs_2_ = bf16[8,32,256]{2,1,0:T(8,128)(2,1)S(1)} collective-permute-done((bf16[8,32,256]{2,1,0:T(8,128)(2,1)S(1)}, bf16[8,32,256]{2,1,0:T(8,128)(2,1)S(1)}, u32[]{:S(2)}, u32[]{:S(2)}) %collective-permute-start.6) | collective-permute-done | bytes 131104 | tf_op jit(solution)/shard_map/ppermute | solution.py:36
  39.6 1.6 %collective-permute-done.4.refs_0_ = bf16[8,32,256]{2,1,0:T(8,128)(2,1)S(1)} collective-permute-done((bf16[8,32,256]{2,1,0:T(8,128)(2,1)S(1)}, bf16[8,32,256]{2,1,0:T(8,128)(2,1)S(1)}, u32[]{:S(2)}, u32[]{:S(2)}) %collective-permute-start.4) | collective-permute-done | bytes 131104 | tf_op jit(solution)/shard_map/ppermute | solution.py:36
  41.2 7.1 %shard_map.105 = (f32[4,128,512]{2,1,0:T(8,128)S(1)}, bf16[8,32,256]{2,1,0:T(8,128)(2,1)S(1)}, bf16[8,32,256]{2,1,0:T(8,128)(2,1)S(1)}, bf16[8,32,256]{2,1,0:T(8,128)(2,1)S(1)}, bf16[8,32,256]{2,1,0:T(8,128)(2,1)S(1)}) custom-call(s32[8,17]{1,0:T(8,128)S(1)} %bitcast.1, s32[8,2]{1,0:T(8,128)S(1)} %pad_add_fusion.span_ref, ...), custom_call_target="tpu_custom_call" | custom-call | flops 1600000000 | bytes 3000000 | tf_op jit(solution)/shard_map/pallas_call | solution.py:264
  48.9 2.5 %collective-permute-start.10 = (bf16[8,32,256]{2,1,0:T(8,128)(2,1)S(1)}, bf16[8,32,256]{2,1,0:T(8,128)(2,1)S(1)}, u32[]{:S(2)}, u32[]{:S(2)}) collective-permute-start(bf16[8,32,256]{2,1,0:T(8,128)(2,1)S(1)} %get-tuple-element.28), channel_id=1, source_target_pairs={{0,6},{1,7},{2,0},{3,1},{4,2},{5,3},{6,4},{7,5},{8,14},{9,15},{10,... | collective-permute-start | bytes 393224 | tf_op jit(solution)/shard_map/ppermute | solution.py:36
  52.0 7.5 %shard_map.106 = (bf16[8,32,1024]{2,1,0:T(8,128)(2,1)S(1)}, bf16[8,32,256]{2,1,0:T(8,128)(2,1)S(1)}, bf16[8,32,256]{2,1,0:T(8,128)(2,1)S(1)}, bf16[8,32,256]{2,1,0:T(8,128)(2,1)S(1)}, bf16[8,32,256]{2,1,0:T(8,128)(2,1)S(1)}) custom-call(s32[8,17]{1,0:T(8,128)S(1)} %bitcast.2, s32[8,2]{1,0:T(8,128)S(1)} %pad_add_fusion.span_ref, ...), custom_call_target="tpu_custom_call" | custom-call | flops 1600000000 | bytes 3000000 | tf_op jit(solution)/shard_map/pallas_call | solution.py:264
  59.5 2.7 %collective-permute-start.7 = (bf16[8,32,256]{2,1,0:T(8,128)(2,1)S(1)}, bf16[8,32,256]{2,1,0:T(8,128)(2,1)S(1)}, u32[]{:S(2)}, u32[]{:S(2)}) collective-permute-start(bf16[8,32,256]{2,1,0:T(8,128)(2,1)S(1)} %get-tuple-element.24), channel_id=1, source_target_pairs={{0,7},{1,0},{2,1},{3,2},{4,3},{5,4},{6,5},{7,6},{8,15},{9,8},{10,9... | collective-permute-start | bytes 393224 | tf_op jit(solution)/shard_map/ppermute | solution.py:36
  62.3 2.1 %collective-permute-start.11 = (bf16[8,32,256]{2,1,0:T(8,128)(2,1)S(1)}, bf16[8,32,256]{2,1,0:T(8,128)(2,1)S(1)}, u32[]{:S(2)}, u32[]{:S(2)}) collective-permute-start(bf16[8,32,256]{2,1,0:T(8,128)(2,1)S(1)} %shard_map.107), channel_id=1, source_target_pairs={{0,6},{1,7},{2,0},{3,1},{4,2},{5,3},{6,4},{7,5},{8,14},{9,15},{10,... | collective-permute-start | bytes 393224 | tf_op jit(solution)/shard_map/ppermute | solution.py:36
  65.6 6.4 %collective-permute-done.8.refs_2_ = bf16[8,32,256]{2,1,0:T(8,128)(2,1)S(1)} collective-permute-done((bf16[8,32,256]{2,1,0:T(8,128)(2,1)S(1)}, bf16[8,32,256]{2,1,0:T(8,128)(2,1)S(1)}, u32[]{:S(2)}, u32[]{:S(2)}) %collective-permute-start.8) | collective-permute-done | bytes 131104 | tf_op jit(solution)/shard_map/ppermute | solution.py:36
  72.0 1.8 %collective-permute-done.13.refs_4_ = bf16[8,32,256]{2,1,0:T(8,128)(2,1)S(1)} collective-permute-done((bf16[8,32,256]{2,1,0:T(8,128)(2,1)S(1)}, bf16[8,32,256]{2,1,0:T(8,128)(2,1)S(1)}, u32[]{:S(2)}, u32[]{:S(2)}) %collective-permute-start.13) | collective-permute-done | bytes 131104 | tf_op jit(solution)/shard_map/ppermute | solution.py:36
  74.7 3.2 %collective-permute-start.14 = (bf16[40,1024]{1,0:T(8,128)(2,1)S(1)}, bf16[40,1024]{1,0:T(8,128)(2,1)S(1)}, u32[]{:S(2)}, u32[]{:S(2)}) collective-permute-start(bf16[40,1024]{1,0:T(8,128)(2,1)S(1)} %get-tuple-element.32), channel_id=1, source_target_pairs={{0,8},{8,16},{16,24},{24,32},{32,40},{40,48},{48,56},{56,0},{1,9},... | collective-permute-start | bytes 245768 | tf_op jit(solution)/shard_map/ppermute | solution.py:48
  79.1 2.0 %collective-permute-start.18 = (bf16[40,1024]{1,0:T(8,128)(2,1)S(1)}, bf16[40,1024]{1,0:T(8,128)(2,1)S(1)}, u32[]{:S(2)}, u32[]{:S(2)}) collective-permute-start(bf16[40,1024]{1,0:T(8,128)(2,1)S(1)} %get-tuple-element.36), channel_id=1, source_target_pairs={{0,40},{8,48},{16,56},{24,0},{32,8},{40,16},{48,24},{56,32},{1,41}... | collective-permute-start | bytes 245768 | tf_op jit(solution)/shard_map/ppermute | solution.py:48
  82.6 1.2 %collective-permute-start.20 = (bf16[40,1024]{1,0:T(8,128)(2,1)S(1)}, bf16[40,1024]{1,0:T(8,128)(2,1)S(1)}, u32[]{:S(2)}, u32[]{:S(2)}) collective-permute-start(bf16[40,1024]{1,0:T(8,128)(2,1)S(1)} %get-tuple-element.38), channel_id=1, source_target_pairs={{0,56},{8,0},{16,8},{24,16},{32,24},{40,32},{48,40},{56,48},{1,57}... | collective-permute-start | bytes 245768 | tf_op jit(solution)/shard_map/ppermute | solution.py:48
  84.4 1.8 %collective-permute-done.18.refs_5_ = bf16[40,1024]{1,0:T(8,128)(2,1)S(1)} collective-permute-done((bf16[40,1024]{1,0:T(8,128)(2,1)S(1)}, bf16[40,1024]{1,0:T(8,128)(2,1)S(1)}, u32[]{:S(2)}, u32[]{:S(2)}) %collective-permute-start.18) | collective-permute-done | bytes 81952 | tf_op jit(solution)/shard_map/ppermute | solution.py:48
  86.2 2.6 %collective-permute-done.20.refs_7_ = bf16[40,1024]{1,0:T(8,128)(2,1)S(1)} collective-permute-done((bf16[40,1024]{1,0:T(8,128)(2,1)S(1)}, bf16[40,1024]{1,0:T(8,128)(2,1)S(1)}, u32[]{:S(2)}, u32[]{:S(2)}) %collective-permute-start.20) | collective-permute-done | bytes 81952 | tf_op jit(solution)/shard_map/ppermute | solution.py:48
  (42 shorter events, 9.8 us)
Async XLA Ops:
  2.2 9.9 %all-to-all-start.1 = ((bf16[8,32,256]{2,1,0:T(8,128)(2,1)}), bf16[8,32,256]{2,1,0:T(8,128)(2,1)S(1)}, u32[]{:S(2)}, u32[]{:S(2)}) async-start(bf16[8,32,256]{2,1,0:T(8,128)(2,1)} %shard_map.104), calls=%async_computation.1 | async-start | bytes 262144 | tf_op jit(solution)/shard_map/all_to_all | solution.py:40
  10.9 4.8 %copy-start = (s32[7]{0:T(128)S(1)}, s32[7]{0:T(128)}, u32[]{:S(2)}) copy-start(s32[7]{0:T(128)} %param.14) | copy-start | bytes 88
  12.1 21.6 %all-to-all-start = ((bf16[8,72,1024]{2,1,0:T(8,128)(2,1)}), bf16[8,72,1024]{2,1,0:T(8,128)(2,1)S(1)}, u32[]{:S(2)}, u32[]{:S(2)}) async-start(bf16[8,72,1024]{2,1,0:T(8,128)(2,1)} %shard_map.103), calls=%async_computation | async-start | bytes 2359296 | tf_op jit(solution)/shard_map/all_to_all | solution.py:40
  16.0 11.1 %collective-permute-start.3 = (bf16[8,32,256]{2,1,0:T(8,128)(2,1)S(1)}, bf16[8,32,256]{2,1,0:T(8,128)(2,1)S(1)}, u32[]{:S(2)}, u32[]{:S(2)}) collective-permute-start(bf16[8,32,256]{2,1,0:T(8,128)(2,1)S(1)} %all-to-all-done.1.refs_0_), channel_id=1, source_target_pairs={{0,2},{1,3},{2,4},{3,5},{4,6},{5,7},{6,0},{7,1},{8,10},{9,11},{10,... | collective-permute-start | bytes 393224 | tf_op jit(solution)/shard_map/ppermute | solution.py:36
  19.4 11.6 %collective-permute-start.2 = (bf16[8,32,256]{2,1,0:T(8,128)(2,1)S(1)}, bf16[8,32,256]{2,1,0:T(8,128)(2,1)S(1)}, u32[]{:S(2)}, u32[]{:S(2)}) collective-permute-start(bf16[8,32,256]{2,1,0:T(8,128)(2,1)S(1)} %all-to-all-done.1.refs_0_), channel_id=1, source_target_pairs={{0,6},{1,7},{2,0},{3,1},{4,2},{5,3},{6,4},{7,5},{8,14},{9,15},{10,... | collective-permute-start | bytes 393224 | tf_op jit(solution)/shard_map/ppermute | solution.py:36
  22.6 29.4 %collective-permute-start.1 = (bf16[8,32,256]{2,1,0:T(8,128)(2,1)S(1)}, bf16[8,32,256]{2,1,0:T(8,128)(2,1)S(1)}, u32[]{:S(2)}, u32[]{:S(2)}) collective-permute-start(bf16[8,32,256]{2,1,0:T(8,128)(2,1)S(1)} %all-to-all-done.1.refs_0_), channel_id=1, source_target_pairs={{0,7},{1,0},{2,1},{3,2},{4,3},{5,4},{6,5},{7,6},{8,15},{9,8},{10,9... | collective-permute-start | bytes 393224 | tf_op jit(solution)/shard_map/ppermute | solution.py:36
  25.0 27.0 %collective-permute-start = (bf16[8,32,256]{2,1,0:T(8,128)(2,1)S(1)}, bf16[8,32,256]{2,1,0:T(8,128)(2,1)S(1)}, u32[]{:S(2)}, u32[]{:S(2)}) collective-permute-start(bf16[8,32,256]{2,1,0:T(8,128)(2,1)S(1)} %all-to-all-done.1.refs_0_), channel_id=1, source_target_pairs={{0,1},{1,2},{2,3},{3,4},{4,5},{5,6},{6,7},{7,0},{8,9},{9,10},{10,1... | collective-permute-start | bytes 393224 | tf_op jit(solution)/shard_map/ppermute | solution.py:36
  27.1 12.4 %collective-permute-start.6 = (bf16[8,32,256]{2,1,0:T(8,128)(2,1)S(1)}, bf16[8,32,256]{2,1,0:T(8,128)(2,1)S(1)}, u32[]{:S(2)}, u32[]{:S(2)}) collective-permute-start(bf16[8,32,256]{2,1,0:T(8,128)(2,1)S(1)} %collective-permute-done.3.refs_3_), channel_id=1, source_target_pairs={{0,2},{1,3},{2,4},{3,5},{4,6},{5,7},{6,0},{7,1},{8,10},{9,11},{10,... | collective-permute-start | bytes 393224 | tf_op jit(solution)/shard_map/ppermute | solution.py:36
  30.4 10.8 %collective-permute-start.4 = (bf16[8,32,256]{2,1,0:T(8,128)(2,1)S(1)}, bf16[8,32,256]{2,1,0:T(8,128)(2,1)S(1)}, u32[]{:S(2)}, u32[]{:S(2)}) collective-permute-start(bf16[8,32,256]{2,1,0:T(8,128)(2,1)S(1)} %collective-permute-done.3.refs_3_), channel_id=1, source_target_pairs={{0,1},{1,2},{2,3},{3,4},{4,5},{5,6},{6,7},{7,0},{8,9},{9,10},{10,1... | collective-permute-start | bytes 393224 | tf_op jit(solution)/shard_map/ppermute | solution.py:36
  30.9 10.2 %collective-permute-start.5 = (bf16[8,32,256]{2,1,0:T(8,128)(2,1)S(1)}, bf16[8,32,256]{2,1,0:T(8,128)(2,1)S(1)}, u32[]{:S(2)}, u32[]{:S(2)}) collective-permute-start(bf16[8,32,256]{2,1,0:T(8,128)(2,1)S(1)} %collective-permute-done.2.refs_3_), channel_id=1, source_target_pairs={{0,7},{1,0},{2,1},{3,2},{4,3},{5,4},{6,5},{7,6},{8,15},{9,8},{10,9... | collective-permute-start | bytes 393224 | tf_op jit(solution)/shard_map/ppermute | solution.py:36
  48.3 13.9 %collective-permute-start.9 = (bf16[8,32,256]{2,1,0:T(8,128)(2,1)S(1)}, bf16[8,32,256]{2,1,0:T(8,128)(2,1)S(1)}, u32[]{:S(2)}, u32[]{:S(2)}) collective-permute-start(bf16[8,32,256]{2,1,0:T(8,128)(2,1)S(1)} %get-tuple-element.27), channel_id=1, source_target_pairs={{0,7},{1,0},{2,1},{3,2},{4,3},{5,4},{6,5},{7,6},{8,15},{9,8},{10,9... | collective-permute-start | bytes 393224 | tf_op jit(solution)/shard_map/ppermute | solution.py:36
  48.9 13.3 %collective-permute-start.10 = (bf16[8,32,256]{2,1,0:T(8,128)(2,1)S(1)}, bf16[8,32,256]{2,1,0:T(8,128)(2,1)S(1)}, u32[]{:S(2)}, u32[]{:S(2)}) collective-permute-start(bf16[8,32,256]{2,1,0:T(8,128)(2,1)S(1)} %get-tuple-element.28), channel_id=1, source_target_pairs={{0,6},{1,7},{2,0},{3,1},{4,2},{5,3},{6,4},{7,5},{8,14},{9,15},{10,... | collective-permute-start | bytes 393224 | tf_op jit(solution)/shard_map/ppermute | solution.py:36
  51.4 13.0 %collective-permute-start.12 = (bf16[8,32,256]{2,1,0:T(8,128)(2,1)S(1)}, bf16[8,32,256]{2,1,0:T(8,128)(2,1)S(1)}, u32[]{:S(2)}, u32[]{:S(2)}) collective-permute-start(bf16[8,32,256]{2,1,0:T(8,128)(2,1)S(1)} %get-tuple-element.30), channel_id=1, source_target_pairs={{0,1},{1,2},{2,3},{3,4},{4,5},{5,6},{6,7},{7,0},{8,9},{9,10},{10,1... | collective-permute-start | bytes 393224 | tf_op jit(solution)/shard_map/ppermute | solution.py:36
  59.5 6.1 %collective-permute-start.7 = (bf16[8,32,256]{2,1,0:T(8,128)(2,1)S(1)}, bf16[8,32,256]{2,1,0:T(8,128)(2,1)S(1)}, u32[]{:S(2)}, u32[]{:S(2)}) collective-permute-start(bf16[8,32,256]{2,1,0:T(8,128)(2,1)S(1)} %get-tuple-element.24), channel_id=1, source_target_pairs={{0,7},{1,0},{2,1},{3,2},{4,3},{5,4},{6,5},{7,6},{8,15},{9,8},{10,9... | collective-permute-start | bytes 393224 | tf_op jit(solution)/shard_map/ppermute | solution.py:36
  62.2 9.8 %collective-permute-start.8 = (bf16[8,32,256]{2,1,0:T(8,128)(2,1)S(1)}, bf16[8,32,256]{2,1,0:T(8,128)(2,1)S(1)}, u32[]{:S(2)}, u32[]{:S(2)}) collective-permute-start(bf16[8,32,256]{2,1,0:T(8,128)(2,1)S(1)} %get-tuple-element.25), channel_id=1, source_target_pairs={{0,1},{1,2},{2,3},{3,4},{4,5},{5,6},{6,7},{7,0},{8,9},{9,10},{10,1... | collective-permute-start | bytes 393224 | tf_op jit(solution)/shard_map/ppermute | solution.py:36
  62.3 9.7 %collective-permute-start.11 = (bf16[8,32,256]{2,1,0:T(8,128)(2,1)S(1)}, bf16[8,32,256]{2,1,0:T(8,128)(2,1)S(1)}, u32[]{:S(2)}, u32[]{:S(2)}) collective-permute-start(bf16[8,32,256]{2,1,0:T(8,128)(2,1)S(1)} %shard_map.107), channel_id=1, source_target_pairs={{0,6},{1,7},{2,0},{3,1},{4,2},{5,3},{6,4},{7,5},{8,14},{9,15},{10,... | collective-permute-start | bytes 393224 | tf_op jit(solution)/shard_map/ppermute | solution.py:36
  64.4 9.4 %collective-permute-start.13 = (bf16[8,32,256]{2,1,0:T(8,128)(2,1)S(1)}, bf16[8,32,256]{2,1,0:T(8,128)(2,1)S(1)}, u32[]{:S(2)}, u32[]{:S(2)}) collective-permute-start(bf16[8,32,256]{2,1,0:T(8,128)(2,1)S(1)} %shard_map.108), channel_id=1, source_target_pairs={{0,2},{1,3},{2,4},{3,5},{4,6},{5,7},{6,0},{7,1},{8,10},{9,11},{10,... | collective-permute-start | bytes 393224 | tf_op jit(solution)/shard_map/ppermute | solution.py:36
  74.7 6.5 %collective-permute-start.14 = (bf16[40,1024]{1,0:T(8,128)(2,1)S(1)}, bf16[40,1024]{1,0:T(8,128)(2,1)S(1)}, u32[]{:S(2)}, u32[]{:S(2)}) collective-permute-start(bf16[40,1024]{1,0:T(8,128)(2,1)S(1)} %get-tuple-element.32), channel_id=1, source_target_pairs={{0,8},{8,16},{16,24},{24,32},{32,40},{40,48},{48,56},{56,0},{1,9},... | collective-permute-start | bytes 245768 | tf_op jit(solution)/shard_map/ppermute | solution.py:48
  77.9 4.7 %collective-permute-start.15 = (bf16[40,1024]{1,0:T(8,128)(2,1)S(1)}, bf16[40,1024]{1,0:T(8,128)(2,1)S(1)}, u32[]{:S(2)}, u32[]{:S(2)}) collective-permute-start(bf16[40,1024]{1,0:T(8,128)(2,1)S(1)} %get-tuple-element.33), channel_id=1, source_target_pairs={{0,16},{8,24},{16,32},{24,40},{32,48},{40,56},{48,0},{56,8},{1,17}... | collective-permute-start | bytes 245768 | tf_op jit(solution)/shard_map/ppermute | solution.py:48
  77.9 6.3 %collective-permute-start.16 = (bf16[40,1024]{1,0:T(8,128)(2,1)S(1)}, bf16[40,1024]{1,0:T(8,128)(2,1)S(1)}, u32[]{:S(2)}, u32[]{:S(2)}) collective-permute-start(bf16[40,1024]{1,0:T(8,128)(2,1)S(1)} %get-tuple-element.34), channel_id=1, source_target_pairs={{0,24},{8,32},{16,40},{24,48},{32,56},{40,0},{48,8},{56,16},{1,25}... | collective-permute-start | bytes 245768 | tf_op jit(solution)/shard_map/ppermute | solution.py:48
  78.9 5.5 %collective-permute-start.17 = (bf16[40,1024]{1,0:T(8,128)(2,1)S(1)}, bf16[40,1024]{1,0:T(8,128)(2,1)S(1)}, u32[]{:S(2)}, u32[]{:S(2)}) collective-permute-start(bf16[40,1024]{1,0:T(8,128)(2,1)S(1)} %get-tuple-element.35), channel_id=1, source_target_pairs={{0,32},{8,40},{16,48},{24,56},{32,0},{40,8},{48,16},{56,24},{1,33}... | collective-permute-start | bytes 245768 | tf_op jit(solution)/shard_map/ppermute | solution.py:48
  79.1 7.1 %collective-permute-start.18 = (bf16[40,1024]{1,0:T(8,128)(2,1)S(1)}, bf16[40,1024]{1,0:T(8,128)(2,1)S(1)}, u32[]{:S(2)}, u32[]{:S(2)}) collective-permute-start(bf16[40,1024]{1,0:T(8,128)(2,1)S(1)} %get-tuple-element.36), channel_id=1, source_target_pairs={{0,40},{8,48},{16,56},{24,0},{32,8},{40,16},{48,24},{56,32},{1,41}... | collective-permute-start | bytes 245768 | tf_op jit(solution)/shard_map/ppermute | solution.py:48
  81.2 5.1 %collective-permute-start.19 = (bf16[40,1024]{1,0:T(8,128)(2,1)S(1)}, bf16[40,1024]{1,0:T(8,128)(2,1)S(1)}, u32[]{:S(2)}, u32[]{:S(2)}) collective-permute-start(bf16[40,1024]{1,0:T(8,128)(2,1)S(1)} %get-tuple-element.37), channel_id=1, source_target_pairs={{0,48},{8,56},{16,0},{24,8},{32,16},{40,24},{48,32},{56,40},{1,49}... | collective-permute-start | bytes 245768 | tf_op jit(solution)/shard_map/ppermute | solution.py:48
  82.6 6.2 %collective-permute-start.20 = (bf16[40,1024]{1,0:T(8,128)(2,1)S(1)}, bf16[40,1024]{1,0:T(8,128)(2,1)S(1)}, u32[]{:S(2)}, u32[]{:S(2)}) collective-permute-start(bf16[40,1024]{1,0:T(8,128)(2,1)S(1)} %get-tuple-element.38), channel_id=1, source_target_pairs={{0,56},{8,0},{16,8},{24,16},{32,24},{40,32},{48,40},{56,48},{1,57}... | collective-permute-start | bytes 245768 | tf_op jit(solution)/shard_map/ppermute | solution.py:48

commit v7 on v6

--- a/solution.py
+++ b/solution.py
@@ -28,8 +28,9 @@
 HEADS = ("xl", "c", "xh")
 F32 = jnp.float32
 BF16 = jnp.bfloat16
-FAR = (3, -3, 4, 2)
-NEAR = (0, 1, -1, -2)
+EARLY = (1, -1)
+FAR = (3, -3, 4)
+LATE = (0, 2, -2)
 
 
 def along_z(value, by):
@@ -141,16 +142,17 @@
         copy.wait()
 
 
-def attention_kernel(offsets, final, keep_ref, span_ref, message_ref, start_ref, *refs):
+def attention_kernel(offsets, first_call, final, keep_ref, message_ref, start_ref, *refs):
     pieces = len(offsets)
     kv_refs, refs = refs[:pieces], refs[pieces:]
-    if final:
+    if not first_call:
         dqt_in_ref, refs = refs[0], refs[1:]
     dq_ref, refs = refs[0], refs[1:]
     dkv_refs, refs = refs[:pieces], refs[pieces:]
     acc_ref, kt_ref, q_ref, g_ref, qt_ref, gt_ref, dqt_ref = refs
     z = lax.axis_index("z")
     sources = [lax.rem(z - off + ZS, ZS) for off in offsets]
+    halves = [source // 4 for source in sources]
     lane_token = lax.rem(lax.broadcasted_iota(jnp.int32, (1, ROWS), 1), TOK)
     sublane = lax.broadcasted_iota(jnp.int32, (TOK, ROWS), 0)
     keys = SPAN * pieces * TOK
@@ -160,127 +162,116 @@
             [kv[b * SPAN + c, :, lanes] for c in range(SPAN) for kv in kv_refs], axis=0
         )
 
-    def prepare(b, _):
+    for b in range(AS // SPAN):
         kt_ref[b] = keys_of(b, pl.ds(0, HD)).T
-        acc_ref[b] = jnp.zeros((keys, 2 * HD), F32)
-        return 0
-
-    lax.fori_loop(0, AS // SPAN, prepare, 0)
-
-    def pair_of_chunks(j, _):
-        lse, delta, start, q_pos = [], [], [], []
+
+    def load(j, slot):
+        vectors = []
         for c in range(PAIR):
             i = j * PAIR + c
             for h in range(GROUP):
                 rows = pl.ds(c * ROWS + h * TOK, TOK)
-                q_ref[rows, :] = message_ref[i, :TOK, h * HD : (h + 1) * HD]
-                g_ref[rows, :] = message_ref[i, TOK : 2 * TOK, h * HD : (h + 1) * HD]
+                q_ref[slot, rows, :] = message_ref[i, :TOK, h * HD : (h + 1) * HD]
+                g_ref[slot, rows, :] = message_ref[i, TOK : 2 * TOK, h * HD : (h + 1) * HD]
             extra = message_ref[i, 2 * TOK :, :ROWS].astype(F32)
-            lse.append(extra[0:1] + extra[1:2])
-            delta.append(extra[2:3] + extra[3:4])
-            start.append(start_ref[i])
-            q_pos.append(i * CHUNK + z * TOK + lane_token)
-        qt_ref[...] = q_ref[...].T
-        gt_ref[...] = g_ref[...].T
-        if final:
-            dqt_ref[...] = dqt_in_ref[j]
+            q_pos = i * CHUNK + z * TOK + lane_token
+            vectors.append((extra[0:1] + extra[1:2], extra[2:3] + extra[3:4], start_ref[i], q_pos))
+        qt_ref[slot] = q_ref[slot].T
+        gt_ref[slot] = g_ref[slot].T
+        return vectors
+
+    def tile(j, b, slot, vectors):
+        reaches_own = (b + 1) * SPAN > j * PAIR
+        scores = jnp.dot(keys_of(b, pl.ds(0, HD)), qt_ref[slot], preferred_element_type=F32)
+        dprobs = jnp.dot(keys_of(b, pl.ds(HD, HD)), gt_ref[slot], preferred_element_type=F32)
+        probs_b, dscores_b = [], []
+        for k in range(SPAN * pieces):
+            a, r = b * SPAN + k // pieces, k % pieces
+            rows = slice(k * TOK, (k + 1) * TOK)
+            probs_row, dscores_row = [], []
+            for c, (lse, delta, start, q_pos) in enumerate(vectors):
+                i = j * PAIR + c
+                columns = slice(c * ROWS, (c + 1) * ROWS)
+                distance = 2 * (i - a) + z // 4 - halves[r]
+                kept = keep_ref[i, jnp.maximum(distance, 0)] > 0
+                shift = lse + jnp.where(kept, 0.0, BIG)
+                probs = jnp.exp2(scores[rows, columns] * (SCALE * LOG2E) - shift)
+                k_pos = a * CHUNK + sources[r] * TOK + sublane
+                allowed = k_pos >= start
+                if reaches_own:
+                    allowed = allowed & (k_pos <= q_pos)
+                probs = jnp.where(allowed, probs, 0.0)
+                probs_row.append(probs.astype(BF16))
+                dscores_row.append((probs * (dprobs[rows, columns] - delta)).astype(BF16))
+            probs_b.append(jnp.concatenate(probs_row, axis=1))
+            dscores_b.append(jnp.concatenate(dscores_row, axis=1))
+        probs_b = jnp.concatenate(probs_b, axis=0)
+        dscores_b = jnp.concatenate(dscores_b, axis=0)
+        dk = jnp.dot(dscores_b, q_ref[slot], preferred_element_type=F32)
+        dv = jnp.dot(probs_b, g_ref[slot], preferred_element_type=F32)
+        if j == b * SPAN // PAIR:
+            acc_ref[b, :, :HD] = dk
+            acc_ref[b, :, HD:] = dv
         else:
-            dqt_ref[...] = jnp.zeros((HD, PAIR * ROWS), F32)
-
-        def tile(b, masked):
-            scores = jnp.dot(keys_of(b, pl.ds(0, HD)), qt_ref[...], preferred_element_type=F32)
-            dprobs = jnp.dot(keys_of(b, pl.ds(HD, HD)), gt_ref[...], preferred_element_type=F32)
-            probs_b, dscores_b = [], []
-            for k in range(SPAN * pieces):
-                a, r = b * SPAN + k // pieces, k % pieces
-                rows = slice(k * TOK, (k + 1) * TOK)
-                probs_row, dscores_row = [], []
-                for c in range(PAIR):
-                    i = j * PAIR + c
-                    columns = slice(c * ROWS, (c + 1) * ROWS)
-                    distance = 2 * (i - a) + z // 4 - sources[r] // 4
-                    kept = keep_ref[i, jnp.maximum(distance, 0)] > 0
-                    shift = lse[c] + jnp.where(kept, 0.0, BIG)
-                    probs = jnp.exp2(scores[rows, columns] * (SCALE * LOG2E) - shift)
-                    if masked:
-                        k_pos = a * CHUNK + sources[r] * TOK + sublane
-                        probs = jnp.where((k_pos >= start[c]) & (k_pos <= q_pos[c]), probs, 0.0)
-                    probs_row.append(probs.astype(BF16))
-                    dscores_row.append((probs * (dprobs[rows, columns] - delta[c])).astype(BF16))
-                probs_b.append(jnp.concatenate(probs_row, axis=1))
-                dscores_b.append(jnp.concatenate(dscores_row, axis=1))
-            probs_b = jnp.concatenate(probs_b, axis=0)
-            dscores_b = jnp.concatenate(dscores_b, axis=0)
-            acc_ref[b, :, :HD] += jnp.dot(dscores_b, q_ref[...], preferred_element_type=F32)
-            acc_ref[b, :, HD:] += jnp.dot(probs_b, g_ref[...], preferred_element_type=F32)
-            dqt_ref[...] += jnp.dot(kt_ref[b], dscores_b, preferred_element_type=F32)
-
-        def step(b, _):
-            reaches_own = (b + 1) * SPAN > j * PAIR
-            masked = reaches_own | (span_ref[j * PAIR + PAIR - 1, 1] > b * SPAN * CHUNK)
-
-            @pl.when(masked)
-            def _():
-                tile(b, True)
-
-            @pl.when(jnp.logical_not(masked))
-            def _():
-                tile(b, False)
-
-            return 0
-
-        first = span_ref[j * PAIR, 0] // (SPAN * CHUNK)
-        lax.fori_loop(first, (j * PAIR + PAIR - 1) // SPAN + 1, step, 0)
+            acc_ref[b, :, :HD] += dk
+            acc_ref[b, :, HD:] += dv
+        dq = jnp.dot(kt_ref[b], dscores_b, preferred_element_type=F32)
+        if b == 0 and first_call:
+            dqt_ref[slot] = dq
+        elif b == 0:
+            dqt_ref[slot] = dqt_in_ref[j] + dq
+        else:
+            dqt_ref[slot] += dq
+
+    for j in range(AS // PAIR):
+        slot = j % 2
+        vectors = load(j, slot)
+        for b in range(j * PAIR // SPAN + 1):
+            tile(j, b, slot, vectors)
         if not final:
-            dq_ref[j] = dqt_ref[...]
-            return 0
-        dq = (dqt_ref[...] * SCALE).T.astype(BF16)
+            dq_ref[j] = dqt_ref[slot]
+            continue
+        dq = (dqt_ref[slot] * SCALE).T.astype(BF16)
         for c in range(PAIR):
             for h in range(GROUP):
                 at = c * ROWS + h * TOK
                 dq_ref[j * PAIR + c, :, h * HD : (h + 1) * HD] = dq[at : at + TOK]
-        return 0
-
-    lax.fori_loop(0, AS // PAIR, pair_of_chunks, 0)
-
-    def finish(b, _):
+
+    for b in range(AS // SPAN):
         for k in range(SPAN * pieces):
             piece = acc_ref[b, k * TOK : (k + 1) * TOK, :]
             out = dkv_refs[k % pieces].at[b * SPAN + k // pieces]
             out[:, :HD] = (piece[:, :HD] * SCALE).astype(BF16)
             out[:, HD:] = piece[:, HD:].astype(BF16)
-        return 0
-
-    lax.fori_loop(0, AS // SPAN, finish, 0)
-
-
-def attention(offsets, scalars, message, start, kv, dqt=None):
-    final = dqt is not None
+
+
+def attention(offsets, keep, message, start, kv, dqt=None, final=False):
+    first_call = dqt is None
     pieces = len(offsets)
     keys = SPAN * pieces * TOK
     rows = PAIR * ROWS
     dqt_shape = jax.ShapeDtypeStruct((AS // PAIR, HD, rows), F32)
     dq_shape = jax.ShapeDtypeStruct((AS, TOK, GROUP * HD), BF16)
     results = pl.pallas_call(
-        functools.partial(attention_kernel, offsets, final),
+        functools.partial(attention_kernel, offsets, first_call, final),
         out_shape=[dq_shape if final else dqt_shape]
         + [jax.ShapeDtypeStruct((AS, TOK, 2 * HD), BF16)] * pieces,
-        in_specs=[in_smem()] * 2 + [in_vmem()] * (2 + pieces + final),
+        in_specs=[in_smem()] + [in_vmem()] * (2 + pieces + (not first_call)),
         out_specs=[in_vmem()] * (1 + pieces),
         scratch_shapes=[
             pltpu.VMEM((AS // SPAN, keys, 2 * HD), F32),
             pltpu.VMEM((AS // SPAN, HD, keys), BF16),
-            pltpu.VMEM((rows, HD), BF16),
-            pltpu.VMEM((rows, HD), BF16),
-            pltpu.VMEM((HD, rows), BF16),
-            pltpu.VMEM((HD, rows), BF16),
-            pltpu.VMEM((HD, rows), F32),
+            pltpu.VMEM((2, rows, HD), BF16),
+            pltpu.VMEM((2, rows, HD), BF16),
+            pltpu.VMEM((2, HD, rows), BF16),
+            pltpu.VMEM((2, HD, rows), BF16),
+            pltpu.VMEM((2, HD, rows), F32),
         ],
         compiler_params=pltpu.CompilerParams(vmem_limit_bytes=24 * 2**20),
         cost_estimate=pl.CostEstimate(
             flops=400000000 * pieces, bytes_accessed=3000000, transcendentals=300000 * pieces
         ),
-    )(*scalars, message, start, *[kv[o] for o in offsets], *([dqt] if final else []))
+    )(keep, message, start, *[kv[o] for o in offsets], *([] if first_call else [dqt]))
     return results[0], dict(zip(offsets, results[1:]))
 
 
@@ -434,15 +425,14 @@
         jnp.where(starts[None, None, :] <= positions[:, :, None], starts[None, None, :], 0), axis=2
     )
     start_of = jnp.maximum(start_of - base, 0)
-    span = jnp.stack([start_of[:, 0], start_of[:, TOK - 1]], axis=1)
-
-    scalars, start = (keep, span), start_of.reshape(AS, 1, ROWS)
-    dqt, part = attention(FAR, scalars, message, start, pieces)
-    from_three, from_four = along_z(part[3], -1), along_z(part[4], -2)
-    from_minus_three = along_z(part[-3], 1)
-    dq, near_part = attention(NEAR, scalars, message, start, pieces, dqt)
-    part.update(near_part)
+
+    start = start_of.reshape(AS, 1, ROWS)
+    dqt, part = attention(EARLY, keep, message, start, pieces)
     one, minus_one = along_z(part[1], -1), along_z(part[-1], 1)
+    dqt, far_part = attention(FAR, keep, message, start, pieces, dqt)
+    from_three, from_four = along_z(far_part[3], -1), along_z(far_part[4], -2)
+    from_minus_three = along_z(far_part[-3], 1)
+    dq, part = attention(LATE, keep, message, start, pieces, dqt, final=True)
     two = along_z(partial_sum(part[2], from_three, from_four), -2)
     minus_two = along_z(partial_sum(part[-2], from_minus_three), 2)
     gradients = pl.pallas_call(

time: 90.1 us -> 86.2 us (0.957)
  starting transfers between devices: 41 us -> 37.5 us
  Pallas kernels: 22.3 us -> 19.9 us
  waiting for transfers between devices: 25.2 us -> 27.2 us
    ppermute x14, starting transfers between devices: 24.5 us -> 21.4 us  [along_z(): return lax.ppermute(value, 'z', [(i, (i + by) % ZS) for i in range(ZS)])]
    pallas_call x2 -> x3, Pallas kernels: 14.6 us -> 12.1 us  [attention(): pl.pallas_call(functools.partial(attention_kernel, offsets, first_call, f...]
    ppermute x14, waiting for transfers between devices: 18.4 us -> 20.3 us  [along_z(): return lax.ppermute(value, 'z', [(i, (i + by) % ZS) for i in range(ZS)])]
  transfers between devices with their start and end apart: 23 -> 23, of which waited for: 13 -> 13; matrix products, arithmetic and copies ran while one was open for 0% -> 0% of each run, Pallas kernels for 21% -> 14%
where the time goes in v7:
time: 86.2 us; the launch traced here: 85.8 us
  starting transfers between devices  37.5 us (44%)
  waiting for transfers between devices  27.2 us (32%)
  Pallas kernels  19.9 us (23%)
  between operations  0.95 us (1%)
    ppermute x14, starting transfers between devices, along_z(): return lax.ppermute(value, 'z', [(i, (i + by) % ZS) for i in range(ZS)])  21.4 us
    ppermute x14, waiting for transfers between devices, along_z(): return lax.ppermute(value, 'z', [(i, (i + by) % ZS) for i in range(ZS)])  20.3 us
    pallas_call x3, Pallas kernels, attention(): pl.pallas_call(functools.partial(attention_kernel, offsets, first_call, f...  12.1 us
    ppermute x7, starting transfers between devices, shifted(): return lax.ppermute(value, HEADS, [(i, (i + by) % AS) for i in range(AS)])  8.19 us
    all_to_all x2, starting transfers between devices, exchange(): return lax.all_to_all(value, HEADS, split_axis=0, concat_axis=0, tiled=True)  7.95 us
    ppermute x7, waiting for transfers between devices, shifted(): return lax.ppermute(value, HEADS, [(i, (i + by) % AS) for i in range(AS)])  5.67 us
    pallas_call x1, Pallas kernels, shards(): pl.pallas_call(pack_queries_kernel, out_shape=jax.ShapeDtypeStruct((AS, 2...  4.35 us
  transfers between devices with their start and end apart: 23, of which 13 were waited for; matrix products, arithmetic and copies ran while one was open for 0% of the time, Pallas kernels for 14%

profile of v7, /device:TPU:8, one launch (start us, length us, event | category | flops | bytes accessed | tf_op | source)
XLA Modules:
  0.0 85.8 jit_solution(12315344550668136688)
XLA Ops:
  0.6 1.6 %shard_map.104 = bf16[8,32,256]{2,1,0:T(8,128)(2,1)} custom-call(bf16[32,1024]{1,0:T(8,128)(2,1)} %k_hbm.1, bf16[32,1024]{1,0:T(8,128)(2,1)} %v_hbm.1), custom_call_target="tpu_custom_call" | custom-call | bytes 262144 | tf_op jit(solution)/shard_map/pallas_call | solution.py:377
  2.2 4.3 %all-to-all-start.1 = ((bf16[8,32,256]{2,1,0:T(8,128)(2,1)}), bf16[8,32,256]{2,1,0:T(8,128)(2,1)S(1)}, u32[]{:S(2)}, u32[]{:S(2)}) async-start(bf16[8,32,256]{2,1,0:T(8,128)(2,1)} %shard_map.104), calls=%async_computation.1 | async-start | bytes 262144 | tf_op jit(solution)/shard_map/all_to_all | solution.py:41
  6.5 4.3 %shard_map.103 = bf16[8,72,1024]{2,1,0:T(8,128)(2,1)} custom-call(bf16[32,8192]{1,0:T(8,128)(2,1)} %q_hbm.1, bf16[32,8192]{1,0:T(8,128)(2,1)} %g_hbm.1, bf16[32,8192]{1,0:T(8,128)(2,1)} %o_hbm.1, f32[32,64]{1,0:T(8,128)} %lse_hbm.1, s32[4,17]{1,0:T(4,128)} %keep_hbm.1), custom_call_target="tpu_custom_call" | custom-call | flops 67108864 | bytes 2800000 | tf_op jit(solution)/shard_map/pallas_call | solution.py:389
  10.9 1.2 %all-to-all-done.1.refs_0_ = bf16[8,32,256]{2,1,0:T(8,128)(2,1)S(1)} async-done(((bf16[8,32,256]{2,1,0:T(8,128)(2,1)}), bf16[8,32,256]{2,1,0:T(8,128)(2,1)S(1)}, u32[]{:S(2)}, u32[]{:S(2)}) %all-to-all-start.1) | async-done | bytes 131104 | tf_op jit(solution)/shard_map/all_to_all | solution.py:41
  12.1 3.6 %all-to-all-start = ((bf16[8,72,1024]{2,1,0:T(8,128)(2,1)}), bf16[8,72,1024]{2,1,0:T(8,128)(2,1)S(1)}, u32[]{:S(2)}, u32[]{:S(2)}) async-start(bf16[8,72,1024]{2,1,0:T(8,128)(2,1)} %shard_map.103), calls=%async_computation | async-start | bytes 2359296 | tf_op jit(solution)/shard_map/all_to_all | solution.py:41
  16.0 6.4 %collective-permute-start.1 = (bf16[8,32,256]{2,1,0:T(8,128)(2,1)S(1)}, bf16[8,32,256]{2,1,0:T(8,128)(2,1)S(1)}, u32[]{:S(2)}, u32[]{:S(2)}) collective-permute-start(bf16[8,32,256]{2,1,0:T(8,128)(2,1)S(1)} %all-to-all-done.1.refs_0_), channel_id=1, source_target_pairs={{0,6},{1,7},{2,0},{3,1},{4,2},{5,3},{6,4},{7,5},{8,14},{9,15},{10,... | collective-permute-start | bytes 393224 | tf_op jit(solution)/shard_map/ppermute | solution.py:37
  22.4 3.8 %collective-permute-start.6 = (bf16[8,32,256]{2,1,0:T(8,128)(2,1)S(1)}, bf16[8,32,256]{2,1,0:T(8,128)(2,1)S(1)}, u32[]{:S(2)}, u32[]{:S(2)}) collective-permute-start(bf16[8,32,256]{2,1,0:T(8,128)(2,1)S(1)} %all-to-all-done.1.refs_0_), channel_id=1, source_target_pairs={{0,7},{1,0},{2,1},{3,2},{4,3},{5,4},{6,5},{7,6},{8,15},{9,8},{10,9... | collective-permute-start | bytes 393224 | tf_op jit(solution)/shard_map/ppermute | solution.py:37
  26.2 6.9 %collective-permute-done.refs_1_ = bf16[8,32,256]{2,1,0:T(8,128)(2,1)S(1)} collective-permute-done((bf16[8,32,256]{2,1,0:T(8,128)(2,1)S(1)}, bf16[8,32,256]{2,1,0:T(8,128)(2,1)S(1)}, u32[]{:S(2)}, u32[]{:S(2)}) %collective-permute-start) | collective-permute-done | bytes 131104 | tf_op jit(solution)/shard_map/ppermute | solution.py:37
  33.1 1.3 %collective-permute-start.2 = (bf16[8,32,256]{2,1,0:T(8,128)(2,1)S(1)}, bf16[8,32,256]{2,1,0:T(8,128)(2,1)S(1)}, u32[]{:S(2)}, u32[]{:S(2)}) collective-permute-start(bf16[8,32,256]{2,1,0:T(8,128)(2,1)S(1)} %collective-permute-done.refs_1_), channel_id=1, source_target_pairs={{0,1},{1,2},{2,3},{3,4},{4,5},{5,6},{6,7},{7,0},{8,9},{9,10},{10,1... | collective-permute-start | bytes 393224 | tf_op jit(solution)/shard_map/ppermute | solution.py:37
  34.3 2.7 %collective-permute-start.3 = (bf16[8,32,256]{2,1,0:T(8,128)(2,1)S(1)}, bf16[8,32,256]{2,1,0:T(8,128)(2,1)S(1)}, u32[]{:S(2)}, u32[]{:S(2)}) collective-permute-start(bf16[8,32,256]{2,1,0:T(8,128)(2,1)S(1)} %collective-permute-done.1.refs_2_), channel_id=1, source_target_pairs={{0,7},{1,0},{2,1},{3,2},{4,3},{5,4},{6,5},{7,6},{8,15},{9,8},{10,9... | collective-permute-start | bytes 393224 | tf_op jit(solution)/shard_map/ppermute | solution.py:37
  37.1 3.5 %shard_map.105 = (f32[4,128,512]{2,1,0:T(8,128)S(1)}, bf16[8,32,256]{2,1,0:T(8,128)(2,1)S(1)}, bf16[8,32,256]{2,1,0:T(8,128)(2,1)S(1)}) custom-call(s32[8,17]{1,0:T(8,128)S(1)} %bitcast.1, bf16[8,72,1024]{2,1,0:T(8,128)(2,1)S(1)} %all-to-all-done.message_ref, s32[8,1,256]{2,1,0:T(1,128)S(1)} %max.18.start_ref, ...), custom_call_target="tpu_custom_call" | custom-call | flops 800000000 | bytes 3000000 | tf_op jit(solution)/shard_map/pallas_call | solution.py:255
  40.6 2.0 %collective-permute-done.4.refs_2_ = bf16[8,32,256]{2,1,0:T(8,128)(2,1)S(1)} collective-permute-done((bf16[8,32,256]{2,1,0:T(8,128)(2,1)S(1)}, bf16[8,32,256]{2,1,0:T(8,128)(2,1)S(1)}, u32[]{:S(2)}, u32[]{:S(2)}) %collective-permute-start.4) | collective-permute-done | bytes 131104 | tf_op jit(solution)/shard_map/ppermute | solution.py:37
  42.6 1.5 %collective-permute-done.2.refs_0_ = bf16[8,32,256]{2,1,0:T(8,128)(2,1)S(1)} collective-permute-done((bf16[8,32,256]{2,1,0:T(8,128)(2,1)S(1)}, bf16[8,32,256]{2,1,0:T(8,128)(2,1)S(1)}, u32[]{:S(2)}, u32[]{:S(2)}) %collective-permute-start.2) | collective-permute-done | bytes 131104 | tf_op jit(solution)/shard_map/ppermute | solution.py:37
  44.1 4.2 %shard_map.106 = (f32[4,128,512]{2,1,0:T(8,128)S(1)}, bf16[8,32,256]{2,1,0:T(8,128)(2,1)S(1)}, bf16[8,32,256]{2,1,0:T(8,128)(2,1)S(1)}, bf16[8,32,256]{2,1,0:T(8,128)(2,1)S(1)}) custom-call(s32[8,17]{1,0:T(8,128)S(1)} %bitcast.2, bf16[8,72,1024]{2,1,0:T(8,128)(2,1)S(1)} %all-to-all-done.message_ref, s32[8,1,256]{2,1,0:T(1,128)S(1)} %max.18.start_ref, ...), custom_call_target="tpu_custom_call" | custom-call | flops 1200000000 | bytes 3000000 | tf_op jit(solution)/shard_map/pallas_call | solution.py:255
  50.5 2.1 %collective-permute-start.7 = (bf16[8,32,256]{2,1,0:T(8,128)(2,1)S(1)}, bf16[8,32,256]{2,1,0:T(8,128)(2,1)S(1)}, u32[]{:S(2)}, u32[]{:S(2)}) collective-permute-start(bf16[8,32,256]{2,1,0:T(8,128)(2,1)S(1)} %get-tuple-element.26), channel_id=1, source_target_pairs={{0,7},{1,0},{2,1},{3,2},{4,3},{5,4},{6,5},{7,6},{8,15},{9,8},{10,9... | collective-permute-start | bytes 393224 | tf_op jit(solution)/shard_map/ppermute | solution.py:37
  52.6 4.4 %shard_map.107 = (bf16[8,32,1024]{2,1,0:T(8,128)(2,1)S(1)}, bf16[8,32,256]{2,1,0:T(8,128)(2,1)S(1)}, bf16[8,32,256]{2,1,0:T(8,128)(2,1)S(1)}, bf16[8,32,256]{2,1,0:T(8,128)(2,1)S(1)}) custom-call(s32[8,17]{1,0:T(8,128)S(1)} %bitcast.3, bf16[8,72,1024]{2,1,0:T(8,128)(2,1)S(1)} %all-to-all-done.message_ref, s32[8,1,256]{2,1,0:T(1,128)S(1)} %max.18.start_ref, ...), custom_call_target="tpu_custom_call" | custom-call | flops 1200000000 | bytes 3000000 | tf_op jit(solution)/shard_map/pallas_call | solution.py:255
  57.0 2.5 %collective-permute-done.10.refs_2_ = bf16[8,32,256]{2,1,0:T(8,128)(2,1)S(1)} collective-permute-done((bf16[8,32,256]{2,1,0:T(8,128)(2,1)S(1)}, bf16[8,32,256]{2,1,0:T(8,128)(2,1)S(1)}, u32[]{:S(2)}, u32[]{:S(2)}) %collective-permute-start.10) | collective-permute-done | bytes 131104 | tf_op jit(solution)/shard_map/ppermute | solution.py:37
  59.5 2.0 %collective-permute-start.11 = (bf16[8,32,256]{2,1,0:T(8,128)(2,1)S(1)}, bf16[8,32,256]{2,1,0:T(8,128)(2,1)S(1)}, u32[]{:S(2)}, u32[]{:S(2)}) collective-permute-start(bf16[8,32,256]{2,1,0:T(8,128)(2,1)S(1)} %shard_map.108), channel_id=1, source_target_pairs={{0,6},{1,7},{2,0},{3,1},{4,2},{5,3},{6,4},{7,5},{8,14},{9,15},{10,... | collective-permute-start | bytes 393224 | tf_op jit(solution)/shard_map/ppermute | solution.py:37
  63.3 3.2 %collective-permute-done.11.refs_3_ = bf16[8,32,256]{2,1,0:T(8,128)(2,1)S(1)} collective-permute-done((bf16[8,32,256]{2,1,0:T(8,128)(2,1)S(1)}, bf16[8,32,256]{2,1,0:T(8,128)(2,1)S(1)}, u32[]{:S(2)}, u32[]{:S(2)}) %collective-permute-start.11) | collective-permute-done | bytes 131104 | tf_op jit(solution)/shard_map/ppermute | solution.py:37
  66.6 3.4 %collective-permute-done.13.refs_4_ = bf16[8,32,256]{2,1,0:T(8,128)(2,1)S(1)} collective-permute-done((bf16[8,32,256]{2,1,0:T(8,128)(2,1)S(1)}, bf16[8,32,256]{2,1,0:T(8,128)(2,1)S(1)}, u32[]{:S(2)}, u32[]{:S(2)}) %collective-permute-start.13) | collective-permute-done | bytes 131104 | tf_op jit(solution)/shard_map/ppermute | solution.py:37
  70.8 2.9 %collective-permute-start.14 = (bf16[40,1024]{1,0:T(8,128)(2,1)S(1)}, bf16[40,1024]{1,0:T(8,128)(2,1)S(1)}, u32[]{:S(2)}, u32[]{:S(2)}) collective-permute-start(bf16[40,1024]{1,0:T(8,128)(2,1)S(1)} %get-tuple-element.34), channel_id=1, source_target_pairs={{0,8},{8,16},{16,24},{24,32},{32,40},{40,48},{48,56},{56,0},{1,9},... | collective-permute-start | bytes 245768 | tf_op jit(solution)/shard_map/ppermute | solution.py:49
  75.0 2.0 %collective-permute-start.18 = (bf16[40,1024]{1,0:T(8,128)(2,1)S(1)}, bf16[40,1024]{1,0:T(8,128)(2,1)S(1)}, u32[]{:S(2)}, u32[]{:S(2)}) collective-permute-start(bf16[40,1024]{1,0:T(8,128)(2,1)S(1)} %get-tuple-element.38), channel_id=1, source_target_pairs={{0,40},{8,48},{16,56},{24,0},{32,8},{40,16},{48,24},{56,32},{1,41}... | collective-permute-start | bytes 245768 | tf_op jit(solution)/shard_map/ppermute | solution.py:49
  80.2 1.8 %collective-permute-done.18.refs_5_ = bf16[40,1024]{1,0:T(8,128)(2,1)S(1)} collective-permute-done((bf16[40,1024]{1,0:T(8,128)(2,1)S(1)}, bf16[40,1024]{1,0:T(8,128)(2,1)S(1)}, u32[]{:S(2)}, u32[]{:S(2)}) %collective-permute-start.18) | collective-permute-done | bytes 81952 | tf_op jit(solution)/shard_map/ppermute | solution.py:49
  82.1 2.6 %collective-permute-done.20.refs_7_ = bf16[40,1024]{1,0:T(8,128)(2,1)S(1)} collective-permute-done((bf16[40,1024]{1,0:T(8,128)(2,1)S(1)}, bf16[40,1024]{1,0:T(8,128)(2,1)S(1)}, u32[]{:S(2)}, u32[]{:S(2)}) %collective-permute-start.20) | collective-permute-done | bytes 81952 | tf_op jit(solution)/shard_map/ppermute | solution.py:49
  (41 shorter events, 10.6 us)
Async XLA Ops:
  2.2 9.9 %all-to-all-start.1 = ((bf16[8,32,256]{2,1,0:T(8,128)(2,1)}), bf16[8,32,256]{2,1,0:T(8,128)(2,1)S(1)}, u32[]{:S(2)}, u32[]{:S(2)}) async-start(bf16[8,32,256]{2,1,0:T(8,128)(2,1)} %shard_map.104), calls=%async_computation.1 | async-start | bytes 262144 | tf_op jit(solution)/shard_map/all_to_all | solution.py:41
  10.9 4.9 %copy-start = (s32[7]{0:T(128)S(1)}, s32[7]{0:T(128)}, u32[]{:S(2)}) copy-start(s32[7]{0:T(128)} %param.14) | copy-start | bytes 88
  12.1 25.0 %all-to-all-start = ((bf16[8,72,1024]{2,1,0:T(8,128)(2,1)}), bf16[8,72,1024]{2,1,0:T(8,128)(2,1)S(1)}, u32[]{:S(2)}, u32[]{:S(2)}) async-start(bf16[8,72,1024]{2,1,0:T(8,128)(2,1)} %shard_map.103), calls=%async_computation | async-start | bytes 2359296 | tf_op jit(solution)/shard_map/all_to_all | solution.py:41
  16.0 18.3 %collective-permute-start.1 = (bf16[8,32,256]{2,1,0:T(8,128)(2,1)S(1)}, bf16[8,32,256]{2,1,0:T(8,128)(2,1)S(1)}, u32[]{:S(2)}, u32[]{:S(2)}) collective-permute-start(bf16[8,32,256]{2,1,0:T(8,128)(2,1)S(1)} %all-to-all-done.1.refs_0_), channel_id=1, source_target_pairs={{0,6},{1,7},{2,0},{3,1},{4,2},{5,3},{6,4},{7,5},{8,14},{9,15},{10,... | collective-permute-start | bytes 393224 | tf_op jit(solution)/shard_map/ppermute | solution.py:37
  22.4 10.7 %collective-permute-start = (bf16[8,32,256]{2,1,0:T(8,128)(2,1)S(1)}, bf16[8,32,256]{2,1,0:T(8,128)(2,1)S(1)}, u32[]{:S(2)}, u32[]{:S(2)}) collective-permute-start(bf16[8,32,256]{2,1,0:T(8,128)(2,1)S(1)} %all-to-all-done.1.refs_0_), channel_id=1, source_target_pairs={{0,2},{1,3},{2,4},{3,5},{4,6},{5,7},{6,0},{7,1},{8,10},{9,11},{10,... | collective-permute-start | bytes 393224 | tf_op jit(solution)/shard_map/ppermute | solution.py:37
  22.4 14.6 %collective-permute-start.6 = (bf16[8,32,256]{2,1,0:T(8,128)(2,1)S(1)}, bf16[8,32,256]{2,1,0:T(8,128)(2,1)S(1)}, u32[]{:S(2)}, u32[]{:S(2)}) collective-permute-start(bf16[8,32,256]{2,1,0:T(8,128)(2,1)S(1)} %all-to-all-done.1.refs_0_), channel_id=1, source_target_pairs={{0,7},{1,0},{2,1},{3,2},{4,3},{5,4},{6,5},{7,6},{8,15},{9,8},{10,9... | collective-permute-start | bytes 393224 | tf_op jit(solution)/shard_map/ppermute | solution.py:37
  26.2 10.9 %collective-permute-start.5 = (bf16[8,32,256]{2,1,0:T(8,128)(2,1)S(1)}, bf16[8,32,256]{2,1,0:T(8,128)(2,1)S(1)}, u32[]{:S(2)}, u32[]{:S(2)}) collective-permute-start(bf16[8,32,256]{2,1,0:T(8,128)(2,1)S(1)} %all-to-all-done.1.refs_0_), channel_id=1, source_target_pairs={{0,1},{1,2},{2,3},{3,4},{4,5},{5,6},{6,7},{7,0},{8,9},{9,10},{10,1... | collective-permute-start | bytes 393224 | tf_op jit(solution)/shard_map/ppermute | solution.py:37
  33.1 9.5 %collective-permute-start.4 = (bf16[8,32,256]{2,1,0:T(8,128)(2,1)S(1)}, bf16[8,32,256]{2,1,0:T(8,128)(2,1)S(1)}, u32[]{:S(2)}, u32[]{:S(2)}) collective-permute-start(bf16[8,32,256]{2,1,0:T(8,128)(2,1)S(1)} %collective-permute-done.refs_1_), channel_id=1, source_target_pairs={{0,2},{1,3},{2,4},{3,5},{4,6},{5,7},{6,0},{7,1},{8,10},{9,11},{10,... | collective-permute-start | bytes 393224 | tf_op jit(solution)/shard_map/ppermute | solution.py:37
  33.1 11.1 %collective-permute-start.2 = (bf16[8,32,256]{2,1,0:T(8,128)(2,1)S(1)}, bf16[8,32,256]{2,1,0:T(8,128)(2,1)S(1)}, u32[]{:S(2)}, u32[]{:S(2)}) collective-permute-start(bf16[8,32,256]{2,1,0:T(8,128)(2,1)S(1)} %collective-permute-done.refs_1_), channel_id=1, source_target_pairs={{0,1},{1,2},{2,3},{3,4},{4,5},{5,6},{6,7},{7,0},{8,9},{9,10},{10,1... | collective-permute-start | bytes 393224 | tf_op jit(solution)/shard_map/ppermute | solution.py:37
  34.3 6.2 %collective-permute-start.3 = (bf16[8,32,256]{2,1,0:T(8,128)(2,1)S(1)}, bf16[8,32,256]{2,1,0:T(8,128)(2,1)S(1)}, u32[]{:S(2)}, u32[]{:S(2)}) collective-permute-start(bf16[8,32,256]{2,1,0:T(8,128)(2,1)S(1)} %collective-permute-done.1.refs_2_), channel_id=1, source_target_pairs={{0,7},{1,0},{2,1},{3,2},{4,3},{5,4},{6,5},{7,6},{8,15},{9,8},{10,9... | collective-permute-start | bytes 393224 | tf_op jit(solution)/shard_map/ppermute | solution.py:37
  48.4 8.6 %collective-permute-start.9 = (bf16[8,32,256]{2,1,0:T(8,128)(2,1)S(1)}, bf16[8,32,256]{2,1,0:T(8,128)(2,1)S(1)}, u32[]{:S(2)}, u32[]{:S(2)}) collective-permute-start(bf16[8,32,256]{2,1,0:T(8,128)(2,1)S(1)} %get-tuple-element.29), channel_id=1, source_target_pairs={{0,7},{1,0},{2,1},{3,2},{4,3},{5,4},{6,5},{7,6},{8,15},{9,8},{10,9... | collective-permute-start | bytes 393224 | tf_op jit(solution)/shard_map/ppermute | solution.py:37
  48.8 10.6 %collective-permute-start.10 = (bf16[8,32,256]{2,1,0:T(8,128)(2,1)S(1)}, bf16[8,32,256]{2,1,0:T(8,128)(2,1)S(1)}, u32[]{:S(2)}, u32[]{:S(2)}) collective-permute-start(bf16[8,32,256]{2,1,0:T(8,128)(2,1)S(1)} %get-tuple-element.30), channel_id=1, source_target_pairs={{0,6},{1,7},{2,0},{3,1},{4,2},{5,3},{6,4},{7,5},{8,14},{9,15},{10,... | collective-permute-start | bytes 393224 | tf_op jit(solution)/shard_map/ppermute | solution.py:37
  49.3 12.2 %collective-permute-start.12 = (bf16[8,32,256]{2,1,0:T(8,128)(2,1)S(1)}, bf16[8,32,256]{2,1,0:T(8,128)(2,1)S(1)}, u32[]{:S(2)}, u32[]{:S(2)}) collective-permute-start(bf16[8,32,256]{2,1,0:T(8,128)(2,1)S(1)} %get-tuple-element.32), channel_id=1, source_target_pairs={{0,1},{1,2},{2,3},{3,4},{4,5},{5,6},{6,7},{7,0},{8,9},{9,10},{10,1... | collective-permute-start | bytes 393224 | tf_op jit(solution)/shard_map/ppermute | solution.py:37
  50.5 12.8 %collective-permute-start.7 = (bf16[8,32,256]{2,1,0:T(8,128)(2,1)S(1)}, bf16[8,32,256]{2,1,0:T(8,128)(2,1)S(1)}, u32[]{:S(2)}, u32[]{:S(2)}) collective-permute-start(bf16[8,32,256]{2,1,0:T(8,128)(2,1)S(1)} %get-tuple-element.26), channel_id=1, source_target_pairs={{0,7},{1,0},{2,1},{3,2},{4,3},{5,4},{6,5},{7,6},{8,15},{9,8},{10,9... | collective-permute-start | bytes 393224 | tf_op jit(solution)/shard_map/ppermute | solution.py:37
  52.6 10.7 %collective-permute-start.8 = (bf16[8,32,256]{2,1,0:T(8,128)(2,1)S(1)}, bf16[8,32,256]{2,1,0:T(8,128)(2,1)S(1)}, u32[]{:S(2)}, u32[]{:S(2)}) collective-permute-start(bf16[8,32,256]{2,1,0:T(8,128)(2,1)S(1)} %get-tuple-element.27), channel_id=1, source_target_pairs={{0,1},{1,2},{2,3},{3,4},{4,5},{5,6},{6,7},{7,0},{8,9},{9,10},{10,1... | collective-permute-start | bytes 393224 | tf_op jit(solution)/shard_map/ppermute | solution.py:37
  59.5 7.1 %collective-permute-start.11 = (bf16[8,32,256]{2,1,0:T(8,128)(2,1)S(1)}, bf16[8,32,256]{2,1,0:T(8,128)(2,1)S(1)}, u32[]{:S(2)}, u32[]{:S(2)}) collective-permute-start(bf16[8,32,256]{2,1,0:T(8,128)(2,1)S(1)} %shard_map.108), channel_id=1, source_target_pairs={{0,6},{1,7},{2,0},{3,1},{4,2},{5,3},{6,4},{7,5},{8,14},{9,15},{10,... | collective-permute-start | bytes 393224 | tf_op jit(solution)/shard_map/ppermute | solution.py:37
  61.5 8.4 %collective-permute-start.13 = (bf16[8,32,256]{2,1,0:T(8,128)(2,1)S(1)}, bf16[8,32,256]{2,1,0:T(8,128)(2,1)S(1)}, u32[]{:S(2)}, u32[]{:S(2)}) collective-permute-start(bf16[8,32,256]{2,1,0:T(8,128)(2,1)S(1)} %shard_map.109), channel_id=1, source_target_pairs={{0,2},{1,3},{2,4},{3,5},{4,6},{5,7},{6,0},{7,1},{8,10},{9,11},{10,... | collective-permute-start | bytes 393224 | tf_op jit(solution)/shard_map/ppermute | solution.py:37
  70.8 6.1 %collective-permute-start.14 = (bf16[40,1024]{1,0:T(8,128)(2,1)S(1)}, bf16[40,1024]{1,0:T(8,128)(2,1)S(1)}, u32[]{:S(2)}, u32[]{:S(2)}) collective-permute-start(bf16[40,1024]{1,0:T(8,128)(2,1)S(1)} %get-tuple-element.34), channel_id=1, source_target_pairs={{0,8},{8,16},{16,24},{24,32},{32,40},{40,48},{48,56},{56,0},{1,9},... | collective-permute-start | bytes 245768 | tf_op jit(solution)/shard_map/ppermute | solution.py:49
  73.7 4.7 %collective-permute-start.15 = (bf16[40,1024]{1,0:T(8,128)(2,1)S(1)}, bf16[40,1024]{1,0:T(8,128)(2,1)S(1)}, u32[]{:S(2)}, u32[]{:S(2)}) collective-permute-start(bf16[40,1024]{1,0:T(8,128)(2,1)S(1)} %get-tuple-element.35), channel_id=1, source_target_pairs={{0,16},{8,24},{16,32},{24,40},{32,48},{40,56},{48,0},{56,8},{1,17}... | collective-permute-start | bytes 245768 | tf_op jit(solution)/shard_map/ppermute | solution.py:49
  73.7 6.2 %collective-permute-start.16 = (bf16[40,1024]{1,0:T(8,128)(2,1)S(1)}, bf16[40,1024]{1,0:T(8,128)(2,1)S(1)}, u32[]{:S(2)}, u32[]{:S(2)}) collective-permute-start(bf16[40,1024]{1,0:T(8,128)(2,1)S(1)} %get-tuple-element.36), channel_id=1, source_target_pairs={{0,24},{8,32},{16,40},{24,48},{32,56},{40,0},{48,8},{56,16},{1,25}... | collective-permute-start | bytes 245768 | tf_op jit(solution)/shard_map/ppermute | solution.py:49
  74.7 5.5 %collective-permute-start.17 = (bf16[40,1024]{1,0:T(8,128)(2,1)S(1)}, bf16[40,1024]{1,0:T(8,128)(2,1)S(1)}, u32[]{:S(2)}, u32[]{:S(2)}) collective-permute-start(bf16[40,1024]{1,0:T(8,128)(2,1)S(1)} %get-tuple-element.37), channel_id=1, source_target_pairs={{0,32},{8,40},{16,48},{24,56},{32,0},{40,8},{48,16},{56,24},{1,33}... | collective-permute-start | bytes 245768 | tf_op jit(solution)/shard_map/ppermute | solution.py:49
  75.0 7.1 %collective-permute-start.18 = (bf16[40,1024]{1,0:T(8,128)(2,1)S(1)}, bf16[40,1024]{1,0:T(8,128)(2,1)S(1)}, u32[]{:S(2)}, u32[]{:S(2)}) collective-permute-start(bf16[40,1024]{1,0:T(8,128)(2,1)S(1)} %get-tuple-element.38), channel_id=1, source_target_pairs={{0,40},{8,48},{16,56},{24,0},{32,8},{40,16},{48,24},{56,32},{1,41}... | collective-permute-start | bytes 245768 | tf_op jit(solution)/shard_map/ppermute | solution.py:49
  77.0 5.1 %collective-permute-start.19 = (bf16[40,1024]{1,0:T(8,128)(2,1)S(1)}, bf16[40,1024]{1,0:T(8,128)(2,1)S(1)}, u32[]{:S(2)}, u32[]{:S(2)}) collective-permute-start(bf16[40,1024]{1,0:T(8,128)(2,1)S(1)} %get-tuple-element.39), channel_id=1, source_target_pairs={{0,48},{8,56},{16,0},{24,8},{32,16},{40,24},{48,32},{56,40},{1,49}... | collective-permute-start | bytes 245768 | tf_op jit(solution)/shard_map/ppermute | solution.py:49
  78.5 6.2 %collective-permute-start.20 = (bf16[40,1024]{1,0:T(8,128)(2,1)S(1)}, bf16[40,1024]{1,0:T(8,128)(2,1)S(1)}, u32[]{:S(2)}, u32[]{:S(2)}) collective-permute-start(bf16[40,1024]{1,0:T(8,128)(2,1)S(1)} %get-tuple-element.40), channel_id=1, source_target_pairs={{0,56},{8,0},{16,8},{24,16},{32,24},{40,32},{48,40},{56,48},{1,57}... | collective-permute-start | bytes 245768 | tf_op jit(solution)/shard_map/ppermute | solution.py:49

commit v8 on v7

--- a/solution.py
+++ b/solution.py
@@ -24,7 +24,7 @@
 BIG = 1e30
 PAIR = 2
 SPAN = 4
-EXTRA = 8
+EXTRA = 16
 HEADS = ("xl", "c", "xh")
 F32 = jnp.float32
 BF16 = jnp.bfloat16
@@ -67,39 +67,32 @@
     return high, (value - high.astype(F32)).astype(BF16)
 
 
-def pack_queries_kernel(
-    q_hbm, g_hbm, o_hbm, lse_hbm, keep_hbm, out_ref, o_ref, lse_ref, keep_ref, row_ref, sems, small
-):
+def pack_queries_kernel(q_hbm, g_hbm, o_hbm, lse_hbm, keep_hbm, out_ref, *refs):
+    q_ref, g_ref, o_ref, lse_ref, keep_ref, row_ref, sems, small = refs
     wide = GROUP * HD
-    copies = [[], []]
     small_copies = [
         pltpu.make_async_copy(lse_hbm, lse_ref, small.at[0]),
         pltpu.make_async_copy(keep_hbm, keep_ref, small.at[1]),
     ]
     for copy in small_copies:
         copy.start()
+    copies = []
     for a in range(AS):
         columns = pl.ds(a * wide, wide)
-        for n, (src, dst) in enumerate(
-            (
-                (g_hbm, out_ref.at[a, pl.ds(TOK, TOK), :]),
-                (o_hbm, o_ref.at[:, columns]),
-            )
-        ):
-            copies[0].append(pltpu.make_async_copy(src.at[:, columns], dst, sems.at[n, a]))
-        copies[1].append(
-            pltpu.make_async_copy(
-                q_hbm.at[:, columns], out_ref.at[a, pl.ds(0, TOK), :], sems.at[2, a]
-            )
+        copies.append(
+            [
+                pltpu.make_async_copy(src.at[:, columns], dst.at[:, columns], sems.at[n, a])
+                for n, (src, dst) in enumerate(((g_hbm, g_ref), (o_hbm, o_ref), (q_hbm, q_ref)))
+            ]
         )
-    for copy in copies[0] + copies[1]:
-        copy.start()
-    ones = jnp.ones((EXTRA, 2 * HD), BF16)
+        for copy in copies[a]:
+            copy.start()
+    ones = jnp.ones((8, 2 * HD), BF16)
     lane = lax.broadcasted_iota(jnp.int32, (TOK, ROWS), 1)
     spread = (lane % TOK == lax.broadcasted_iota(jnp.int32, (TOK, ROWS), 0)).astype(F32).astype(BF16)
     head_lane = lax.broadcasted_iota(jnp.int32, (GROUP, ROWS), 1) // TOK
     own_head = head_lane == lax.broadcasted_iota(jnp.int32, (GROUP, ROWS), 0)
-    row = lax.broadcasted_iota(jnp.int32, (EXTRA, ROWS), 0)
+    row = lax.broadcasted_iota(jnp.int32, (EXTRA, HD), 0)
     for copy in small_copies:
         copy.wait()
     place = lax.axis_index("xh") * 2 + lax.axis_index("z") // 4
@@ -113,10 +106,14 @@
     lower = split(scaled - high.astype(F32) - low.astype(F32))[0]
     lse_all = sum(jnp.dot(p, spread, preferred_element_type=F32) for p in (high, low, lower))
     for a in range(AS):
-        copies[0][2 * a].wait()
-        copies[0][2 * a + 1].wait()
+        for copy in copies[a]:
+            copy.wait()
         columns = slice(a * wide, (a + 1) * wide)
-        product = out_ref[a, TOK : 2 * TOK, :].astype(F32) * o_ref[:, columns].astype(F32)
+        for h in range(GROUP):
+            head = slice((a * GROUP + h) * HD, (a * GROUP + h + 1) * HD)
+            out_ref[a, h * TOK : (h + 1) * TOK, :] = q_ref[:, head]
+            out_ref[a, ROWS + h * TOK : ROWS + (h + 1) * TOK, :] = g_ref[:, head]
+        product = g_ref[:, columns].astype(F32) * o_ref[:, columns].astype(F32)
         high, low = split(product)
         stacked = jnp.concatenate(
             [
@@ -131,15 +128,12 @@
         lse = jnp.sum(
             jnp.where(own_head, lse_all[a * GROUP : (a + 1) * GROUP], 0.0), axis=0, keepdims=True
         )
-        lse_high, lse_low = split(lse)
-        delta_high, delta_low = split(delta)
-        extra = jnp.zeros((EXTRA, ROWS), F32)
-        for n, part in enumerate((lse_high, lse_low, delta_high, delta_low, flags)):
-            extra = jnp.where(row == n, part.astype(F32), extra)
-        out_ref[a, 2 * TOK :, :ROWS] = extra.astype(BF16)
-        out_ref[a, 2 * TOK :, ROWS:] = jnp.zeros((EXTRA, wide - ROWS), BF16)
-    for copy in copies[1]:
-        copy.wait()
+        parts = [p.astype(F32) for p in split(lse) + split(delta)]
+        extra = jnp.where(row == 8, flags, 0.0)
+        for n, part in enumerate(parts):
+            extra = jnp.where(row == 2 * n, part[:, :HD], extra)
+            extra = jnp.where(row == 2 * n + 1, part[:, HD:], extra)
+        out_ref[a, 2 * ROWS :, :] = extra.astype(BF16)
 
 
 def attention_kernel(offsets, first_call, final, keep_ref, message_ref, start_ref, *refs):
@@ -149,7 +143,7 @@
         dqt_in_ref, refs = refs[0], refs[1:]
     dq_ref, refs = refs[0], refs[1:]
     dkv_refs, refs = refs[:pieces], refs[pieces:]
-    acc_ref, kt_ref, q_ref, g_ref, qt_ref, gt_ref, dqt_ref = refs
+    acc_ref, kt_ref, qt_ref, gt_ref, dqt_ref = refs
     z = lax.axis_index("z")
     sources = [lax.rem(z - off + ZS, ZS) for off in offsets]
     halves = [source // 4 for source in sources]
@@ -165,19 +159,22 @@
     for b in range(AS // SPAN):
         kt_ref[b] = keys_of(b, pl.ds(0, HD)).T
 
+    def rows_of(j, first):
+        return jnp.concatenate(
+            [message_ref[j * PAIR + c, first : first + ROWS, :] for c in range(PAIR)], axis=0
+        )
+
     def load(j, slot):
         vectors = []
         for c in range(PAIR):
             i = j * PAIR + c
-            for h in range(GROUP):
-                rows = pl.ds(c * ROWS + h * TOK, TOK)
-                q_ref[slot, rows, :] = message_ref[i, :TOK, h * HD : (h + 1) * HD]
-                g_ref[slot, rows, :] = message_ref[i, TOK : 2 * TOK, h * HD : (h + 1) * HD]
-            extra = message_ref[i, 2 * TOK :, :ROWS].astype(F32)
-            q_pos = i * CHUNK + z * TOK + lane_token
-            vectors.append((extra[0:1] + extra[1:2], extra[2:3] + extra[3:4], start_ref[i], q_pos))
-        qt_ref[slot] = q_ref[slot].T
-        gt_ref[slot] = g_ref[slot].T
+            extra = message_ref[i, 2 * ROWS :, :].astype(F32)
+            summed = [extra[n : n + 1] + extra[n + 2 : n + 3] for n in (0, 1, 4, 5)]
+            lse = jnp.concatenate(summed[:2], axis=1)
+            delta = jnp.concatenate(summed[2:], axis=1)
+            vectors.append((lse, delta, start_ref[i], i * CHUNK + z * TOK + lane_token))
+        qt_ref[slot] = rows_of(j, 0).T
+        gt_ref[slot] = rows_of(j, ROWS).T
         return vectors
 
     def tile(j, b, slot, vectors):
@@ -207,8 +204,8 @@
             dscores_b.append(jnp.concatenate(dscores_row, axis=1))
         probs_b = jnp.concatenate(probs_b, axis=0)
         dscores_b = jnp.concatenate(dscores_b, axis=0)
-        dk = jnp.dot(dscores_b, q_ref[slot], preferred_element_type=F32)
-        dv = jnp.dot(probs_b, g_ref[slot], preferred_element_type=F32)
+        dk = jnp.dot(dscores_b, rows_of(j, 0), preferred_element_type=F32)
+        dv = jnp.dot(probs_b, rows_of(j, ROWS), preferred_element_type=F32)
         if j == b * SPAN // PAIR:
             acc_ref[b, :, :HD] = dk
             acc_ref[b, :, HD:] = dv
@@ -261,8 +258,6 @@
         scratch_shapes=[
             pltpu.VMEM((AS // SPAN, keys, 2 * HD), F32),
             pltpu.VMEM((AS // SPAN, HD, keys), BF16),
-            pltpu.VMEM((2, rows, HD), BF16),
-            pltpu.VMEM((2, rows, HD), BF16),
             pltpu.VMEM((2, HD, rows), BF16),
             pltpu.VMEM((2, HD, rows), BF16),
             pltpu.VMEM((2, HD, rows), F32),
@@ -282,17 +277,9 @@
     refs[-1][...] = total.astype(BF16)
 
 
-def pack_gradients_kernel(dq_ref, *refs):
-    pieces, out_refs, (total_ref, sems) = refs[:5], refs[5 : 5 + AS], refs[5 + AS :]
+def pack_gradients_kernel(*refs):
+    pieces, out_refs, (total_ref,) = refs[:5], refs[5 : 5 + AS], refs[5 + AS :]
     me = own_place()
-    copies = []
-    for k, out_ref in enumerate(out_refs):
-        there = lax.rem(me + k, AS)
-        copies.append(
-            pltpu.make_async_copy(dq_ref.at[there], out_ref.at[pl.ds(0, TOK), :], sems.at[k])
-        )
-    for copy in copies:
-        copy.start()
     total = pieces[0][...].astype(F32)
     for piece in pieces[1:]:
         total = total + piece[...].astype(F32)
@@ -301,36 +288,31 @@
         there = lax.rem(me + k, AS)
         for n in range(TOK // 8):
             columns = slice(n * 2 * HD, (n + 1) * 2 * HD)
-            out_ref[TOK:, columns] = total_ref[there, n * 8 : (n + 1) * 8, :]
+            out_ref[:, columns] = total_ref[there, n * 8 : (n + 1) * 8, :]
+
+
+def unpack_queries_kernel(in_ref, out_hbm, sems):
+    wide = GROUP * HD
+    copies = [
+        pltpu.make_async_copy(in_ref.at[a], out_hbm.at[:, pl.ds(a * wide, wide)], sems.at[a])
+        for a in range(AS)
+    ]
+    for copy in copies:
+        copy.start()
     for copy in copies:
         copy.wait()
 
 
 def unpack_gradients_kernel(*refs):
-    in_refs, (dq_hbm, dk_hbm, dv_hbm, dk_ref, dv_ref, sems) = refs[:AS], refs[AS:]
-    wide = GROUP * HD
+    in_refs, (dk_ref, dv_ref) = refs[:AS], refs[AS:]
     me = own_place()
-    copies = []
-    for k, in_ref in enumerate(in_refs):
-        a = lax.rem(me - k + AS, AS)
-        columns = pl.ds(pl.multiple_of(a * wide, wide), wide)
-        copies.append(
-            pltpu.make_async_copy(in_ref.at[pl.ds(0, TOK), :], dq_hbm.at[:, columns], sems.at[k])
-        )
-        copies[-1].start()
     for k, in_ref in enumerate(in_refs):
         a = lax.rem(me - k + AS, AS)
         columns = pl.ds(pl.multiple_of(a * HD, HD), HD)
         for n in range(TOK // 8):
             rows = slice(n * 8, (n + 1) * 8)
-            dk_ref[rows, columns] = in_ref[TOK:, 2 * n * HD : (2 * n + 1) * HD]
-            dv_ref[rows, columns] = in_ref[TOK:, (2 * n + 1) * HD : (2 * n + 2) * HD]
-    copies.append(pltpu.make_async_copy(dk_ref, dk_hbm, sems.at[AS]))
-    copies.append(pltpu.make_async_copy(dv_ref, dv_hbm, sems.at[AS + 1]))
-    copies[-2].start()
-    copies[-1].start()
-    for copy in copies:
-        copy.wait()
+            dk_ref[rows, columns] = in_ref[:, 2 * n * HD : (2 * n + 1) * HD]
+            dv_ref[rows, columns] = in_ref[:, (2 * n + 1) * HD : (2 * n + 2) * HD]
 
 
 def in_hbm():
@@ -388,14 +370,16 @@
     reach = block_keep.shape[1]
     message_send = pl.pallas_call(
         pack_queries_kernel,
-        out_shape=jax.ShapeDtypeStruct((AS, 2 * TOK + EXTRA, columns), BF16),
+        out_shape=jax.ShapeDtypeStruct((AS, 2 * ROWS + EXTRA, HD), BF16),
         in_specs=[in_hbm()] * 5,
         out_specs=in_vmem(),
         scratch_shapes=[
             pltpu.VMEM((TOK, AS * columns), BF16),
+            pltpu.VMEM((TOK, AS * columns), BF16),
+            pltpu.VMEM((TOK, AS * columns), BF16),
             pltpu.VMEM(lse.shape, F32),
             pltpu.VMEM(block_keep.shape, i32),
-            pltpu.VMEM((8, ROWS), F32),
+            pltpu.VMEM((8, HD), F32),
             dma((3, AS)),
             dma((2,)),
         ],
@@ -411,7 +395,7 @@
     pieces[-3] = along_z(pieces[-2], -1)
     pieces[4] = along_z(pieces[2], 2)
 
-    keep = message[:, 2 * TOK + 4, :reach].astype(i32)
+    keep = message[:, 2 * ROWS + 8, :reach].astype(i32)
     ends = jnp.arange(doc_lengths.shape[0], dtype=i32)
     starts = jnp.sum(jnp.where(ends[None, :] < ends[:, None], doc_lengths[None, :], 0), axis=1)
     base = lax.axis_index("y").astype(i32) * WINDOW
@@ -432,33 +416,42 @@
     dqt, far_part = attention(FAR, keep, message, start, pieces, dqt)
     from_three, from_four = along_z(far_part[3], -1), along_z(far_part[4], -2)
     from_minus_three = along_z(far_part[-3], 1)
-    dq, part = attention(LATE, keep, message, start, pieces, dqt, final=True)
-    two = along_z(partial_sum(part[2], from_three, from_four), -2)
-    minus_two = along_z(partial_sum(part[-2], from_minus_three), 2)
+    dqt, one, minus_one = lax.optimization_barrier((dqt, one, minus_one))
+    dq, late_part = attention(LATE, keep, message, start, pieces, dqt, final=True)
+    two = along_z(partial_sum(late_part[2], from_three, from_four), -2)
+    minus_two = along_z(partial_sum(late_part[-2], from_minus_three), 2)
+    dq_back = exchange(dq)
+    returned = (late_part[0], one, minus_one, two, minus_two)
+    query_grad = pl.pallas_call(
+        unpack_queries_kernel,
+        out_shape=jax.ShapeDtypeStruct((TOK, AS * columns), BF16),
+        in_specs=[in_vmem()],
+        out_specs=in_hbm(),
+        scratch_shapes=[dma((AS,))],
+        compiler_params=small_kernel,
+        cost_estimate=pl.CostEstimate(flops=0, bytes_accessed=1048576, transcendentals=0),
+    )(dq_back)
     gradients = pl.pallas_call(
         pack_gradients_kernel,
-        out_shape=[jax.ShapeDtypeStruct((TOK + 8, columns), BF16)] * AS,
-        in_specs=[in_vmem()] * 6,
+        out_shape=[jax.ShapeDtypeStruct((8, columns), BF16)] * AS,
+        in_specs=[in_vmem()] * 5,
         out_specs=[in_vmem()] * AS,
-        scratch_shapes=[pltpu.VMEM((AS, TOK, 2 * HD), BF16), dma((AS,))],
+        scratch_shapes=[pltpu.VMEM((AS, TOK, 2 * HD), BF16)],
         compiler_params=small_kernel,
-        cost_estimate=pl.CostEstimate(flops=400000, bytes_accessed=1900000, transcendentals=0),
-    )(dq, part[0], one, minus_one, two, minus_two)
+        cost_estimate=pl.CostEstimate(flops=5000000000, bytes_accessed=900000, transcendentals=0),
+    )(*returned)
     gradients = [gradients[0]] + [shifted(gradients[k], k) for k in range(1, AS)]
+    query_grad, gradients = lax.optimization_barrier((query_grad, gradients))
     half = jax.ShapeDtypeStruct((TOK, KVH * HD), BF16)
-    return pl.pallas_call(
+    key_grad, value_grad = pl.pallas_call(
         unpack_gradients_kernel,
-        out_shape=[jax.ShapeDtypeStruct((TOK, AS * columns), BF16), half, half],
+        out_shape=[half, half],
         in_specs=[in_vmem()] * AS,
-        out_specs=[in_hbm()] * 3,
-        scratch_shapes=[
-            pltpu.VMEM(half.shape, BF16),
-            pltpu.VMEM(half.shape, BF16),
-            dma((AS + 2,)),
-        ],
+        out_specs=[in_vmem()] * 2,
         compiler_params=small_kernel,
-        cost_estimate=pl.CostEstimate(flops=0, bytes_accessed=1300000, transcendentals=0),
+        cost_estimate=pl.CostEstimate(flops=0, bytes_accessed=262144, transcendentals=0),
     )(*gradients)
+    return (query_grad, key_grad, value_grad)
 
 
 def solution(mesh):

time: 86.2 us -> 82.7 us (0.959)
  waiting for transfers between devices: 27.2 us -> 16.9 us
  starting transfers between devices: 37.5 us -> 43.8 us
    ppermute x14, waiting for transfers between devices: 20.3 us -> 12.8 us  [along_z(): return lax.ppermute(value, 'z', [(i, (i + by) % ZS) for i in range(ZS)])]
    all_to_all x2 -> x3, starting transfers between devices: 7.95 us -> 12.3 us  [exchange(): return lax.all_to_all(value, HEADS, split_axis=0, concat_axis=0, tiled=True)]
    ppermute x7, waiting for transfers between devices: 5.67 us -> 2.99 us  [shifted(): return lax.ppermute(value, HEADS, [(i, (i + by) % AS) for i in range(AS)])]
    ppermute x14, starting transfers between devices: 21.4 us -> 22.7 us  [along_z(): return lax.ppermute(value, 'z', [(i, (i + by) % ZS) for i in range(ZS)])]
    pallas_call x2 -> x3, Pallas kernels: 1.79 us -> 1.66 us  [the longest x1 0.85 us: shards(): pl.pallas_call(unpack_queries_kernel, out_shape=jax.ShapeDtypeStruct((TOK...]
  transfers between devices with their start and end apart: 23 -> 24, of which waited for: 13 -> 7; matrix products, arithmetic and copies ran while one was open for 0% -> 0% of each run, Pallas kernels for 14% -> 22%
where the time goes in v8:
time: 82.7 us; the launch traced here: 82 us
  starting transfers between devices  43.8 us (53%)
  Pallas kernels  20.3 us (25%)
  waiting for transfers between devices  16.9 us (20%)
    ppermute x14, starting transfers between devices, along_z(): return lax.ppermute(value, 'z', [(i, (i + by) % ZS) for i in range(ZS)])  22.7 us
    ppermute x14, waiting for transfers between devices, along_z(): return lax.ppermute(value, 'z', [(i, (i + by) % ZS) for i in range(ZS)])  12.8 us
    pallas_call x3, Pallas kernels, attention(): pl.pallas_call(functools.partial(attention_kernel, offsets, first_call, f...  12.5 us
    all_to_all x3, starting transfers between devices, exchange(): return lax.all_to_all(value, HEADS, split_axis=0, concat_axis=0, tiled=True)  12.3 us
    ppermute x7, starting transfers between devices, shifted(): return lax.ppermute(value, HEADS, [(i, (i + by) % AS) for i in range(AS)])  8.8 us
    pallas_call x1, Pallas kernels, shards(): pl.pallas_call(pack_queries_kernel, out_shape=jax.ShapeDtypeStruct((AS, 2...  4.49 us
    ppermute x7, waiting for transfers between devices, shifted(): return lax.ppermute(value, HEADS, [(i, (i + by) % AS) for i in range(AS)])  2.99 us
  transfers between devices with their start and end apart: 24, of which 7 were waited for; matrix products, arithmetic and copies ran while one was open for 0% of the time, Pallas kernels for 22%

profile of v8, /device:TPU:8, one launch (start us, length us, event | category | flops | bytes accessed | tf_op | source)
XLA Modules:
  0.0 82.0 jit_solution(6251996453577157121)
XLA Ops:
  0.6 1.6 %shard_map.104 = bf16[8,32,256]{2,1,0:T(8,128)(2,1)} custom-call(bf16[32,1024]{1,0:T(8,128)(2,1)} %k_hbm.1, bf16[32,1024]{1,0:T(8,128)(2,1)} %v_hbm.1), custom_call_target="tpu_custom_call" | custom-call | bytes 262144 | tf_op jit(solution)/shard_map/pallas_call | solution.py:359
  2.2 4.3 %all-to-all-start.1 = ((bf16[8,32,256]{2,1,0:T(8,128)(2,1)}), bf16[8,32,256]{2,1,0:T(8,128)(2,1)S(1)}, u32[]{:S(2)}, u32[]{:S(2)}) async-start(bf16[8,32,256]{2,1,0:T(8,128)(2,1)} %shard_map.104), calls=%async_computation.1 | async-start | bytes 262144 | tf_op jit(solution)/shard_map/all_to_all | solution.py:41
  6.5 4.5 %shard_map.103 = bf16[8,528,128]{2,1,0:T(8,128)(2,1)} custom-call(bf16[32,8192]{1,0:T(8,128)(2,1)} %q_hbm.1, bf16[32,8192]{1,0:T(8,128)(2,1)} %g_hbm.1, bf16[32,8192]{1,0:T(8,128)(2,1)} %o_hbm.1, f32[32,64]{1,0:T(8,128)} %lse_hbm.1, s32[4,17]{1,0:T(4,128)} %keep_hbm.1), custom_call_target="tpu_custom_call" | custom-call | flops 67108864 | bytes 2800000 | tf_op jit(solution)/shard_map/pallas_call | solution.py:371
  12.1 3.8 %all-to-all-start = ((bf16[8,528,128]{2,1,0:T(8,128)(2,1)}), bf16[8,528,128]{2,1,0:T(8,128)(2,1)S(1)}, u32[]{:S(2)}, u32[]{:S(2)}) async-start(bf16[8,528,128]{2,1,0:T(8,128)(2,1)} %shard_map.103), calls=%async_computation | async-start | bytes 2162688 | tf_op jit(solution)/shard_map/all_to_all | solution.py:41
  16.1 6.4 %collective-permute-start.1 = (bf16[8,32,256]{2,1,0:T(8,128)(2,1)S(1)}, bf16[8,32,256]{2,1,0:T(8,128)(2,1)S(1)}, u32[]{:S(2)}, u32[]{:S(2)}) collective-permute-start(bf16[8,32,256]{2,1,0:T(8,128)(2,1)S(1)} %all-to-all-done.1.refs_0_), channel_id=1, source_target_pairs={{0,6},{1,7},{2,0},{3,1},{4,2},{5,3},{6,4},{7,5},{8,14},{9,15},{10,... | collective-permute-start | bytes 393224 | tf_op jit(solution)/shard_map/ppermute | solution.py:37
  22.5 3.8 %collective-permute-start.6 = (bf16[8,32,256]{2,1,0:T(8,128)(2,1)S(1)}, bf16[8,32,256]{2,1,0:T(8,128)(2,1)S(1)}, u32[]{:S(2)}, u32[]{:S(2)}) collective-permute-start(bf16[8,32,256]{2,1,0:T(8,128)(2,1)S(1)} %all-to-all-done.1.refs_0_), channel_id=1, source_target_pairs={{0,7},{1,0},{2,1},{3,2},{4,3},{5,4},{6,5},{7,6},{8,15},{9,8},{10,9... | collective-permute-start | bytes 393224 | tf_op jit(solution)/shard_map/ppermute | solution.py:37
  26.3 6.9 %collective-permute-done.refs_1_ = bf16[8,32,256]{2,1,0:T(8,128)(2,1)S(1)} collective-permute-done((bf16[8,32,256]{2,1,0:T(8,128)(2,1)S(1)}, bf16[8,32,256]{2,1,0:T(8,128)(2,1)S(1)}, u32[]{:S(2)}, u32[]{:S(2)}) %collective-permute-start) | collective-permute-done | bytes 131104 | tf_op jit(solution)/shard_map/ppermute | solution.py:37
  33.2 1.3 %collective-permute-start.2 = (bf16[8,32,256]{2,1,0:T(8,128)(2,1)S(1)}, bf16[8,32,256]{2,1,0:T(8,128)(2,1)S(1)}, u32[]{:S(2)}, u32[]{:S(2)}) collective-permute-start(bf16[8,32,256]{2,1,0:T(8,128)(2,1)S(1)} %collective-permute-done.refs_1_), channel_id=1, source_target_pairs={{0,1},{1,2},{2,3},{3,4},{4,5},{5,6},{6,7},{7,0},{8,9},{9,10},{10,1... | collective-permute-start | bytes 393224 | tf_op jit(solution)/shard_map/ppermute | solution.py:37
  34.5 2.7 %collective-permute-start.3 = (bf16[8,32,256]{2,1,0:T(8,128)(2,1)S(1)}, bf16[8,32,256]{2,1,0:T(8,128)(2,1)S(1)}, u32[]{:S(2)}, u32[]{:S(2)}) collective-permute-start(bf16[8,32,256]{2,1,0:T(8,128)(2,1)S(1)} %collective-permute-done.1.refs_2_), channel_id=1, source_target_pairs={{0,7},{1,0},{2,1},{3,2},{4,3},{5,4},{6,5},{7,6},{8,15},{9,8},{10,9... | collective-permute-start | bytes 393224 | tf_op jit(solution)/shard_map/ppermute | solution.py:37
  37.2 3.4 %shard_map.105 = (f32[4,128,512]{2,1,0:T(8,128)S(1)}, bf16[8,32,256]{2,1,0:T(8,128)(2,1)S(1)}, bf16[8,32,256]{2,1,0:T(8,128)(2,1)S(1)}) custom-call(s32[8,17]{1,0:T(8,128)S(1)} %bitcast.1, bf16[8,528,128]{2,1,0:T(8,128)(2,1)S(1)} %all-to-all-done.message_ref, s32[8,1,256]{2,1,0:T(1,128)S(1)} %max.18.start_ref, ...), custom_call_target="tpu_custom_call" | custom-call | flops 800000000 | bytes 3000000 | tf_op jit(solution)/shard_map/pallas_call | solution.py:252
  40.6 2.1 %collective-permute-start.7 = (bf16[8,32,256]{2,1,0:T(8,128)(2,1)S(1)}, bf16[8,32,256]{2,1,0:T(8,128)(2,1)S(1)}, u32[]{:S(2)}, u32[]{:S(2)}) collective-permute-start(bf16[8,32,256]{2,1,0:T(8,128)(2,1)S(1)} %get-tuple-element.38), channel_id=1, source_target_pairs={{0,7},{1,0},{2,1},{3,2},{4,3},{5,4},{6,5},{7,6},{8,15},{9,8},{10,9... | collective-permute-start | bytes 393224 | tf_op jit(solution)/shard_map/ppermute | solution.py:37
  42.7 1.5 %collective-permute-done.2.refs_0_ = bf16[8,32,256]{2,1,0:T(8,128)(2,1)S(1)} collective-permute-done((bf16[8,32,256]{2,1,0:T(8,128)(2,1)S(1)}, bf16[8,32,256]{2,1,0:T(8,128)(2,1)S(1)}, u32[]{:S(2)}, u32[]{:S(2)}) %collective-permute-start.2) | collective-permute-done | bytes 131104 | tf_op jit(solution)/shard_map/ppermute | solution.py:37
  44.3 4.1 %shard_map.106 = (f32[4,128,512]{2,1,0:T(8,128)S(1)}, bf16[8,32,256]{2,1,0:T(8,128)(2,1)S(1)}, bf16[8,32,256]{2,1,0:T(8,128)(2,1)S(1)}, bf16[8,32,256]{2,1,0:T(8,128)(2,1)S(1)}) custom-call(s32[8,17]{1,0:T(8,128)S(1)} %bitcast.2, bf16[8,528,128]{2,1,0:T(8,128)(2,1)S(1)} %all-to-all-done.message_ref, s32[8,1,256]{2,1,0:T(1,128)S(1)} %max.18.start_ref, ...), custom_call_target="tpu_custom_call" | custom-call | flops 1200000000 | bytes 3000000 | tf_op jit(solution)/shard_map/pallas_call | solution.py:252
  48.4 1.8 %collective-permute-start.9 = (bf16[8,32,256]{2,1,0:T(8,128)(2,1)S(1)}, bf16[8,32,256]{2,1,0:T(8,128)(2,1)S(1)}, u32[]{:S(2)}, u32[]{:S(2)}) collective-permute-start(bf16[8,32,256]{2,1,0:T(8,128)(2,1)S(1)} %get-tuple-element.46), channel_id=1, source_target_pairs={{0,7},{1,0},{2,1},{3,2},{4,3},{5,4},{6,5},{7,6},{8,15},{9,8},{10,9... | collective-permute-start | bytes 393224 | tf_op jit(solution)/shard_map/ppermute | solution.py:37
  50.2 1.6 %collective-permute-start.12 = (bf16[8,32,256]{2,1,0:T(8,128)(2,1)S(1)}, bf16[8,32,256]{2,1,0:T(8,128)(2,1)S(1)}, u32[]{:S(2)}, u32[]{:S(2)}) collective-permute-start(bf16[8,32,256]{2,1,0:T(8,128)(2,1)S(1)} %get-tuple-element.49), channel_id=1, source_target_pairs={{0,1},{1,2},{2,3},{3,4},{4,5},{5,6},{6,7},{7,0},{8,9},{9,10},{10,1... | collective-permute-start | bytes 393224 | tf_op jit(solution)/shard_map/ppermute | solution.py:37
  51.7 5.0 %shard_map.107 = (bf16[8,32,1024]{2,1,0:T(8,128)(2,1)}, bf16[8,32,256]{2,1,0:T(8,128)(2,1)S(1)}, bf16[8,32,256]{2,1,0:T(8,128)(2,1)S(1)}, bf16[8,32,256]{2,1,0:T(8,128)(2,1)S(1)}) custom-call(s32[8,17]{1,0:T(8,128)S(1)} %bitcast.3, bf16[8,528,128]{2,1,0:T(8,128)(2,1)S(1)} %all-to-all-done.message_ref, s32[8,1,256]{2,1,0:T(1,128)S(1)} %max.18.start_ref, ...), custom_call_target="tpu_custom_call" | custom-call | flops 1200000000 | bytes 3000000 | tf_op jit(solution)/shard_map/pallas_call | solution.py:252
  57.9 3.2 %collective-permute-start.11 = (bf16[8,32,256]{2,1,0:T(8,128)(2,1)S(1)}, bf16[8,32,256]{2,1,0:T(8,128)(2,1)S(1)}, u32[]{:S(2)}, u32[]{:S(2)}) collective-permute-start(bf16[8,32,256]{2,1,0:T(8,128)(2,1)S(1)} %shard_map.109), channel_id=1, source_target_pairs={{0,6},{1,7},{2,0},{3,1},{4,2},{5,3},{6,4},{7,5},{8,14},{9,15},{10,... | collective-permute-start | bytes 393224 | tf_op jit(solution)/shard_map/ppermute | solution.py:37
  61.2 4.2 %all-to-all-start.2 = ((bf16[8,32,1024]{2,1,0:T(8,128)(2,1)}), bf16[8,32,1024]{2,1,0:T(8,128)(2,1)S(1)}, u32[]{:S(2)}, u32[]{:S(2)}) async-start(bf16[8,32,1024]{2,1,0:T(8,128)(2,1)} %get-tuple-element.41), calls=%async_computation.2 | async-start | bytes 1048576 | tf_op jit(solution)/shard_map/all_to_all | solution.py:41
  65.4 3.2 %collective-permute-done.13.refs_4_ = bf16[8,32,256]{2,1,0:T(8,128)(2,1)S(1)} collective-permute-done((bf16[8,32,256]{2,1,0:T(8,128)(2,1)S(1)}, bf16[8,32,256]{2,1,0:T(8,128)(2,1)S(1)}, u32[]{:S(2)}, u32[]{:S(2)}) %collective-permute-start.13) | collective-permute-done | bytes 131104 | tf_op jit(solution)/shard_map/ppermute | solution.py:37
  68.7 3.3 %collective-permute-start.14 = (bf16[8,1024]{1,0:T(8,128)(2,1)S(1)}, bf16[8,1024]{1,0:T(8,128)(2,1)S(1)}, u32[]{:S(2)}, u32[]{:S(2)}) collective-permute-start(bf16[8,1024]{1,0:T(8,128)(2,1)S(1)} %get-tuple-element.51), channel_id=1, source_target_pairs={{0,8},{8,16},{16,24},{24,32},{32,40},{40,48},{48,56},{56,0},{1,9},... | collective-permute-start | bytes 49160 | tf_op jit(solution)/shard_map/ppermute | solution.py:49
  72.0 1.2 %collective-permute-start.16 = (bf16[8,1024]{1,0:T(8,128)(2,1)S(1)}, bf16[8,1024]{1,0:T(8,128)(2,1)S(1)}, u32[]{:S(2)}, u32[]{:S(2)}) collective-permute-start(bf16[8,1024]{1,0:T(8,128)(2,1)S(1)} %get-tuple-element.53), channel_id=1, source_target_pairs={{0,24},{8,32},{16,40},{24,48},{32,56},{40,0},{48,8},{56,16},{1,25}... | collective-permute-start | bytes 49160 | tf_op jit(solution)/shard_map/ppermute | solution.py:49
  73.4 1.8 %collective-permute-start.18 = (bf16[8,1024]{1,0:T(8,128)(2,1)S(1)}, bf16[8,1024]{1,0:T(8,128)(2,1)S(1)}, u32[]{:S(2)}, u32[]{:S(2)}) collective-permute-start(bf16[8,1024]{1,0:T(8,128)(2,1)S(1)} %get-tuple-element.55), channel_id=1, source_target_pairs={{0,40},{8,48},{16,56},{24,0},{32,8},{40,16},{48,24},{56,32},{1,41}... | collective-permute-start | bytes 49160 | tf_op jit(solution)/shard_map/ppermute | solution.py:49
  76.1 1.6 %collective-permute-start.20 = (bf16[8,1024]{1,0:T(8,128)(2,1)S(1)}, bf16[8,1024]{1,0:T(8,128)(2,1)S(1)}, u32[]{:S(2)}, u32[]{:S(2)}) collective-permute-start(bf16[8,1024]{1,0:T(8,128)(2,1)S(1)} %get-tuple-element.57), channel_id=1, source_target_pairs={{0,56},{8,0},{16,8},{24,16},{32,24},{40,32},{48,40},{56,48},{1,57}... | collective-permute-start | bytes 49160 | tf_op jit(solution)/shard_map/ppermute | solution.py:49
  78.6 2.8 %collective-permute-done.20.refs_7_ = bf16[8,1024]{1,0:T(8,128)(2,1)S(1)} collective-permute-done((bf16[8,1024]{1,0:T(8,128)(2,1)S(1)}, bf16[8,1024]{1,0:T(8,128)(2,1)S(1)}, u32[]{:S(2)}, u32[]{:S(2)}) %collective-permute-start.20) | collective-permute-done | bytes 16416 | tf_op jit(solution)/shard_map/ppermute | solution.py:49
  (44 shorter events, 5.5 us)
Async XLA Ops:
  2.2 9.9 %all-to-all-start.1 = ((bf16[8,32,256]{2,1,0:T(8,128)(2,1)}), bf16[8,32,256]{2,1,0:T(8,128)(2,1)S(1)}, u32[]{:S(2)}, u32[]{:S(2)}) async-start(bf16[8,32,256]{2,1,0:T(8,128)(2,1)} %shard_map.104), calls=%async_computation.1 | async-start | bytes 262144 | tf_op jit(solution)/shard_map/all_to_all | solution.py:41
  12.1 25.1 %all-to-all-start = ((bf16[8,528,128]{2,1,0:T(8,128)(2,1)}), bf16[8,528,128]{2,1,0:T(8,128)(2,1)S(1)}, u32[]{:S(2)}, u32[]{:S(2)}) async-start(bf16[8,528,128]{2,1,0:T(8,128)(2,1)} %shard_map.103), calls=%async_computation | async-start | bytes 2162688 | tf_op jit(solution)/shard_map/all_to_all | solution.py:41
  16.1 18.3 %collective-permute-start.1 = (bf16[8,32,256]{2,1,0:T(8,128)(2,1)S(1)}, bf16[8,32,256]{2,1,0:T(8,128)(2,1)S(1)}, u32[]{:S(2)}, u32[]{:S(2)}) collective-permute-start(bf16[8,32,256]{2,1,0:T(8,128)(2,1)S(1)} %all-to-all-done.1.refs_0_), channel_id=1, source_target_pairs={{0,6},{1,7},{2,0},{3,1},{4,2},{5,3},{6,4},{7,5},{8,14},{9,15},{10,... | collective-permute-start | bytes 393224 | tf_op jit(solution)/shard_map/ppermute | solution.py:37
  22.5 10.7 %collective-permute-start = (bf16[8,32,256]{2,1,0:T(8,128)(2,1)S(1)}, bf16[8,32,256]{2,1,0:T(8,128)(2,1)S(1)}, u32[]{:S(2)}, u32[]{:S(2)}) collective-permute-start(bf16[8,32,256]{2,1,0:T(8,128)(2,1)S(1)} %all-to-all-done.1.refs_0_), channel_id=1, source_target_pairs={{0,2},{1,3},{2,4},{3,5},{4,6},{5,7},{6,0},{7,1},{8,10},{9,11},{10,... | collective-permute-start | bytes 393224 | tf_op jit(solution)/shard_map/ppermute | solution.py:37
  22.5 14.6 %collective-permute-start.6 = (bf16[8,32,256]{2,1,0:T(8,128)(2,1)S(1)}, bf16[8,32,256]{2,1,0:T(8,128)(2,1)S(1)}, u32[]{:S(2)}, u32[]{:S(2)}) collective-permute-start(bf16[8,32,256]{2,1,0:T(8,128)(2,1)S(1)} %all-to-all-done.1.refs_0_), channel_id=1, source_target_pairs={{0,7},{1,0},{2,1},{3,2},{4,3},{5,4},{6,5},{7,6},{8,15},{9,8},{10,9... | collective-permute-start | bytes 393224 | tf_op jit(solution)/shard_map/ppermute | solution.py:37
  26.3 10.9 %collective-permute-start.5 = (bf16[8,32,256]{2,1,0:T(8,128)(2,1)S(1)}, bf16[8,32,256]{2,1,0:T(8,128)(2,1)S(1)}, u32[]{:S(2)}, u32[]{:S(2)}) collective-permute-start(bf16[8,32,256]{2,1,0:T(8,128)(2,1)S(1)} %all-to-all-done.1.refs_0_), channel_id=1, source_target_pairs={{0,1},{1,2},{2,3},{3,4},{4,5},{5,6},{6,7},{7,0},{8,9},{9,10},{10,1... | collective-permute-start | bytes 393224 | tf_op jit(solution)/shard_map/ppermute | solution.py:37
  33.2 9.5 %collective-permute-start.4 = (bf16[8,32,256]{2,1,0:T(8,128)(2,1)S(1)}, bf16[8,32,256]{2,1,0:T(8,128)(2,1)S(1)}, u32[]{:S(2)}, u32[]{:S(2)}) collective-permute-start(bf16[8,32,256]{2,1,0:T(8,128)(2,1)S(1)} %collective-permute-done.refs_1_), channel_id=1, source_target_pairs={{0,2},{1,3},{2,4},{3,5},{4,6},{5,7},{6,0},{7,1},{8,10},{9,11},{10,... | collective-permute-start | bytes 393224 | tf_op jit(solution)/shard_map/ppermute | solution.py:37
  33.2 11.1 %collective-permute-start.2 = (bf16[8,32,256]{2,1,0:T(8,128)(2,1)S(1)}, bf16[8,32,256]{2,1,0:T(8,128)(2,1)S(1)}, u32[]{:S(2)}, u32[]{:S(2)}) collective-permute-start(bf16[8,32,256]{2,1,0:T(8,128)(2,1)S(1)} %collective-permute-done.refs_1_), channel_id=1, source_target_pairs={{0,1},{1,2},{2,3},{3,4},{4,5},{5,6},{6,7},{7,0},{8,9},{9,10},{10,1... | collective-permute-start | bytes 393224 | tf_op jit(solution)/shard_map/ppermute | solution.py:37
  34.5 8.2 %collective-permute-start.3 = (bf16[8,32,256]{2,1,0:T(8,128)(2,1)S(1)}, bf16[8,32,256]{2,1,0:T(8,128)(2,1)S(1)}, u32[]{:S(2)}, u32[]{:S(2)}) collective-permute-start(bf16[8,32,256]{2,1,0:T(8,128)(2,1)S(1)} %collective-permute-done.1.refs_2_), channel_id=1, source_target_pairs={{0,7},{1,0},{2,1},{3,2},{4,3},{5,4},{6,5},{7,6},{8,15},{9,8},{10,9... | collective-permute-start | bytes 393224 | tf_op jit(solution)/shard_map/ppermute | solution.py:37
  40.6 11.1 %collective-permute-start.7 = (bf16[8,32,256]{2,1,0:T(8,128)(2,1)S(1)}, bf16[8,32,256]{2,1,0:T(8,128)(2,1)S(1)}, u32[]{:S(2)}, u32[]{:S(2)}) collective-permute-start(bf16[8,32,256]{2,1,0:T(8,128)(2,1)S(1)} %get-tuple-element.38), channel_id=1, source_target_pairs={{0,7},{1,0},{2,1},{3,2},{4,3},{5,4},{6,5},{7,6},{8,15},{9,8},{10,9... | collective-permute-start | bytes 393224 | tf_op jit(solution)/shard_map/ppermute | solution.py:37
  42.7 9.0 %collective-permute-start.8 = (bf16[8,32,256]{2,1,0:T(8,128)(2,1)S(1)}, bf16[8,32,256]{2,1,0:T(8,128)(2,1)S(1)}, u32[]{:S(2)}, u32[]{:S(2)}) collective-permute-start(bf16[8,32,256]{2,1,0:T(8,128)(2,1)S(1)} %get-tuple-element.39), channel_id=1, source_target_pairs={{0,1},{1,2},{2,3},{3,4},{4,5},{5,6},{6,7},{7,0},{8,9},{9,10},{10,1... | collective-permute-start | bytes 393224 | tf_op jit(solution)/shard_map/ppermute | solution.py:37
  48.4 8.3 %collective-permute-start.9 = (bf16[8,32,256]{2,1,0:T(8,128)(2,1)S(1)}, bf16[8,32,256]{2,1,0:T(8,128)(2,1)S(1)}, u32[]{:S(2)}, u32[]{:S(2)}) collective-permute-start(bf16[8,32,256]{2,1,0:T(8,128)(2,1)S(1)} %get-tuple-element.46), channel_id=1, source_target_pairs={{0,7},{1,0},{2,1},{3,2},{4,3},{5,4},{6,5},{7,6},{8,15},{9,8},{10,9... | collective-permute-start | bytes 393224 | tf_op jit(solution)/shard_map/ppermute | solution.py:37
  50.1 7.7 %collective-permute-start.10 = (bf16[8,32,256]{2,1,0:T(8,128)(2,1)S(1)}, bf16[8,32,256]{2,1,0:T(8,128)(2,1)S(1)}, u32[]{:S(2)}, u32[]{:S(2)}) collective-permute-start(bf16[8,32,256]{2,1,0:T(8,128)(2,1)S(1)} %get-tuple-element.47), channel_id=1, source_target_pairs={{0,6},{1,7},{2,0},{3,1},{4,2},{5,3},{6,4},{7,5},{8,14},{9,15},{10,... | collective-permute-start | bytes 393224 | tf_op jit(solution)/shard_map/ppermute | solution.py:37
  50.2 10.9 %collective-permute-start.12 = (bf16[8,32,256]{2,1,0:T(8,128)(2,1)S(1)}, bf16[8,32,256]{2,1,0:T(8,128)(2,1)S(1)}, u32[]{:S(2)}, u32[]{:S(2)}) collective-permute-start(bf16[8,32,256]{2,1,0:T(8,128)(2,1)S(1)} %get-tuple-element.49), channel_id=1, source_target_pairs={{0,1},{1,2},{2,3},{3,4},{4,5},{5,6},{6,7},{7,0},{8,9},{9,10},{10,1... | collective-permute-start | bytes 393224 | tf_op jit(solution)/shard_map/ppermute | solution.py:37
  57.9 7.5 %collective-permute-start.11 = (bf16[8,32,256]{2,1,0:T(8,128)(2,1)S(1)}, bf16[8,32,256]{2,1,0:T(8,128)(2,1)S(1)}, u32[]{:S(2)}, u32[]{:S(2)}) collective-permute-start(bf16[8,32,256]{2,1,0:T(8,128)(2,1)S(1)} %shard_map.109), channel_id=1, source_target_pairs={{0,6},{1,7},{2,0},{3,1},{4,2},{5,3},{6,4},{7,5},{8,14},{9,15},{10,... | collective-permute-start | bytes 393224 | tf_op jit(solution)/shard_map/ppermute | solution.py:37
  61.1 7.5 %collective-permute-start.13 = (bf16[8,32,256]{2,1,0:T(8,128)(2,1)S(1)}, bf16[8,32,256]{2,1,0:T(8,128)(2,1)S(1)}, u32[]{:S(2)}, u32[]{:S(2)}) collective-permute-start(bf16[8,32,256]{2,1,0:T(8,128)(2,1)S(1)} %shard_map.110), channel_id=1, source_target_pairs={{0,2},{1,3},{2,4},{3,5},{4,6},{5,7},{6,0},{7,1},{8,10},{9,11},{10,... | collective-permute-start | bytes 393224 | tf_op jit(solution)/shard_map/ppermute | solution.py:37
  61.2 16.5 %all-to-all-start.2 = ((bf16[8,32,1024]{2,1,0:T(8,128)(2,1)}), bf16[8,32,1024]{2,1,0:T(8,128)(2,1)S(1)}, u32[]{:S(2)}, u32[]{:S(2)}) async-start(bf16[8,32,1024]{2,1,0:T(8,128)(2,1)} %get-tuple-element.41), calls=%async_computation.2 | async-start | bytes 1048576 | tf_op jit(solution)/shard_map/all_to_all | solution.py:41
  68.7 6.7 %collective-permute-start.14 = (bf16[8,1024]{1,0:T(8,128)(2,1)S(1)}, bf16[8,1024]{1,0:T(8,128)(2,1)S(1)}, u32[]{:S(2)}, u32[]{:S(2)}) collective-permute-start(bf16[8,1024]{1,0:T(8,128)(2,1)S(1)} %get-tuple-element.51), channel_id=1, source_target_pairs={{0,8},{8,16},{16,24},{24,32},{32,40},{40,48},{48,56},{56,0},{1,9},... | collective-permute-start | bytes 49160 | tf_op jit(solution)/shard_map/ppermute | solution.py:49
  72.0 4.1 %collective-permute-start.15 = (bf16[8,1024]{1,0:T(8,128)(2,1)S(1)}, bf16[8,1024]{1,0:T(8,128)(2,1)S(1)}, u32[]{:S(2)}, u32[]{:S(2)}) collective-permute-start(bf16[8,1024]{1,0:T(8,128)(2,1)S(1)} %get-tuple-element.52), channel_id=1, source_target_pairs={{0,16},{8,24},{16,32},{24,40},{32,48},{40,56},{48,0},{56,8},{1,17}... | collective-permute-start | bytes 49160 | tf_op jit(solution)/shard_map/ppermute | solution.py:49
  72.0 6.6 %collective-permute-start.16 = (bf16[8,1024]{1,0:T(8,128)(2,1)S(1)}, bf16[8,1024]{1,0:T(8,128)(2,1)S(1)}, u32[]{:S(2)}, u32[]{:S(2)}) collective-permute-start(bf16[8,1024]{1,0:T(8,128)(2,1)S(1)} %get-tuple-element.53), channel_id=1, source_target_pairs={{0,24},{8,32},{16,40},{24,48},{32,56},{40,0},{48,8},{56,16},{1,25}... | collective-permute-start | bytes 49160 | tf_op jit(solution)/shard_map/ppermute | solution.py:49
  73.2 5.4 %collective-permute-start.17 = (bf16[8,1024]{1,0:T(8,128)(2,1)S(1)}, bf16[8,1024]{1,0:T(8,128)(2,1)S(1)}, u32[]{:S(2)}, u32[]{:S(2)}) collective-permute-start(bf16[8,1024]{1,0:T(8,128)(2,1)S(1)} %get-tuple-element.54), channel_id=1, source_target_pairs={{0,32},{8,40},{16,48},{24,56},{32,0},{40,8},{48,16},{56,24},{1,33}... | collective-permute-start | bytes 49160 | tf_op jit(solution)/shard_map/ppermute | solution.py:49
  73.4 5.1 %collective-permute-start.18 = (bf16[8,1024]{1,0:T(8,128)(2,1)S(1)}, bf16[8,1024]{1,0:T(8,128)(2,1)S(1)}, u32[]{:S(2)}, u32[]{:S(2)}) collective-permute-start(bf16[8,1024]{1,0:T(8,128)(2,1)S(1)} %get-tuple-element.55), channel_id=1, source_target_pairs={{0,40},{8,48},{16,56},{24,0},{32,8},{40,16},{48,24},{56,32},{1,41}... | collective-permute-start | bytes 49160 | tf_op jit(solution)/shard_map/ppermute | solution.py:49
  75.4 3.2 %collective-permute-start.19 = (bf16[8,1024]{1,0:T(8,128)(2,1)S(1)}, bf16[8,1024]{1,0:T(8,128)(2,1)S(1)}, u32[]{:S(2)}, u32[]{:S(2)}) collective-permute-start(bf16[8,1024]{1,0:T(8,128)(2,1)S(1)} %get-tuple-element.56), channel_id=1, source_target_pairs={{0,48},{8,56},{16,0},{24,8},{32,16},{40,24},{48,32},{56,40},{1,49}... | collective-permute-start | bytes 49160 | tf_op jit(solution)/shard_map/ppermute | solution.py:49
  76.1 5.2 %collective-permute-start.20 = (bf16[8,1024]{1,0:T(8,128)(2,1)S(1)}, bf16[8,1024]{1,0:T(8,128)(2,1)S(1)}, u32[]{:S(2)}, u32[]{:S(2)}) collective-permute-start(bf16[8,1024]{1,0:T(8,128)(2,1)S(1)} %get-tuple-element.57), channel_id=1, source_target_pairs={{0,56},{8,0},{16,8},{24,16},{32,24},{40,32},{48,40},{56,48},{1,57}... | collective-permute-start | bytes 49160 | tf_op jit(solution)/shard_map/ppermute | solution.py:49
  (1 other events, 4.9 us)

commit v9 on v8

--- a/solution.py
+++ b/solution.py
@@ -28,9 +28,9 @@
 HEADS = ("xl", "c", "xh")
 F32 = jnp.float32
 BF16 = jnp.bfloat16
-EARLY = (1, -1)
+EARLY = (0, 1, -1)
 FAR = (3, -3, 4)
-LATE = (0, 2, -2)
+LATE = (2, -2)
 
 
 def along_z(value, by):
@@ -421,7 +421,7 @@
     two = along_z(partial_sum(late_part[2], from_three, from_four), -2)
     minus_two = along_z(partial_sum(late_part[-2], from_minus_three), 2)
     dq_back = exchange(dq)
-    returned = (late_part[0], one, minus_one, two, minus_two)
+    returned = (part[0], one, minus_one, two, minus_two)
     query_grad = pl.pallas_call(
         unpack_queries_kernel,
         out_shape=jax.ShapeDtypeStruct((TOK, AS * columns), BF16),

time: 82.7 us -> 83 us (level)
    ppermute x14, starting transfers between devices: 22.7 us -> 23.7 us  [along_z(): return lax.ppermute(value, 'z', [(i, (i + by) % ZS) for i in range(ZS)])]
    ppermute x7, starting transfers between devices: 8.8 us -> 7.81 us  [shifted(): return lax.ppermute(value, HEADS, [(i, (i + by) % AS) for i in range(AS)])]
where the time goes in v9:
time: 83 us; the launch traced here: 82.5 us
  starting transfers between devices  43.3 us (52%)
  Pallas kernels  20.3 us (24%)
  waiting for transfers between devices  17.7 us (21%)
    ppermute x14, starting transfers between devices, along_z(): return lax.ppermute(value, 'z', [(i, (i + by) % ZS) for i in range(ZS)])  23.7 us
    ppermute x14, waiting for transfers between devices, along_z(): return lax.ppermute(value, 'z', [(i, (i + by) % ZS) for i in range(ZS)])  12.9 us
    pallas_call x3, Pallas kernels, attention(): pl.pallas_call(functools.partial(attention_kernel, offsets, first_call, f...  12.5 us
    all_to_all x3, starting transfers between devices, exchange(): return lax.all_to_all(value, HEADS, split_axis=0, concat_axis=0, tiled=True)  11.8 us
    ppermute x7, starting transfers between devices, shifted(): return lax.ppermute(value, HEADS, [(i, (i + by) % AS) for i in range(AS)])  7.81 us
    pallas_call x1, Pallas kernels, shards(): pl.pallas_call(pack_queries_kernel, out_shape=jax.ShapeDtypeStruct((AS, 2...  4.49 us
    ppermute x7, waiting for transfers between devices, shifted(): return lax.ppermute(value, HEADS, [(i, (i + by) % AS) for i in range(AS)])  3.75 us
  transfers between devices with their start and end apart: 24, of which 7 were waited for; matrix products, arithmetic and copies ran while one was open for 0% of the time, Pallas kernels for 22%

profile of v9, /device:TPU:8, one launch (start us, length us, event | category | flops | bytes accessed | tf_op | source)
XLA Modules:
  0.0 82.5 jit_solution(1365657468250702151)
XLA Ops:
  0.6 1.6 %shard_map.104 = bf16[8,32,256]{2,1,0:T(8,128)(2,1)} custom-call(bf16[32,1024]{1,0:T(8,128)(2,1)} %k_hbm.1, bf16[32,1024]{1,0:T(8,128)(2,1)} %v_hbm.1), custom_call_target="tpu_custom_call" | custom-call | bytes 262144 | tf_op jit(solution)/shard_map/pallas_call | solution.py:359
  2.2 4.3 %all-to-all-start.1 = ((bf16[8,32,256]{2,1,0:T(8,128)(2,1)}), bf16[8,32,256]{2,1,0:T(8,128)(2,1)S(1)}, u32[]{:S(2)}, u32[]{:S(2)}) async-start(bf16[8,32,256]{2,1,0:T(8,128)(2,1)} %shard_map.104), calls=%async_computation.1 | async-start | bytes 262144 | tf_op jit(solution)/shard_map/all_to_all | solution.py:41
  6.5 4.5 %shard_map.103 = bf16[8,528,128]{2,1,0:T(8,128)(2,1)} custom-call(bf16[32,8192]{1,0:T(8,128)(2,1)} %q_hbm.1, bf16[32,8192]{1,0:T(8,128)(2,1)} %g_hbm.1, bf16[32,8192]{1,0:T(8,128)(2,1)} %o_hbm.1, f32[32,64]{1,0:T(8,128)} %lse_hbm.1, s32[4,17]{1,0:T(4,128)} %keep_hbm.1), custom_call_target="tpu_custom_call" | custom-call | flops 67108864 | bytes 2800000 | tf_op jit(solution)/shard_map/pallas_call | solution.py:371
  11.0 1.0 %all-to-all-done.1.refs_0_ = bf16[8,32,256]{2,1,0:T(8,128)(2,1)S(1)} async-done(((bf16[8,32,256]{2,1,0:T(8,128)(2,1)}), bf16[8,32,256]{2,1,0:T(8,128)(2,1)S(1)}, u32[]{:S(2)}, u32[]{:S(2)}) %all-to-all-start.1) | async-done | bytes 131104 | tf_op jit(solution)/shard_map/all_to_all | solution.py:41
  12.1 3.8 %all-to-all-start = ((bf16[8,528,128]{2,1,0:T(8,128)(2,1)}), bf16[8,528,128]{2,1,0:T(8,128)(2,1)S(1)}, u32[]{:S(2)}, u32[]{:S(2)}) async-start(bf16[8,528,128]{2,1,0:T(8,128)(2,1)} %shard_map.103), calls=%async_computation | async-start | bytes 2162688 | tf_op jit(solution)/shard_map/all_to_all | solution.py:41
  16.1 6.4 %collective-permute-start.1 = (bf16[8,32,256]{2,1,0:T(8,128)(2,1)S(1)}, bf16[8,32,256]{2,1,0:T(8,128)(2,1)S(1)}, u32[]{:S(2)}, u32[]{:S(2)}) collective-permute-start(bf16[8,32,256]{2,1,0:T(8,128)(2,1)S(1)} %all-to-all-done.1.refs_0_), channel_id=1, source_target_pairs={{0,6},{1,7},{2,0},{3,1},{4,2},{5,3},{6,4},{7,5},{8,14},{9,15},{10,... | collective-permute-start | bytes 393224 | tf_op jit(solution)/shard_map/ppermute | solution.py:37
  22.5 3.8 %collective-permute-start.6 = (bf16[8,32,256]{2,1,0:T(8,128)(2,1)S(1)}, bf16[8,32,256]{2,1,0:T(8,128)(2,1)S(1)}, u32[]{:S(2)}, u32[]{:S(2)}) collective-permute-start(bf16[8,32,256]{2,1,0:T(8,128)(2,1)S(1)} %all-to-all-done.1.refs_0_), channel_id=1, source_target_pairs={{0,7},{1,0},{2,1},{3,2},{4,3},{5,4},{6,5},{7,6},{8,15},{9,8},{10,9... | collective-permute-start | bytes 393224 | tf_op jit(solution)/shard_map/ppermute | solution.py:37
  26.3 6.9 %collective-permute-done.refs_0_ = bf16[8,32,256]{2,1,0:T(8,128)(2,1)S(1)} collective-permute-done((bf16[8,32,256]{2,1,0:T(8,128)(2,1)S(1)}, bf16[8,32,256]{2,1,0:T(8,128)(2,1)S(1)}, u32[]{:S(2)}, u32[]{:S(2)}) %collective-permute-start) | collective-permute-done | bytes 131104 | tf_op jit(solution)/shard_map/ppermute | solution.py:37
  33.2 1.3 %collective-permute-start.2 = (bf16[8,32,256]{2,1,0:T(8,128)(2,1)S(1)}, bf16[8,32,256]{2,1,0:T(8,128)(2,1)S(1)}, u32[]{:S(2)}, u32[]{:S(2)}) collective-permute-start(bf16[8,32,256]{2,1,0:T(8,128)(2,1)S(1)} %collective-permute-done.refs_0_), channel_id=1, source_target_pairs={{0,1},{1,2},{2,3},{3,4},{4,5},{5,6},{6,7},{7,0},{8,9},{9,10},{10,1... | collective-permute-start | bytes 393224 | tf_op jit(solution)/shard_map/ppermute | solution.py:37
  34.5 2.7 %collective-permute-start.3 = (bf16[8,32,256]{2,1,0:T(8,128)(2,1)S(1)}, bf16[8,32,256]{2,1,0:T(8,128)(2,1)S(1)}, u32[]{:S(2)}, u32[]{:S(2)}) collective-permute-start(bf16[8,32,256]{2,1,0:T(8,128)(2,1)S(1)} %collective-permute-done.1.refs_1_), channel_id=1, source_target_pairs={{0,7},{1,0},{2,1},{3,2},{4,3},{5,4},{6,5},{7,6},{8,15},{9,8},{10,9... | collective-permute-start | bytes 393224 | tf_op jit(solution)/shard_map/ppermute | solution.py:37
  37.2 4.1 %shard_map.105 = (f32[4,128,512]{2,1,0:T(8,128)S(1)}, bf16[8,32,256]{2,1,0:T(8,128)(2,1)S(1)}, bf16[8,32,256]{2,1,0:T(8,128)(2,1)S(1)}, bf16[8,32,256]{2,1,0:T(8,128)(2,1)S(1)}) custom-call(s32[8,17]{1,0:T(8,128)S(1)} %bitcast.1, bf16[8,528,128]{2,1,0:T(8,128)(2,1)S(1)} %all-to-all-done.message_ref, s32[8,1,256]{2,1,0:T(1,128)S(1)} %max.18.start_ref, ...), custom_call_target="tpu_custom_call" | custom-call | flops 1200000000 | bytes 3000000 | tf_op jit(solution)/shard_map/pallas_call | solution.py:252
  41.3 2.1 %collective-permute-start.7 = (bf16[8,32,256]{2,1,0:T(8,128)(2,1)S(1)}, bf16[8,32,256]{2,1,0:T(8,128)(2,1)S(1)}, u32[]{:S(2)}, u32[]{:S(2)}) collective-permute-start(bf16[8,32,256]{2,1,0:T(8,128)(2,1)S(1)} %get-tuple-element.38), channel_id=1, source_target_pairs={{0,7},{1,0},{2,1},{3,2},{4,3},{5,4},{6,5},{7,6},{8,15},{9,8},{10,9... | collective-permute-start | bytes 393224 | tf_op jit(solution)/shard_map/ppermute | solution.py:37
  44.3 4.1 %shard_map.106 = (f32[4,128,512]{2,1,0:T(8,128)S(1)}, bf16[8,32,256]{2,1,0:T(8,128)(2,1)S(1)}, bf16[8,32,256]{2,1,0:T(8,128)(2,1)S(1)}, bf16[8,32,256]{2,1,0:T(8,128)(2,1)S(1)}) custom-call(s32[8,17]{1,0:T(8,128)S(1)} %bitcast.2, bf16[8,528,128]{2,1,0:T(8,128)(2,1)S(1)} %all-to-all-done.message_ref, s32[8,1,256]{2,1,0:T(1,128)S(1)} %max.18.start_ref, ...), custom_call_target="tpu_custom_call" | custom-call | flops 1200000000 | bytes 3000000 | tf_op jit(solution)/shard_map/pallas_call | solution.py:252
  48.4 2.5 %collective-permute-start.9 = (bf16[8,32,256]{2,1,0:T(8,128)(2,1)S(1)}, bf16[8,32,256]{2,1,0:T(8,128)(2,1)S(1)}, u32[]{:S(2)}, u32[]{:S(2)}) collective-permute-start(bf16[8,32,256]{2,1,0:T(8,128)(2,1)S(1)} %get-tuple-element.46), channel_id=1, source_target_pairs={{0,7},{1,0},{2,1},{3,2},{4,3},{5,4},{6,5},{7,6},{8,15},{9,8},{10,9... | collective-permute-start | bytes 393224 | tf_op jit(solution)/shard_map/ppermute | solution.py:37
  50.9 1.6 %collective-permute-start.12 = (bf16[8,32,256]{2,1,0:T(8,128)(2,1)S(1)}, bf16[8,32,256]{2,1,0:T(8,128)(2,1)S(1)}, u32[]{:S(2)}, u32[]{:S(2)}) collective-permute-start(bf16[8,32,256]{2,1,0:T(8,128)(2,1)S(1)} %get-tuple-element.49), channel_id=1, source_target_pairs={{0,1},{1,2},{2,3},{3,4},{4,5},{5,6},{6,7},{7,0},{8,9},{9,10},{10,1... | collective-permute-start | bytes 393224 | tf_op jit(solution)/shard_map/ppermute | solution.py:37
  52.4 4.3 %shard_map.107 = (bf16[8,32,1024]{2,1,0:T(8,128)(2,1)}, bf16[8,32,256]{2,1,0:T(8,128)(2,1)S(1)}, bf16[8,32,256]{2,1,0:T(8,128)(2,1)S(1)}) custom-call(s32[8,17]{1,0:T(8,128)S(1)} %bitcast.3, bf16[8,528,128]{2,1,0:T(8,128)(2,1)S(1)} %all-to-all-done.message_ref, s32[8,1,256]{2,1,0:T(1,128)S(1)} %max.18.start_ref, ...), custom_call_target="tpu_custom_call" | custom-call | flops 800000000 | bytes 3000000 | tf_op jit(solution)/shard_map/pallas_call | solution.py:252
  56.7 1.8 %collective-permute-done.10.refs_2_ = bf16[8,32,256]{2,1,0:T(8,128)(2,1)S(1)} collective-permute-done((bf16[8,32,256]{2,1,0:T(8,128)(2,1)S(1)}, bf16[8,32,256]{2,1,0:T(8,128)(2,1)S(1)}, u32[]{:S(2)}, u32[]{:S(2)}) %collective-permute-start.10) | collective-permute-done | bytes 131104 | tf_op jit(solution)/shard_map/ppermute | solution.py:37
  58.6 3.4 %collective-permute-start.11 = (bf16[8,32,256]{2,1,0:T(8,128)(2,1)S(1)}, bf16[8,32,256]{2,1,0:T(8,128)(2,1)S(1)}, u32[]{:S(2)}, u32[]{:S(2)}) collective-permute-start(bf16[8,32,256]{2,1,0:T(8,128)(2,1)S(1)} %shard_map.109), channel_id=1, source_target_pairs={{0,6},{1,7},{2,0},{3,1},{4,2},{5,3},{6,4},{7,5},{8,14},{9,15},{10,... | collective-permute-start | bytes 393224 | tf_op jit(solution)/shard_map/ppermute | solution.py:37
  62.2 3.7 %all-to-all-start.2 = ((bf16[8,32,1024]{2,1,0:T(8,128)(2,1)}), bf16[8,32,1024]{2,1,0:T(8,128)(2,1)S(1)}, u32[]{:S(2)}, u32[]{:S(2)}) async-start(bf16[8,32,1024]{2,1,0:T(8,128)(2,1)} %get-tuple-element.41), calls=%async_computation.2 | async-start | bytes 1048576 | tf_op jit(solution)/shard_map/all_to_all | solution.py:41
  65.9 3.3 %collective-permute-done.13.refs_4_ = bf16[8,32,256]{2,1,0:T(8,128)(2,1)S(1)} collective-permute-done((bf16[8,32,256]{2,1,0:T(8,128)(2,1)S(1)}, bf16[8,32,256]{2,1,0:T(8,128)(2,1)S(1)}, u32[]{:S(2)}, u32[]{:S(2)}) %collective-permute-start.13) | collective-permute-done | bytes 131104 | tf_op jit(solution)/shard_map/ppermute | solution.py:37
  69.4 2.5 %collective-permute-start.14 = (bf16[8,1024]{1,0:T(8,128)(2,1)S(1)}, bf16[8,1024]{1,0:T(8,128)(2,1)S(1)}, u32[]{:S(2)}, u32[]{:S(2)}) collective-permute-start(bf16[8,1024]{1,0:T(8,128)(2,1)S(1)} %get-tuple-element.51), channel_id=1, source_target_pairs={{0,8},{8,16},{16,24},{24,32},{32,40},{40,48},{48,56},{56,0},{1,9},... | collective-permute-start | bytes 49160 | tf_op jit(solution)/shard_map/ppermute | solution.py:49
  73.3 1.8 %collective-permute-start.18 = (bf16[8,1024]{1,0:T(8,128)(2,1)S(1)}, bf16[8,1024]{1,0:T(8,128)(2,1)S(1)}, u32[]{:S(2)}, u32[]{:S(2)}) collective-permute-start(bf16[8,1024]{1,0:T(8,128)(2,1)S(1)} %get-tuple-element.55), channel_id=1, source_target_pairs={{0,40},{8,48},{16,56},{24,0},{32,8},{40,16},{48,24},{56,32},{1,41}... | collective-permute-start | bytes 49160 | tf_op jit(solution)/shard_map/ppermute | solution.py:49
  76.6 1.5 %collective-permute-start.20 = (bf16[8,1024]{1,0:T(8,128)(2,1)S(1)}, bf16[8,1024]{1,0:T(8,128)(2,1)S(1)}, u32[]{:S(2)}, u32[]{:S(2)}) collective-permute-start(bf16[8,1024]{1,0:T(8,128)(2,1)S(1)} %get-tuple-element.57), channel_id=1, source_target_pairs={{0,56},{8,0},{16,8},{24,16},{32,24},{40,32},{48,40},{56,48},{1,57}... | collective-permute-start | bytes 49160 | tf_op jit(solution)/shard_map/ppermute | solution.py:49
  78.9 2.9 %collective-permute-done.20.refs_7_ = bf16[8,1024]{1,0:T(8,128)(2,1)S(1)} collective-permute-done((bf16[8,1024]{1,0:T(8,128)(2,1)S(1)}, bf16[8,1024]{1,0:T(8,128)(2,1)S(1)}, u32[]{:S(2)}, u32[]{:S(2)}) %collective-permute-start.20) | collective-permute-done | bytes 16416 | tf_op jit(solution)/shard_map/ppermute | solution.py:49
  (44 shorter events, 5.9 us)
Async XLA Ops:
  2.2 9.9 %all-to-all-start.1 = ((bf16[8,32,256]{2,1,0:T(8,128)(2,1)}), bf16[8,32,256]{2,1,0:T(8,128)(2,1)S(1)}, u32[]{:S(2)}, u32[]{:S(2)}) async-start(bf16[8,32,256]{2,1,0:T(8,128)(2,1)} %shard_map.104), calls=%async_computation.1 | async-start | bytes 262144 | tf_op jit(solution)/shard_map/all_to_all | solution.py:41
  12.1 25.1 %all-to-all-start = ((bf16[8,528,128]{2,1,0:T(8,128)(2,1)}), bf16[8,528,128]{2,1,0:T(8,128)(2,1)S(1)}, u32[]{:S(2)}, u32[]{:S(2)}) async-start(bf16[8,528,128]{2,1,0:T(8,128)(2,1)} %shard_map.103), calls=%async_computation | async-start | bytes 2162688 | tf_op jit(solution)/shard_map/all_to_all | solution.py:41
  16.1 18.3 %collective-permute-start.1 = (bf16[8,32,256]{2,1,0:T(8,128)(2,1)S(1)}, bf16[8,32,256]{2,1,0:T(8,128)(2,1)S(1)}, u32[]{:S(2)}, u32[]{:S(2)}) collective-permute-start(bf16[8,32,256]{2,1,0:T(8,128)(2,1)S(1)} %all-to-all-done.1.refs_0_), channel_id=1, source_target_pairs={{0,6},{1,7},{2,0},{3,1},{4,2},{5,3},{6,4},{7,5},{8,14},{9,15},{10,... | collective-permute-start | bytes 393224 | tf_op jit(solution)/shard_map/ppermute | solution.py:37
  22.5 10.7 %collective-permute-start = (bf16[8,32,256]{2,1,0:T(8,128)(2,1)S(1)}, bf16[8,32,256]{2,1,0:T(8,128)(2,1)S(1)}, u32[]{:S(2)}, u32[]{:S(2)}) collective-permute-start(bf16[8,32,256]{2,1,0:T(8,128)(2,1)S(1)} %all-to-all-done.1.refs_0_), channel_id=1, source_target_pairs={{0,2},{1,3},{2,4},{3,5},{4,6},{5,7},{6,0},{7,1},{8,10},{9,11},{10,... | collective-permute-start | bytes 393224 | tf_op jit(solution)/shard_map/ppermute | solution.py:37
  22.5 14.6 %collective-permute-start.6 = (bf16[8,32,256]{2,1,0:T(8,128)(2,1)S(1)}, bf16[8,32,256]{2,1,0:T(8,128)(2,1)S(1)}, u32[]{:S(2)}, u32[]{:S(2)}) collective-permute-start(bf16[8,32,256]{2,1,0:T(8,128)(2,1)S(1)} %all-to-all-done.1.refs_0_), channel_id=1, source_target_pairs={{0,7},{1,0},{2,1},{3,2},{4,3},{5,4},{6,5},{7,6},{8,15},{9,8},{10,9... | collective-permute-start | bytes 393224 | tf_op jit(solution)/shard_map/ppermute | solution.py:37
  26.3 10.9 %collective-permute-start.5 = (bf16[8,32,256]{2,1,0:T(8,128)(2,1)S(1)}, bf16[8,32,256]{2,1,0:T(8,128)(2,1)S(1)}, u32[]{:S(2)}, u32[]{:S(2)}) collective-permute-start(bf16[8,32,256]{2,1,0:T(8,128)(2,1)S(1)} %all-to-all-done.1.refs_0_), channel_id=1, source_target_pairs={{0,1},{1,2},{2,3},{3,4},{4,5},{5,6},{6,7},{7,0},{8,9},{9,10},{10,1... | collective-permute-start | bytes 393224 | tf_op jit(solution)/shard_map/ppermute | solution.py:37
  33.2 10.2 %collective-permute-start.4 = (bf16[8,32,256]{2,1,0:T(8,128)(2,1)S(1)}, bf16[8,32,256]{2,1,0:T(8,128)(2,1)S(1)}, u32[]{:S(2)}, u32[]{:S(2)}) collective-permute-start(bf16[8,32,256]{2,1,0:T(8,128)(2,1)S(1)} %collective-permute-done.refs_0_), channel_id=1, source_target_pairs={{0,2},{1,3},{2,4},{3,5},{4,6},{5,7},{6,0},{7,1},{8,10},{9,11},{10,... | collective-permute-start | bytes 393224 | tf_op jit(solution)/shard_map/ppermute | solution.py:37
  33.2 11.1 %collective-permute-start.2 = (bf16[8,32,256]{2,1,0:T(8,128)(2,1)S(1)}, bf16[8,32,256]{2,1,0:T(8,128)(2,1)S(1)}, u32[]{:S(2)}, u32[]{:S(2)}) collective-permute-start(bf16[8,32,256]{2,1,0:T(8,128)(2,1)S(1)} %collective-permute-done.refs_0_), channel_id=1, source_target_pairs={{0,1},{1,2},{2,3},{3,4},{4,5},{5,6},{6,7},{7,0},{8,9},{9,10},{10,1... | collective-permute-start | bytes 393224 | tf_op jit(solution)/shard_map/ppermute | solution.py:37
  34.5 8.9 %collective-permute-start.3 = (bf16[8,32,256]{2,1,0:T(8,128)(2,1)S(1)}, bf16[8,32,256]{2,1,0:T(8,128)(2,1)S(1)}, u32[]{:S(2)}, u32[]{:S(2)}) collective-permute-start(bf16[8,32,256]{2,1,0:T(8,128)(2,1)S(1)} %collective-permute-done.1.refs_1_), channel_id=1, source_target_pairs={{0,7},{1,0},{2,1},{3,2},{4,3},{5,4},{6,5},{7,6},{8,15},{9,8},{10,9... | collective-permute-start | bytes 393224 | tf_op jit(solution)/shard_map/ppermute | solution.py:37
  41.3 11.1 %collective-permute-start.7 = (bf16[8,32,256]{2,1,0:T(8,128)(2,1)S(1)}, bf16[8,32,256]{2,1,0:T(8,128)(2,1)S(1)}, u32[]{:S(2)}, u32[]{:S(2)}) collective-permute-start(bf16[8,32,256]{2,1,0:T(8,128)(2,1)S(1)} %get-tuple-element.38), channel_id=1, source_target_pairs={{0,7},{1,0},{2,1},{3,2},{4,3},{5,4},{6,5},{7,6},{8,15},{9,8},{10,9... | collective-permute-start | bytes 393224 | tf_op jit(solution)/shard_map/ppermute | solution.py:37
  43.4 9.0 %collective-permute-start.8 = (bf16[8,32,256]{2,1,0:T(8,128)(2,1)S(1)}, bf16[8,32,256]{2,1,0:T(8,128)(2,1)S(1)}, u32[]{:S(2)}, u32[]{:S(2)}) collective-permute-start(bf16[8,32,256]{2,1,0:T(8,128)(2,1)S(1)} %get-tuple-element.39), channel_id=1, source_target_pairs={{0,1},{1,2},{2,3},{3,4},{4,5},{5,6},{6,7},{7,0},{8,9},{9,10},{10,1... | collective-permute-start | bytes 393224 | tf_op jit(solution)/shard_map/ppermute | solution.py:37
  48.4 8.3 %collective-permute-start.9 = (bf16[8,32,256]{2,1,0:T(8,128)(2,1)S(1)}, bf16[8,32,256]{2,1,0:T(8,128)(2,1)S(1)}, u32[]{:S(2)}, u32[]{:S(2)}) collective-permute-start(bf16[8,32,256]{2,1,0:T(8,128)(2,1)S(1)} %get-tuple-element.46), channel_id=1, source_target_pairs={{0,7},{1,0},{2,1},{3,2},{4,3},{5,4},{6,5},{7,6},{8,15},{9,8},{10,9... | collective-permute-start | bytes 393224 | tf_op jit(solution)/shard_map/ppermute | solution.py:37
  50.9 7.7 %collective-permute-start.10 = (bf16[8,32,256]{2,1,0:T(8,128)(2,1)S(1)}, bf16[8,32,256]{2,1,0:T(8,128)(2,1)S(1)}, u32[]{:S(2)}, u32[]{:S(2)}) collective-permute-start(bf16[8,32,256]{2,1,0:T(8,128)(2,1)S(1)} %get-tuple-element.47), channel_id=1, source_target_pairs={{0,6},{1,7},{2,0},{3,1},{4,2},{5,3},{6,4},{7,5},{8,14},{9,15},{10,... | collective-permute-start | bytes 393224 | tf_op jit(solution)/shard_map/ppermute | solution.py:37
  50.9 11.2 %collective-permute-start.12 = (bf16[8,32,256]{2,1,0:T(8,128)(2,1)S(1)}, bf16[8,32,256]{2,1,0:T(8,128)(2,1)S(1)}, u32[]{:S(2)}, u32[]{:S(2)}) collective-permute-start(bf16[8,32,256]{2,1,0:T(8,128)(2,1)S(1)} %get-tuple-element.49), channel_id=1, source_target_pairs={{0,1},{1,2},{2,3},{3,4},{4,5},{5,6},{6,7},{7,0},{8,9},{9,10},{10,1... | collective-permute-start | bytes 393224 | tf_op jit(solution)/shard_map/ppermute | solution.py:37
  58.6 7.3 %collective-permute-start.11 = (bf16[8,32,256]{2,1,0:T(8,128)(2,1)S(1)}, bf16[8,32,256]{2,1,0:T(8,128)(2,1)S(1)}, u32[]{:S(2)}, u32[]{:S(2)}) collective-permute-start(bf16[8,32,256]{2,1,0:T(8,128)(2,1)S(1)} %shard_map.109), channel_id=1, source_target_pairs={{0,6},{1,7},{2,0},{3,1},{4,2},{5,3},{6,4},{7,5},{8,14},{9,15},{10,... | collective-permute-start | bytes 393224 | tf_op jit(solution)/shard_map/ppermute | solution.py:37
  62.1 7.2 %collective-permute-start.13 = (bf16[8,32,256]{2,1,0:T(8,128)(2,1)S(1)}, bf16[8,32,256]{2,1,0:T(8,128)(2,1)S(1)}, u32[]{:S(2)}, u32[]{:S(2)}) collective-permute-start(bf16[8,32,256]{2,1,0:T(8,128)(2,1)S(1)} %shard_map.110), channel_id=1, source_target_pairs={{0,2},{1,3},{2,4},{3,5},{4,6},{5,7},{6,0},{7,1},{8,10},{9,11},{10,... | collective-permute-start | bytes 393224 | tf_op jit(solution)/shard_map/ppermute | solution.py:37
  62.2 15.9 %all-to-all-start.2 = ((bf16[8,32,1024]{2,1,0:T(8,128)(2,1)}), bf16[8,32,1024]{2,1,0:T(8,128)(2,1)S(1)}, u32[]{:S(2)}, u32[]{:S(2)}) async-start(bf16[8,32,1024]{2,1,0:T(8,128)(2,1)} %get-tuple-element.41), calls=%async_computation.2 | async-start | bytes 1048576 | tf_op jit(solution)/shard_map/all_to_all | solution.py:41
  69.4 6.6 %collective-permute-start.14 = (bf16[8,1024]{1,0:T(8,128)(2,1)S(1)}, bf16[8,1024]{1,0:T(8,128)(2,1)S(1)}, u32[]{:S(2)}, u32[]{:S(2)}) collective-permute-start(bf16[8,1024]{1,0:T(8,128)(2,1)S(1)} %get-tuple-element.51), channel_id=1, source_target_pairs={{0,8},{8,16},{16,24},{24,32},{32,40},{40,48},{48,56},{56,0},{1,9},... | collective-permute-start | bytes 49160 | tf_op jit(solution)/shard_map/ppermute | solution.py:49
  71.9 4.7 %collective-permute-start.15 = (bf16[8,1024]{1,0:T(8,128)(2,1)S(1)}, bf16[8,1024]{1,0:T(8,128)(2,1)S(1)}, u32[]{:S(2)}, u32[]{:S(2)}) collective-permute-start(bf16[8,1024]{1,0:T(8,128)(2,1)S(1)} %get-tuple-element.52), channel_id=1, source_target_pairs={{0,16},{8,24},{16,32},{24,40},{32,48},{40,56},{48,0},{56,8},{1,17}... | collective-permute-start | bytes 49160 | tf_op jit(solution)/shard_map/ppermute | solution.py:49
  71.9 7.0 %collective-permute-start.16 = (bf16[8,1024]{1,0:T(8,128)(2,1)S(1)}, bf16[8,1024]{1,0:T(8,128)(2,1)S(1)}, u32[]{:S(2)}, u32[]{:S(2)}) collective-permute-start(bf16[8,1024]{1,0:T(8,128)(2,1)S(1)} %get-tuple-element.53), channel_id=1, source_target_pairs={{0,24},{8,32},{16,40},{24,48},{32,56},{40,0},{48,8},{56,16},{1,25}... | collective-permute-start | bytes 49160 | tf_op jit(solution)/shard_map/ppermute | solution.py:49
  72.8 6.1 %collective-permute-start.17 = (bf16[8,1024]{1,0:T(8,128)(2,1)S(1)}, bf16[8,1024]{1,0:T(8,128)(2,1)S(1)}, u32[]{:S(2)}, u32[]{:S(2)}) collective-permute-start(bf16[8,1024]{1,0:T(8,128)(2,1)S(1)} %get-tuple-element.54), channel_id=1, source_target_pairs={{0,32},{8,40},{16,48},{24,56},{32,0},{40,8},{48,16},{56,24},{1,33}... | collective-permute-start | bytes 49160 | tf_op jit(solution)/shard_map/ppermute | solution.py:49
  73.3 5.6 %collective-permute-start.18 = (bf16[8,1024]{1,0:T(8,128)(2,1)S(1)}, bf16[8,1024]{1,0:T(8,128)(2,1)S(1)}, u32[]{:S(2)}, u32[]{:S(2)}) collective-permute-start(bf16[8,1024]{1,0:T(8,128)(2,1)S(1)} %get-tuple-element.55), channel_id=1, source_target_pairs={{0,40},{8,48},{16,56},{24,0},{32,8},{40,16},{48,24},{56,32},{1,41}... | collective-permute-start | bytes 49160 | tf_op jit(solution)/shard_map/ppermute | solution.py:49
  76.0 3.0 %collective-permute-start.19 = (bf16[8,1024]{1,0:T(8,128)(2,1)S(1)}, bf16[8,1024]{1,0:T(8,128)(2,1)S(1)}, u32[]{:S(2)}, u32[]{:S(2)}) collective-permute-start(bf16[8,1024]{1,0:T(8,128)(2,1)S(1)} %get-tuple-element.56), channel_id=1, source_target_pairs={{0,48},{8,56},{16,0},{24,8},{32,16},{40,24},{48,32},{56,40},{1,49}... | collective-permute-start | bytes 49160 | tf_op jit(solution)/shard_map/ppermute | solution.py:49
  76.6 5.2 %collective-permute-start.20 = (bf16[8,1024]{1,0:T(8,128)(2,1)S(1)}, bf16[8,1024]{1,0:T(8,128)(2,1)S(1)}, u32[]{:S(2)}, u32[]{:S(2)}) collective-permute-start(bf16[8,1024]{1,0:T(8,128)(2,1)S(1)} %get-tuple-element.57), channel_id=1, source_target_pairs={{0,56},{8,0},{16,8},{24,16},{32,24},{40,32},{48,40},{56,48},{1,57}... | collective-permute-start | bytes 49160 | tf_op jit(solution)/shard_map/ppermute | solution.py:49
  (1 other events, 4.9 us)
